TPU v7x, 128 devices: a whole 4x4x4 slice. The times are simulated.
128 devices in a mesh: dp: 8 (over y, x_hi), fsdp: 16 (over z, x_lo, core).
Axes of the slice: x: 4 (x_hi: 2, x_lo: 2; x = x_hi * 2 + x_lo), y: 4, z: 4, core: 2. Of those that a mesh axis runs over, the one named last changes fastest.
Arguments:
- tokens: bfloat16 [49152, 8192], P(('dp', 'fsdp')), may hold values from -6 to 6
- frozen_value_weight: bfloat16 [8192, 1024], P('fsdp'), may hold values from -0.0625 to 0.0625
- adapter_down_weight: bfloat16 [32, 8192, 64], P('dp', 'fsdp'), may hold values from -0.0625 to 0.0625
- adapter_up_weight: bfloat16 [32, 64, 1024], P('dp', None, 'fsdp'), may hold values from -0.75 to 0.75
- output_gradient: bfloat16 [49152, 1024], P(('dp', 'fsdp')), may hold values from -6 to 6
- adapter_per_block: int32 [384], P(('dp', 'fsdp')), may hold values from 0 to 31, as said below
- block_live_count: int32 [384], P(('dp', 'fsdp')), may hold values from 1 to 128
Outputs:
- values: bfloat16 [49152, 1024], P(('dp', 'fsdp'))
- input_gradient: bfloat16 [49152, 8192], P(('dp', 'fsdp'))
- grad_down: float32 [32, 8192, 64], P('dp', 'fsdp')
- grad_up: float32 [32, 64, 1024], P('dp', None, 'fsdp')
Inputs may be any that keep to these rules, and one draw needn't show every extreme that they name: `adapter_per_block`: within the blocks of one device the adapter numbers never fall.
All inputs are finite; a program needn't handle non-finite values.
Results may differ from a plain program's by a relative error of at most 0.0038.
Values may be sent and summed in bfloat16 or wider, within the bound.
No kernel may reach another device: no remote copies, remote signals or barrier semaphores. Data moves between devices by JAX's collectives and lax.ppermute only.
A program may use at most 192 MiB of HBM per device.

v0:
```python
import jax
import jax.numpy as jnp
from jax import lax
from jax.sharding import PartitionSpec as P

adapter_scale = 0.5


def in_one_piece(arrays, axis, dim, along):
    ends, at = ([], 0)
    for a in arrays[:-1]:
        at += a.shape[along]
        ends.append(at)
    both = jnp.concatenate(arrays, axis=along)
    return tuple(jnp.split(lax.all_gather(both, axis, axis=dim, tiled=True), ends, axis=along))


def rows_first(arrays, axis, dims):
    turned = [jnp.moveaxis(a, dim, 0) for a, dim in zip(arrays, dims)]
    both = jnp.concatenate([t.reshape(len(t), -1) for t in turned], axis=1)
    result, at, outs = (lax.all_gather(both, axis, axis=0, tiled=True), 0, [])
    for t, dim in zip(turned, dims):
        piece = result[:, at : at + t[0].size].reshape(-1, *t.shape[1:])
        outs.append(jnp.moveaxis(piece, 0, dim))
        at += t[0].size
    return tuple(outs)


def cut_along(x, dim, devices):
    before, after = (x.shape[:dim], x.shape[dim + 1 :])
    return jnp.moveaxis(x.reshape(*before, devices, -1, *after), dim, 0)


def cut_rows(length, count):
    turn = length // count
    if turn >= 8:
        turn -= turn % 8
    return [turn * k for k in range(1, count)]


def in_order(parts, dim):
    parts = jnp.moveaxis(parts, 0, dim)
    dims = parts.shape
    return parts.reshape(*dims[:dim], dims[dim] * dims[dim + 1], *dims[dim + 2 :])


def several_exchanges(x, axis, pieces, split_dim, concat_dim):
    parts = cut_along(x, split_dim, lax.axis_size(axis))
    widest = max(range(1, max(2, parts.ndim - 1)), key=lambda d: parts.shape[d])
    outs = []
    for piece in jnp.split(parts, cut_rows(parts.shape[widest], pieces), axis=widest):
        if piece.size:
            outs.append(lax.all_to_all(piece, axis, split_axis=0, concat_axis=0, tiled=True))
    return in_order(jnp.concatenate(outs, axis=widest), concat_dim)


def in_one_piece_2(arrays, axis, dim, along):
    widths = [a.shape[along] for a in arrays]
    both = jnp.concatenate(arrays, axis=along)
    result = lax.psum_scatter(both, axis, scatter_dimension=dim, tiled=True)
    return tuple(jnp.split(result, [sum(widths[:k]) for k in range(1, len(widths))], axis=along))


def body(
    tokens,
    frozen_value_weight,
    adapter_down_weight,
    adapter_up_weight,
    output_gradient,
    adapter_per_block,
    block_live_count,
):
    count_dev = tokens.shape[0]
    per_dev = adapter_per_block.shape[0]
    block_rows = count_dev // per_dev
    adapter_list = adapter_down_weight.shape[0] * lax.axis_size("dp")
    piece = lax.all_gather(frozen_value_weight, "fsdp", axis=0, tiled=True)
    forward_pass = jnp.dot(tokens, piece, preferred_element_type=jnp.float32)
    portion_gradient = lax.dot_general(
        output_gradient, piece, (((1,), (1,)), ((), ())), preferred_element_type=jnp.float32
    )
    down_all, up_all = in_one_piece((adapter_down_weight, adapter_up_weight), "dp", 0, 1)
    ids_all, fill_all = rows_first((adapter_per_block, block_live_count), "fsdp", (0, 0))
    positions = jnp.arange(block_rows, dtype=jnp.int32)
    catalog = jnp.arange(adapter_list, dtype=jnp.int32)
    live_slot_mask = (positions[None, :] < fill_all[:, None]).astype(jnp.float32)[:, :, None]
    choose = (ids_all[:, None] == catalog[None, :]).astype(jnp.float32)
    down_per_block = down_all[ids_all]
    group_blocks = ids_all.shape[0]
    group_rows = group_blocks * block_rows
    x_group, dy_group = (
        lax.all_to_all(tokens, "fsdp", split_axis=1, concat_axis=0, tiled=True),
        lax.all_to_all(output_gradient, "fsdp", split_axis=1, concat_axis=0, tiled=True),
    )
    input_per_block = x_group.reshape(group_blocks, block_rows, -1)
    dy_blocks = dy_group.reshape(group_blocks, block_rows, -1)
    up_per_block = up_all[ids_all]
    down_partial = jnp.einsum(
        "gzq,gqx->gzx", input_per_block, down_per_block, preferred_element_type=jnp.float32
    )
    up_partial = jnp.einsum(
        "bkc,brc->bkr", dy_blocks, up_per_block, preferred_element_type=jnp.float32
    )
    down_total, up_total = lax.psum((down_partial, up_partial), "fsdp")
    reduced_down_output = (down_total * live_slot_mask).astype(jnp.bfloat16)
    reduced_output_gradient = (up_total * live_slot_mask).astype(jnp.bfloat16)
    raised_rows = (
        jnp.einsum(
            "bkr,brc->bkc", reduced_down_output, up_per_block, preferred_element_type=jnp.float32
        )
        .astype(jnp.bfloat16)
        .reshape(group_rows, -1)
    )
    spread_input = (
        jnp.einsum(
            "qjz,qaz->qja",
            reduced_output_gradient,
            down_per_block,
            preferred_element_type=jnp.float32,
        )
        .astype(jnp.bfloat16)
        .reshape(group_rows, -1)
    )
    raised_resident, input_resident = (
        several_exchanges(raised_rows, "fsdp", 2, 0, 1),
        several_exchanges(spread_input, "fsdp", 2, 0, 1),
    )
    up_terms = jnp.einsum(
        "bkr,bkc->brc", reduced_down_output, dy_blocks, preferred_element_type=jnp.float32
    )
    up_gradient = jnp.einsum("ba,brc->arc", choose, up_terms, precision=lax.Precision.HIGHEST)
    down_gradient_terms = jnp.einsum(
        "uia,uiw->uaw", input_per_block, reduced_output_gradient, preferred_element_type=jnp.float32
    )
    down_gradient = jnp.einsum(
        "ba,bdr->adr", choose, down_gradient_terms, precision=lax.Precision.HIGHEST
    )
    grad_down, grad_up = in_one_piece_2(
        (adapter_scale * down_gradient, adapter_scale * up_gradient), "dp", 0, 1
    )
    values = (forward_pass + adapter_scale * raised_resident.astype(jnp.float32)).astype(
        jnp.bfloat16
    )
    input_gradient = (portion_gradient + adapter_scale * input_resident.astype(jnp.float32)).astype(
        jnp.bfloat16
    )
    return (values, input_gradient, grad_down, grad_up)


def solution(mesh):
    placed = (
        P(("dp", "fsdp"), None),
        P("fsdp", None),
        P("dp", "fsdp", None),
        P("dp", None, "fsdp"),
        P(("dp", "fsdp"), None),
        P(("dp", "fsdp")),
        P(("dp", "fsdp")),
    )
    return jax.shard_map(
        body,
        mesh=mesh,
        in_specs=placed,
        out_specs=(
            P(("dp", "fsdp"), None),
            P(("dp", "fsdp"), None),
            P("dp", "fsdp", None),
            P("dp", None, "fsdp"),
        ),
        check_vma=False,
    )
```

profile of v0, /device:TPU:0, one launch (start us, length us, event | category | flops | bytes accessed | tf_op | source)
XLA Modules:
  0.0 558.1 jit_solution(6873364627100419224)
XLA Ops:
  7.2 2.3 copy.42
  9.5 6.4 %all-to-all-start.3 = ((bf16[384,16,64]{0,2,1:T(8,128)(2,1)}), bf16[384,16,64]{0,2,1:T(8,128)(2,1)S(1)}, u32[]{:S(2)}, u32[]{:S(2)}) async-start(bf16[384,16,64]{0,2,1:T(8,128)(2,1)} %bitcast.10), calls=%async_computation.3 | async-start | bytes 1572864 | tf_op jit(solution)/shard_map/all_to_all | solution.py:93
  15.9 6.2 %copy.68 = bf16[48,16,8,512]{3,2,0,1:T(8,128)(2,1)} copy(bf16[48,16,8,512]{3,2,1,0:T(8,128)(2,1)} %bitcast.57) | data formatting | bytes 12582912 | tf_op jit(solution)/shard_map/all_to_all | solution.py:92
  22.1 7.6 %all-to-all-done.3 = bf16[384,16,64]{0,2,1:T(8,128)(2,1)S(1)} async-done(((bf16[384,16,64]{0,2,1:T(8,128)(2,1)}), bf16[384,16,64]{0,2,1:T(8,128)(2,1)S(1)}, u32[]{:S(2)}, u32[]{:S(2)}) %all-to-all-start.3) | async-done | bytes 786464 | tf_op jit(solution)/shard_map/all_to_all | solution.py:93
  29.7 4.8 all-to-all-start
  35.5 99.5 %all-gather = s32[16,3,2]{1,2,0:T(2,128)S(1)} all-gather(s32[1,3,2]{1,2,0:T(2,128)S(1)} %add_bitcast_fusion), channel_id=1, replica_groups=mesh['dp'=8,'fsdp'=16] {'fsdp'}, dimensions={0}, use_global_device_ids=true | all-gather | bytes 408 | tf_op jit(solution)/shard_map/all_gather | solution.py:21
  141.2 2.3 gather_fusion
  143.6 3.0 convolution_bitcast_fusion.1
  146.5 6.2 %convolution_bitcast_fusion.2 = f32[48,128,64]{1,2,0:T(8,128)} fusion(bf16[48,512,64]{1,2,0:T(8,128)(2,1)S(1)} %gather_fusion, bf16[48,128,512]{2,1,0:T(8,128)(2,1)} %bitcast.5), kind=kOutput, calls=%fused_computation.16 | convolution fusion | flops 402653184 | bytes 11010048 | tf_op jit(solution)/shard_map/gzq,gqx->gzx/dot_general | solution.py:98
  153.0 129.5 %all-reduce.3.cloned.1.call-done = (f32[48,128,64]{1,2,0:T(8,128)}, f32[48,128,64]{1,2,0:T(8,128)}) async-done(((f32[48,128,64]{1,2,0:T(8,128)}, f32[48,128,64]{1,2,0:T(8,128)}), (f32[48,128,64]{1,2,0:T(8,128)}, f32[48,128,64]{1,2,0:T(8,128)})) %all-reduce.3.cloned.1.call-update) | async-done | bytes 3145744 | tf_op jit(solution)/shard_map/psum | solution.py:104
  282.5 3.3 fusion.5
  285.8 3.2 copy.54
  288.9 4.4 convolution_bitcast_fusion
  294.0 6.7 %fusion.2 = f32[32,512,64]{1,0,2:T(8,128)S(1)} fusion(f32[48,512,64]{1,2,0:T(8,128)S(1)} %convolution_bitcast_fusion, s32[48]{0:T(128)S(1)} %get-tuple-element.22), kind=kOutput, calls=%fused_computation.10 | convolution fusion | flops 605029888 | bytes 10485952 | tf_op jit(solution)/shard_map/ba,bdr->adr/dot_general | solution.py:135
  301.3 5.6 %copy.51 = f32[32,576,64]{1,2,0:T(8,128)} copy(f32[32,576,64]{1,0,2:T(8,128)S(1)} %pad_maximum_fusion) | data formatting | bytes 9437184 | tf_op jit(solution)/shard_map/concatenate | solution.py:59
  313.1 2.3 fusion.16
  316.3 4.3 all-to-all-start.1
  322.6 5.9 %convolution_convert_fusion = bf16[48,128,512]{2,1,0:T(8,128)(2,1)} fusion(bf16[48,512,64]{1,2,0:T(8,128)(2,1)S(1)} %gather_fusion, f32[48,128,64]{1,2,0:T(8,128)} %get-tuple-element.17, f32[48,128]{1,0:T(8,128)S(1)} %fusion.8), kind=kOutput, calls=%fused_computation.8 | convolution fusion | flops 406585344 | bytes 11034624 | tf_op jit(solution)/shard_map/qjz,qaz->qja/dot_general | solution.py:115
  328.5 4.2 all-to-all-done.1
  332.7 3.6 all-to-all-start.2
  336.3 6.5 %fusion.15 = (bf16[16,192,512]{2,1,0:T(8,128)(2,1)}, bf16[16,192,512]{2,1,0:T(8,128)(2,1)}) fusion(bf16[16,384,512]{2,1,0:T(8,128)(2,1)} %bitcast.55), kind=kLoop, calls=%fused_computation.35 | loop fusion | bytes 12582912 | tf_op jit(solution)/shard_map/split | solution.py:51
  342.8 7.3 %all-to-all-done.2 = bf16[16,192,64]{1,2,0:T(8,128)(2,1)S(1)} async-done(((bf16[16,192,64]{1,2,0:T(8,128)(2,1)}), bf16[16,192,64]{1,2,0:T(8,128)(2,1)S(1)}, u32[]{:S(2)}, u32[]{:S(2)}) %all-to-all-start.2) | async-done | bytes 393248 | tf_op jit(solution)/shard_map/all_to_all | solution.py:53
  350.9 49.4 %all_to_all.52 = bf16[16,192,512]{2,1,0:T(8,128)(2,1)S(1)} all-to-all(bf16[16,192,512]{2,1,0:T(8,128)(2,1)} %get-tuple-element.18), channel_id=1, replica_groups=mesh['dp'=8,'fsdp'=16] {'fsdp'}, dimensions={0} | all-to-all | bytes 6291456 | tf_op jit(solution)/shard_map/all_to_all | solution.py:53
  400.4 4.5 all-to-all-start.5
  404.9 2.7 convert_multiply_fusion
  407.5 3.0 copy.41
  410.6 42.6 %all-to-all-done.5 = bf16[16,192,512]{2,1,0:T(8,128)(2,1)} async-done(((bf16[16,192,512]{2,1,0:T(8,128)(2,1)}), bf16[16,192,512]{2,1,0:T(8,128)(2,1)}, u32[]{:S(2)}, u32[]{:S(2)}) %all-to-all-start.5) | async-done | bytes 3145760 | tf_op jit(solution)/shard_map/all_to_all | solution.py:53
  453.2 8.2 %multiply_bitcast_fusion = f32[16,48,8,512]{3,2,1,0:T(8,128)} fusion(bf16[16,192,512]{2,1,0:T(8,128)(2,1)} %all-to-all-done.5, bf16[16,192,512]{2,1,0:T(8,128)(2,1)S(1)} %all_to_all.52), kind=kLoop, calls=%fused_computation.3 | loop fusion | flops 15728640 | bytes 18874368
  461.4 11.7 %copy.58 = f32[16,48,8,512]{3,2,0,1:T(8,128)} copy(f32[16,48,8,512]{3,2,1,0:T(8,128)} %multiply_bitcast_fusion) | data formatting | bytes 25165824 | tf_op jit(solution)/shard_map/mul | solution.py:144
  476.7 47.6 %all-gather.4.cloned.1.call-done = bf16[8192,1024]{1,0:T(8,128)(2,1)} async-done(((bf16[512,1024]{1,0:T(8,128)(2,1)}), bf16[8192,1024]{1,0:T(8,128)(2,1)}) %all-gather.4.cloned.1.call-update) | async-done | bytes 16777232 | tf_op jit(solution)/shard_map/all_gather | solution.py:77
  524.3 12.8 %add_convert_fusion.1 = bf16[384,1024]{1,0:T(8,128)(2,1)} fusion(f32[384,1024]{1,0:T(8,128)S(1)} %copy-done.3, bf16[384,8192]{1,0:T(8,128)(2,1)} %param.7, bf16[8192,1024]{1,0:T(8,128)(2,1)} %all-gather.4.cloned.1.call-done), kind=kOutput, calls=%fused_computation.12 | convolution fusion | flops 6443237376 | bytes 25427968 | tf_op jit(solution)/shard_map/dot_general | solution.py:78
  537.1 14.5 %add_convert_fusion = bf16[384,8192]{1,0:T(8,128)(2,1)} fusion(f32[384,8192]{1,0:T(8,128)} %bitcast.56, bf16[384,1024]{1,0:T(8,128)(2,1)S(1)} %copy-done.4, bf16[8192,1024]{1,0:T(8,128)(2,1)} %all-gather.4.cloned.1.call-done), kind=kOutput, calls=%fused_computation.2 | convolution fusion | flops 6448742400 | bytes 36438016 | tf_op jit(solution)/shard_map/dot_general | solution.py:79
  (52 shorter events, 22.3 us)
Async XLA Ops:
  9.5 20.2 %all-to-all-start.3 = ((bf16[384,16,64]{0,2,1:T(8,128)(2,1)}), bf16[384,16,64]{0,2,1:T(8,128)(2,1)S(1)}, u32[]{:S(2)}, u32[]{:S(2)}) async-start(bf16[384,16,64]{0,2,1:T(8,128)(2,1)} %bitcast.10), calls=%async_computation.3 | async-start | bytes 1572864 | tf_op jit(solution)/shard_map/all_to_all | solution.py:93
  29.6 4.9 copy-start.6
  29.6 5.0 copy-start.5
  29.6 5.8 %copy-start.7 = (s32[3]{0:T(128)S(1)}, s32[3]{0:T(128)}, u32[]{:S(2)}) copy-start(s32[3]{0:T(128)} %param.13) | copy-start | bytes 40
  29.7 5.8 %copy-start.8 = (s32[3]{0:T(128)S(1)}, s32[3]{0:T(128)}, u32[]{:S(2)}) copy-start(s32[3]{0:T(128)} %param.12) | copy-start | bytes 40
  29.7 116.9 %all-to-all-start = ((bf16[384,16,512]{2,0,1:T(8,128)(2,1)}), bf16[384,16,512]{2,0,1:T(8,128)(2,1)}, u32[]{:S(2)}, u32[]{:S(2)}) async-start(bf16[384,16,512]{2,0,1:T(8,128)(2,1)} %bitcast.54), calls=%async_computation | async-start | bytes 12582912 | tf_op jit(solution)/shard_map/all_to_all | solution.py:92
  34.5 102.4 %all-gather.6.cloned.1.call-start = ((), (), s32[]{:S(2)}) async-start(), calls=%async_computation.8 | async-start | bytes 2949120 | tf_op jit(solution)/shard_map/all_gather | solution.py:15
  35.4 247.0 %all-reduce.3.cloned.1.call-start = ((), (), s32[]{:S(2)}) async-start(), calls=%async_computation.10 | async-start | bytes 6291456 | tf_op jit(solution)/shard_map/psum | solution.py:104
  136.8 2.8 copy-start.1
  152.7 320.4 %reduce-scatter.2.cloned.1.call-start = ((), (), s32[]{:S(2)}) async-start(), calls=%async_computation.9 | async-start | bytes 5898240 | tf_op jit(solution)/shard_map/reduce_scatter | solution.py:60
  288.9 4.4 copy-start
  307.0 217.3 %all-gather.4.cloned.1.call-start = ((), (), s32[]{:S(2)}) async-start(), calls=%async_computation.7 | async-start | bytes 17825792 | tf_op jit(solution)/shard_map/all_gather | solution.py:77
  316.3 16.4 %all-to-all-start.1 = ((bf16[16,192,64]{1,2,0:T(8,128)(2,1)}), bf16[16,192,64]{1,2,0:T(8,128)(2,1)}, u32[]{:S(2)}, u32[]{:S(2)}) async-start(bf16[16,192,64]{1,2,0:T(8,128)(2,1)} %copy.39), calls=%async_computation.1 | async-start | bytes 1048576 | tf_op jit(solution)/shard_map/all_to_all | solution.py:53
  332.7 17.4 %all-to-all-start.2 = ((bf16[16,192,64]{1,2,0:T(8,128)(2,1)}), bf16[16,192,64]{1,2,0:T(8,128)(2,1)S(1)}, u32[]{:S(2)}, u32[]{:S(2)}) async-start(bf16[16,192,64]{1,2,0:T(8,128)(2,1)} %copy.40), calls=%async_computation.2 | async-start | bytes 1048576 | tf_op jit(solution)/shard_map/all_to_all | solution.py:53
  350.1 0.8 copy-start.2
  400.4 52.8 %all-to-all-start.5 = ((bf16[16,192,512]{2,1,0:T(8,128)(2,1)}), bf16[16,192,512]{2,1,0:T(8,128)(2,1)}, u32[]{:S(2)}, u32[]{:S(2)}) async-start(bf16[16,192,512]{2,1,0:T(8,128)(2,1)} %get-tuple-element.19), calls=%async_computation.5 | async-start | bytes 6291456 | tf_op jit(solution)/shard_map/all_to_all | solution.py:53
  461.4 62.9 %copy-start.3 = (f32[384,1024]{1,0:T(8,128)S(1)}, f32[384,1024]{1,0:T(8,128)}, u32[]{:S(2)}) copy-start(f32[384,1024]{1,0:T(8,128)} %copy.41) | copy-start | bytes 4718596
  476.7 60.4 %copy-start.4 = (bf16[384,1024]{1,0:T(8,128)(2,1)S(1)}, bf16[384,1024]{1,0:T(8,128)(2,1)}, u32[]{:S(2)}) copy-start(bf16[384,1024]{1,0:T(8,128)(2,1)} %param.11) | copy-start | bytes 2359300
Sparse Core Ops, SparseCore 0:
  38.2 77.5 all-gather.5
  152.8 129.5 all-reduce.2
  307.1 116.4 reduce-scatter.1
  425.2 99.0 all-gather.3
where the time goes:
time: 560 us; the launch traced here: 558 us
  waiting for transfers between devices  239 us (43%)
  blocking collectives  149 us (27%)
  local copies, waits for them, and re-layouts  60.3 us (11%)
  matrix products  59.4 us (11%)
  starting transfers between devices  23.9 us (4%)
  between operations  13.9 us (2%)
  other arithmetic  12.3 us (2%)
    psum x1, waiting for transfers between devices, body(): down_total, up_total = lax.psum((down_partial, up_partial), 'fsdp')  129 us
    all_gather x1, blocking collectives, rows_first(): result, at, outs = (lax.all_gather(both, axis, axis=0, tiled=True), 0, [])  99.5 us
    all_to_all x3, waiting for transfers between devices, several_exchanges(): lax.all_to_all(piece, axis, split_axis=0, concat_axis=0, tiled=True)  54.1 us
    all_to_all x1, blocking collectives, several_exchanges(): lax.all_to_all(piece, axis, split_axis=0, concat_axis=0, tiled=True)  49.4 us
    all_gather x1, waiting for transfers between devices, body(): piece = lax.all_gather(frozen_value_weight, 'fsdp', axis=0, tiled=True)  47.6 us
    dot_general x1, matrix products, body(): lax.dot_general(output_gradient, piece, (((1,), (1,)), ((), ())), preferr...  14.5 us
    dot_general x1, matrix products, body(): forward_pass = jnp.dot(tokens, piece, preferred_element_type=jnp.float32)  12.8 us
    all_to_all x3, starting transfers between devices, several_exchanges(): lax.all_to_all(piece, axis, split_axis=0, concat_axis=0, tiled=True)  12.3 us
  transfers between devices with their start and end apart: 9, of which 6 were waited for; matrix products, arithmetic and copies ran while one was open for 13% of the time, Pallas kernels for 0%

commit v1 on v0

v1 whole, which is shorter than its diff:
```python
import functools

import jax
import jax.numpy as jnp
from jax import lax
from jax.experimental import pallas as pl
from jax.experimental.pallas import tpu as pltpu
from jax.sharding import Mesh
from jax.sharding import PartitionSpec as P

DP = ("y", "xh")
FSDP = ("z", "xl", "c")
X = ("xh", "xl")
SCALE = 0.5
F32 = jnp.float32
BF16 = jnp.bfloat16


def nt(a, b):
    return lax.dot_general(a, b, (((1,), (1,)), ((), ())), preferred_element_type=F32)


def tn(a, b):
    return lax.dot_general(a, b, (((0,), (0,)), ((), ())), preferred_element_type=F32)


def nn(a, b):
    return jnp.dot(a, b, preferred_element_type=F32)


def shift(x, axis, by):
    return lax.ppermute(x, axis, [(i, (i + by) % 4) for i in range(4)])


def ring(x, axis):
    one, three = shift(x, axis, 1), shift(x, axis, -1)
    half = x.shape[0] // 2
    two = jnp.concatenate([shift(one[:half], axis, 1), shift(three[half:], axis, -1)], axis=0)
    return jnp.stack([x, one, two, three])


def ring_small(x, axis):
    return jnp.stack([x, shift(x, axis, 1), shift(x, axis, 2), shift(x, axis, -1)])


def live_rows(fill_ref, b, rows):
    return (lax.broadcasted_iota(jnp.int32, (rows, 1), 0) < fill_ref[b]).astype(F32)


def low_v_kernel(blocks, fill_ref, x_ref, dy_ref, up_ref, v_ref, g_ref):
    rows = dy_ref.shape[0] // blocks

    @pl.when(pl.program_id(0) == 0)
    def _():
        for b in range(blocks):
            at = pl.ds(b * rows, rows)
            up = up_ref[:, :, b].reshape(-1, up_ref.shape[-1])
            v = nn(dy_ref[at, :], up) * live_rows(fill_ref, b, rows)
            v_ref[at, :] = v.astype(BF16)

    for b in range(blocks):
        at = pl.ds(b * rows, rows)
        g_ref[0, b] = tn(v_ref[at, :], x_ref[at, :]).astype(BF16)


def low_u_kernel(blocks, steps, fill_ref, x_ref, dy_ref, down_ref, u_ref, g_ref, acc_ref):
    rows = dy_ref.shape[0] // blocks
    f = pl.program_id(0)

    @pl.when(f == 0)
    def _():
        acc_ref[...] = jnp.zeros_like(acc_ref)

    for b in range(blocks):
        at = pl.ds(b * rows, rows)
        acc_ref[at, :] += nt(x_ref[at, :], down_ref[0, 0, b])

    @pl.when(f == steps - 1)
    def _():
        for b in range(blocks):
            at = pl.ds(b * rows, rows)
            u = (acc_ref[at, :] * live_rows(fill_ref, b, rows)).astype(BF16)
            u_ref[at, :] = u
            g = tn(dy_ref[at, :], u).astype(BF16)
            g_ref[:, b] = g.reshape(g_ref.shape[0], g_ref.shape[2], g_ref.shape[3])


def base_kernel(blocks, steps, x_ref, dy_ref, w_ref, u_ref, v_ref, up_ref, down_ref, y_ref, dx_ref, acc_ref):
    rows = dy_ref.shape[0] // blocks
    f = pl.program_id(0)

    @pl.when(f == 0)
    def _():
        acc_ref[...] = jnp.zeros_like(acc_ref)

    acc_ref[...] += nn(x_ref[...], w_ref[...])
    wide = nt(dy_ref[...], w_ref[...])
    for b in range(blocks):
        at = pl.ds(b * rows, rows)
        pulled = nn(v_ref[at, :], down_ref[0, 0, b]).astype(BF16).astype(F32)
        dx_ref[at, :] = (wide[b * rows : (b + 1) * rows, :] + SCALE * pulled).astype(BF16)

    @pl.when(f == steps - 1)
    def _():
        for b in range(blocks):
            at = pl.ds(b * rows, rows)
            up = up_ref[:, :, b].reshape(-1, up_ref.shape[-1])
            lifted = nt(u_ref[at, :], up).astype(BF16).astype(F32)
            y_ref[at, :] = (acc_ref[at, :] + SCALE * lifted).astype(BF16)


def sum_kernel(members, blocks, ids_ref, g_ref, h_ref, go_ref, ho_ref, gacc_ref, hacc_ref):
    gacc_ref[...] = jnp.zeros_like(gacc_ref)
    hacc_ref[...] = jnp.zeros_like(hacc_ref)

    @pl.loop(0, members)
    def _(m):
        for b in range(blocks):
            a = ids_ref[m, b]
            gacc_ref[a] += g_ref[m, b].astype(F32)
            hacc_ref[a] += h_ref[m, b].astype(F32)

    go_ref[...] = gacc_ref[...].astype(BF16)
    ho_ref[...] = hacc_ref[...].astype(BF16)


PARAMS = pltpu.CompilerParams(vmem_limit_bytes=48 * 1024 * 1024)
VMEM = pl.BlockSpec(memory_space=pltpu.VMEM)


def whole(shape):
    zeros = (0,) * len(shape)
    return pl.BlockSpec(shape, lambda f, *_: zeros)


def body(tokens, weight, down, up, dy, ids, fill):
    rows_dev, width = tokens.shape
    value = dy.shape[1]
    blocks = ids.shape[0]
    slots, feats, rank = down.shape
    cols = up.shape[2]
    zs, xls, cs = (lax.axis_size(a) for a in FSDP)
    steps = zs * xls * cs
    adapters = slots * lax.axis_size(DP)
    x_at, y_at, xl_at = lax.axis_index(X), lax.axis_index("y"), lax.axis_index("xl")

    w_full = lax.all_gather(weight, FSDP, axis=0, tiled=True)

    ids_out = jnp.broadcast_to(jnp.pad(ids, (0, 128 - blocks)), (steps, 8, 128))
    ids_all = lax.all_to_all(ids_out, FSDP, split_axis=0, concat_axis=0, tiled=True)[:, 0, :blocks]

    up_t = jnp.swapaxes(up, 1, 2)
    up_plane = ring_small(ring_small(up_t, X), "y")
    down_t = jnp.swapaxes(down, 1, 2)
    half = slots // 2
    first = ring(jnp.moveaxis(ring_small(down_t[:half], X), 0, 0), "y")
    second = ring(ring_small(down_t[half:], "y"), X)

    mine = lax.dynamic_index_in_dim(ids_all.reshape(zs, xls, cs, blocks), xl_at, 1, keepdims=False)
    want = mine.reshape(zs * cs, 1, blocks)
    owner, slot = want // slots, want % slots
    xl_src = jnp.arange(xls, dtype=jnp.int32)[None, :, None]
    oy = (y_at - owner // 2) % 4
    ox = (x_at - (2 * (owner % 2) + xl_src)) % 4
    up_pick = up_plane.reshape(-1, cols, rank)[(oy * 4 + ox) * slots + slot]
    up_recv = lax.all_to_all(up_pick, ("z", "c"), split_axis=0, concat_axis=0, tiled=True)
    both = jnp.concatenate([first.reshape(-1, rank, feats), second.reshape(-1, rank, feats)], axis=0)
    in_first = (oy * 4 + ox) * half + slot
    in_second = first.shape[0] * first.shape[1] * half + (ox * 4 + oy) * half + slot - half
    down_pick = both[jnp.where(slot < half, in_first, in_second)]
    down_recv = lax.all_to_all(down_pick, ("z", "c"), split_axis=0, concat_axis=0, tiled=True)

    def down_at(f, *_):
        return (f // (xls * cs) * cs + f % cs, f // cs % xls, 0, 0, 0)

    up_mine = jnp.swapaxes(up_recv.reshape(zs, cs, xls, blocks, cols, rank), 1, 2)
    up_mine = up_mine.reshape(1, steps, blocks, cols, rank)

    smem = pl.BlockSpec(memory_space=pltpu.SMEM)
    x_spec = pl.BlockSpec((rows_dev, feats), lambda f, *_: (0, f))
    down_spec = pl.BlockSpec((1, 1, blocks, rank, feats), down_at)
    low_v, grad_d = pl.pallas_call(
        functools.partial(low_v_kernel, blocks),
        grid=(steps,),
        in_specs=[smem, x_spec, whole(dy.shape), whole(up_mine.shape)],
        out_specs=[whole((rows_dev, rank)), pl.BlockSpec((1, blocks, rank, feats), lambda f: (f, 0, 0, 0))],
        out_shape=[
            jax.ShapeDtypeStruct((rows_dev, rank), BF16),
            jax.ShapeDtypeStruct((steps, blocks, rank, feats), BF16),
        ],
        compiler_params=PARAMS,
        name="low_v",
    )(fill, tokens, dy, up_mine)
    grad_d = lax.all_to_all(grad_d, FSDP, split_axis=0, concat_axis=0, tiled=True)

    low_u, grad_u = pl.pallas_call(
        functools.partial(low_u_kernel, blocks, steps),
        grid=(steps,),
        in_specs=[smem, x_spec, whole(dy.shape), down_spec],
        out_specs=[whole((rows_dev, rank)), whole((steps, blocks, cols, rank))],
        out_shape=[
            jax.ShapeDtypeStruct((rows_dev, rank), BF16),
            jax.ShapeDtypeStruct((steps, blocks, cols, rank), BF16),
        ],
        scratch_shapes=[pltpu.VMEM((rows_dev, rank), F32)],
        compiler_params=PARAMS,
        name="low_u",
    )(fill, tokens, dy, down_recv)
    grad_u = lax.all_to_all(grad_u, FSDP, split_axis=0, concat_axis=0, tiled=True)

    sum_d, sum_u = pl.pallas_call(
        functools.partial(sum_kernel, steps, blocks),
        in_specs=[smem, VMEM, VMEM],
        out_specs=[VMEM, VMEM],
        out_shape=[
            jax.ShapeDtypeStruct((adapters, rank, feats), BF16),
            jax.ShapeDtypeStruct((adapters, cols, rank), BF16),
        ],
        scratch_shapes=[pltpu.VMEM((adapters, rank, feats), F32), pltpu.VMEM((adapters, cols, rank), F32)],
        compiler_params=PARAMS,
        name="sum_blocks",
    )(ids_all, grad_d, grad_u)
    part_d = lax.all_to_all(sum_d, DP, split_axis=0, concat_axis=0, tiled=True)
    part_u = lax.all_to_all(sum_u, DP, split_axis=0, concat_axis=0, tiled=True)

    values, input_gradient = pl.pallas_call(
        functools.partial(base_kernel, blocks, steps),
        grid=(steps,),
        in_specs=[
            x_spec,
            whole(dy.shape),
            pl.BlockSpec((feats, value), lambda f: (f, 0)),
            whole(low_u.shape),
            whole(low_v.shape),
            whole(up_mine.shape),
            down_spec,
        ],
        out_specs=[whole((rows_dev, value)), pl.BlockSpec((rows_dev, feats), lambda f: (0, f))],
        out_shape=[
            jax.ShapeDtypeStruct((rows_dev, value), BF16),
            jax.ShapeDtypeStruct((rows_dev, width), BF16),
        ],
        scratch_shapes=[pltpu.VMEM((rows_dev, value), F32)],
        compiler_params=PARAMS,
        name="base",
    )(tokens, dy, w_full, low_u, low_v, up_mine, down_recv)

    grad_down = SCALE * part_d.reshape(-1, slots, rank, feats).astype(F32).sum(0)
    grad_up = SCALE * part_u.reshape(-1, slots, cols, rank).astype(F32).sum(0)
    return values, input_gradient, jnp.swapaxes(grad_down, 1, 2), jnp.swapaxes(grad_up, 1, 2)


def solution(mesh):
    fine = Mesh(mesh.devices.reshape(4, 2, 4, 2, 2), DP + FSDP)
    every = DP + FSDP
    placed = (
        P(every, None),
        P(FSDP, None),
        P(DP, FSDP, None),
        P(DP, None, FSDP),
        P(every, None),
        P(every),
        P(every),
    )
    return jax.shard_map(
        body,
        mesh=fine,
        in_specs=placed,
        out_specs=(P(every, None), P(every, None), P(DP, FSDP, None), P(DP, None, FSDP)),
        check_vma=False,
    )
```

time: 560 us -> 327 us (0.58)
  blocking collectives: 149 us -> 15.1 us
  waiting for transfers between devices: 239 us -> 127 us
  matrix products: 59.4 us -> 0 us
  Pallas kernels: 0 us -> 48.9 us
  starting transfers between devices: 23.9 us -> 63.6 us
  local copies, waits for them, and re-layouts: 60.3 us -> 42.1 us
    psum x1 -> x0, waiting for transfers between devices: 129 us -> none  [body(): down_total, up_total = lax.psum((down_partial, up_partial), 'fsdp')]
    all_gather x1 -> x0, blocking collectives: 99.5 us -> none  [rows_first(): result, at, outs = (lax.all_gather(both, axis, axis=0, tiled=True), 0, [])]
    dot_general x10 -> x0, matrix products: 59.4 us -> none  [the longest x1 14.5 us: body(): lax.dot_general(output_gradient, piece, (((1,), (1,)), ((), ())), preferr...]
    pallas_call x0 -> x4, Pallas kernels: none -> 48.9 us  [the longest x1 23.7 us: body(): pl.pallas_call(functools.partial(base_kernel, blocks, steps), grid=(steps...]
    all_gather x2 -> x1, waiting for transfers between devices: 47.6 us -> 0.01 us  [body(): w_full = lax.all_gather(weight, FSDP, axis=0, tiled=True)]
    ppermute x0 -> x20, waiting for transfers between devices: none -> 47.2 us  [shift(): return lax.ppermute(x, axis, [(i, (i + by) % 4) for i in range(4)])]
    all_to_all x1, blocking collectives: 49.4 us -> 15.1 us  [body(): part_u = lax.all_to_all(sum_u, DP, split_axis=0, concat_axis=0, tiled=True)]
    ppermute x0 -> x20, starting transfers between devices: none -> 33.3 us  [shift(): return lax.ppermute(x, axis, [(i, (i + by) % 4) for i in range(4)])]
  transfers between devices with their start and end apart: 9 -> 27, of which waited for: 6 -> 14; matrix products, arithmetic and copies ran while one was open for 13% -> 14% of each run, Pallas kernels for 0% -> 8%
where the time goes in v1:
time: 327 us; the launch traced here: 325 us
  waiting for transfers between devices  127 us (39%)
  starting transfers between devices  63.6 us (19%)
  Pallas kernels  48.9 us (15%)
  local copies, waits for them, and re-layouts  42.1 us (13%)
  blocking collectives  15.1 us (5%)
  between operations  14.3 us (4%)
  other arithmetic  14 us (4%)
    ppermute x20, waiting for transfers between devices, shift(): return lax.ppermute(x, axis, [(i, (i + by) % 4) for i in range(4)])  47.2 us
    all_to_all x1, waiting for transfers between devices, body(): lax.all_to_all(grad_d, FSDP, split_axis=0, concat_axis=0, tiled=True)  36.4 us
    ppermute x20, starting transfers between devices, shift(): return lax.ppermute(x, axis, [(i, (i + by) % 4) for i in range(4)])  33.3 us
    unnamed x31, local copies, waits for them, and re-layouts  25.9 us
    pallas_call x1, Pallas kernels, body(): pl.pallas_call(functools.partial(base_kernel, blocks, steps), grid=(steps...  23.7 us
    all_to_all x1, waiting for transfers between devices, body(): part_d = lax.all_to_all(sum_d, DP, split_axis=0, concat_axis=0, tiled=True)  23 us
    all_to_all x1, waiting for transfers between devices, body(): lax.all_to_all(down_pick, ('z', 'c'), split_axis=0, concat_axis=0, tiled=...  18.6 us
    all_to_all x1, blocking collectives, body(): part_u = lax.all_to_all(sum_u, DP, split_axis=0, concat_axis=0, tiled=True)  15.1 us
  transfers between devices with their start and end apart: 27, of which 14 were waited for; matrix products, arithmetic and copies ran while one was open for 14% of the time, Pallas kernels for 8%

profile of v1, /device:TPU:0, one launch (start us, length us, event | category | flops | bytes accessed | tf_op | source)
XLA Modules:
  0.0 324.9 jit_solution(8125717372450816850)
XLA Ops:
  10.6 2.7 collective-permute-start.1
  16.0 5.4 %all-to-all-start = ((s32[16,8,128]{2,1,0:T(8,128)}), s32[16,8,128]{2,1,0:T(8,128)S(1)}, u32[]{:S(2)}, u32[]{:S(2)}) async-start(s32[16,8,128]{2,1,0:T(8,128)} %broadcast_in_dim.14), calls=%async_computation | async-start | bytes 131072 | tf_op jit(solution)/shard_map/all_to_all | solution.py:150
  23.1 2.9 collective-permute-start.8
  36.9 7.5 %collective-permute-done.3 = bf16[4,2,64,512]{3,2,1,0:T(8,128)(2,1)S(1)} collective-permute-done((bf16[4,2,64,512]{3,2,1,0:T(8,128)(2,1)}, bf16[4,2,64,512]{3,2,1,0:T(8,128)(2,1)S(1)}, u32[]{:S(2)}, u32[]{:S(2)}) %collective-permute-start.3) | collective-permute-done | bytes 524320 | tf_op jit(solution)/shard_map/ppermute | solution.py:32
  45.2 3.2 collective-permute-start.6
  48.4 10.0 %collective-permute-done.10 = bf16[4,2,64,512]{3,2,1,0:T(8,128)(2,1)S(1)} collective-permute-done((bf16[4,2,64,512]{3,2,1,0:T(8,128)(2,1)}, bf16[4,2,64,512]{3,2,1,0:T(8,128)(2,1)S(1)}, u32[]{:S(2)}, u32[]{:S(2)}) %collective-permute-start.10) | collective-permute-done | bytes 524320 | tf_op jit(solution)/shard_map/ppermute | solution.py:32
  64.3 8.9 %collective-permute-done.11 = bf16[2,2,64,512]{3,2,1,0:T(8,128)(2,1)} collective-permute-done((bf16[2,2,64,512]{3,2,1,0:T(8,128)(2,1)}, bf16[2,2,64,512]{3,2,1,0:T(8,128)(2,1)}, u32[]{:S(2)}, u32[]{:S(2)}) %collective-permute-start.11) | collective-permute-done | bytes 262176 | tf_op jit(solution)/shard_map/ppermute | solution.py:32
  73.3 3.1 collective-permute-done.13
  80.4 4.8 %gather_fusion = bf16[48,64,512]{2,1,0:T(8,128)(2,1)} fusion(bf16[64,64,512]{2,1,0:T(8,128)(2,1)} %pad_maximum_fusion, s32[1024]{0:T(1024)S(1)} %pad_clamp_fusion.1), kind=kCustom, calls=%fused_computation | custom fusion | bytes 6291648 | tf_op jit(solution)/shard_map/gather | solution.py:170
  85.2 4.4 %all-to-all-start.1 = ((bf16[8,2,3,64,512]{4,3,2,1,0:T(8,128)(2,1)}), bf16[8,2,3,64,512]{4,3,2,1,0:T(8,128)(2,1)S(1)}, u32[]{:S(2)}, u32[]{:S(2)}) async-start(bf16[8,2,3,64,512]{4,3,2,1,0:T(8,128)(2,1)} %bitcast.61), calls=%async_computation.1 | async-start | bytes 6291456 | tf_op jit(solution)/shard_map/all_to_all | solution.py:171
  90.5 2.5 collective-permute-start.16
  93.0 3.0 collective-permute-done.14
  97.5 3.1 collective-permute-done.16
  106.6 5.4 %collective-permute-done.17 = bf16[4,4,64,64]{2,3,1,0:T(8,128)(2,1)} collective-permute-done((bf16[4,4,64,64]{2,3,1,0:T(8,128)(2,1)}, bf16[4,4,64,64]{2,3,1,0:T(8,128)(2,1)}, u32[]{:S(2)}, u32[]{:S(2)}) %collective-permute-start.17) | collective-permute-done | bytes 131104 | tf_op jit(solution)/shard_map/ppermute | solution.py:32
  112.0 4.2 %collective-permute-done.18 = bf16[4,4,64,64]{2,3,1,0:T(8,128)(2,1)} collective-permute-done((bf16[4,4,64,64]{2,3,1,0:T(8,128)(2,1)}, bf16[4,4,64,64]{2,3,1,0:T(8,128)(2,1)}, u32[]{:S(2)}, u32[]{:S(2)}) %collective-permute-start.18) | collective-permute-done | bytes 131104 | tf_op jit(solution)/shard_map/ppermute | solution.py:32
  121.4 2.8 gather_fusion.1
  124.2 2.7 reshape.354
  126.9 18.6 %all-to-all-done.1.down_ref = bf16[8,2,3,64,512]{4,3,2,1,0:T(8,128)(2,1)S(1)} async-done(((bf16[8,2,3,64,512]{4,3,2,1,0:T(8,128)(2,1)}), bf16[8,2,3,64,512]{4,3,2,1,0:T(8,128)(2,1)S(1)}, u32[]{:S(2)}, u32[]{:S(2)}) %all-to-all-start.1) | async-done | bytes 3145760 | tf_op jit(solution)/shard_map/all_to_all | solution.py:171
  145.5 5.4 %all-to-all-start.2 = ((bf16[8,2,12288]{2,1,0:T(2,128)(2,1)}), bf16[8,2,12288]{2,1,0:T(2,128)(2,1)}, u32[]{:S(2)}, u32[]{:S(2)}) async-start(bf16[8,2,12288]{2,1,0:T(2,128)(2,1)} %reshape.354), calls=%async_computation.2 | async-start | bytes 786432 | tf_op jit(solution)/shard_map/all_to_all | solution.py:166
  152.1 11.1 %low_u.1 = (bf16[384,64]{1,0:T(8,128)(2,1)S(1)}, bf16[16,3,64,64]{3,2,1,0:T(8,128)(2,1)S(1)}) custom-call(s32[3]{0:T(128)S(1)} %copy-done.10, bf16[384,8192]{1,0:T(8,128)(2,1)} %x_ref.5, bf16[384,1024]{1,0:T(8,128)(2,1)S(1)} %copy-done, bf16[8,2,3,64,512]{4,3,2,1,0:T(8,128)(2,1)S(1)} %all-to-all-done.1.down_ref), custom_call_target="tpu_custom_call" | custom-call | tf_op jit(solution)/shard_map/low_u/pallas_call | solution.py:196
  164.1 2.7 reshape.356
  166.8 5.0 %all-to-all-start.4 = ((bf16[16,2,6144]{2,1,0:T(2,128)(2,1)}), bf16[16,2,6144]{2,1,0:T(2,128)(2,1)}, u32[]{:S(2)}, u32[]{:S(2)}) async-start(bf16[16,2,6144]{2,1,0:T(2,128)(2,1)} %reshape.356), calls=%async_computation.4 | async-start | bytes 786432 | tf_op jit(solution)/shard_map/all_to_all | solution.py:209
  171.7 2.7 reshape.355
  175.8 10.8 %low_v.1 = (bf16[384,64]{1,0:T(8,128)(2,1)S(1)}, bf16[16,3,64,512]{3,2,1,0:T(8,128)(2,1)S(1)}) custom-call(s32[3]{0:T(128)S(1)} %copy-done.10, bf16[384,8192]{1,0:T(8,128)(2,1)} %x_ref.5, bf16[384,1024]{1,0:T(8,128)(2,1)S(1)} %copy-done.1, bf16[1,16,3,64,64]{4,3,2,1,0:T(8,128)(2,1)S(1)} %bitcast.59), custom_call_target="tpu_custom_call" | custom-call | tf_op jit(solution)/shard_map/low_v/pallas_call | solution.py:182
  189.1 5.7 %all-to-all-start.3 = ((bf16[16,3,64,512]{3,2,1,0:T(8,128)(2,1)}), bf16[16,3,64,512]{3,2,1,0:T(8,128)(2,1)}, u32[]{:S(2)}, u32[]{:S(2)}) async-start(bf16[16,3,64,512]{3,2,1,0:T(8,128)(2,1)} %copy-done.5), calls=%async_computation.3 | async-start | bytes 6291456 | tf_op jit(solution)/shard_map/all_to_all | solution.py:194
  194.9 2.7 reshape.357.h_ref
  197.7 36.4 %all-to-all-done.3.g_ref = bf16[16,3,64,512]{3,2,1,0:T(8,128)(2,1)} async-done(((bf16[16,3,64,512]{3,2,1,0:T(8,128)(2,1)}), bf16[16,3,64,512]{3,2,1,0:T(8,128)(2,1)}, u32[]{:S(2)}, u32[]{:S(2)}) %all-to-all-start.3) | async-done | bytes 3145760 | tf_op jit(solution)/shard_map/all_to_all | solution.py:194
  235.2 3.3 %sum_blocks.1 = (bf16[32,64,512]{2,1,0:T(8,128)(2,1)S(1)}, bf16[32,64,64]{2,1,0:T(8,128)(2,1)S(1)}) custom-call(s32[16,3]{1,0:T(8,128)S(1)} %copy.25.ids_ref, bf16[16,3,64,512]{3,2,1,0:T(8,128)(2,1)} %all-to-all-done.3.g_ref, bf16[16,3,64,64]{3,2,1,0:T(8,128)(2,1)S(1)} %copy-done.6), custom_call_target="tpu_custom_call" | custom-call | tf_op jit(solution)/shard_map/sum_blocks/pallas_call | solution.py:211
  242.7 15.1 %all_to_all.35 = bf16[8,2,8192]{2,1,0:T(2,128)(2,1)} all-to-all(bf16[8,2,8192]{2,1,0:T(2,128)(2,1)} %reshape.358), channel_id=1, replica_groups=mesh['y'=4,'xh'=2,'z'=4,'xl'=2,'c'=2] {'y','xh'}, dimensions={0} | all-to-all | bytes 524288 | tf_op jit(solution)/shard_map/all_to_all | solution.py:224
  257.8 4.4 %all-to-all-start.5 = ((bf16[32,64,512]{2,1,0:T(8,128)(2,1)}), bf16[32,64,512]{2,1,0:T(8,128)(2,1)}, u32[]{:S(2)}, u32[]{:S(2)}) async-start(bf16[32,64,512]{2,1,0:T(8,128)(2,1)} %copy-done.7), calls=%async_computation.5 | async-start | bytes 4194304 | tf_op jit(solution)/shard_map/all_to_all | solution.py:223
  266.3 23.0 %all-to-all-done.5 = bf16[32,64,512]{2,1,0:T(8,128)(2,1)} async-done(((bf16[32,64,512]{2,1,0:T(8,128)(2,1)}), bf16[32,64,512]{2,1,0:T(8,128)(2,1)}, u32[]{:S(2)}, u32[]{:S(2)}) %all-to-all-start.5) | async-done | bytes 2097184 | tf_op jit(solution)/shard_map/all_to_all | solution.py:223
  294.4 23.7 %base.1 = (bf16[384,1024]{1,0:T(8,128)(2,1)}, bf16[384,8192]{1,0:T(8,128)(2,1)}) custom-call(bf16[384,8192]{1,0:T(8,128)(2,1)} %x_ref.5, bf16[384,1024]{1,0:T(8,128)(2,1)S(1)} %copy-done.2, bf16[8192,1024]{1,0:T(8,128)(2,1)} %all-gather.2.cloned.1.call-done.w_ref, bf16[384,64]{1,0:T(8,128)(2,1)S(1)} %get-tuple-element.12.u_ref, ...), custom_call_target="tpu_custom_call" | custom-call | tf_op jit(solution)/shard_map/base/pallas_call | solution.py:226
  (96 shorter events, 63.3 us)
Async XLA Ops:
  7.2 284.9 %all-gather.2.cloned.1.call-start = ((), (), s32[]{:S(2)}) async-start(), calls=%async_computation.7 | async-start | bytes 17825792 | tf_op jit(solution)/shard_map/all_gather | solution.py:147
  8.9 17.1 %collective-permute-start = (bf16[2,64,512]{2,1,0:T(8,128)(2,1)S(1)}, bf16[2,64,512]{2,1,0:T(8,128)(2,1)S(1)}, u32[]{:S(2)}, u32[]{:S(2)}) collective-permute-start(bf16[2,64,512]{2,1,0:T(8,128)(2,1)S(1)} %get-tuple-element.37), channel_id=1, source_target_pairs={{0,2},{2,16},{16,18},{18,0},{1,3},{3,17},{17,19},{19,1},{4,6},{6,2... | collective-permute-start | bytes 393224 | tf_op jit(solution)/shard_map/ppermute | solution.py:32
  10.6 17.9 %collective-permute-start.1 = (bf16[2,64,512]{2,1,0:T(8,128)(2,1)S(1)}, bf16[2,64,512]{2,1,0:T(8,128)(2,1)S(1)}, u32[]{:S(2)}, u32[]{:S(2)}) collective-permute-start(bf16[2,64,512]{2,1,0:T(8,128)(2,1)S(1)} %get-tuple-element.37), channel_id=1, source_target_pairs={{0,16},{2,18},{16,0},{18,2},{1,17},{3,19},{17,1},{19,3},{4,20},{6,... | collective-permute-start | bytes 393224 | tf_op jit(solution)/shard_map/ppermute | solution.py:32
  13.3 15.2 %collective-permute-start.2 = (bf16[2,64,512]{2,1,0:T(8,128)(2,1)S(1)}, bf16[2,64,512]{2,1,0:T(8,128)(2,1)S(1)}, u32[]{:S(2)}, u32[]{:S(2)}) collective-permute-start(bf16[2,64,512]{2,1,0:T(8,128)(2,1)S(1)} %get-tuple-element.37), channel_id=1, source_target_pairs={{0,18},{2,0},{16,2},{18,16},{1,19},{3,1},{17,3},{19,17},{4,22},{6,... | collective-permute-start | bytes 393224 | tf_op jit(solution)/shard_map/ppermute | solution.py:32
  16.0 12.2 %all-to-all-start = ((s32[16,8,128]{2,1,0:T(8,128)}), s32[16,8,128]{2,1,0:T(8,128)S(1)}, u32[]{:S(2)}, u32[]{:S(2)}) async-start(s32[16,8,128]{2,1,0:T(8,128)} %broadcast_in_dim.14), calls=%async_computation | async-start | bytes 131072 | tf_op jit(solution)/shard_map/all_to_all | solution.py:150
  21.5 11.1 %collective-permute-start.7 = (bf16[2,64,512]{2,1,0:T(8,128)(2,1)S(1)}, bf16[2,64,512]{2,1,0:T(8,128)(2,1)S(1)}, u32[]{:S(2)}, u32[]{:S(2)}) collective-permute-start(bf16[2,64,512]{2,1,0:T(8,128)(2,1)S(1)} %get-tuple-element.36), channel_id=1, source_target_pairs={{0,32},{32,64},{64,96},{96,0},{1,33},{33,65},{65,97},{97,1},{2,34}... | collective-permute-start | bytes 393224 | tf_op jit(solution)/shard_map/ppermute | solution.py:32
  23.1 9.5 %collective-permute-start.8 = (bf16[2,64,512]{2,1,0:T(8,128)(2,1)S(1)}, bf16[2,64,512]{2,1,0:T(8,128)(2,1)S(1)}, u32[]{:S(2)}, u32[]{:S(2)}) collective-permute-start(bf16[2,64,512]{2,1,0:T(8,128)(2,1)S(1)} %get-tuple-element.36), channel_id=1, source_target_pairs={{0,64},{32,96},{64,0},{96,32},{1,65},{33,97},{65,1},{97,33},{2,66}... | collective-permute-start | bytes 393224 | tf_op jit(solution)/shard_map/ppermute | solution.py:32
  26.0 6.6 %collective-permute-start.9 = (bf16[2,64,512]{2,1,0:T(8,128)(2,1)S(1)}, bf16[2,64,512]{2,1,0:T(8,128)(2,1)S(1)}, u32[]{:S(2)}, u32[]{:S(2)}) collective-permute-start(bf16[2,64,512]{2,1,0:T(8,128)(2,1)S(1)} %get-tuple-element.36), channel_id=1, source_target_pairs={{0,96},{32,0},{64,32},{96,64},{1,97},{33,1},{65,33},{97,65},{2,98}... | collective-permute-start | bytes 393224 | tf_op jit(solution)/shard_map/ppermute | solution.py:32
  29.3 15.0 %collective-permute-start.3 = (bf16[4,2,64,512]{3,2,1,0:T(8,128)(2,1)}, bf16[4,2,64,512]{3,2,1,0:T(8,128)(2,1)S(1)}, u32[]{:S(2)}, u32[]{:S(2)}) collective-permute-start(bf16[4,2,64,512]{3,2,1,0:T(8,128)(2,1)} %get-tuple-element.29), channel_id=1, source_target_pairs={{0,32},{32,64},{64,96},{96,0},{1,33},{33,65},{65,97},{97,1},{2,34}... | collective-permute-start | bytes 1572872 | tf_op jit(solution)/shard_map/ppermute | solution.py:32
  30.9 13.6 %collective-permute-start.5 = (bf16[4,2,64,512]{3,2,1,0:T(8,128)(2,1)}, bf16[4,2,64,512]{3,2,1,0:T(8,128)(2,1)S(1)}, u32[]{:S(2)}, u32[]{:S(2)}) collective-permute-start(bf16[4,2,64,512]{3,2,1,0:T(8,128)(2,1)} %get-tuple-element.29), channel_id=1, source_target_pairs={{0,96},{32,0},{64,32},{96,64},{1,97},{33,1},{65,33},{97,65},{2,98}... | collective-permute-start | bytes 1572872 | tf_op jit(solution)/shard_map/ppermute | solution.py:32
  33.5 24.9 %collective-permute-start.10 = (bf16[4,2,64,512]{3,2,1,0:T(8,128)(2,1)}, bf16[4,2,64,512]{3,2,1,0:T(8,128)(2,1)S(1)}, u32[]{:S(2)}, u32[]{:S(2)}) collective-permute-start(bf16[4,2,64,512]{3,2,1,0:T(8,128)(2,1)} %get-tuple-element.31), channel_id=1, source_target_pairs={{0,2},{2,16},{16,18},{18,0},{1,3},{3,17},{17,19},{19,1},{4,6},{6,2... | collective-permute-start | bytes 1572872 | tf_op jit(solution)/shard_map/ppermute | solution.py:32
  35.1 26.4 %collective-permute-start.12 = (bf16[4,2,64,512]{3,2,1,0:T(8,128)(2,1)}, bf16[4,2,64,512]{3,2,1,0:T(8,128)(2,1)S(1)}, u32[]{:S(2)}, u32[]{:S(2)}) collective-permute-start(bf16[4,2,64,512]{3,2,1,0:T(8,128)(2,1)} %get-tuple-element.31), channel_id=1, source_target_pairs={{0,18},{2,0},{16,2},{18,16},{1,19},{3,1},{17,3},{19,17},{4,22},{6,... | collective-permute-start | bytes 1572872 | tf_op jit(solution)/shard_map/ppermute | solution.py:32
  44.4 18.9 %collective-permute-start.4 = (bf16[2,2,64,512]{3,2,1,0:T(8,128)(2,1)S(1)}, bf16[2,2,64,512]{3,2,1,0:T(8,128)(2,1)}, u32[]{:S(2)}, u32[]{:S(2)}) collective-permute-start(bf16[2,2,64,512]{3,2,1,0:T(8,128)(2,1)S(1)} %slice.33), channel_id=1, source_target_pairs={{0,32},{32,64},{64,96},{96,0},{1,33},{33,65},{65,97},{97,1},{2,34}... | collective-permute-start | bytes 786440 | tf_op jit(solution)/shard_map/ppermute | solution.py:32
  45.2 18.0 %collective-permute-start.6 = (bf16[2,2,64,512]{3,2,1,0:T(8,128)(2,1)}, bf16[2,2,64,512]{3,2,1,0:T(8,128)(2,1)}, u32[]{:S(2)}, u32[]{:S(2)}) collective-permute-start(bf16[2,2,64,512]{3,2,1,0:T(8,128)(2,1)} %slice.34), channel_id=1, source_target_pairs={{0,96},{32,0},{64,32},{96,64},{1,97},{33,1},{65,33},{97,65},{2,98}... | collective-permute-start | bytes 786440 | tf_op jit(solution)/shard_map/ppermute | solution.py:32
  59.1 14.2 %collective-permute-start.11 = (bf16[2,2,64,512]{3,2,1,0:T(8,128)(2,1)}, bf16[2,2,64,512]{3,2,1,0:T(8,128)(2,1)}, u32[]{:S(2)}, u32[]{:S(2)}) collective-permute-start(bf16[2,2,64,512]{3,2,1,0:T(8,128)(2,1)} %slice.36), channel_id=1, source_target_pairs={{0,2},{2,16},{16,18},{18,0},{1,3},{3,17},{17,19},{19,1},{4,6},{6,2... | collective-permute-start | bytes 786440 | tf_op jit(solution)/shard_map/ppermute | solution.py:32
  62.2 14.2 %collective-permute-start.13 = (bf16[2,2,64,512]{3,2,1,0:T(8,128)(2,1)}, bf16[2,2,64,512]{3,2,1,0:T(8,128)(2,1)}, u32[]{:S(2)}, u32[]{:S(2)}) collective-permute-start(bf16[2,2,64,512]{3,2,1,0:T(8,128)(2,1)} %slice.37), channel_id=1, source_target_pairs={{0,18},{2,0},{16,2},{18,16},{1,19},{3,1},{17,3},{19,17},{4,22},{6,... | collective-permute-start | bytes 786440 | tf_op jit(solution)/shard_map/ppermute | solution.py:32
  85.2 4.4 %copy-start.11 = (bf16[4,64,64]{2,1,0:T(8,128)(2,1)S(1)}, bf16[4,64,64]{2,1,0:T(8,128)(2,1)}, u32[]{:S(2)}) copy-start(bf16[4,64,64]{2,1,0:T(8,128)(2,1)} %param.10) | copy-start | bytes 98308
  85.2 60.3 %all-to-all-start.1 = ((bf16[8,2,3,64,512]{4,3,2,1,0:T(8,128)(2,1)}), bf16[8,2,3,64,512]{4,3,2,1,0:T(8,128)(2,1)S(1)}, u32[]{:S(2)}, u32[]{:S(2)}) async-start(bf16[8,2,3,64,512]{4,3,2,1,0:T(8,128)(2,1)} %bitcast.61), calls=%async_computation.1 | async-start | bytes 6291456 | tf_op jit(solution)/shard_map/all_to_all | solution.py:171
  89.6 6.4 %collective-permute-start.14 = (bf16[4,64,64]{1,2,0:T(8,128)(2,1)S(1)}, bf16[4,64,64]{1,2,0:T(8,128)(2,1)S(1)}, u32[]{:S(2)}, u32[]{:S(2)}) collective-permute-start(bf16[4,64,64]{1,2,0:T(8,128)(2,1)S(1)} %bitcast.79), channel_id=1, source_target_pairs={{0,2},{2,16},{16,18},{18,0},{1,3},{3,17},{17,19},{19,1},{4,6},{6,2... | collective-permute-start | bytes 98312 | tf_op jit(solution)/shard_map/ppermute | solution.py:32
  89.6 7.8 %collective-permute-start.15 = (bf16[4,64,64]{1,2,0:T(8,128)(2,1)S(1)}, bf16[4,64,64]{1,2,0:T(8,128)(2,1)S(1)}, u32[]{:S(2)}, u32[]{:S(2)}) collective-permute-start(bf16[4,64,64]{1,2,0:T(8,128)(2,1)S(1)} %bitcast.80), channel_id=1, source_target_pairs={{0,16},{2,18},{16,0},{18,2},{1,17},{3,19},{17,1},{19,3},{4,20},{6,... | collective-permute-start | bytes 98312 | tf_op jit(solution)/shard_map/ppermute | solution.py:32
  90.5 10.1 %collective-permute-start.16 = (bf16[4,64,64]{1,2,0:T(8,128)(2,1)S(1)}, bf16[4,64,64]{1,2,0:T(8,128)(2,1)S(1)}, u32[]{:S(2)}, u32[]{:S(2)}) collective-permute-start(bf16[4,64,64]{1,2,0:T(8,128)(2,1)S(1)} %bitcast.81), channel_id=1, source_target_pairs={{0,18},{2,0},{16,2},{18,16},{1,19},{3,1},{17,3},{19,17},{4,22},{6,... | collective-permute-start | bytes 98312 | tf_op jit(solution)/shard_map/ppermute | solution.py:32
  101.3 10.7 %collective-permute-start.17 = (bf16[4,4,64,64]{2,3,1,0:T(8,128)(2,1)}, bf16[4,4,64,64]{2,3,1,0:T(8,128)(2,1)}, u32[]{:S(2)}, u32[]{:S(2)}) collective-permute-start(bf16[4,4,64,64]{2,3,1,0:T(8,128)(2,1)} %get-tuple-element.33), channel_id=1, source_target_pairs={{0,32},{32,64},{64,96},{96,0},{1,33},{33,65},{65,97},{97,1},{2,34}... | collective-permute-start | bytes 393224 | tf_op jit(solution)/shard_map/ppermute | solution.py:32
  102.6 13.6 %collective-permute-start.18 = (bf16[4,4,64,64]{2,3,1,0:T(8,128)(2,1)}, bf16[4,4,64,64]{2,3,1,0:T(8,128)(2,1)}, u32[]{:S(2)}, u32[]{:S(2)}) collective-permute-start(bf16[4,4,64,64]{2,3,1,0:T(8,128)(2,1)} %get-tuple-element.33), channel_id=1, source_target_pairs={{0,64},{32,96},{64,0},{96,32},{1,65},{33,97},{65,1},{97,33},{2,66}... | collective-permute-start | bytes 393224 | tf_op jit(solution)/shard_map/ppermute | solution.py:32
  104.7 12.1 %collective-permute-start.19 = (bf16[4,4,64,64]{2,3,1,0:T(8,128)(2,1)}, bf16[4,4,64,64]{2,3,1,0:T(8,128)(2,1)}, u32[]{:S(2)}, u32[]{:S(2)}) collective-permute-start(bf16[4,4,64,64]{2,3,1,0:T(8,128)(2,1)} %get-tuple-element.33), channel_id=1, source_target_pairs={{0,96},{32,0},{64,32},{96,64},{1,97},{33,1},{65,33},{97,65},{2,98}... | collective-permute-start | bytes 393224 | tf_op jit(solution)/shard_map/ppermute | solution.py:32
  121.4 29.6 %copy-start.10 = (s32[3]{0:T(128)S(1)}, s32[3]{0:T(128)}, u32[]{:S(2)}) copy-start(s32[3]{0:T(128)} %fill_ref.3) | copy-start | bytes 40
  145.5 21.2 %all-to-all-start.2 = ((bf16[8,2,12288]{2,1,0:T(2,128)(2,1)}), bf16[8,2,12288]{2,1,0:T(2,128)(2,1)}, u32[]{:S(2)}, u32[]{:S(2)}) async-start(bf16[8,2,12288]{2,1,0:T(2,128)(2,1)} %reshape.354), calls=%async_computation.2 | async-start | bytes 786432 | tf_op jit(solution)/shard_map/all_to_all | solution.py:166
  166.8 22.4 %all-to-all-start.4 = ((bf16[16,2,6144]{2,1,0:T(2,128)(2,1)}), bf16[16,2,6144]{2,1,0:T(2,128)(2,1)}, u32[]{:S(2)}, u32[]{:S(2)}) async-start(bf16[16,2,6144]{2,1,0:T(2,128)(2,1)} %reshape.356), calls=%async_computation.4 | async-start | bytes 786432 | tf_op jit(solution)/shard_map/all_to_all | solution.py:209
  174.4 1.4 copy-start.1
  187.5 1.7 copy-start.5
  189.1 44.9 %all-to-all-start.3 = ((bf16[16,3,64,512]{3,2,1,0:T(8,128)(2,1)}), bf16[16,3,64,512]{3,2,1,0:T(8,128)(2,1)}, u32[]{:S(2)}, u32[]{:S(2)}) async-start(bf16[16,3,64,512]{3,2,1,0:T(8,128)(2,1)} %copy-done.5), calls=%async_computation.3 | async-start | bytes 6291456 | tf_op jit(solution)/shard_map/all_to_all | solution.py:194
  238.4 1.3 copy-start.7
  257.8 31.5 %all-to-all-start.5 = ((bf16[32,64,512]{2,1,0:T(8,128)(2,1)}), bf16[32,64,512]{2,1,0:T(8,128)(2,1)}, u32[]{:S(2)}, u32[]{:S(2)}) async-start(bf16[32,64,512]{2,1,0:T(8,128)(2,1)} %copy-done.7), calls=%async_computation.5 | async-start | bytes 4194304 | tf_op jit(solution)/shard_map/all_to_all | solution.py:223
  (7 other events, 7.1 us)
Sparse Core Ops, SparseCore 0:
  9.7 124.2 all-gather.1

commit v2 on v1

v2 whole, which is shorter than its diff:
```python
import functools

import jax
import jax.numpy as jnp
from jax import lax
from jax.experimental import pallas as pl
from jax.experimental.pallas import tpu as pltpu
from jax.sharding import Mesh
from jax.sharding import PartitionSpec as P

DP = ("y", "xh")
FSDP = ("z", "xl", "c")
SCALE = 0.5
PACK = 4
F32 = jnp.float32
BF16 = jnp.bfloat16
after = lax.optimization_barrier


def nt(a, b):
    return lax.dot_general(a, b, (((1,), (1,)), ((), ())), preferred_element_type=F32)


def tn(a, b):
    return lax.dot_general(a, b, (((0,), (0,)), ((), ())), preferred_element_type=F32)


def nn(a, b):
    return jnp.dot(a, b, preferred_element_type=F32)


def shift(x, axis, by):
    n = lax.axis_size(axis)
    return lax.ppermute(x, axis, [(i, (i + by) % n) for i in range(n)])


def exchange(x, axis):
    return lax.all_to_all(x, axis, split_axis=0, concat_axis=0, tiled=True)


def live_rows(fill_ref, b, rows):
    return (lax.broadcasted_iota(jnp.int32, (rows, 1), 0) < fill_ref[b]).astype(F32)


def pack(a):
    n = a.shape[0] // PACK
    return jnp.concatenate([a[k * n : (k + 1) * n] for k in range(PACK)], axis=1)


def unpack(a):
    r = a.shape[1] // PACK
    return jnp.concatenate([a[:, k * r : (k + 1) * r] for k in range(PACK)], axis=0)


def first_kernel(blocks, per, fill_ref, x_ref, dy_ref, a_ref, v_ref, up_ref, g_ref):
    rows = dy_ref.shape[0] // blocks
    rank = v_ref.shape[1]
    half = a_ref.shape[3]
    cols = up_ref.shape[1] // a_ref.shape[0]

    @pl.when(pl.program_id(0) == 0)
    def _():
        for b in range(blocks):
            at = pl.ds(b * rows, rows)
            for f in range(a_ref.shape[0]):
                up_ref[b, pl.ds(f * cols, cols), :] = unpack(a_ref[f, b, rank:, :])
            v = nn(dy_ref[at, :], up_ref[b]) * live_rows(fill_ref, b, rows)
            v_ref[at, :] = v.astype(BF16)

    for b in range(blocks):
        at = pl.ds(b * rows, rows)
        for j in range(per):
            g_ref[j, b] = tn(v_ref[at, :], x_ref[at, pl.ds(2 * j * half, half)]).astype(BF16)


def second_kernel(blocks, per, fill_ref, x_ref, dy_ref, v_ref, a_ref, b_ref, u_ref, g_ref, acc_ref):
    rows = dy_ref.shape[0] // blocks
    rank = v_ref.shape[1]
    half = a_ref.shape[3]
    cols = dy_ref.shape[1] // a_ref.shape[0]
    step = pl.program_id(0)

    @pl.when(step == 0)
    def _():
        acc_ref[...] = jnp.zeros_like(acc_ref)

    for b in range(blocks):
        at = pl.ds(b * rows, rows)
        total = acc_ref[at, :]
        for j in range(per):
            f = step * per + j
            x_b = x_ref[at, pl.ds((2 * j + 1) * half, half)]
            total += nt(x_ref[at, pl.ds(2 * j * half, half)], a_ref[f, b, :rank, :])
            total += nt(x_b, b_ref[f, b])
            g_ref[f, b, :rank, :] = tn(v_ref[at, :], x_b).astype(BF16)
        acc_ref[at, :] = total

    @pl.when(step == pl.num_programs(0) - 1)
    def _():
        for b in range(blocks):
            at = pl.ds(b * rows, rows)
            u = (acc_ref[at, :] * live_rows(fill_ref, b, rows)).astype(BF16)
            u_ref[at, :] = u
            g = tn(dy_ref[at, :], u).astype(BF16)
            for f in range(a_ref.shape[0]):
                g_ref[f, b, rank:, :] = pack(g[f * cols : (f + 1) * cols])


def base_kernel(blocks, per, x_ref, dy_ref, w_ref, u_ref, v_ref, up_ref, a_ref, b_ref, y_ref, dx_ref, acc_ref):
    rows = dy_ref.shape[0] // blocks
    rank = v_ref.shape[1]
    half = a_ref.shape[3]
    step = pl.program_id(0)

    @pl.when(step == 0)
    def _():
        acc_ref[...] = jnp.zeros_like(acc_ref)

    acc_ref[...] += nn(x_ref[...], w_ref[...])
    wide = nt(dy_ref[...], w_ref[...])
    for b in range(blocks):
        at = pl.ds(b * rows, rows)
        v = v_ref[at, :]
        for j in range(per):
            f = step * per + j
            for k, low in ((2 * j, a_ref[f, b, :rank, :]), (2 * j + 1, b_ref[f, b])):
                pulled = nn(v, low).astype(BF16).astype(F32)
                own = wide[b * rows : (b + 1) * rows, k * half : (k + 1) * half]
                dx_ref[at, pl.ds(k * half, half)] = (own + SCALE * pulled).astype(BF16)

    @pl.when(step == pl.num_programs(0) - 1)
    def _():
        for b in range(blocks):
            at = pl.ds(b * rows, rows)
            lifted = nt(u_ref[at, :], up_ref[b]).astype(BF16).astype(F32)
            y_ref[at, :] = (acc_ref[at, :] + SCALE * lifted).astype(BF16)


def sum_kernel(ids_ref, g_ref, o_ref, acc_ref):
    members, blocks = g_ref.shape[:2]
    acc_ref[...] = jnp.zeros_like(acc_ref)

    @pl.loop(0, members)
    def _(m):
        for b in range(blocks):
            acc_ref[ids_ref[m, b]] += g_ref[m, b].astype(F32)

    o_ref[...] = acc_ref[...].astype(BF16)


PARAMS = pltpu.CompilerParams(vmem_limit_bytes=48 * 1024 * 1024)
VMEM = pl.BlockSpec(memory_space=pltpu.VMEM)
SMEM = pl.BlockSpec(memory_space=pltpu.SMEM)


def cost(flops, size):
    return pl.CostEstimate(flops=flops, bytes_accessed=size, transcendentals=0)


def whole(shape):
    zeros = (0,) * len(shape)
    return pl.BlockSpec(shape, lambda i: zeros)


def sum_blocks(ids_all, g, adapters):
    shape = (adapters,) + g.shape[2:]
    return pl.pallas_call(
        sum_kernel,
        in_specs=[SMEM, VMEM],
        out_specs=VMEM,
        out_shape=jax.ShapeDtypeStruct(shape, BF16),
        scratch_shapes=[pltpu.VMEM(shape, F32)],
        compiler_params=PARAMS,
        cost_estimate=cost(g.size, 4 * g.size),
        name="sum_blocks",
    )(ids_all, g)


def body(tokens, weight, down, up, dy, ids, fill):
    rows_dev, width = tokens.shape
    value = dy.shape[1]
    blocks = ids.shape[0]
    slots, feats, rank = down.shape
    cols = up.shape[2]
    half = feats // 2
    ys, xhs = lax.axis_size("y"), lax.axis_size("xh")
    steps = lax.axis_size(FSDP)
    adapters = slots * ys * xhs
    y_at, xh_at = lax.axis_index("y"), lax.axis_index("xh")
    up_rows = cols // PACK

    w_full = lax.all_gather(weight, FSDP, axis=0, tiled=True)

    ids_out = jnp.broadcast_to(jnp.pad(ids, (0, 128 - blocks)), (steps, 8, 128))
    ids_all = exchange(ids_out, FSDP)[:, 0, :blocks]

    down_t = jnp.swapaxes(down, 1, 2)
    up_t = jnp.swapaxes(up, 1, 2).reshape(slots, PACK, up_rows, rank)
    up_packed = jnp.swapaxes(up_t, 1, 2).reshape(slots, up_rows, PACK * rank)
    own_a = jnp.concatenate([down_t[:, :, :half], up_packed], axis=1)
    own_b = down_t[:, :, half:]

    def over_y(x):
        one, three = shift(x, "y", 1), shift(x, "y", -1)
        mid = slots // 2
        lo, hi = shift(one[:, :mid], "y", 1), shift(three[:, mid:], "y", -1)
        return jnp.stack([x, one, jnp.concatenate([lo, hi], axis=1), three])

    def over_x(x):
        return jnp.stack([x, shift(x, "xh", 1)])

    x_a = over_x(own_a)
    own_b, x_a = after((own_b, x_a))
    x_b = over_x(own_b)
    all_a = over_y(x_a)
    x_b, all_a = after((x_b, all_a))
    all_b = over_y(x_b)

    want = ids_all.reshape(steps * blocks)
    owner = want // slots
    oy, ox = (y_at - owner // xhs) % ys, (xh_at - owner % xhs) % xhs
    at = (oy * xhs + ox) * slots + want % slots

    def pick(x):
        return x.reshape(adapters, *x.shape[3:])[at].reshape(steps, blocks, *x.shape[3:])

    pick_a = pick(all_a)
    all_b, pick_a = after((all_b, pick_a))
    low_a = exchange(pick_a, FSDP)
    low_b = exchange(pick(all_b), FSDP)

    grid = 4
    per = steps // grid
    x_spec = pl.BlockSpec((rows_dev, per * feats), lambda i: (0, i))
    low_v, up_mine, grad_a = pl.pallas_call(
        functools.partial(first_kernel, blocks, per),
        grid=(grid,),
        in_specs=[SMEM, x_spec, whole(dy.shape), whole(low_a.shape)],
        out_specs=[
            whole((rows_dev, rank)),
            whole((blocks, value, rank)),
            pl.BlockSpec((per, blocks, rank, half), lambda i: (i, 0, 0, 0)),
        ],
        out_shape=[
            jax.ShapeDtypeStruct((rows_dev, rank), BF16),
            jax.ShapeDtypeStruct((blocks, value, rank), BF16),
            jax.ShapeDtypeStruct((steps, blocks, rank, half), BF16),
        ],
        compiler_params=PARAMS,
        cost_estimate=cost(rows_dev * rank * (width + 2 * value), 12 << 20),
        name="first",
    )(fill, tokens, dy, low_a)
    grad_a, low_b = after((grad_a, low_b))
    back_a = exchange(grad_a, FSDP)

    low_u, grad_b = pl.pallas_call(
        functools.partial(second_kernel, blocks, per),
        grid=(grid,),
        in_specs=[SMEM, x_spec, whole(dy.shape), whole(low_v.shape), whole(low_a.shape), whole(low_b.shape)],
        out_specs=[whole((rows_dev, rank)), whole((steps, blocks, rank + up_rows, half))],
        out_shape=[
            jax.ShapeDtypeStruct((rows_dev, rank), BF16),
            jax.ShapeDtypeStruct((steps, blocks, rank + up_rows, half), BF16),
        ],
        scratch_shapes=[pltpu.VMEM((rows_dev, rank), F32)],
        compiler_params=PARAMS,
        cost_estimate=cost(rows_dev * rank * (3 * width + 2 * value), 14 << 20),
        name="second",
    )(fill, tokens, dy, low_v, low_a, low_b)
    grad_b, back_a = after((grad_b, back_a))
    back_b = exchange(grad_b, FSDP)

    sums = jnp.concatenate(
        [sum_blocks(ids_all, back_a, adapters), sum_blocks(ids_all, back_b, adapters)], axis=1
    )
    part = exchange(sums, DP)

    grid = 8
    per = steps // grid
    x_spec = pl.BlockSpec((rows_dev, per * feats), lambda i: (0, i))
    values, input_gradient = pl.pallas_call(
        functools.partial(base_kernel, blocks, per),
        grid=(grid,),
        in_specs=[
            x_spec,
            whole(dy.shape),
            pl.BlockSpec((per * feats, value), lambda i: (i, 0)),
            whole(low_u.shape),
            whole(low_v.shape),
            whole(up_mine.shape),
            whole(low_a.shape),
            whole(low_b.shape),
        ],
        out_specs=[whole((rows_dev, value)), x_spec],
        out_shape=[
            jax.ShapeDtypeStruct((rows_dev, value), BF16),
            jax.ShapeDtypeStruct((rows_dev, width), BF16),
        ],
        scratch_shapes=[pltpu.VMEM((rows_dev, value), F32)],
        compiler_params=PARAMS,
        cost_estimate=cost(4 * rows_dev * width * value, 36 << 20),
        name="base",
    )(tokens, dy, w_full, low_u, low_v, up_mine, low_a, low_b)

    part, values, input_gradient = after((part, values, input_gradient))
    total = SCALE * part.reshape(ys * xhs, slots, -1, half).astype(F32).sum(0)
    grad_down = jnp.concatenate([total[:, :rank], total[:, rank : 2 * rank]], axis=2)
    grad_up = total[:, 2 * rank :].reshape(slots, up_rows, PACK, rank)
    grad_up = jnp.transpose(grad_up, (0, 3, 2, 1)).reshape(slots, rank, cols)
    return values, input_gradient, jnp.swapaxes(grad_down, 1, 2), grad_up


def solution(mesh):
    fine = Mesh(mesh.devices.reshape(4, 2, 4, 2, 2), DP + FSDP)
    every = DP + FSDP
    placed = (
        P(every, None),
        P(FSDP, None),
        P(DP, FSDP, None),
        P(DP, None, FSDP),
        P(every, None),
        P(every),
        P(every),
    )
    return jax.shard_map(
        body,
        mesh=fine,
        in_specs=placed,
        out_specs=(P(every, None), P(every, None), P(DP, FSDP, None), P(DP, None, FSDP)),
        check_vma=False,
    )
```

time: 327 us -> 256 us (0.78)
  local copies, waits for them, and re-layouts: 42.1 us -> 20.8 us
  Pallas kernels: 48.9 us -> 33.4 us
  blocking collectives: 15.1 us -> 0 us
  starting transfers between devices: 63.6 us -> 50 us
  other arithmetic: 14 us -> 5.04 us
  waiting for transfers between devices: 127 us -> 131 us
    all_to_all x6, waiting for transfers between devices: 78.9 us -> 116 us  [exchange(): return lax.all_to_all(x, axis, split_axis=0, concat_axis=0, tiled=True)]
    ppermute x20 -> x10, waiting for transfers between devices: 47.2 us -> 14 us  [shift(): return lax.ppermute(x, axis, [(i, (i + by) % n) for i in range(n)])]
    pallas_call x4 -> x5, Pallas kernels: 48.9 us -> 33.4 us  [the longest x1 20 us: body(): pl.pallas_call(functools.partial(base_kernel, blocks, per), grid=(grid,),...]
    all_to_all x1 -> x0, blocking collectives: 15.1 us -> none  [body(): part_u = lax.all_to_all(sum_u, DP, split_axis=0, concat_axis=0, tiled=True)]
    ppermute x20 -> x10, starting transfers between devices: 33.3 us -> 20.5 us  [shift(): return lax.ppermute(x, axis, [(i, (i + by) % n) for i in range(n)])]
    unnamed x31 -> x44, local copies, waits for them, and re-layouts: 25.9 us -> 14.8 us
    another operation x8 -> x7, other arithmetic: 7.58 us -> 0.44 us  [the longest x4 0.36 us: over_y(): return jnp.stack([x, one, jnp.concatenate([lo, hi], axis=1), three])]
    gather x2, local copies, waits for them, and re-layouts: 7.6 us -> 3.9 us  [pick(): x.reshape(adapters, *x.shape[3:])[at].reshape(steps, blocks, *x.shape[3:])]
  transfers between devices with their start and end apart: 27 -> 17, of which waited for: 14 -> 11; matrix products, arithmetic and copies ran while one was open for 14% -> 3% of each run, Pallas kernels for 8% -> 13%
where the time goes in v2:
time: 256 us; the launch traced here: 255 us
  waiting for transfers between devices  131 us (51%)
  starting transfers between devices  50 us (20%)
  Pallas kernels  33.4 us (13%)
  local copies, waits for them, and re-layouts  20.8 us (8%)
  between operations  14.4 us (6%)
  other arithmetic  5.04 us (2%)
    all_to_all x6, waiting for transfers between devices, exchange(): return lax.all_to_all(x, axis, split_axis=0, concat_axis=0, tiled=True)  116 us
    all_to_all x6, starting transfers between devices, exchange(): return lax.all_to_all(x, axis, split_axis=0, concat_axis=0, tiled=True)  29.5 us
    ppermute x10, starting transfers between devices, shift(): return lax.ppermute(x, axis, [(i, (i + by) % n) for i in range(n)])  20.5 us
    pallas_call x1, Pallas kernels, body(): pl.pallas_call(functools.partial(base_kernel, blocks, per), grid=(grid,),...  20 us
    unnamed x44, local copies, waits for them, and re-layouts  14.8 us
    ppermute x10, waiting for transfers between devices, shift(): return lax.ppermute(x, axis, [(i, (i + by) % n) for i in range(n)])  14 us
    pallas_call x1, Pallas kernels, body(): pl.pallas_call(functools.partial(second_kernel, blocks, per), grid=(grid,...  6.17 us
  transfers between devices with their start and end apart: 17, of which 11 were waited for; matrix products, arithmetic and copies ran while one was open for 3% of the time, Pallas kernels for 13%

profile of v2, /device:TPU:0, one launch (start us, length us, event | category | flops | bytes accessed | tf_op | source)
XLA Modules:
  0.0 254.5 jit_solution(156023280295031105)
XLA Ops:
  10.0 3.2 %collective-permute-start = (bf16[4,80,256]{2,1,0:T(8,128)(2,1)S(1)}, bf16[4,80,256]{2,1,0:T(8,128)(2,1)S(1)}, u32[]{:S(2)}, u32[]{:S(2)}) collective-permute-start(bf16[4,80,256]{2,1,0:T(8,128)(2,1)S(1)} %get-tuple-element.61), channel_id=1, source_target_pairs={{0,16},{16,0},{1,17},{17,1},{2,18},{18,2},{3,19},{19,3},{4,20},{20... | collective-permute-start | bytes 491528 | tf_op jit(solution)/shard_map/ppermute | solution.py:34
  13.2 4.2 %collective-permute-done = bf16[4,80,256]{2,1,0:T(8,128)(2,1)S(1)} collective-permute-done((bf16[4,80,256]{2,1,0:T(8,128)(2,1)S(1)}, bf16[4,80,256]{2,1,0:T(8,128)(2,1)S(1)}, u32[]{:S(2)}, u32[]{:S(2)}) %collective-permute-start) | collective-permute-done | bytes 163872 | tf_op jit(solution)/shard_map/ppermute | solution.py:34
  17.4 3.3 %collective-permute-start.4 = (bf16[2,4,80,256]{3,2,1,0:T(8,128)(2,1)S(1)}, bf16[2,4,80,256]{3,2,1,0:T(8,128)(2,1)S(1)}, u32[]{:S(2)}, u32[]{:S(2)}) collective-permute-start(bf16[2,4,80,256]{3,2,1,0:T(8,128)(2,1)S(1)} %pad_maximum_fusion.3), channel_id=1, source_target_pairs={{0,96},{32,0},{64,32},{96,64},{1,97},{33,1},{65,33},{97,65},{2,98}... | collective-permute-start | bytes 983048 | tf_op jit(solution)/shard_map/ppermute | solution.py:34
  20.7 3.0 %collective-permute-start.1 = (bf16[4,64,256]{2,1,0:T(8,128)(2,1)S(1)}, bf16[4,64,256]{2,1,0:T(8,128)(2,1)S(1)}, u32[]{:S(2)}, u32[]{:S(2)}) collective-permute-start(bf16[4,64,256]{2,1,0:T(8,128)(2,1)S(1)} %get-tuple-element.24), channel_id=1, source_target_pairs={{0,16},{16,0},{1,17},{17,1},{2,18},{18,2},{3,19},{19,3},{4,20},{20... | collective-permute-start | bytes 393224 | tf_op jit(solution)/shard_map/ppermute | solution.py:34
  23.8 3.1 %collective-permute-done.4 = bf16[2,4,80,256]{3,2,1,0:T(8,128)(2,1)S(1)} collective-permute-done((bf16[2,4,80,256]{3,2,1,0:T(8,128)(2,1)S(1)}, bf16[2,4,80,256]{3,2,1,0:T(8,128)(2,1)S(1)}, u32[]{:S(2)}, u32[]{:S(2)}) %collective-permute-start.4) | collective-permute-done | bytes 327712 | tf_op jit(solution)/shard_map/ppermute | solution.py:34
  26.9 3.8 %collective-permute-start.5 = (bf16[2,2,80,256]{3,2,1,0:T(8,128)(2,1)S(1)}, bf16[2,2,80,256]{3,2,1,0:T(8,128)(2,1)S(1)}, u32[]{:S(2)}, u32[]{:S(2)}) collective-permute-start(bf16[2,2,80,256]{3,2,1,0:T(8,128)(2,1)S(1)} %slice.48), channel_id=1, source_target_pairs={{0,96},{32,0},{64,32},{96,64},{1,97},{33,1},{65,33},{97,65},{2,98}... | collective-permute-start | bytes 491528 | tf_op jit(solution)/shard_map/ppermute | solution.py:34
  31.4 6.3 %all-to-all-start = ((s32[16,8,128]{2,1,0:T(8,128)}), s32[16,8,128]{2,1,0:T(8,128)S(1)}, u32[]{:S(2)}, u32[]{:S(2)}) async-start(s32[16,8,128]{2,1,0:T(8,128)} %broadcast_in_dim.2), calls=%async_computation | async-start | bytes 131072 | tf_op jit(solution)/shard_map/all_to_all | solution.py:38
  38.0 3.3 %collective-permute-start.8 = (bf16[2,4,64,256]{3,2,1,0:T(8,128)(2,1)S(1)}, bf16[2,4,64,256]{3,2,1,0:T(8,128)(2,1)S(1)}, u32[]{:S(2)}, u32[]{:S(2)}) collective-permute-start(bf16[2,4,64,256]{3,2,1,0:T(8,128)(2,1)S(1)} %pad_maximum_fusion.4), channel_id=1, source_target_pairs={{0,96},{32,0},{64,32},{96,64},{1,97},{33,1},{65,33},{97,65},{2,98}... | collective-permute-start | bytes 786440 | tf_op jit(solution)/shard_map/ppermute | solution.py:34
  41.3 3.4 %all-to-all-done = s32[16,8,128]{2,1,0:T(8,128)S(1)} async-done(((s32[16,8,128]{2,1,0:T(8,128)}), s32[16,8,128]{2,1,0:T(8,128)S(1)}, u32[]{:S(2)}, u32[]{:S(2)}) %all-to-all-start) | async-done | bytes 65568 | tf_op jit(solution)/shard_map/all_to_all | solution.py:38
  44.8 2.6 %collective-permute-done.8 = bf16[2,4,64,256]{3,2,1,0:T(8,128)(2,1)S(1)} collective-permute-done((bf16[2,4,64,256]{3,2,1,0:T(8,128)(2,1)S(1)}, bf16[2,4,64,256]{3,2,1,0:T(8,128)(2,1)S(1)}, u32[]{:S(2)}, u32[]{:S(2)}) %collective-permute-start.8) | collective-permute-done | bytes 262176 | tf_op jit(solution)/shard_map/ppermute | solution.py:34
  47.5 3.8 %collective-permute-start.9 = (bf16[2,2,64,256]{3,2,1,0:T(8,128)(2,1)S(1)}, bf16[2,2,64,256]{3,2,1,0:T(8,128)(2,1)S(1)}, u32[]{:S(2)}, u32[]{:S(2)}) collective-permute-start(bf16[2,2,64,256]{3,2,1,0:T(8,128)(2,1)S(1)} %slice.50), channel_id=1, source_target_pairs={{0,96},{32,0},{64,32},{96,64},{1,97},{33,1},{65,33},{97,65},{2,98}... | collective-permute-start | bytes 393224 | tf_op jit(solution)/shard_map/ppermute | solution.py:34
  51.4 2.0 gather_fusion
  53.8 3.7 %collective-permute-done.7 = bf16[2,2,64,256]{3,2,1,0:T(8,128)(2,1)S(1)} collective-permute-done((bf16[2,2,64,256]{3,2,1,0:T(8,128)(2,1)S(1)}, bf16[2,2,64,256]{3,2,1,0:T(8,128)(2,1)S(1)}, u32[]{:S(2)}, u32[]{:S(2)}) %collective-permute-start.7) | collective-permute-done | bytes 131104 | tf_op jit(solution)/shard_map/ppermute | solution.py:34
  57.7 5.4 %all-to-all-start.1 = ((bf16[16,3,80,256]{3,2,1,0:T(8,128)(2,1)}), bf16[16,3,80,256]{3,2,1,0:T(8,128)(2,1)S(1)}, u32[]{:S(2)}, u32[]{:S(2)}) async-start(bf16[16,3,80,256]{3,2,1,0:T(8,128)(2,1)} %bitcast.37), calls=%async_computation.1 | async-start | bytes 3932160 | tf_op jit(solution)/shard_map/all_to_all | solution.py:38
  63.1 1.9 gather_fusion.1
  65.0 45.8 %all-to-all-done.1.a_ref = bf16[16,3,80,256]{3,2,1,0:T(8,128)(2,1)S(1)} async-done(((bf16[16,3,80,256]{3,2,1,0:T(8,128)(2,1)}), bf16[16,3,80,256]{3,2,1,0:T(8,128)(2,1)S(1)}, u32[]{:S(2)}, u32[]{:S(2)}) %all-to-all-start.1) | async-done | bytes 1966112 | tf_op jit(solution)/shard_map/all_to_all | solution.py:38
  110.8 3.7 %all-to-all-start.2 = ((bf16[16,3,64,256]{3,2,1,0:T(8,128)(2,1)}), bf16[16,3,64,256]{3,2,1,0:T(8,128)(2,1)S(1)}, u32[]{:S(2)}, u32[]{:S(2)}) async-start(bf16[16,3,64,256]{3,2,1,0:T(8,128)(2,1)} %bitcast.39), calls=%async_computation.2 | async-start | bytes 3145728 | tf_op jit(solution)/shard_map/all_to_all | solution.py:38
  115.7 4.6 %first.1 = (bf16[384,64]{1,0:T(8,128)(2,1)S(1)}, bf16[3,1024,64]{2,1,0:T(8,128)(2,1)S(1)}, bf16[16,3,64,256]{3,2,1,0:T(8,128)(2,1)S(1)}) custom-call(s32[3]{0:T(128)S(1)} %copy-done.15, bf16[384,8192]{1,0:T(8,128)(2,1)} %x_ref.5, bf16[384,1024]{1,0:T(8,128)(2,1)S(1)} %copy-done.7, bf16[16,3,80,256]{3,2,1,0:T(8,128)(2,1)S(1)} %all-to-all-done.1.a_ref), custom_call_target="tpu_custom_call" | custom-call | flops 251658240 | bytes 12582912 | tf_op jit(solution)/shard_map/first/pallas_call | solution.py:235
  122.9 22.8 %all-to-all-done.2.b_ref = bf16[16,3,64,256]{3,2,1,0:T(8,128)(2,1)S(1)} async-done(((bf16[16,3,64,256]{3,2,1,0:T(8,128)(2,1)}), bf16[16,3,64,256]{3,2,1,0:T(8,128)(2,1)S(1)}, u32[]{:S(2)}, u32[]{:S(2)}) %all-to-all-start.2) | async-done | bytes 1572896 | tf_op jit(solution)/shard_map/all_to_all | solution.py:38
  146.9 3.8 %all-to-all-start.3 = ((bf16[16,3,64,256]{3,2,1,0:T(8,128)(2,1)}), bf16[16,3,64,256]{3,2,1,0:T(8,128)(2,1)S(1)}, u32[]{:S(2)}, u32[]{:S(2)}) async-start(bf16[16,3,64,256]{3,2,1,0:T(8,128)(2,1)} %copy-done.11), calls=%async_computation.3 | async-start | bytes 3145728 | tf_op jit(solution)/shard_map/all_to_all | solution.py:38
  151.9 6.2 %second.1 = (bf16[384,64]{1,0:T(8,128)(2,1)S(1)}, bf16[16,3,80,256]{3,2,1,0:T(8,128)(2,1)S(1)}) custom-call(s32[3]{0:T(128)S(1)} %copy-done.15, bf16[384,8192]{1,0:T(8,128)(2,1)} %x_ref.5, bf16[384,1024]{1,0:T(8,128)(2,1)S(1)} %copy-done.8, bf16[384,64]{1,0:T(8,128)(2,1)S(1)} %copy-done.13, bf16[16,3,80,256]{3,2,1,0:T(8,128)(2,1)} %copy-done, ...), custom_call_target="tpu_custom_call" | custom-call | flops 654311424 | bytes 14680064 | tf_op jit(solution)/shard_map/second/pallas_call | solution.py:256
  158.1 1.3 copy-done.10
  160.0 12.9 %all-to-all-done.3.g_ref = bf16[16,3,64,256]{3,2,1,0:T(8,128)(2,1)S(1)} async-done(((bf16[16,3,64,256]{3,2,1,0:T(8,128)(2,1)}), bf16[16,3,64,256]{3,2,1,0:T(8,128)(2,1)S(1)}, u32[]{:S(2)}, u32[]{:S(2)}) %all-to-all-start.3) | async-done | bytes 1572896 | tf_op jit(solution)/shard_map/all_to_all | solution.py:38
  173.0 3.7 %all-to-all-start.4 = ((bf16[16,3,80,256]{3,2,1,0:T(8,128)(2,1)}), bf16[16,3,80,256]{3,2,1,0:T(8,128)(2,1)S(1)}, u32[]{:S(2)}, u32[]{:S(2)}) async-start(bf16[16,3,80,256]{3,2,1,0:T(8,128)(2,1)} %copy-done.10), calls=%async_computation.4 | async-start | bytes 3932160 | tf_op jit(solution)/shard_map/all_to_all | solution.py:38
  176.7 1.3 sum_blocks.2
  179.0 24.2 %all-to-all-done.4.g_ref = bf16[16,3,80,256]{3,2,1,0:T(8,128)(2,1)S(1)} async-done(((bf16[16,3,80,256]{3,2,1,0:T(8,128)(2,1)}), bf16[16,3,80,256]{3,2,1,0:T(8,128)(2,1)S(1)}, u32[]{:S(2)}, u32[]{:S(2)}) %all-to-all-start.4) | async-done | bytes 1966112 | tf_op jit(solution)/shard_map/all_to_all | solution.py:38
  203.2 1.4 sum_blocks.3
  204.6 1.6 pad_maximum_fusion
  206.2 6.4 %all-to-all-start.5 = ((bf16[32,144,256]{2,1,0:T(8,128)(2,1)}), bf16[32,144,256]{2,1,0:T(8,128)(2,1)}, u32[]{:S(2)}, u32[]{:S(2)}) async-start(bf16[32,144,256]{2,1,0:T(8,128)(2,1)} %pad_maximum_fusion), calls=%async_computation.5 | async-start | bytes 4718592 | tf_op jit(solution)/shard_map/all_to_all | solution.py:38
  216.7 20.0 %base.1 = (bf16[384,1024]{1,0:T(8,128)(2,1)}, bf16[384,8192]{1,0:T(8,128)(2,1)}) custom-call(bf16[384,8192]{1,0:T(8,128)(2,1)} %x_ref.5, bf16[384,1024]{1,0:T(8,128)(2,1)S(1)} %copy-done.9, bf16[8192,1024]{1,0:T(8,128)(2,1)} %all-gather.2.cloned.1.call-done.w_ref, bf16[384,64]{1,0:T(8,128)(2,1)S(1)} %copy-done.19, bf16[384,64]{1,0:T(8,128)(2,1)S(1)} %copy-done.14, ...), custom_call_target="tpu_custom_call" | custom-call | flops 12884901888 | bytes 37748736 | tf_op jit(solution)/shard_map/base/pallas_call | solution.py:281
  236.7 7.1 %all-to-all-done.5 = bf16[32,144,256]{2,1,0:T(8,128)(2,1)} async-done(((bf16[32,144,256]{2,1,0:T(8,128)(2,1)}), bf16[32,144,256]{2,1,0:T(8,128)(2,1)}, u32[]{:S(2)}, u32[]{:S(2)}) %all-to-all-start.5) | async-done | bytes 2359328 | tf_op jit(solution)/shard_map/all_to_all | solution.py:38
  243.8 2.0 convert_reduce_fusion
  (82 shorter events, 18.2 us)
Async XLA Ops:
  7.2 23.6 %copy-start.20 = (s32[3]{0:T(128)S(1)}, s32[3]{0:T(128)}, u32[]{:S(2)}) copy-start(s32[3]{0:T(128)} %param.12) | copy-start | bytes 40
  7.2 205.4 %all-gather.2.cloned.1.call-start = ((), (), s32[]{:S(2)}) async-start(), calls=%async_computation.6 | async-start | bytes 17825792 | tf_op jit(solution)/shard_map/all_gather | solution.py:192
  10.0 7.4 %collective-permute-start = (bf16[4,80,256]{2,1,0:T(8,128)(2,1)S(1)}, bf16[4,80,256]{2,1,0:T(8,128)(2,1)S(1)}, u32[]{:S(2)}, u32[]{:S(2)}) collective-permute-start(bf16[4,80,256]{2,1,0:T(8,128)(2,1)S(1)} %get-tuple-element.61), channel_id=1, source_target_pairs={{0,16},{16,0},{1,17},{17,1},{2,18},{18,2},{3,19},{19,3},{4,20},{20... | collective-permute-start | bytes 491528 | tf_op jit(solution)/shard_map/ppermute | solution.py:34
  17.4 9.4 %collective-permute-start.4 = (bf16[2,4,80,256]{3,2,1,0:T(8,128)(2,1)S(1)}, bf16[2,4,80,256]{3,2,1,0:T(8,128)(2,1)S(1)}, u32[]{:S(2)}, u32[]{:S(2)}) collective-permute-start(bf16[2,4,80,256]{3,2,1,0:T(8,128)(2,1)S(1)} %pad_maximum_fusion.3), channel_id=1, source_target_pairs={{0,96},{32,0},{64,32},{96,64},{1,97},{33,1},{65,33},{97,65},{2,98}... | collective-permute-start | bytes 983048 | tf_op jit(solution)/shard_map/ppermute | solution.py:34
  20.7 9.9 %collective-permute-start.2 = (bf16[2,4,80,256]{3,2,1,0:T(8,128)(2,1)S(1)}, bf16[2,4,80,256]{3,2,1,0:T(8,128)(2,1)S(1)}, u32[]{:S(2)}, u32[]{:S(2)}) collective-permute-start(bf16[2,4,80,256]{3,2,1,0:T(8,128)(2,1)S(1)} %pad_maximum_fusion.3), channel_id=1, source_target_pairs={{0,32},{32,64},{64,96},{96,0},{1,33},{33,65},{65,97},{97,1},{2,34}... | collective-permute-start | bytes 983048 | tf_op jit(solution)/shard_map/ppermute | solution.py:34
  20.7 17.0 %collective-permute-start.1 = (bf16[4,64,256]{2,1,0:T(8,128)(2,1)S(1)}, bf16[4,64,256]{2,1,0:T(8,128)(2,1)S(1)}, u32[]{:S(2)}, u32[]{:S(2)}) collective-permute-start(bf16[4,64,256]{2,1,0:T(8,128)(2,1)S(1)} %get-tuple-element.24), channel_id=1, source_target_pairs={{0,16},{16,0},{1,17},{17,1},{2,18},{18,2},{3,19},{19,3},{4,20},{20... | collective-permute-start | bytes 393224 | tf_op jit(solution)/shard_map/ppermute | solution.py:34
  26.9 10.9 %collective-permute-start.5 = (bf16[2,2,80,256]{3,2,1,0:T(8,128)(2,1)S(1)}, bf16[2,2,80,256]{3,2,1,0:T(8,128)(2,1)S(1)}, u32[]{:S(2)}, u32[]{:S(2)}) collective-permute-start(bf16[2,2,80,256]{3,2,1,0:T(8,128)(2,1)S(1)} %slice.48), channel_id=1, source_target_pairs={{0,96},{32,0},{64,32},{96,64},{1,97},{33,1},{65,33},{97,65},{2,98}... | collective-permute-start | bytes 491528 | tf_op jit(solution)/shard_map/ppermute | solution.py:34
  30.6 7.2 %collective-permute-start.3 = (bf16[2,2,80,256]{3,2,1,0:T(8,128)(2,1)S(1)}, bf16[2,2,80,256]{3,2,1,0:T(8,128)(2,1)S(1)}, u32[]{:S(2)}, u32[]{:S(2)}) collective-permute-start(bf16[2,2,80,256]{3,2,1,0:T(8,128)(2,1)S(1)} %slice.47), channel_id=1, source_target_pairs={{0,32},{32,64},{64,96},{96,0},{1,33},{33,65},{65,97},{97,1},{2,34}... | collective-permute-start | bytes 491528 | tf_op jit(solution)/shard_map/ppermute | solution.py:34
  31.4 13.3 %all-to-all-start = ((s32[16,8,128]{2,1,0:T(8,128)}), s32[16,8,128]{2,1,0:T(8,128)S(1)}, u32[]{:S(2)}, u32[]{:S(2)}) async-start(s32[16,8,128]{2,1,0:T(8,128)} %broadcast_in_dim.2), calls=%async_computation | async-start | bytes 131072 | tf_op jit(solution)/shard_map/all_to_all | solution.py:38
  38.0 9.4 %collective-permute-start.8 = (bf16[2,4,64,256]{3,2,1,0:T(8,128)(2,1)S(1)}, bf16[2,4,64,256]{3,2,1,0:T(8,128)(2,1)S(1)}, u32[]{:S(2)}, u32[]{:S(2)}) collective-permute-start(bf16[2,4,64,256]{3,2,1,0:T(8,128)(2,1)S(1)} %pad_maximum_fusion.4), channel_id=1, source_target_pairs={{0,96},{32,0},{64,32},{96,64},{1,97},{33,1},{65,33},{97,65},{2,98}... | collective-permute-start | bytes 786440 | tf_op jit(solution)/shard_map/ppermute | solution.py:34
  41.3 9.9 %collective-permute-start.6 = (bf16[2,4,64,256]{3,2,1,0:T(8,128)(2,1)S(1)}, bf16[2,4,64,256]{3,2,1,0:T(8,128)(2,1)S(1)}, u32[]{:S(2)}, u32[]{:S(2)}) collective-permute-start(bf16[2,4,64,256]{3,2,1,0:T(8,128)(2,1)S(1)} %pad_maximum_fusion.4), channel_id=1, source_target_pairs={{0,32},{32,64},{64,96},{96,0},{1,33},{33,65},{65,97},{97,1},{2,34}... | collective-permute-start | bytes 786440 | tf_op jit(solution)/shard_map/ppermute | solution.py:34
  47.5 6.3 %collective-permute-start.9 = (bf16[2,2,64,256]{3,2,1,0:T(8,128)(2,1)S(1)}, bf16[2,2,64,256]{3,2,1,0:T(8,128)(2,1)S(1)}, u32[]{:S(2)}, u32[]{:S(2)}) collective-permute-start(bf16[2,2,64,256]{3,2,1,0:T(8,128)(2,1)S(1)} %slice.50), channel_id=1, source_target_pairs={{0,96},{32,0},{64,32},{96,64},{1,97},{33,1},{65,33},{97,65},{2,98}... | collective-permute-start | bytes 393224 | tf_op jit(solution)/shard_map/ppermute | solution.py:34
  51.2 6.2 %collective-permute-start.7 = (bf16[2,2,64,256]{3,2,1,0:T(8,128)(2,1)S(1)}, bf16[2,2,64,256]{3,2,1,0:T(8,128)(2,1)S(1)}, u32[]{:S(2)}, u32[]{:S(2)}) collective-permute-start(bf16[2,2,64,256]{3,2,1,0:T(8,128)(2,1)S(1)} %slice.49), channel_id=1, source_target_pairs={{0,32},{32,64},{64,96},{96,0},{1,33},{33,65},{65,97},{97,1},{2,34}... | collective-permute-start | bytes 393224 | tf_op jit(solution)/shard_map/ppermute | solution.py:34
  57.7 53.1 %all-to-all-start.1 = ((bf16[16,3,80,256]{3,2,1,0:T(8,128)(2,1)}), bf16[16,3,80,256]{3,2,1,0:T(8,128)(2,1)S(1)}, u32[]{:S(2)}, u32[]{:S(2)}) async-start(bf16[16,3,80,256]{3,2,1,0:T(8,128)(2,1)} %bitcast.37), calls=%async_computation.1 | async-start | bytes 3932160 | tf_op jit(solution)/shard_map/all_to_all | solution.py:38
  65.0 49.5 %copy-start.15 = (s32[3]{0:T(128)S(1)}, s32[3]{0:T(128)}, u32[]{:S(2)}) copy-start(s32[3]{0:T(128)} %fill_ref.3) | copy-start | bytes 40
  110.8 9.4 %copy-start = (bf16[16,3,80,256]{3,2,1,0:T(8,128)(2,1)}, bf16[16,3,80,256]{3,2,1,0:T(8,128)(2,1)S(1)}, u32[]{:S(2)}) copy-start(bf16[16,3,80,256]{3,2,1,0:T(8,128)(2,1)S(1)} %all-to-all-done.1.a_ref) | copy-start | bytes 5898244
  110.8 34.9 %all-to-all-start.2 = ((bf16[16,3,64,256]{3,2,1,0:T(8,128)(2,1)}), bf16[16,3,64,256]{3,2,1,0:T(8,128)(2,1)S(1)}, u32[]{:S(2)}, u32[]{:S(2)}) async-start(bf16[16,3,64,256]{3,2,1,0:T(8,128)(2,1)} %bitcast.39), calls=%async_computation.2 | async-start | bytes 3145728 | tf_op jit(solution)/shard_map/all_to_all | solution.py:38
  114.5 1.1 copy-start.7
  120.2 1.1 copy-start.11
  145.7 1.2 copy-start.2
  146.9 3.9 %copy-start.13 = (bf16[384,64]{1,0:T(8,128)(2,1)S(1)}, bf16[384,64]{1,0:T(8,128)(2,1)}, u32[]{:S(2)}) copy-start(bf16[384,64]{1,0:T(8,128)(2,1)} %copy-done.12) | copy-start | bytes 147460
  146.9 3.9 %copy-start.3 = (bf16[16,3,64,256]{3,2,1,0:T(8,128)(2,1)S(1)}, bf16[16,3,64,256]{3,2,1,0:T(8,128)(2,1)}, u32[]{:S(2)}) copy-start(bf16[16,3,64,256]{3,2,1,0:T(8,128)(2,1)} %copy-done.2) | copy-start | bytes 4718596
  146.9 26.1 %all-to-all-start.3 = ((bf16[16,3,64,256]{3,2,1,0:T(8,128)(2,1)}), bf16[16,3,64,256]{3,2,1,0:T(8,128)(2,1)S(1)}, u32[]{:S(2)}, u32[]{:S(2)}) async-start(bf16[16,3,64,256]{3,2,1,0:T(8,128)(2,1)} %copy-done.11), calls=%async_computation.3 | async-start | bytes 3145728 | tf_op jit(solution)/shard_map/all_to_all | solution.py:38
  150.8 1.1 copy-start.8
  158.1 1.3 copy-start.10
  173.0 30.2 %all-to-all-start.4 = ((bf16[16,3,80,256]{3,2,1,0:T(8,128)(2,1)}), bf16[16,3,80,256]{3,2,1,0:T(8,128)(2,1)S(1)}, u32[]{:S(2)}, u32[]{:S(2)}) async-start(bf16[16,3,80,256]{3,2,1,0:T(8,128)(2,1)} %copy-done.10), calls=%async_computation.4 | async-start | bytes 3932160 | tf_op jit(solution)/shard_map/all_to_all | solution.py:38
  203.2 1.4 copy-start.6
  206.2 6.4 %copy-start.1 = (bf16[16,3,80,256]{3,2,1,0:T(8,128)(2,1)S(1)}, bf16[16,3,80,256]{3,2,1,0:T(8,128)(2,1)}, u32[]{:S(2)}) copy-start(bf16[16,3,80,256]{3,2,1,0:T(8,128)(2,1)} %copy-done) | copy-start | bytes 5898244
  206.2 6.4 %copy-start.4 = (bf16[16,3,64,256]{3,2,1,0:T(8,128)(2,1)S(1)}, bf16[16,3,64,256]{3,2,1,0:T(8,128)(2,1)}, u32[]{:S(2)}) copy-start(bf16[16,3,64,256]{3,2,1,0:T(8,128)(2,1)} %copy-done.2) | copy-start | bytes 4718596
  206.2 37.6 %all-to-all-start.5 = ((bf16[32,144,256]{2,1,0:T(8,128)(2,1)}), bf16[32,144,256]{2,1,0:T(8,128)(2,1)}, u32[]{:S(2)}, u32[]{:S(2)}) async-start(bf16[32,144,256]{2,1,0:T(8,128)(2,1)} %pad_maximum_fusion), calls=%async_computation.5 | async-start | bytes 4718592 | tf_op jit(solution)/shard_map/all_to_all | solution.py:38
  212.6 1.1 copy-start.9
  214.7 1.1 copy-start.17
  (6 other events, 4.9 us)
Sparse Core Ops, SparseCore 0:
  9.7 130.5 all-gather.1

commit v3 on v2

--- a/solution.py
+++ b/solution.py
@@ -10,11 +10,11 @@
 
 DP = ("y", "xh")
 FSDP = ("z", "xl", "c")
+X = ("xh", "xl")
 SCALE = 0.5
 PACK = 4
 F32 = jnp.float32
 BF16 = jnp.bfloat16
-after = lax.optimization_barrier
 
 
 def nt(a, b):
@@ -34,8 +34,16 @@
     return lax.ppermute(x, axis, [(i, (i + by) % n) for i in range(n)])
 
 
+def gate(x, *needed):
+    return lax.optimization_barrier((x, *needed))[0]
+
+
 def exchange(x, axis):
     return lax.all_to_all(x, axis, split_axis=0, concat_axis=0, tiled=True)
+
+
+def hbm(x):
+    return pltpu.with_memory_space_constraint(x, pltpu.HBM)
 
 
 def live_rows(fill_ref, b, rows):
@@ -106,29 +114,47 @@
                 g_ref[f, b, rank:, :] = pack(g[f * cols : (f + 1) * cols])
 
 
-def base_kernel(blocks, per, x_ref, dy_ref, w_ref, u_ref, v_ref, up_ref, a_ref, b_ref, y_ref, dx_ref, acc_ref):
+def base_kernel(blocks, pieces, f_ref, x_ref, dy_ref, u_ref, v_ref, up_ref, a_ref, b_ref, *refs):
+    w_refs, (y_ref, dx_ref, acc_ref, w_buf, sem) = refs[:pieces], refs[pieces:]
     rows = dy_ref.shape[0] // blocks
     rank = v_ref.shape[1]
     half = a_ref.shape[3]
-    step = pl.program_id(0)
+    step, steps = pl.program_id(0), pl.num_programs(0)
+    feats = w_buf.shape[1]
+    per = steps // pieces
+
+    def fetch(i):
+        for k, w_ref in enumerate(w_refs):
+
+            @pl.when(i // per == k)
+            def _():
+                at = pl.ds(pl.multiple_of(i % per * feats, feats), feats)
+                pltpu.make_async_copy(w_ref.at[at], w_buf.at[i % 2], sem.at[i % 2]).start()
 
     @pl.when(step == 0)
     def _():
         acc_ref[...] = jnp.zeros_like(acc_ref)
-
-    acc_ref[...] += nn(x_ref[...], w_ref[...])
-    wide = nt(dy_ref[...], w_ref[...])
+        fetch(step)
+
+    @pl.when(step + 1 < steps)
+    def _():
+        fetch(step + 1)
+
+    slot = step % 2
+    pltpu.make_async_copy(w_refs[0].at[pl.ds(0, feats)], w_buf.at[slot], sem.at[slot]).wait()
+    f = f_ref[step]
+    w = w_buf[slot]
+    acc_ref[...] += nn(x_ref[...], w)
+    wide = nt(dy_ref[...], w)
     for b in range(blocks):
         at = pl.ds(b * rows, rows)
         v = v_ref[at, :]
-        for j in range(per):
-            f = step * per + j
-            for k, low in ((2 * j, a_ref[f, b, :rank, :]), (2 * j + 1, b_ref[f, b])):
-                pulled = nn(v, low).astype(BF16).astype(F32)
-                own = wide[b * rows : (b + 1) * rows, k * half : (k + 1) * half]
-                dx_ref[at, pl.ds(k * half, half)] = (own + SCALE * pulled).astype(BF16)
-
-    @pl.when(step == pl.num_programs(0) - 1)
+        for k, low in enumerate((a_ref[f, b, :rank, :], b_ref[f, b])):
+            pulled = nn(v, low).astype(BF16).astype(F32)
+            own = wide[b * rows : (b + 1) * rows, k * half : (k + 1) * half]
+            dx_ref[at, pl.ds(k * half, half)] = (own + SCALE * pulled).astype(BF16)
+
+    @pl.when(step == steps - 1)
     def _():
         for b in range(blocks):
             at = pl.ds(b * rows, rows)
@@ -136,8 +162,9 @@
             y_ref[at, :] = (acc_ref[at, :] + SCALE * lifted).astype(BF16)
 
 
-def sum_kernel(ids_ref, g_ref, o_ref, acc_ref):
+def sum_kernel(ids_ref, to_ref, g_ref, *refs):
     members, blocks = g_ref.shape[:2]
+    acc_ref = refs[-1]
     acc_ref[...] = jnp.zeros_like(acc_ref)
 
     @pl.loop(0, members)
@@ -145,10 +172,18 @@
         for b in range(blocks):
             acc_ref[ids_ref[m, b]] += g_ref[m, b].astype(F32)
 
-    o_ref[...] = acc_ref[...].astype(BF16)
-
-
-PARAMS = pltpu.CompilerParams(vmem_limit_bytes=48 * 1024 * 1024)
+    if len(refs) == 2:
+        refs[0][...] = acc_ref[...].astype(BF16)
+    else:
+        for k, o_ref in enumerate(refs[:-1]):
+            slots = o_ref.shape[0]
+            o_ref[...] = acc_ref[pl.ds(to_ref[k] * slots, slots)].astype(BF16)
+
+
+def vmem(mib):
+    return pltpu.CompilerParams(vmem_limit_bytes=mib * 1024 * 1024)
+
+
 VMEM = pl.BlockSpec(memory_space=pltpu.VMEM)
 SMEM = pl.BlockSpec(memory_space=pltpu.SMEM)
 
@@ -159,21 +194,22 @@
 
 def whole(shape):
     zeros = (0,) * len(shape)
-    return pl.BlockSpec(shape, lambda i: zeros)
-
-
-def sum_blocks(ids_all, g, adapters):
+    return pl.BlockSpec(shape, lambda i, *_: zeros)
+
+
+def sum_blocks(ids_all, to, g, adapters, pieces):
     shape = (adapters,) + g.shape[2:]
+    piece = pltpu.HBM((adapters // pieces,) + g.shape[2:], BF16)
     return pl.pallas_call(
         sum_kernel,
-        in_specs=[SMEM, VMEM],
-        out_specs=VMEM,
-        out_shape=jax.ShapeDtypeStruct(shape, BF16),
+        in_specs=[SMEM, SMEM, VMEM],
+        out_specs=[VMEM] * pieces,
+        out_shape=[piece] * pieces,
         scratch_shapes=[pltpu.VMEM(shape, F32)],
-        compiler_params=PARAMS,
+        compiler_params=vmem(12),
         cost_estimate=cost(g.size, 4 * g.size),
         name="sum_blocks",
-    )(ids_all, g)
+    )(ids_all, to, g)
 
 
 def body(tokens, weight, down, up, dy, ids, fill):
@@ -187,9 +223,10 @@
     steps = lax.axis_size(FSDP)
     adapters = slots * ys * xhs
     y_at, xh_at = lax.axis_index("y"), lax.axis_index("xh")
+    z_at, xl_at, c_at = (lax.axis_index(a) for a in FSDP)
     up_rows = cols // PACK
 
-    w_full = lax.all_gather(weight, FSDP, axis=0, tiled=True)
+    w_back, w_next = shift(weight, "z", 1), shift(weight, "z", -1)
 
     ids_out = jnp.broadcast_to(jnp.pad(ids, (0, 128 - blocks)), (steps, 8, 128))
     ids_all = exchange(ids_out, FSDP)[:, 0, :blocks]
@@ -209,12 +246,8 @@
     def over_x(x):
         return jnp.stack([x, shift(x, "xh", 1)])
 
-    x_a = over_x(own_a)
-    own_b, x_a = after((own_b, x_a))
-    x_b = over_x(own_b)
+    x_a = over_x(gate(own_a, ids_out))
     all_a = over_y(x_a)
-    x_b, all_a = after((x_b, all_a))
-    all_b = over_y(x_b)
 
     want = ids_all.reshape(steps * blocks)
     owner = want // slots
@@ -224,10 +257,20 @@
     def pick(x):
         return x.reshape(adapters, *x.shape[3:])[at].reshape(steps, blocks, *x.shape[3:])
 
-    pick_a = pick(all_a)
-    all_b, pick_a = after((all_b, pick_a))
+    pick_a = pick(gate(all_a, w_back, w_next))
     low_a = exchange(pick_a, FSDP)
-    low_b = exchange(pick(all_b), FSDP)
+    x_b = over_x(gate(own_b, x_a))
+    all_b = over_y(gate(x_b, pick_a))
+    pick_b = pick(all_b)
+    low_b = exchange(pick_b, FSDP)
+
+    mid = feats // 2
+    w_lo = shift(gate(w_back, pick_a)[:mid], "z", 1)
+    w_hi = shift(gate(w_next, pick_a)[mid:], "z", -1)
+    near = jnp.concatenate([weight, w_next])
+    far = jnp.concatenate([w_back, w_lo, w_hi])
+    low_a, near, far = lax.optimization_barrier((low_a, near, far, pick_b))[:3]
+    near_x, far_x = shift(near, X, 1), shift(far, X, -1)
 
     grid = 4
     per = steps // grid
@@ -242,16 +285,16 @@
             pl.BlockSpec((per, blocks, rank, half), lambda i: (i, 0, 0, 0)),
         ],
         out_shape=[
-            jax.ShapeDtypeStruct((rows_dev, rank), BF16),
-            jax.ShapeDtypeStruct((blocks, value, rank), BF16),
-            jax.ShapeDtypeStruct((steps, blocks, rank, half), BF16),
+            pltpu.HBM((rows_dev, rank), BF16),
+            pltpu.HBM((blocks, value, rank), BF16),
+            pltpu.HBM((steps, blocks, rank, half), BF16),
         ],
-        compiler_params=PARAMS,
+        compiler_params=vmem(16),
         cost_estimate=cost(rows_dev * rank * (width + 2 * value), 12 << 20),
         name="first",
-    )(fill, tokens, dy, low_a)
-    grad_a, low_b = after((grad_a, low_b))
-    back_a = exchange(grad_a, FSDP)
+    )(fill, hbm(tokens), hbm(dy), low_a)
+    near, far = lax.optimization_barrier((near, far, low_b))[:2]
+    back_a = exchange(gate(grad_a, low_b), FSDP)
 
     low_u, grad_b = pl.pallas_call(
         functools.partial(second_kernel, blocks, per),
@@ -259,53 +302,75 @@
         in_specs=[SMEM, x_spec, whole(dy.shape), whole(low_v.shape), whole(low_a.shape), whole(low_b.shape)],
         out_specs=[whole((rows_dev, rank)), whole((steps, blocks, rank + up_rows, half))],
         out_shape=[
-            jax.ShapeDtypeStruct((rows_dev, rank), BF16),
-            jax.ShapeDtypeStruct((steps, blocks, rank + up_rows, half), BF16),
+            pltpu.HBM((rows_dev, rank), BF16),
+            pltpu.HBM((steps, blocks, rank + up_rows, half), BF16),
         ],
         scratch_shapes=[pltpu.VMEM((rows_dev, rank), F32)],
-        compiler_params=PARAMS,
+        compiler_params=vmem(20),
         cost_estimate=cost(rows_dev * rank * (3 * width + 2 * value), 14 << 20),
         name="second",
-    )(fill, tokens, dy, low_v, low_a, low_b)
-    grad_b, back_a = after((grad_b, back_a))
-    back_b = exchange(grad_b, FSDP)
-
-    sums = jnp.concatenate(
-        [sum_blocks(ids_all, back_a, adapters), sum_blocks(ids_all, back_b, adapters)], axis=1
-    )
-    part = exchange(sums, DP)
-
-    grid = 8
-    per = steps // grid
-    x_spec = pl.BlockSpec((rows_dev, per * feats), lambda i: (0, i))
+    )(fill, hbm(tokens), hbm(dy), hbm(low_v), low_a, low_b)
+    back_b = exchange(gate(grad_b, back_a), FSDP)
+    w_own = [near, far, near_x, far_x]
+    w_other = [shift(w, "c", 1) for w in (near, far, gate(near_x, low_u), gate(far_x, low_u))]
+    w_all = w_own + w_other
+    order = [
+        (z_at + dz) % 4 * 4 + (xl_at + dx) % 2 * 2 + (c_at + dc) % 2
+        for dc in (0, 1)
+        for dx in (0, 1)
+        for dz in (0, 1, 3, 2)
+    ]
+
+    peers = [(i, j) for i in range(ys) for j in range(xhs)]
+    to = jnp.stack([(y_at + i) % ys * xhs + (xh_at + j) % xhs for i, j in peers])
+    sums = sum_blocks(ids_all, to, gate(back_a, *w_other), adapters, len(peers))
+    part_a = [sums[0]]
+    for (i, j), piece in zip(peers[1:], sums[1:]):
+        moves = [(a * xhs + b, (a + i) % ys * xhs + (b + j) % xhs) for a, b in peers]
+        part_a.append(lax.ppermute(piece, DP, moves))
+
     values, input_gradient = pl.pallas_call(
-        functools.partial(base_kernel, blocks, per),
-        grid=(grid,),
-        in_specs=[
-            x_spec,
-            whole(dy.shape),
-            pl.BlockSpec((per * feats, value), lambda i: (i, 0)),
-            whole(low_u.shape),
-            whole(low_v.shape),
-            whole(up_mine.shape),
-            whole(low_a.shape),
-            whole(low_b.shape),
-        ],
-        out_specs=[whole((rows_dev, value)), x_spec],
-        out_shape=[
-            jax.ShapeDtypeStruct((rows_dev, value), BF16),
-            jax.ShapeDtypeStruct((rows_dev, width), BF16),
-        ],
-        scratch_shapes=[pltpu.VMEM((rows_dev, value), F32)],
-        compiler_params=PARAMS,
+        functools.partial(base_kernel, blocks, len(w_all)),
+        grid_spec=pltpu.PrefetchScalarGridSpec(
+            num_scalar_prefetch=1,
+            grid=(steps,),
+            in_specs=[
+                pl.BlockSpec((rows_dev, feats), lambda i, f: (0, f[i])),
+                whole(dy.shape),
+                whole(low_u.shape),
+                whole(low_v.shape),
+                whole(up_mine.shape),
+                whole(low_a.shape),
+                whole(low_b.shape),
+            ]
+            + [pl.BlockSpec(memory_space=pltpu.HBM)] * len(w_all),
+            out_specs=[
+                whole((rows_dev, value)),
+                pl.BlockSpec((rows_dev, feats), lambda i, f: (0, f[i])),
+            ],
+            scratch_shapes=[
+                pltpu.VMEM((rows_dev, value), F32),
+                pltpu.VMEM((2, feats, value), BF16),
+                pltpu.SemaphoreType.DMA((2,)),
+            ],
+        ),
+        out_shape=[pltpu.HBM((rows_dev, value), BF16), pltpu.HBM((rows_dev, width), BF16)],
+        compiler_params=vmem(28),
         cost_estimate=cost(4 * rows_dev * width * value, 36 << 20),
         name="base",
-    )(tokens, dy, w_full, low_u, low_v, up_mine, low_a, low_b)
-
-    part, values, input_gradient = after((part, values, input_gradient))
-    total = SCALE * part.reshape(ys * xhs, slots, -1, half).astype(F32).sum(0)
-    grad_down = jnp.concatenate([total[:, :rank], total[:, rank : 2 * rank]], axis=2)
-    grad_up = total[:, 2 * rank :].reshape(slots, up_rows, PACK, rank)
+    )(
+        jnp.stack(order),
+        *(hbm(a) for a in (tokens, dy, low_u, low_v, up_mine)),
+        low_a,
+        low_b,
+        *(hbm(a) for a in w_all),
+    )
+
+    sum_b = sum_blocks(ids_all, to, gate(back_b, *part_a), adapters, 1)[0]
+    part_b = gate(exchange(sum_b, DP), values).reshape(ys * xhs, slots, -1, half).astype(F32)
+    total_a, total_b = SCALE * sum(p.astype(F32) for p in part_a), SCALE * part_b.sum(0)
+    grad_down = jnp.concatenate([total_a, total_b[:, :rank]], axis=2)
+    grad_up = total_b[:, rank:].reshape(slots, up_rows, PACK, rank)
     grad_up = jnp.transpose(grad_up, (0, 3, 2, 1)).reshape(slots, rank, cols)
     return values, input_gradient, jnp.swapaxes(grad_down, 1, 2), grad_up
 

time: 256 us -> 273 us (1.066)
  starting transfers between devices: 50 us -> 67.7 us
  between operations: 14.4 us -> 1.13 us
  Pallas kernels: 33.4 us -> 44.1 us
  local copies, waits for them, and re-layouts: 20.8 us -> 14.5 us
  other arithmetic: 5.04 us -> 11 us
    all_to_all x6, waiting for transfers between devices: 116 us -> 27.6 us  [exchange(): return lax.all_to_all(x, axis, split_axis=0, concat_axis=0, tiled=True)]
    ppermute x10 -> x20, waiting for transfers between devices: 14 us -> 78.8 us  [shift(): return lax.ppermute(x, axis, [(i, (i + by) % n) for i in range(n)])]
    ppermute x0 -> x7, waiting for transfers between devices: none -> 25.1 us  [body(): part_a.append(lax.ppermute(piece, DP, moves))]
    ppermute x0 -> x7, starting transfers between devices: none -> 11.1 us  [body(): part_a.append(lax.ppermute(piece, DP, moves))]
    unnamed x44 -> x38, local copies, waits for them, and re-layouts: 14.8 us -> 4.99 us
    pallas_call x3, Pallas kernels: 22.7 us -> 31.3 us  [the longest x1 25.6 us: body(): pl.pallas_call(functools.partial(base_kernel, blocks, len(w_all)), grid_s...]
    ppermute x10 -> x20, starting transfers between devices: 20.5 us -> 28.6 us  [shift(): return lax.ppermute(x, axis, [(i, (i + by) % n) for i in range(n)])]
    concatenate x1 -> x3, other arithmetic: 1.61 us -> 5.98 us  [the longest x1 3.14 us: body(): near = jnp.concatenate([weight, w_next])]
  transfers between devices with their start and end apart: 17 -> 33, of which waited for: 11 -> 13; matrix products, arithmetic and copies ran while one was open for 3% -> 5% of each run, Pallas kernels for 13% -> 15%
where the time goes in v3:
time: 273 us; the launch traced here: 270 us
  waiting for transfers between devices  132 us (48%)
  starting transfers between devices  67.7 us (25%)
  Pallas kernels  44.1 us (16%)
  local copies, waits for them, and re-layouts  14.5 us (5%)
  other arithmetic  11 us (4%)
    ppermute x20, waiting for transfers between devices, shift(): return lax.ppermute(x, axis, [(i, (i + by) % n) for i in range(n)])  78.8 us
    ppermute x20, starting transfers between devices, shift(): return lax.ppermute(x, axis, [(i, (i + by) % n) for i in range(n)])  28.6 us
    all_to_all x6, starting transfers between devices, exchange(): return lax.all_to_all(x, axis, split_axis=0, concat_axis=0, tiled=True)  28 us
    all_to_all x6, waiting for transfers between devices, exchange(): return lax.all_to_all(x, axis, split_axis=0, concat_axis=0, tiled=True)  27.6 us
    pallas_call x1, Pallas kernels, body(): pl.pallas_call(functools.partial(base_kernel, blocks, len(w_all)), grid_s...  25.6 us
    ppermute x7, waiting for transfers between devices, body(): part_a.append(lax.ppermute(piece, DP, moves))  25.1 us
    ppermute x7, starting transfers between devices, body(): part_a.append(lax.ppermute(piece, DP, moves))  11.1 us
    pallas_call x1, Pallas kernels, body(): pl.pallas_call(functools.partial(second_kernel, blocks, per), grid=(grid,...  7.06 us
  transfers between devices with their start and end apart: 33, of which 13 were waited for; matrix products, arithmetic and copies ran while one was open for 5% of the time, Pallas kernels for 15%

profile of v3, /device:TPU:0, one launch (start us, length us, event | category | flops | bytes accessed | tf_op | source)
XLA Modules:
  0.0 269.9 jit_solution(2040012165010678903)
XLA Ops:
  4.0 3.1 %collective-permute-start = (bf16[4,80,256]{2,1,0:T(8,128)(2,1)S(1)}, bf16[4,80,256]{2,1,0:T(8,128)(2,1)S(1)}, u32[]{:S(2)}, u32[]{:S(2)}) collective-permute-start(bf16[4,80,256]{2,1,0:T(8,128)(2,1)S(1)} %pad_maximum_fusion.6), channel_id=1, source_target_pairs={{0,16},{16,0},{1,17},{17,1},{2,18},{18,2},{3,19},{19,3},{4,20},{20... | collective-permute-start | bytes 491528 | tf_op jit(solution)/shard_map/ppermute | solution.py:34
  7.1 1.9 collective-permute-start.5
  9.0 2.1 collective-permute-start.6
  14.8 6.5 %all-to-all-start = ((s32[16,8,128]{2,1,0:T(8,128)}), s32[16,8,128]{2,1,0:T(8,128)S(1)}, u32[]{:S(2)}, u32[]{:S(2)}) async-start(s32[16,8,128]{2,1,0:T(8,128)} %broadcast_in_dim.2), calls=%async_computation | async-start | bytes 131072 | tf_op jit(solution)/shard_map/all_to_all | solution.py:42
  21.3 14.8 %all-to-all-done = s32[16,8,128]{2,1,0:T(8,128)S(1)} async-done(((s32[16,8,128]{2,1,0:T(8,128)}), s32[16,8,128]{2,1,0:T(8,128)S(1)}, u32[]{:S(2)}, u32[]{:S(2)}) %all-to-all-start) | async-done | bytes 65568 | tf_op jit(solution)/shard_map/all_to_all | solution.py:42
  39.6 4.1 %collective-permute-done.2 = bf16[2,2,80,256]{3,2,1,0:T(8,128)(2,1)S(1)} collective-permute-done((bf16[2,2,80,256]{3,2,1,0:T(8,128)(2,1)S(1)}, bf16[2,2,80,256]{3,2,1,0:T(8,128)(2,1)S(1)}, u32[]{:S(2)}, u32[]{:S(2)}) %collective-permute-start.2) | collective-permute-done | bytes 163872 | tf_op jit(solution)/shard_map/ppermute | solution.py:34
  45.1 2.0 gather_fusion
  47.1 3.7 %all-to-all-start.1 = ((bf16[16,3,80,256]{3,2,1,0:T(8,128)(2,1)}), bf16[16,3,80,256]{3,2,1,0:T(8,128)(2,1)S(1)}, u32[]{:S(2)}, u32[]{:S(2)}) async-start(bf16[16,3,80,256]{3,2,1,0:T(8,128)(2,1)} %bitcast.62), calls=%async_computation.1 | async-start | bytes 3932160 | tf_op jit(solution)/shard_map/all_to_all | solution.py:42
  52.5 26.7 %collective-permute-done.9 = bf16[4,64,256]{2,1,0:T(8,128)(2,1)S(1)} collective-permute-done((bf16[4,64,256]{2,1,0:T(8,128)(2,1)S(1)}, bf16[4,64,256]{2,1,0:T(8,128)(2,1)S(1)}, u32[]{:S(2)}, u32[]{:S(2)}) %collective-permute-start.9) | collective-permute-done | bytes 131104 | tf_op jit(solution)/shard_map/ppermute | solution.py:34
  82.5 6.1 %collective-permute-done.10 = bf16[2,4,64,256]{3,2,1,0:T(8,128)(2,1)S(1)} collective-permute-done((bf16[2,4,64,256]{3,2,1,0:T(8,128)(2,1)S(1)}, bf16[2,4,64,256]{3,2,1,0:T(8,128)(2,1)S(1)}, u32[]{:S(2)}, u32[]{:S(2)}) %collective-permute-start.10) | collective-permute-done | bytes 262176 | tf_op jit(solution)/shard_map/ppermute | solution.py:34
  89.1 3.0 %collective-permute-start.13 = (bf16[2,2,64,256]{3,2,1,0:T(8,128)(2,1)S(1)}, bf16[2,2,64,256]{3,2,1,0:T(8,128)(2,1)S(1)}, u32[]{:S(2)}, u32[]{:S(2)}) collective-permute-start(bf16[2,2,64,256]{3,2,1,0:T(8,128)(2,1)S(1)} %slice.54), channel_id=1, source_target_pairs={{0,96},{32,0},{64,32},{96,64},{1,97},{33,1},{65,33},{97,65},{2,98}... | collective-permute-start | bytes 393224 | tf_op jit(solution)/shard_map/ppermute | solution.py:34
  94.8 3.1 %collective-permute-start.8 = (bf16[256,1024]{1,0:T(8,128)(2,1)}, bf16[256,1024]{1,0:T(8,128)(2,1)}, u32[]{:S(2)}, u32[]{:S(2)}) collective-permute-start(bf16[256,1024]{1,0:T(8,128)(2,1)} %slice.38), channel_id=1, source_target_pairs={{0,12},{4,0},{8,4},{12,8},{1,13},{5,1},{9,5},{13,9},{2,14},{6,2},{... | collective-permute-start | bytes 1572872 | tf_op jit(solution)/shard_map/ppermute | solution.py:34
  100.0 3.7 %all-to-all-start.2 = ((bf16[16,3,64,256]{3,2,1,0:T(8,128)(2,1)}), bf16[16,3,64,256]{3,2,1,0:T(8,128)(2,1)S(1)}, u32[]{:S(2)}, u32[]{:S(2)}) async-start(bf16[16,3,64,256]{3,2,1,0:T(8,128)(2,1)} %bitcast.64), calls=%async_computation.2 | async-start | bytes 3145728 | tf_op jit(solution)/shard_map/all_to_all | solution.py:42
  103.7 3.1 %pad_maximum_fusion.refs_0_ = bf16[1024,1024]{1,0:T(8,128)(2,1)} fusion(bf16[512,1024]{1,0:T(8,128)(2,1)} %collective-permute-done.6, bf16[512,1024]{1,0:T(8,128)(2,1)} %param.8), kind=kLoop, calls=%fused_computation.3 | loop fusion | flops 4194304 | bytes 4194304 | tf_op jit(solution)/shard_map/concatenate | solution.py:270
  106.9 15.8 %collective-permute-done.8 = bf16[256,1024]{1,0:T(8,128)(2,1)} collective-permute-done((bf16[256,1024]{1,0:T(8,128)(2,1)}, bf16[256,1024]{1,0:T(8,128)(2,1)}, u32[]{:S(2)}, u32[]{:S(2)}) %collective-permute-start.8) | collective-permute-done | bytes 524320 | tf_op jit(solution)/shard_map/ppermute | solution.py:34
  122.7 2.8 %pad_maximum_fusion.1.refs_1_ = bf16[1024,1024]{1,0:T(8,128)(2,1)} fusion(bf16[256,1024]{1,0:T(8,128)(2,1)} %collective-permute-done.8, bf16[256,1024]{1,0:T(8,128)(2,1)} %collective-permute-done.7, bf16[512,1024]{1,0:T(8,128)(2,1)S(1)} %copy-done.5), kind=kLoop, calls=%fused_computation.4 | loop fusion | flops 6291456 | bytes 4194304 | tf_op jit(solution)/shard_map/concatenate | solution.py:271
  127.5 5.8 %first.1 = (bf16[384,64]{1,0:T(8,128)(2,1)}, bf16[3,1024,64]{2,1,0:T(8,128)(2,1)}, bf16[16,3,64,256]{3,2,1,0:T(8,128)(2,1)}) custom-call(s32[3]{0:T(128)S(1)} %copy-done.3, bf16[384,8192]{1,0:T(8,128)(2,1)} %x_ref.5, bf16[384,1024]{1,0:T(8,128)(2,1)} %dy_ref.5, bf16[16,3,80,256]{3,2,1,0:T(8,128)(2,1)S(1)} %all-to-all-done.1.a_ref), custom_call_target="tpu_custom_call" | custom-call | flops 251658240 | bytes 12582912 | tf_op jit(solution)/shard_map/first/pallas_call | solution.py:278
  134.4 5.0 %all-to-all-start.3 = ((bf16[16,3,64,256]{3,2,1,0:T(8,128)(2,1)}), bf16[16,3,64,256]{3,2,1,0:T(8,128)(2,1)S(1)}, u32[]{:S(2)}, u32[]{:S(2)}) async-start(bf16[16,3,64,256]{3,2,1,0:T(8,128)(2,1)} %get-tuple-element.56), calls=%async_computation.3 | async-start | bytes 3145728 | tf_op jit(solution)/shard_map/all_to_all | solution.py:42
  141.5 7.1 %second.1 = (bf16[384,64]{1,0:T(8,128)(2,1)}, bf16[16,3,80,256]{3,2,1,0:T(8,128)(2,1)}) custom-call(s32[3]{0:T(128)S(1)} %copy-done.3, bf16[384,8192]{1,0:T(8,128)(2,1)} %x_ref.5, bf16[384,1024]{1,0:T(8,128)(2,1)} %dy_ref.5, bf16[384,64]{1,0:T(8,128)(2,1)} %get-tuple-element.44.v_ref, bf16[16,3,80,256]{3,2,1,0:T(8,128)(2,1)S(1)} %all-to-all-done.1.a_ref, ...), custom_call_target="tpu_custom_call" | custom-call | flops 654311424 | bytes 14680064 | tf_op jit(solution)/shard_map/second/pallas_call | solution.py:299
  148.5 25.8 %collective-permute-done.15.refs_3_ = bf16[1024,1024]{1,0:T(8,128)(2,1)} collective-permute-done((bf16[1024,1024]{1,0:T(8,128)(2,1)}, bf16[1024,1024]{1,0:T(8,128)(2,1)}, u32[]{:S(2)}, u32[]{:S(2)}) %collective-permute-start.15) | collective-permute-done | bytes 2097184 | tf_op jit(solution)/shard_map/ppermute | solution.py:34
  174.9 12.8 %all-to-all-done.3.g_ref = bf16[16,3,64,256]{3,2,1,0:T(8,128)(2,1)S(1)} async-done(((bf16[16,3,64,256]{3,2,1,0:T(8,128)(2,1)}), bf16[16,3,64,256]{3,2,1,0:T(8,128)(2,1)S(1)}, u32[]{:S(2)}, u32[]{:S(2)}) %all-to-all-start.3) | async-done | bytes 1572896 | tf_op jit(solution)/shard_map/all_to_all | solution.py:42
  187.7 4.6 %all-to-all-start.4 = ((bf16[16,3,80,256]{3,2,1,0:T(8,128)(2,1)}), bf16[16,3,80,256]{3,2,1,0:T(8,128)(2,1)}, u32[]{:S(2)}, u32[]{:S(2)}) async-start(bf16[16,3,80,256]{3,2,1,0:T(8,128)(2,1)} %get-tuple-element.67), calls=%async_computation.4 | async-start | bytes 3932160 | tf_op jit(solution)/shard_map/all_to_all | solution.py:42
  192.5 2.3 sum_blocks.2
  194.8 2.6 collective-permute-start.20
  198.2 4.3 %collective-permute-start.23 = (bf16[4,64,256]{2,1,0:T(8,128)(2,1)}, bf16[4,64,256]{2,1,0:T(8,128)(2,1)S(1)}, u32[]{:S(2)}, u32[]{:S(2)}) collective-permute-start(bf16[4,64,256]{2,1,0:T(8,128)(2,1)} %get-tuple-element.62), channel_id=1, source_target_pairs={{0,64},{16,80},{32,96},{48,112},{64,0},{80,16},{96,32},{112,48},{1... | collective-permute-start | bytes 393224 | tf_op jit(solution)/shard_map/ppermute | solution.py:330
  202.5 2.0 collective-permute-start.24
  204.5 17.3 %collective-permute-done.20 = bf16[4,64,256]{2,1,0:T(8,128)(2,1)} collective-permute-done((bf16[4,64,256]{2,1,0:T(8,128)(2,1)}, bf16[4,64,256]{2,1,0:T(8,128)(2,1)}, u32[]{:S(2)}, u32[]{:S(2)}) %collective-permute-start.20) | collective-permute-done | bytes 131104 | tf_op jit(solution)/shard_map/ppermute | solution.py:330
  223.3 2.4 collective-permute-done.22
  227.5 3.6 %collective-permute-done.25 = bf16[4,64,256]{2,1,0:T(8,128)(2,1)S(1)} collective-permute-done((bf16[4,64,256]{2,1,0:T(8,128)(2,1)}, bf16[4,64,256]{2,1,0:T(8,128)(2,1)S(1)}, u32[]{:S(2)}, u32[]{:S(2)}) %collective-permute-start.25) | collective-permute-done | bytes 131104 | tf_op jit(solution)/shard_map/ppermute | solution.py:330
  231.8 3.4 %sum_blocks.3 = bf16[32,80,256]{2,1,0:T(8,128)(2,1)} custom-call(s32[16,3]{1,0:T(8,128)S(1)} %bitcast.60, s32[8]{0:T(128)S(1)} %stack.167.to_ref, bf16[16,3,80,256]{3,2,1,0:T(8,128)(2,1)} %all-to-all-done.4.g_ref), custom_call_target="tpu_custom_call" | custom-call | flops 983040 | bytes 3932160 | tf_op jit(solution)/shard_map/sum_blocks/pallas_call | solution.py:203
  235.2 4.4 %all-to-all-start.5 = ((bf16[32,80,256]{2,1,0:T(8,128)(2,1)}), bf16[32,80,256]{2,1,0:T(8,128)(2,1)}, u32[]{:S(2)}, u32[]{:S(2)}) async-start(bf16[32,80,256]{2,1,0:T(8,128)(2,1)} %sum_blocks.3), calls=%async_computation.5 | async-start | bytes 2621440 | tf_op jit(solution)/shard_map/all_to_all | solution.py:42
  239.7 25.6 %base.1 = (bf16[384,1024]{1,0:T(8,128)(2,1)}, bf16[384,8192]{1,0:T(8,128)(2,1)}) custom-call(s32[16]{0:T(128)S(1)} %stack.142.f_ref, bf16[384,8192]{1,0:T(8,128)(2,1)} %x_ref.5, bf16[384,1024]{1,0:T(8,128)(2,1)} %dy_ref.5, bf16[384,64]{1,0:T(8,128)(2,1)} %get-tuple-element.45.u_ref, bf16[384,64]{1,0:T(8,128)(2,1)} %get-tuple-element.44.v_ref, ...), custom_call_target="tpu_custom_call" | custom-call | flops 12884901888 | bytes 37748736 | tf_op jit(solution)/shard_map/base/pallas_call | solution.py:332
  (113 shorter events, 37.1 us)
Async XLA Ops:
  4.0 7.3 %collective-permute-start = (bf16[4,80,256]{2,1,0:T(8,128)(2,1)S(1)}, bf16[4,80,256]{2,1,0:T(8,128)(2,1)S(1)}, u32[]{:S(2)}, u32[]{:S(2)}) collective-permute-start(bf16[4,80,256]{2,1,0:T(8,128)(2,1)S(1)} %pad_maximum_fusion.6), channel_id=1, source_target_pairs={{0,16},{16,0},{1,17},{17,1},{2,18},{18,2},{3,19},{19,3},{4,20},{20... | collective-permute-start | bytes 491528 | tf_op jit(solution)/shard_map/ppermute | solution.py:34
  7.1 37.9 %collective-permute-start.5 = (bf16[512,1024]{1,0:T(8,128)(2,1)}, bf16[512,1024]{1,0:T(8,128)(2,1)S(1)}, u32[]{:S(2)}, u32[]{:S(2)}) collective-permute-start(bf16[512,1024]{1,0:T(8,128)(2,1)} %param.8), channel_id=1, source_target_pairs={{0,4},{4,8},{8,12},{12,0},{1,5},{5,9},{9,13},{13,1},{2,6},{6,10},{... | collective-permute-start | bytes 3145736 | tf_op jit(solution)/shard_map/ppermute | solution.py:34
  9.0 36.0 %collective-permute-start.6 = (bf16[512,1024]{1,0:T(8,128)(2,1)}, bf16[512,1024]{1,0:T(8,128)(2,1)}, u32[]{:S(2)}, u32[]{:S(2)}) collective-permute-start(bf16[512,1024]{1,0:T(8,128)(2,1)} %param.8), channel_id=1, source_target_pairs={{0,12},{4,0},{8,4},{12,8},{1,13},{5,1},{9,5},{13,9},{2,14},{6,2},{... | collective-permute-start | bytes 3145736 | tf_op jit(solution)/shard_map/ppermute | solution.py:34
  11.4 24.8 %collective-permute-start.1 = (bf16[2,4,80,256]{3,2,1,0:T(8,128)(2,1)S(1)}, bf16[2,4,80,256]{3,2,1,0:T(8,128)(2,1)S(1)}, u32[]{:S(2)}, u32[]{:S(2)}) collective-permute-start(bf16[2,4,80,256]{3,2,1,0:T(8,128)(2,1)S(1)} %get-tuple-element.83), channel_id=1, source_target_pairs={{0,32},{32,64},{64,96},{96,0},{1,33},{33,65},{65,97},{97,1},{2,34}... | collective-permute-start | bytes 983048 | tf_op jit(solution)/shard_map/ppermute | solution.py:34
  13.2 24.6 %collective-permute-start.3 = (bf16[2,4,80,256]{3,2,1,0:T(8,128)(2,1)S(1)}, bf16[2,4,80,256]{3,2,1,0:T(8,128)(2,1)S(1)}, u32[]{:S(2)}, u32[]{:S(2)}) collective-permute-start(bf16[2,4,80,256]{3,2,1,0:T(8,128)(2,1)S(1)} %get-tuple-element.83), channel_id=1, source_target_pairs={{0,96},{32,0},{64,32},{96,64},{1,97},{33,1},{65,33},{97,65},{2,98}... | collective-permute-start | bytes 983048 | tf_op jit(solution)/shard_map/ppermute | solution.py:34
  14.8 21.3 %all-to-all-start = ((s32[16,8,128]{2,1,0:T(8,128)}), s32[16,8,128]{2,1,0:T(8,128)S(1)}, u32[]{:S(2)}, u32[]{:S(2)}) async-start(s32[16,8,128]{2,1,0:T(8,128)} %broadcast_in_dim.2), calls=%async_computation | async-start | bytes 131072 | tf_op jit(solution)/shard_map/all_to_all | solution.py:42
  36.2 7.6 %collective-permute-start.2 = (bf16[2,2,80,256]{3,2,1,0:T(8,128)(2,1)S(1)}, bf16[2,2,80,256]{3,2,1,0:T(8,128)(2,1)S(1)}, u32[]{:S(2)}, u32[]{:S(2)}) collective-permute-start(bf16[2,2,80,256]{3,2,1,0:T(8,128)(2,1)S(1)} %slice.49), channel_id=1, source_target_pairs={{0,32},{32,64},{64,96},{96,0},{1,33},{33,65},{65,97},{97,1},{2,34}... | collective-permute-start | bytes 491528 | tf_op jit(solution)/shard_map/ppermute | solution.py:34
  47.1 52.9 %all-to-all-start.1 = ((bf16[16,3,80,256]{3,2,1,0:T(8,128)(2,1)}), bf16[16,3,80,256]{3,2,1,0:T(8,128)(2,1)S(1)}, u32[]{:S(2)}, u32[]{:S(2)}) async-start(bf16[16,3,80,256]{3,2,1,0:T(8,128)(2,1)} %bitcast.62), calls=%async_computation.1 | async-start | bytes 3932160 | tf_op jit(solution)/shard_map/all_to_all | solution.py:42
  50.8 28.3 %collective-permute-start.9 = (bf16[4,64,256]{2,1,0:T(8,128)(2,1)S(1)}, bf16[4,64,256]{2,1,0:T(8,128)(2,1)S(1)}, u32[]{:S(2)}, u32[]{:S(2)}) collective-permute-start(bf16[4,64,256]{2,1,0:T(8,128)(2,1)S(1)} %get-tuple-element.41), channel_id=1, source_target_pairs={{0,16},{16,0},{1,17},{17,1},{2,18},{18,2},{3,19},{19,3},{4,20},{20... | collective-permute-start | bytes 393224 | tf_op jit(solution)/shard_map/ppermute | solution.py:34
  79.2 9.4 %collective-permute-start.10 = (bf16[2,4,64,256]{3,2,1,0:T(8,128)(2,1)S(1)}, bf16[2,4,64,256]{3,2,1,0:T(8,128)(2,1)S(1)}, u32[]{:S(2)}, u32[]{:S(2)}) collective-permute-start(bf16[2,4,64,256]{3,2,1,0:T(8,128)(2,1)S(1)} %pad_maximum_fusion.5), channel_id=1, source_target_pairs={{0,32},{32,64},{64,96},{96,0},{1,33},{33,65},{65,97},{97,1},{2,34}... | collective-permute-start | bytes 786440 | tf_op jit(solution)/shard_map/ppermute | solution.py:34
  80.8 8.2 %collective-permute-start.12 = (bf16[2,4,64,256]{3,2,1,0:T(8,128)(2,1)S(1)}, bf16[2,4,64,256]{3,2,1,0:T(8,128)(2,1)S(1)}, u32[]{:S(2)}, u32[]{:S(2)}) collective-permute-start(bf16[2,4,64,256]{3,2,1,0:T(8,128)(2,1)S(1)} %pad_maximum_fusion.5), channel_id=1, source_target_pairs={{0,96},{32,0},{64,32},{96,64},{1,97},{33,1},{65,33},{97,65},{2,98}... | collective-permute-start | bytes 786440 | tf_op jit(solution)/shard_map/ppermute | solution.py:34
  88.6 9.3 %collective-permute-start.11 = (bf16[2,2,64,256]{3,2,1,0:T(8,128)(2,1)S(1)}, bf16[2,2,64,256]{3,2,1,0:T(8,128)(2,1)S(1)}, u32[]{:S(2)}, u32[]{:S(2)}) collective-permute-start(bf16[2,2,64,256]{3,2,1,0:T(8,128)(2,1)S(1)} %slice.53), channel_id=1, source_target_pairs={{0,32},{32,64},{64,96},{96,0},{1,33},{33,65},{65,97},{97,1},{2,34}... | collective-permute-start | bytes 393224 | tf_op jit(solution)/shard_map/ppermute | solution.py:34
  89.1 8.9 %collective-permute-start.13 = (bf16[2,2,64,256]{3,2,1,0:T(8,128)(2,1)S(1)}, bf16[2,2,64,256]{3,2,1,0:T(8,128)(2,1)S(1)}, u32[]{:S(2)}, u32[]{:S(2)}) collective-permute-start(bf16[2,2,64,256]{3,2,1,0:T(8,128)(2,1)S(1)} %slice.54), channel_id=1, source_target_pairs={{0,96},{32,0},{64,32},{96,64},{1,97},{33,1},{65,33},{97,65},{2,98}... | collective-permute-start | bytes 393224 | tf_op jit(solution)/shard_map/ppermute | solution.py:34
  92.9 14.0 %collective-permute-start.7 = (bf16[256,1024]{1,0:T(8,128)(2,1)}, bf16[256,1024]{1,0:T(8,128)(2,1)}, u32[]{:S(2)}, u32[]{:S(2)}) collective-permute-start(bf16[256,1024]{1,0:T(8,128)(2,1)} %slice.37), channel_id=1, source_target_pairs={{0,4},{4,8},{8,12},{12,0},{1,5},{5,9},{9,13},{13,1},{2,6},{6,10},{... | collective-permute-start | bytes 1572872 | tf_op jit(solution)/shard_map/ppermute | solution.py:34
  94.8 27.8 %collective-permute-start.8 = (bf16[256,1024]{1,0:T(8,128)(2,1)}, bf16[256,1024]{1,0:T(8,128)(2,1)}, u32[]{:S(2)}, u32[]{:S(2)}) collective-permute-start(bf16[256,1024]{1,0:T(8,128)(2,1)} %slice.38), channel_id=1, source_target_pairs={{0,12},{4,0},{8,4},{12,8},{1,13},{5,1},{9,5},{13,9},{2,14},{6,2},{... | collective-permute-start | bytes 1572872 | tf_op jit(solution)/shard_map/ppermute | solution.py:34
  100.0 33.3 %all-to-all-start.2 = ((bf16[16,3,64,256]{3,2,1,0:T(8,128)(2,1)}), bf16[16,3,64,256]{3,2,1,0:T(8,128)(2,1)S(1)}, u32[]{:S(2)}, u32[]{:S(2)}) async-start(bf16[16,3,64,256]{3,2,1,0:T(8,128)(2,1)} %bitcast.64), calls=%async_computation.2 | async-start | bytes 3145728 | tf_op jit(solution)/shard_map/all_to_all | solution.py:42
  125.5 48.9 %collective-permute-start.15 = (bf16[1024,1024]{1,0:T(8,128)(2,1)}, bf16[1024,1024]{1,0:T(8,128)(2,1)}, u32[]{:S(2)}, u32[]{:S(2)}) collective-permute-start(bf16[1024,1024]{1,0:T(8,128)(2,1)} %pad_maximum_fusion.1.refs_1_), channel_id=1, source_target_pairs={{0,18},{2,0},{16,2},{18,16},{1,19},{3,1},{17,3},{19,17},{4,22},{6,... | collective-permute-start | bytes 6291464 | tf_op jit(solution)/shard_map/ppermute | solution.py:34
  127.3 47.1 %collective-permute-start.14 = (bf16[1024,1024]{1,0:T(8,128)(2,1)}, bf16[1024,1024]{1,0:T(8,128)(2,1)}, u32[]{:S(2)}, u32[]{:S(2)}) collective-permute-start(bf16[1024,1024]{1,0:T(8,128)(2,1)} %pad_maximum_fusion.refs_0_), channel_id=1, source_target_pairs={{0,2},{2,16},{16,18},{18,0},{1,3},{3,17},{17,19},{19,1},{4,6},{6,2... | collective-permute-start | bytes 6291464 | tf_op jit(solution)/shard_map/ppermute | solution.py:34
  134.4 53.3 %all-to-all-start.3 = ((bf16[16,3,64,256]{3,2,1,0:T(8,128)(2,1)}), bf16[16,3,64,256]{3,2,1,0:T(8,128)(2,1)S(1)}, u32[]{:S(2)}, u32[]{:S(2)}) async-start(bf16[16,3,64,256]{3,2,1,0:T(8,128)(2,1)} %get-tuple-element.56), calls=%async_computation.3 | async-start | bytes 3145728 | tf_op jit(solution)/shard_map/all_to_all | solution.py:42
  139.5 53.0 %collective-permute-start.16 = (bf16[1024,1024]{1,0:T(8,128)(2,1)}, bf16[1024,1024]{1,0:T(8,128)(2,1)}, u32[]{:S(2)}, u32[]{:S(2)}) collective-permute-start(bf16[1024,1024]{1,0:T(8,128)(2,1)} %pad_maximum_fusion.refs_0_), channel_id=1, source_target_pairs={{0,1},{1,0},{2,3},{3,2},{4,5},{5,4},{6,7},{7,6},{8,9},{9,8},{10,11... | collective-permute-start | bytes 6291464 | tf_op jit(solution)/shard_map/ppermute | solution.py:34
  139.9 52.6 %collective-permute-start.17 = (bf16[1024,1024]{1,0:T(8,128)(2,1)}, bf16[1024,1024]{1,0:T(8,128)(2,1)}, u32[]{:S(2)}, u32[]{:S(2)}) collective-permute-start(bf16[1024,1024]{1,0:T(8,128)(2,1)} %pad_maximum_fusion.1.refs_1_), channel_id=1, source_target_pairs={{0,1},{1,0},{2,3},{3,2},{4,5},{5,4},{6,7},{7,6},{8,9},{9,8},{10,11... | collective-permute-start | bytes 6291464 | tf_op jit(solution)/shard_map/ppermute | solution.py:34
  174.4 18.1 %collective-permute-start.19 = (bf16[1024,1024]{1,0:T(8,128)(2,1)}, bf16[1024,1024]{1,0:T(8,128)(2,1)}, u32[]{:S(2)}, u32[]{:S(2)}) collective-permute-start(bf16[1024,1024]{1,0:T(8,128)(2,1)} %collective-permute-done.15.refs_3_), channel_id=1, source_target_pairs={{0,1},{1,0},{2,3},{3,2},{4,5},{5,4},{6,7},{7,6},{8,9},{9,8},{10,11... | collective-permute-start | bytes 6291464 | tf_op jit(solution)/shard_map/ppermute | solution.py:34
  174.4 18.2 %collective-permute-start.18 = (bf16[1024,1024]{1,0:T(8,128)(2,1)}, bf16[1024,1024]{1,0:T(8,128)(2,1)}, u32[]{:S(2)}, u32[]{:S(2)}) collective-permute-start(bf16[1024,1024]{1,0:T(8,128)(2,1)} %collective-permute-done.14.refs_2_), channel_id=1, source_target_pairs={{0,1},{1,0},{2,3},{3,2},{4,5},{5,4},{6,7},{7,6},{8,9},{9,8},{10,11... | collective-permute-start | bytes 6291464 | tf_op jit(solution)/shard_map/ppermute | solution.py:34
  187.7 35.6 %all-to-all-start.4 = ((bf16[16,3,80,256]{3,2,1,0:T(8,128)(2,1)}), bf16[16,3,80,256]{3,2,1,0:T(8,128)(2,1)}, u32[]{:S(2)}, u32[]{:S(2)}) async-start(bf16[16,3,80,256]{3,2,1,0:T(8,128)(2,1)} %get-tuple-element.67), calls=%async_computation.4 | async-start | bytes 3932160 | tf_op jit(solution)/shard_map/all_to_all | solution.py:42
  194.8 27.0 %collective-permute-start.20 = (bf16[4,64,256]{2,1,0:T(8,128)(2,1)}, bf16[4,64,256]{2,1,0:T(8,128)(2,1)}, u32[]{:S(2)}, u32[]{:S(2)}) collective-permute-start(bf16[4,64,256]{2,1,0:T(8,128)(2,1)} %get-tuple-element.59), channel_id=1, source_target_pairs={{0,16},{16,0},{32,48},{48,32},{64,80},{80,64},{96,112},{112,96},{1... | collective-permute-start | bytes 393224 | tf_op jit(solution)/shard_map/ppermute | solution.py:330
  197.4 25.5 %collective-permute-start.21 = (bf16[4,64,256]{2,1,0:T(8,128)(2,1)}, bf16[4,64,256]{2,1,0:T(8,128)(2,1)}, u32[]{:S(2)}, u32[]{:S(2)}) collective-permute-start(bf16[4,64,256]{2,1,0:T(8,128)(2,1)} %get-tuple-element.60), channel_id=1, source_target_pairs={{0,32},{16,48},{32,64},{48,80},{64,96},{80,112},{96,0},{112,16},{1... | collective-permute-start | bytes 393224 | tf_op jit(solution)/shard_map/ppermute | solution.py:330
  197.4 28.3 %collective-permute-start.22 = (bf16[4,64,256]{2,1,0:T(8,128)(2,1)}, bf16[4,64,256]{2,1,0:T(8,128)(2,1)S(1)}, u32[]{:S(2)}, u32[]{:S(2)}) collective-permute-start(bf16[4,64,256]{2,1,0:T(8,128)(2,1)} %get-tuple-element.61), channel_id=1, source_target_pairs={{0,48},{16,32},{32,80},{48,64},{64,112},{80,96},{96,16},{112,0},{1... | collective-permute-start | bytes 393224 | tf_op jit(solution)/shard_map/ppermute | solution.py:330
  198.2 27.5 %collective-permute-start.23 = (bf16[4,64,256]{2,1,0:T(8,128)(2,1)}, bf16[4,64,256]{2,1,0:T(8,128)(2,1)S(1)}, u32[]{:S(2)}, u32[]{:S(2)}) collective-permute-start(bf16[4,64,256]{2,1,0:T(8,128)(2,1)} %get-tuple-element.62), channel_id=1, source_target_pairs={{0,64},{16,80},{32,96},{48,112},{64,0},{80,16},{96,32},{112,48},{1... | collective-permute-start | bytes 393224 | tf_op jit(solution)/shard_map/ppermute | solution.py:330
  202.5 25.0 %collective-permute-start.24 = (bf16[4,64,256]{2,1,0:T(8,128)(2,1)}, bf16[4,64,256]{2,1,0:T(8,128)(2,1)S(1)}, u32[]{:S(2)}, u32[]{:S(2)}) collective-permute-start(bf16[4,64,256]{2,1,0:T(8,128)(2,1)} %get-tuple-element.63), channel_id=1, source_target_pairs={{0,80},{16,64},{32,112},{48,96},{64,16},{80,0},{96,48},{112,32},{1... | collective-permute-start | bytes 393224 | tf_op jit(solution)/shard_map/ppermute | solution.py:330
  221.8 9.3 %collective-permute-start.25 = (bf16[4,64,256]{2,1,0:T(8,128)(2,1)}, bf16[4,64,256]{2,1,0:T(8,128)(2,1)S(1)}, u32[]{:S(2)}, u32[]{:S(2)}) collective-permute-start(bf16[4,64,256]{2,1,0:T(8,128)(2,1)} %get-tuple-element.64), channel_id=1, source_target_pairs={{0,96},{16,112},{32,0},{48,16},{64,32},{80,48},{96,64},{112,80},{1... | collective-permute-start | bytes 393224 | tf_op jit(solution)/shard_map/ppermute | solution.py:330
  222.9 8.2 %collective-permute-start.26 = (bf16[4,64,256]{2,1,0:T(8,128)(2,1)}, bf16[4,64,256]{2,1,0:T(8,128)(2,1)S(1)}, u32[]{:S(2)}, u32[]{:S(2)}) collective-permute-start(bf16[4,64,256]{2,1,0:T(8,128)(2,1)} %get-tuple-element.65), channel_id=1, source_target_pairs={{0,112},{16,96},{32,16},{48,0},{64,48},{80,32},{96,80},{112,64},{1... | collective-permute-start | bytes 393224 | tf_op jit(solution)/shard_map/ppermute | solution.py:330
  235.2 31.3 %all-to-all-start.5 = ((bf16[32,80,256]{2,1,0:T(8,128)(2,1)}), bf16[32,80,256]{2,1,0:T(8,128)(2,1)}, u32[]{:S(2)}, u32[]{:S(2)}) async-start(bf16[32,80,256]{2,1,0:T(8,128)(2,1)} %sum_blocks.3), calls=%async_computation.5 | async-start | bytes 2621440 | tf_op jit(solution)/shard_map/all_to_all | solution.py:42
  (19 other events, 275.6 us)

commit v4 on v3

v4 whole, which is shorter than its diff:
```python
import functools

import jax
import jax.numpy as jnp
from jax import lax
from jax.experimental import pallas as pl
from jax.experimental.pallas import tpu as pltpu
from jax.sharding import Mesh
from jax.sharding import PartitionSpec as P

DP = ("y", "xh")
FSDP = ("z", "xl", "c")
X = ("xh", "xl")
SCALE = 0.5
F32 = jnp.float32
BF16 = jnp.bfloat16


def nt(a, b):
    return lax.dot_general(a, b, (((1,), (1,)), ((), ())), preferred_element_type=F32)


def tn(a, b):
    return lax.dot_general(a, b, (((0,), (0,)), ((), ())), preferred_element_type=F32)


def nn(a, b):
    return jnp.dot(a, b, preferred_element_type=F32)


def shift(x, axis, by):
    n = lax.axis_size(axis)
    return lax.ppermute(x, axis, [(i, (i + by) % n) for i in range(n)])


def gate(x, *needed):
    return lax.optimization_barrier((x, *needed))[0]


def exchange(x, axis):
    return lax.all_to_all(x, axis, split_axis=0, concat_axis=0, tiled=True)


def hbm(x):
    return pltpu.with_memory_space_constraint(x, pltpu.HBM)


def live_rows(fill_ref, b, rows):
    return (lax.broadcasted_iota(jnp.int32, (rows, 1), 0) < fill_ref[b]).astype(F32)


def pack(a, k):
    n = a.shape[0] // k
    return jnp.concatenate([a[i * n : (i + 1) * n] for i in range(k)], axis=1)


def unpack(a, k):
    r = a.shape[1] // k
    return jnp.concatenate([a[:, i * r : (i + 1) * r] for i in range(k)], axis=0)


def low_kernel(blocks, per, fill_ref, x_ref, dy_ref, packed_ref, down_ref, v_ref, u_ref, up_ref, g_ref, acc_ref):
    rows = dy_ref.shape[0] // blocks
    rank, feats = down_ref.shape[2:]
    steps = g_ref.shape[0]
    cols = dy_ref.shape[1] // steps
    step = pl.program_id(0)

    @pl.when(step == 0)
    def _():
        acc_ref[...] = jnp.zeros_like(acc_ref)
        for b in range(blocks):
            at = pl.ds(b * rows, rows)
            for f in range(steps):
                up_ref[b, pl.ds(f * cols, cols), :] = unpack(packed_ref[f, b], cols // packed_ref.shape[2])
            v = nn(dy_ref[at, :], up_ref[b]) * live_rows(fill_ref, b, rows)
            v_ref[at, :] = v.astype(BF16)

    for b in range(blocks):
        at = pl.ds(b * rows, rows)
        v = v_ref[at, :]
        total = acc_ref[at, :]
        for j in range(per):
            x = x_ref[at, pl.ds(j * feats, feats)]
            total += nt(x, down_ref[j, b])
            g_ref[step * per + j, b, :rank, :] = tn(v, x).astype(BF16)
        acc_ref[at, :] = total

    @pl.when(step == pl.num_programs(0) - 1)
    def _():
        for b in range(blocks):
            at = pl.ds(b * rows, rows)
            u = (acc_ref[at, :] * live_rows(fill_ref, b, rows)).astype(BF16)
            u_ref[at, :] = u
            g = tn(dy_ref[at, :], u).astype(BF16)
            for f in range(steps):
                g_ref[f, b, rank:, :] = pack(g[f * cols : (f + 1) * cols], feats // rank)


def base_kernel(blocks, pieces, f_ref, x_ref, dy_ref, u_ref, v_ref, up_ref, down_ref, *refs):
    w_refs, (y_ref, dx_ref, acc_ref, w_buf, sem) = refs[:pieces], refs[pieces:]
    rows = dy_ref.shape[0] // blocks
    step, steps = pl.program_id(0), pl.num_programs(0)
    feats = w_buf.shape[1]
    per = steps // pieces

    def fetch(i):
        for k, w_ref in enumerate(w_refs):

            @pl.when(i // per == k)
            def _():
                at = pl.ds(pl.multiple_of(i % per * feats, feats), feats)
                pltpu.make_async_copy(w_ref.at[at], w_buf.at[i % 2], sem.at[i % 2]).start()

    @pl.when(step == 0)
    def _():
        acc_ref[...] = jnp.zeros_like(acc_ref)
        fetch(step)

    @pl.when(step + 1 < steps)
    def _():
        fetch(step + 1)

    slot = step % 2
    pltpu.make_async_copy(w_refs[0].at[pl.ds(0, feats)], w_buf.at[slot], sem.at[slot]).wait()
    w = w_buf[slot]
    acc_ref[...] += nn(x_ref[...], w)
    wide = nt(dy_ref[...], w)
    for b in range(blocks):
        at = pl.ds(b * rows, rows)
        pulled = nn(v_ref[at, :], down_ref[0, b]).astype(BF16).astype(F32)
        dx_ref[at, :] = (wide[b * rows : (b + 1) * rows, :] + SCALE * pulled).astype(BF16)

    @pl.when(step == steps - 1)
    def _():
        for b in range(blocks):
            at = pl.ds(b * rows, rows)
            lifted = nt(u_ref[at, :], up_ref[b]).astype(BF16).astype(F32)
            y_ref[at, :] = (acc_ref[at, :] + SCALE * lifted).astype(BF16)


def sum_kernel(ids_ref, g_ref, o_ref, acc_ref):
    members, blocks = g_ref.shape[:2]
    acc_ref[...] = jnp.zeros_like(acc_ref)

    @pl.loop(0, members)
    def _(m):
        for b in range(blocks):
            acc_ref[ids_ref[m, b]] += g_ref[m, b].astype(F32)

    o_ref[...] = acc_ref[...].astype(BF16)


def vmem(mib):
    return pltpu.CompilerParams(vmem_limit_bytes=mib * 1024 * 1024)


VMEM = pl.BlockSpec(memory_space=pltpu.VMEM)
SMEM = pl.BlockSpec(memory_space=pltpu.SMEM)


def cost(flops, size):
    return pl.CostEstimate(flops=flops, bytes_accessed=size, transcendentals=0)


def whole(shape):
    zeros = (0,) * len(shape)
    return pl.BlockSpec(shape, lambda i, *_: zeros)


def sum_blocks(ids_all, g, adapters):
    shape = (adapters,) + g.shape[2:]
    return pl.pallas_call(
        sum_kernel,
        in_specs=[SMEM, VMEM],
        out_specs=VMEM,
        out_shape=pltpu.HBM(shape, BF16),
        scratch_shapes=[pltpu.VMEM(shape, F32)],
        compiler_params=vmem(16),
        cost_estimate=cost(g.size, 4 * g.size),
        name="sum_blocks",
    )(ids_all, g)


def body(tokens, weight, down, up, dy, ids, fill):
    rows_dev, width = tokens.shape
    value = dy.shape[1]
    blocks = ids.shape[0]
    slots, feats, rank = down.shape
    cols = up.shape[2]
    ys, xhs = lax.axis_size("y"), lax.axis_size("xh")
    steps = lax.axis_size(FSDP)
    adapters = slots * ys * xhs
    y_at, xh_at = lax.axis_index("y"), lax.axis_index("xh")
    z_at, xl_at, c_at = (lax.axis_index(a) for a in FSDP)
    w_back, w_next = shift(weight, "z", 1), shift(weight, "z", -1)
    mid = feats // 2
    w_lo, w_hi = shift(w_back[:mid], "z", 1), shift(w_next[mid:], "z", -1)

    ids_out = jnp.broadcast_to(jnp.pad(ids, (0, 128 - blocks)), (steps, 8, 128))
    ids_all = exchange(ids_out, FSDP)

    folds = feats // rank
    up_t = jnp.swapaxes(up, 1, 2).reshape(slots, folds, cols // folds, rank)
    up_packed = jnp.swapaxes(up_t, 1, 2).reshape(slots, cols // folds, feats)
    own = jnp.concatenate([jnp.swapaxes(down, 1, 2), up_packed], axis=1)
    x_all = jnp.stack([own, shift(own, "xh", 1)])
    one, three = shift(x_all, "y", 1), shift(x_all, "y", -1)
    lo, hi = shift(one[:, : slots // 2], "y", 1), shift(three[:, slots // 2 :], "y", -1)
    every = jnp.stack([x_all, one, jnp.concatenate([lo, hi], axis=1), three])

    ids_all = gate(ids_all, lo, hi)[:, 0, :blocks]
    want = ids_all.reshape(steps * blocks)
    owner = want // slots
    oy, ox = (y_at - owner // xhs) % ys, (xh_at - owner % xhs) % xhs
    at = (oy * xhs + ox) * slots + want % slots
    every = gate(every, w_lo, w_hi)
    picked = every.reshape(adapters, *own.shape[1:])[at].reshape(steps, blocks, *own.shape[1:])
    low = exchange(picked, FSDP)

    near = jnp.concatenate([gate(weight, picked), w_next])
    far = jnp.concatenate([gate(w_back, picked), w_lo, w_hi])
    across = [(0, 3), (3, 0), (1, 2), (2, 1)]
    near_x = lax.ppermute(near, X, across)
    low = gate(low, near_x)

    grid = 4
    per = steps // grid
    x_spec = pl.BlockSpec((rows_dev, per * feats), lambda i: (0, i))
    up_rows = cols // folds
    low_v, low_u, up_mine, grads = pl.pallas_call(
        functools.partial(low_kernel, blocks, per),
        grid=(grid,),
        in_specs=[
            SMEM,
            x_spec,
            whole(dy.shape),
            pl.BlockSpec((steps, blocks, up_rows, feats), lambda i: (0, 0, rank // up_rows, 0)),
            pl.BlockSpec((per, blocks, rank, feats), lambda i: (i, 0, 0, 0)),
        ],
        out_specs=[
            whole((rows_dev, rank)),
            whole((rows_dev, rank)),
            whole((blocks, value, rank)),
            whole(low.shape),
        ],
        out_shape=[
            pltpu.HBM((rows_dev, rank), BF16),
            pltpu.HBM((rows_dev, rank), BF16),
            pltpu.HBM((blocks, value, rank), BF16),
            pltpu.HBM(low.shape, BF16),
        ],
        scratch_shapes=[pltpu.VMEM((rows_dev, rank), F32)],
        compiler_params=vmem(24),
        cost_estimate=cost(rows_dev * rank * 4 * (width + value), 16 << 20),
        name="low",
    )(fill, *(hbm(a) for a in (tokens, dy, low, low)))
    far_x = lax.ppermute(gate(far, low_u), X, across)
    back = exchange(grads, FSDP)

    w_own = [near, far, near_x, far_x]
    w_other = [shift(gate(w, low_u), "c", 1) for w in w_own]
    w_all = w_own + w_other
    order = [
        (z_at + dz) % 4 * 4 + (xl_at + dx) % 2 * 2 + (c_at + dc) % 2
        for dc in (0, 1)
        for dx in (0, 1)
        for dz in (0, 1, 3, 2)
    ]


    values, input_gradient = pl.pallas_call(
        functools.partial(base_kernel, blocks, len(w_all)),
        grid_spec=pltpu.PrefetchScalarGridSpec(
            num_scalar_prefetch=1,
            grid=(steps,),
            in_specs=[
                pl.BlockSpec((rows_dev, feats), lambda i, f: (0, f[i])),
                whole(dy.shape),
                whole(low_u.shape),
                whole(low_v.shape),
                whole(up_mine.shape),
                pl.BlockSpec((1, blocks, rank, feats), lambda i, f: (f[i], 0, 0, 0)),
            ]
            + [pl.BlockSpec(memory_space=pltpu.HBM)] * len(w_all),
            out_specs=[
                whole((rows_dev, value)),
                pl.BlockSpec((rows_dev, feats), lambda i, f: (0, f[i])),
            ],
            scratch_shapes=[
                pltpu.VMEM((rows_dev, value), F32),
                pltpu.VMEM((2, feats, value), BF16),
                pltpu.SemaphoreType.DMA((2,)),
            ],
        ),
        out_shape=[pltpu.HBM((rows_dev, value), BF16), pltpu.HBM((rows_dev, width), BF16)],
        compiler_params=vmem(28),
        cost_estimate=cost(4 * rows_dev * width * value, 36 << 20),
        name="base",
    )(
        jnp.stack(order),
        *(hbm(a) for a in (tokens, dy, low_u, low_v, up_mine, low)),
        *(hbm(a) for a in w_all),
    )

    part = exchange(sum_blocks(ids_all, back, adapters), DP)
    part = gate(part, values).reshape(ys * xhs, slots, *own.shape[1:])
    total = SCALE * part.astype(F32).sum(0)
    grad_down = total[:, :rank]
    grad_up = total[:, rank:].reshape(slots, up_rows, folds, rank)
    grad_up = jnp.transpose(grad_up, (0, 3, 2, 1)).reshape(slots, rank, cols)
    return values, input_gradient, jnp.swapaxes(grad_down, 1, 2), grad_up


def solution(mesh):
    fine = Mesh(mesh.devices.reshape(4, 2, 4, 2, 2), DP + FSDP)
    every = DP + FSDP
    placed = (
        P(every, None),
        P(FSDP, None),
        P(DP, FSDP, None),
        P(DP, None, FSDP),
        P(every, None),
        P(every),
        P(every),
    )
    return jax.shard_map(
        body,
        mesh=fine,
        in_specs=placed,
        out_specs=(P(every, None), P(every, None), P(DP, FSDP, None), P(DP, None, FSDP)),
        check_vma=False,
    )
```

time: 273 us -> 220 us (0.81)
  starting transfers between devices: 67.7 us -> 43.9 us
  waiting for transfers between devices: 132 us -> 114 us
  other arithmetic: 11 us -> 3.97 us
  Pallas kernels: 44.1 us -> 38.9 us
    ppermute x7 -> x2, waiting for transfers between devices: 25.1 us -> 81.7 us  [the longest x1 41.3 us: body(): near_x = lax.ppermute(near, X, across)]
    ppermute x20 -> x13, waiting for transfers between devices: 78.8 us -> 24.3 us  [shift(): return lax.ppermute(x, axis, [(i, (i + by) % n) for i in range(n)])]
    all_to_all x6 -> x4, waiting for transfers between devices: 27.6 us -> 8.01 us  [exchange(): return lax.all_to_all(x, axis, split_axis=0, concat_axis=0, tiled=True)]
    ppermute x20 -> x13, starting transfers between devices: 28.6 us -> 18 us  [shift(): return lax.ppermute(x, axis, [(i, (i + by) % n) for i in range(n)])]
    all_to_all x6 -> x4, starting transfers between devices: 28 us -> 19.7 us  [exchange(): return lax.all_to_all(x, axis, split_axis=0, concat_axis=0, tiled=True)]
    concatenate x3 -> x0, other arithmetic: 5.98 us -> none  [the longest x1 3.14 us: body(): near = jnp.concatenate([weight, w_next])]
    pallas_call x4 -> x2, Pallas kernels: 18.5 us -> 12.7 us  [the longest x1 9.37 us: body(): pl.pallas_call(functools.partial(low_kernel, blocks, per), grid=(grid,),...]
    ppermute x7 -> x2, starting transfers between devices: 11.1 us -> 6.17 us  [the longest x1 3.22 us: body(): near_x = lax.ppermute(near, X, across)]
  transfers between devices with their start and end apart: 33 -> 19, of which waited for: 13 -> 9; matrix products, arithmetic and copies ran while one was open for 5% -> 6% of each run, Pallas kernels for 15% -> 14%
where the time goes in v4:
time: 220 us; the launch traced here: 218 us
  waiting for transfers between devices  114 us (52%)
  starting transfers between devices  43.9 us (20%)
  Pallas kernels  38.9 us (18%)
  local copies, waits for them, and re-layouts  16.6 us (8%)
  other arithmetic  3.97 us (2%)
    ppermute x1, waiting for transfers between devices, body(): near_x = lax.ppermute(near, X, across)  41.3 us
    ppermute x1, waiting for transfers between devices, body(): far_x = lax.ppermute(gate(far, low_u), X, across)  40.4 us
    pallas_call x1, Pallas kernels, body(): pl.pallas_call(functools.partial(base_kernel, blocks, len(w_all)), grid_s...  26.2 us
    ppermute x13, waiting for transfers between devices, shift(): return lax.ppermute(x, axis, [(i, (i + by) % n) for i in range(n)])  24.3 us
    all_to_all x4, starting transfers between devices, exchange(): return lax.all_to_all(x, axis, split_axis=0, concat_axis=0, tiled=True)  19.7 us
    ppermute x13, starting transfers between devices, shift(): return lax.ppermute(x, axis, [(i, (i + by) % n) for i in range(n)])  18 us
    pallas_call x1, Pallas kernels, body(): pl.pallas_call(functools.partial(low_kernel, blocks, per), grid=(grid,),...  9.37 us
    all_to_all x4, waiting for transfers between devices, exchange(): return lax.all_to_all(x, axis, split_axis=0, concat_axis=0, tiled=True)  8.01 us
  transfers between devices with their start and end apart: 19, of which 9 were waited for; matrix products, arithmetic and copies ran while one was open for 6% of the time, Pallas kernels for 14%

profile of v4, /device:TPU:0, one launch (start us, length us, event | category | flops | bytes accessed | tf_op | source)
XLA Modules:
  0.0 218.3 jit_solution(5369831221298045281)
XLA Ops:
  2.7 3.2 %collective-permute-start = (bf16[4,72,512]{2,1,0:T(8,128)(2,1)S(1)}, bf16[4,72,512]{2,1,0:T(8,128)(2,1)S(1)}, u32[]{:S(2)}, u32[]{:S(2)}) collective-permute-start(bf16[4,72,512]{2,1,0:T(8,128)(2,1)S(1)} %get-tuple-element.51), channel_id=1, source_target_pairs={{0,16},{16,0},{1,17},{17,1},{2,18},{18,2},{3,19},{19,3},{4,20},{20... | collective-permute-start | bytes 884744 | tf_op jit(solution)/shard_map/ppermute | solution.py:33
  5.9 1.9 collective-permute-start.5
  7.8 2.1 collective-permute-start.7
  10.0 3.0 %collective-permute-done = bf16[4,72,512]{2,1,0:T(8,128)(2,1)S(1)} collective-permute-done((bf16[4,72,512]{2,1,0:T(8,128)(2,1)S(1)}, bf16[4,72,512]{2,1,0:T(8,128)(2,1)S(1)}, u32[]{:S(2)}, u32[]{:S(2)}) %collective-permute-start) | collective-permute-done | bytes 294944 | tf_op jit(solution)/shard_map/ppermute | solution.py:33
  13.0 1.9 collective-permute-start.1
  14.9 1.5 collective-permute-start.3
  16.4 12.4 %collective-permute-done.1 = bf16[2,4,72,512]{3,2,1,0:T(8,128)(2,1)S(1)} collective-permute-done((bf16[2,4,72,512]{3,2,1,0:T(8,128)(2,1)S(1)}, bf16[2,4,72,512]{3,2,1,0:T(8,128)(2,1)S(1)}, u32[]{:S(2)}, u32[]{:S(2)}) %collective-permute-start.1) | collective-permute-done | bytes 589856 | tf_op jit(solution)/shard_map/ppermute | solution.py:33
  29.8 1.7 slice.31
  31.5 2.9 %collective-permute-start.4 = (bf16[2,2,72,512]{3,2,1,0:T(8,128)(2,1)}, bf16[2,2,72,512]{3,2,1,0:T(8,128)(2,1)}, u32[]{:S(2)}, u32[]{:S(2)}) collective-permute-start(bf16[2,2,72,512]{3,2,1,0:T(8,128)(2,1)} %slice.31), channel_id=1, source_target_pairs={{0,96},{32,0},{64,32},{96,64},{1,97},{33,1},{65,33},{97,65},{2,98}... | collective-permute-start | bytes 884744 | tf_op jit(solution)/shard_map/ppermute | solution.py:33
  35.1 6.3 %all-to-all-start = ((s32[16,8,128]{2,1,0:T(8,128)}), s32[16,8,128]{2,1,0:T(8,128)S(1)}, u32[]{:S(2)}, u32[]{:S(2)}) async-start(s32[16,8,128]{2,1,0:T(8,128)} %broadcast_in_dim.4), calls=%async_computation | async-start | bytes 131072 | tf_op jit(solution)/shard_map/all_to_all | solution.py:41
  42.4 1.9 collective-permute-start.6
  45.2 1.3 collective-permute-start.8
  46.5 1.1 all-to-all-done
  47.8 1.1 maximum_bitcast_fusion
  48.9 1.4 pad_maximum_fusion
  50.3 8.2 %collective-permute-done.6 = bf16[256,1024]{1,0:T(8,128)(2,1)} collective-permute-done((bf16[256,1024]{1,0:T(8,128)(2,1)}, bf16[256,1024]{1,0:T(8,128)(2,1)}, u32[]{:S(2)}, u32[]{:S(2)}) %collective-permute-start.6) | collective-permute-done | bytes 524320 | tf_op jit(solution)/shard_map/ppermute | solution.py:33
  59.2 2.7 %gather_fusion = bf16[48,72,512]{2,1,0:T(8,128)(2,1)} fusion(bf16[32,72,512]{2,1,0:T(8,128)(2,1)S(1)} %bitcast.47, s32[1024]{0:T(1024)S(1)} %pad_clamp_fusion), kind=kCustom, calls=%fused_computation | custom fusion | bytes 7078080 | tf_op jit(solution)/shard_map/gather | solution.py:218
  61.9 5.4 %all-to-all-start.1 = ((bf16[16,3,72,512]{3,2,1,0:T(8,128)(2,1)}), bf16[16,3,72,512]{3,2,1,0:T(8,128)(2,1)}, u32[]{:S(2)}, u32[]{:S(2)}) async-start(bf16[16,3,72,512]{3,2,1,0:T(8,128)(2,1)} %bitcast.48), calls=%async_computation.1 | async-start | bytes 7077888 | tf_op jit(solution)/shard_map/all_to_all | solution.py:41
  67.4 1.1 copy-done.4
  68.6 3.2 %collective-permute-start.9 = (bf16[1024,1024]{1,0:T(8,128)(2,1)S(1)}, bf16[1024,1024]{1,0:T(8,128)(2,1)}, u32[]{:S(2)}, u32[]{:S(2)}) collective-permute-start(bf16[1024,1024]{1,0:T(8,128)(2,1)S(1)} %constant_dynamic-update-slice_fusion.refs_0_), channel_id=1, source_target_pairs={{0,18},{18,0},{2,16},{16,2},{1,19},{19,1},{3,17},{17,3},{4,22},{22... | collective-permute-start | bytes 6291464 | tf_op jit(solution)/shard_map/ppermute | solution.py:224
  72.9 1.9 constant_dynamic-update-slice_fusion.3
  74.8 1.9 constant_dynamic-update-slice_fusion.2.refs_1_
  76.7 41.3 %collective-permute-done.9.refs_2_ = bf16[1024,1024]{1,0:T(8,128)(2,1)} collective-permute-done((bf16[1024,1024]{1,0:T(8,128)(2,1)S(1)}, bf16[1024,1024]{1,0:T(8,128)(2,1)}, u32[]{:S(2)}, u32[]{:S(2)}) %collective-permute-start.9) | collective-permute-done | bytes 2097184 | tf_op jit(solution)/shard_map/ppermute | solution.py:224
  117.9 9.4 %low.1 = (bf16[384,64]{1,0:T(8,128)(2,1)}, bf16[384,64]{1,0:T(8,128)(2,1)}, bf16[3,1024,64]{2,1,0:T(8,128)(2,1)}, bf16[16,3,72,512]{3,2,1,0:T(8,128)(2,1)}) custom-call(s32[3]{0:T(128)S(1)} %copy-done, bf16[384,8192]{1,0:T(8,128)(2,1)} %x_ref.3, bf16[384,1024]{1,0:T(8,128)(2,1)} %dy_ref.3, bf16[16,3,72,512]{3,2,1,0:T(8,128)(2,1)} %all-to-all-done.1.packed_ref.down_ref, ...), custom_call_target="tpu_custom_call" | custom-call | flops 905969664 | bytes 16777216 | tf_op jit(solution)/shard_map/low/pallas_call | solution.py:231
  127.3 2.9 %collective-permute-start.10 = (bf16[1024,1024]{1,0:T(8,128)(2,1)}, bf16[1024,1024]{1,0:T(8,128)(2,1)}, u32[]{:S(2)}, u32[]{:S(2)}) collective-permute-start(bf16[1024,1024]{1,0:T(8,128)(2,1)} %constant_dynamic-update-slice_fusion.2.refs_1_), channel_id=1, source_target_pairs={{0,18},{18,0},{2,16},{16,2},{1,19},{19,1},{3,17},{17,3},{4,22},{22... | collective-permute-start | bytes 6291464 | tf_op jit(solution)/shard_map/ppermute | solution.py:258
  130.3 4.3 %all-to-all-start.2 = ((bf16[16,3,72,512]{3,2,1,0:T(8,128)(2,1)}), bf16[16,3,72,512]{3,2,1,0:T(8,128)(2,1)S(1)}, u32[]{:S(2)}, u32[]{:S(2)}) async-start(bf16[16,3,72,512]{3,2,1,0:T(8,128)(2,1)} %get-tuple-element.34), calls=%async_computation.2 | async-start | bytes 7077888 | tf_op jit(solution)/shard_map/all_to_all | solution.py:41
  135.5 40.4 %collective-permute-done.10.refs_3_ = bf16[1024,1024]{1,0:T(8,128)(2,1)} collective-permute-done((bf16[1024,1024]{1,0:T(8,128)(2,1)}, bf16[1024,1024]{1,0:T(8,128)(2,1)}, u32[]{:S(2)}, u32[]{:S(2)}) %collective-permute-start.10) | collective-permute-done | bytes 2097184 | tf_op jit(solution)/shard_map/ppermute | solution.py:258
  175.9 2.0 all-to-all-done.2.g_ref
  177.9 3.3 %sum_blocks.1 = bf16[32,72,512]{2,1,0:T(8,128)(2,1)} custom-call(s32[16,3]{1,0:T(8,128)S(1)} %bitcast.46, bf16[16,3,72,512]{3,2,1,0:T(8,128)(2,1)S(1)} %all-to-all-done.2.g_ref), custom_call_target="tpu_custom_call" | custom-call | flops 1769472 | bytes 7077888 | tf_op jit(solution)/shard_map/sum_blocks/pallas_call | solution.py:173
  181.2 3.6 %all-to-all-start.3 = ((bf16[32,72,512]{2,1,0:T(8,128)(2,1)}), bf16[32,72,512]{2,1,0:T(8,128)(2,1)S(1)}, u32[]{:S(2)}, u32[]{:S(2)}) async-start(bf16[32,72,512]{2,1,0:T(8,128)(2,1)} %sum_blocks.1), calls=%async_computation.3 | async-start | bytes 4718592 | tf_op jit(solution)/shard_map/all_to_all | solution.py:41
  185.1 26.2 %base.1 = (bf16[384,1024]{1,0:T(8,128)(2,1)}, bf16[384,8192]{1,0:T(8,128)(2,1)}) custom-call(s32[16]{0:T(128)S(1)} %stack.91.f_ref, bf16[384,8192]{1,0:T(8,128)(2,1)} %x_ref.3, bf16[384,1024]{1,0:T(8,128)(2,1)} %dy_ref.3, bf16[384,64]{1,0:T(8,128)(2,1)} %get-tuple-element.24.u_ref, bf16[384,64]{1,0:T(8,128)(2,1)} %get-tuple-element.25.v_ref, ...), custom_call_target="tpu_custom_call" | custom-call | flops 12884901888 | bytes 37748736 | tf_op jit(solution)/shard_map/base/pallas_call | solution.py:272
  211.3 4.9 %all-to-all-done.3 = bf16[32,72,512]{2,1,0:T(8,128)(2,1)S(1)} async-done(((bf16[32,72,512]{2,1,0:T(8,128)(2,1)}), bf16[32,72,512]{2,1,0:T(8,128)(2,1)S(1)}, u32[]{:S(2)}, u32[]{:S(2)}) %all-to-all-start.3) | async-done | bytes 2359328 | tf_op jit(solution)/shard_map/all_to_all | solution.py:41
  (56 shorter events, 10.8 us)
Async XLA Ops:
  0.6 33.8 %copy-start.7 = (s32[3]{0:T(128)S(1)}, s32[3]{0:T(128)}, u32[]{:S(2)}) copy-start(s32[3]{0:T(128)} %param.12) | copy-start | bytes 40
  2.7 10.2 %collective-permute-start = (bf16[4,72,512]{2,1,0:T(8,128)(2,1)S(1)}, bf16[4,72,512]{2,1,0:T(8,128)(2,1)S(1)}, u32[]{:S(2)}, u32[]{:S(2)}) collective-permute-start(bf16[4,72,512]{2,1,0:T(8,128)(2,1)S(1)} %get-tuple-element.51), channel_id=1, source_target_pairs={{0,16},{16,0},{1,17},{17,1},{2,18},{18,2},{3,19},{19,3},{4,20},{20... | collective-permute-start | bytes 884744 | tf_op jit(solution)/shard_map/ppermute | solution.py:33
  5.9 35.5 %collective-permute-start.5 = (bf16[512,1024]{1,0:T(8,128)(2,1)}, bf16[512,1024]{1,0:T(8,128)(2,1)S(1)}, u32[]{:S(2)}, u32[]{:S(2)}) collective-permute-start(bf16[512,1024]{1,0:T(8,128)(2,1)} %param.8), channel_id=1, source_target_pairs={{0,4},{4,8},{8,12},{12,0},{1,5},{5,9},{9,13},{13,1},{2,6},{6,10},{... | collective-permute-start | bytes 3145736 | tf_op jit(solution)/shard_map/ppermute | solution.py:33
  7.8 36.5 %collective-permute-start.7 = (bf16[512,1024]{1,0:T(8,128)(2,1)}, bf16[512,1024]{1,0:T(8,128)(2,1)S(1)}, u32[]{:S(2)}, u32[]{:S(2)}) collective-permute-start(bf16[512,1024]{1,0:T(8,128)(2,1)} %param.8), channel_id=1, source_target_pairs={{0,12},{4,0},{8,4},{12,8},{1,13},{5,1},{9,5},{13,9},{2,14},{6,2},{... | collective-permute-start | bytes 3145736 | tf_op jit(solution)/shard_map/ppermute | solution.py:33
  13.0 15.8 %collective-permute-start.1 = (bf16[2,4,72,512]{3,2,1,0:T(8,128)(2,1)S(1)}, bf16[2,4,72,512]{3,2,1,0:T(8,128)(2,1)S(1)}, u32[]{:S(2)}, u32[]{:S(2)}) collective-permute-start(bf16[2,4,72,512]{3,2,1,0:T(8,128)(2,1)S(1)} %get-tuple-element.49), channel_id=1, source_target_pairs={{0,32},{32,64},{64,96},{96,0},{1,33},{33,65},{65,97},{97,1},{2,34}... | collective-permute-start | bytes 1769480 | tf_op jit(solution)/shard_map/ppermute | solution.py:33
  14.9 14.9 %collective-permute-start.3 = (bf16[2,4,72,512]{3,2,1,0:T(8,128)(2,1)S(1)}, bf16[2,4,72,512]{3,2,1,0:T(8,128)(2,1)}, u32[]{:S(2)}, u32[]{:S(2)}) collective-permute-start(bf16[2,4,72,512]{3,2,1,0:T(8,128)(2,1)S(1)} %get-tuple-element.49), channel_id=1, source_target_pairs={{0,96},{32,0},{64,32},{96,64},{1,97},{33,1},{65,33},{97,65},{2,98}... | collective-permute-start | bytes 1769480 | tf_op jit(solution)/shard_map/ppermute | solution.py:33
  29.5 18.1 %collective-permute-start.2 = (bf16[2,2,72,512]{3,2,1,0:T(8,128)(2,1)}, bf16[2,2,72,512]{3,2,1,0:T(8,128)(2,1)}, u32[]{:S(2)}, u32[]{:S(2)}) collective-permute-start(bf16[2,2,72,512]{3,2,1,0:T(8,128)(2,1)} %slice.30), channel_id=1, source_target_pairs={{0,32},{32,64},{64,96},{96,0},{1,33},{33,65},{65,97},{97,1},{2,34}... | collective-permute-start | bytes 884744 | tf_op jit(solution)/shard_map/ppermute | solution.py:33
  31.5 16.1 %collective-permute-start.4 = (bf16[2,2,72,512]{3,2,1,0:T(8,128)(2,1)}, bf16[2,2,72,512]{3,2,1,0:T(8,128)(2,1)}, u32[]{:S(2)}, u32[]{:S(2)}) collective-permute-start(bf16[2,2,72,512]{3,2,1,0:T(8,128)(2,1)} %slice.31), channel_id=1, source_target_pairs={{0,96},{32,0},{64,32},{96,64},{1,97},{33,1},{65,33},{97,65},{2,98}... | collective-permute-start | bytes 884744 | tf_op jit(solution)/shard_map/ppermute | solution.py:33
  35.1 12.5 %all-to-all-start = ((s32[16,8,128]{2,1,0:T(8,128)}), s32[16,8,128]{2,1,0:T(8,128)S(1)}, u32[]{:S(2)}, u32[]{:S(2)}) async-start(s32[16,8,128]{2,1,0:T(8,128)} %broadcast_in_dim.4), calls=%async_computation | async-start | bytes 131072 | tf_op jit(solution)/shard_map/all_to_all | solution.py:41
  41.5 6.2 %copy-start.1 = (bf16[512,1024]{1,0:T(8,128)(2,1)}, bf16[512,1024]{1,0:T(8,128)(2,1)S(1)}, u32[]{:S(2)}) copy-start(bf16[512,1024]{1,0:T(8,128)(2,1)S(1)} %collective-permute-done.5) | copy-start | bytes 3145732
  42.4 16.1 %collective-permute-start.6 = (bf16[256,1024]{1,0:T(8,128)(2,1)}, bf16[256,1024]{1,0:T(8,128)(2,1)}, u32[]{:S(2)}, u32[]{:S(2)}) collective-permute-start(bf16[256,1024]{1,0:T(8,128)(2,1)} %slice.32), channel_id=1, source_target_pairs={{0,4},{4,8},{8,12},{12,0},{1,5},{5,9},{9,13},{13,1},{2,6},{6,10},{... | collective-permute-start | bytes 1572872 | tf_op jit(solution)/shard_map/ppermute | solution.py:33
  44.3 4.6 %copy-start.3 = (bf16[512,1024]{1,0:T(8,128)(2,1)}, bf16[512,1024]{1,0:T(8,128)(2,1)S(1)}, u32[]{:S(2)}) copy-start(bf16[512,1024]{1,0:T(8,128)(2,1)S(1)} %collective-permute-done.7) | copy-start | bytes 3145732
  45.2 14.0 %collective-permute-start.8 = (bf16[256,1024]{1,0:T(8,128)(2,1)}, bf16[256,1024]{1,0:T(8,128)(2,1)}, u32[]{:S(2)}, u32[]{:S(2)}) collective-permute-start(bf16[256,1024]{1,0:T(8,128)(2,1)} %slice.33), channel_id=1, source_target_pairs={{0,12},{4,0},{8,4},{12,8},{1,13},{5,1},{9,5},{13,9},{2,14},{6,2},{... | collective-permute-start | bytes 1572872 | tf_op jit(solution)/shard_map/ppermute | solution.py:33
  61.9 5.5 %copy-start.5 = (bf16[512,1024]{1,0:T(8,128)(2,1)S(1)}, bf16[512,1024]{1,0:T(8,128)(2,1)}, u32[]{:S(2)}) copy-start(bf16[512,1024]{1,0:T(8,128)(2,1)} %param.8) | copy-start | bytes 3145732
  61.9 56.1 %all-to-all-start.1 = ((bf16[16,3,72,512]{3,2,1,0:T(8,128)(2,1)}), bf16[16,3,72,512]{3,2,1,0:T(8,128)(2,1)}, u32[]{:S(2)}, u32[]{:S(2)}) async-start(bf16[16,3,72,512]{3,2,1,0:T(8,128)(2,1)} %bitcast.48), calls=%async_computation.1 | async-start | bytes 7077888 | tf_op jit(solution)/shard_map/all_to_all | solution.py:41
  67.3 1.2 copy-start.4
  67.3 4.5 %copy-start.2 = (bf16[512,1024]{1,0:T(8,128)(2,1)S(1)}, bf16[512,1024]{1,0:T(8,128)(2,1)}, u32[]{:S(2)}) copy-start(bf16[512,1024]{1,0:T(8,128)(2,1)} %copy-done.1) | copy-start | bytes 3145732
  68.6 4.3 %copy-start.6 = (bf16[1024,1024]{1,0:T(8,128)(2,1)}, bf16[1024,1024]{1,0:T(8,128)(2,1)S(1)}, u32[]{:S(2)}) copy-start(bf16[1024,1024]{1,0:T(8,128)(2,1)S(1)} %constant_dynamic-update-slice_fusion.refs_0_) | copy-start | bytes 6291460
  68.6 49.3 %copy-start = (s32[3]{0:T(128)S(1)}, s32[3]{0:T(128)}, u32[]{:S(2)}) copy-start(s32[3]{0:T(128)} %fill_ref.1) | copy-start | bytes 40
  68.6 49.3 %collective-permute-start.9 = (bf16[1024,1024]{1,0:T(8,128)(2,1)S(1)}, bf16[1024,1024]{1,0:T(8,128)(2,1)}, u32[]{:S(2)}, u32[]{:S(2)}) collective-permute-start(bf16[1024,1024]{1,0:T(8,128)(2,1)S(1)} %constant_dynamic-update-slice_fusion.refs_0_), channel_id=1, source_target_pairs={{0,18},{18,0},{2,16},{16,2},{1,19},{19,1},{3,17},{17,3},{4,22},{22... | collective-permute-start | bytes 6291464 | tf_op jit(solution)/shard_map/ppermute | solution.py:224
  127.3 48.6 %collective-permute-start.10 = (bf16[1024,1024]{1,0:T(8,128)(2,1)}, bf16[1024,1024]{1,0:T(8,128)(2,1)}, u32[]{:S(2)}, u32[]{:S(2)}) collective-permute-start(bf16[1024,1024]{1,0:T(8,128)(2,1)} %constant_dynamic-update-slice_fusion.2.refs_1_), channel_id=1, source_target_pairs={{0,18},{18,0},{2,16},{16,2},{1,19},{19,1},{3,17},{17,3},{4,22},{22... | collective-permute-start | bytes 6291464 | tf_op jit(solution)/shard_map/ppermute | solution.py:258
  130.3 47.7 %all-to-all-start.2 = ((bf16[16,3,72,512]{3,2,1,0:T(8,128)(2,1)}), bf16[16,3,72,512]{3,2,1,0:T(8,128)(2,1)S(1)}, u32[]{:S(2)}, u32[]{:S(2)}) async-start(bf16[16,3,72,512]{3,2,1,0:T(8,128)(2,1)} %get-tuple-element.34), calls=%async_computation.2 | async-start | bytes 7077888 | tf_op jit(solution)/shard_map/all_to_all | solution.py:41
  134.6 50.4 %collective-permute-start.12 = (bf16[1024,1024]{1,0:T(8,128)(2,1)}, bf16[1024,1024]{1,0:T(8,128)(2,1)}, u32[]{:S(2)}, u32[]{:S(2)}) collective-permute-start(bf16[1024,1024]{1,0:T(8,128)(2,1)} %constant_dynamic-update-slice_fusion.2.refs_1_), channel_id=1, source_target_pairs={{0,1},{1,0},{2,3},{3,2},{4,5},{5,4},{6,7},{7,6},{8,9},{9,8},{10,11... | collective-permute-start | bytes 6291464 | tf_op jit(solution)/shard_map/ppermute | solution.py:33
  135.0 50.0 %collective-permute-start.11 = (bf16[1024,1024]{1,0:T(8,128)(2,1)}, bf16[1024,1024]{1,0:T(8,128)(2,1)}, u32[]{:S(2)}, u32[]{:S(2)}) collective-permute-start(bf16[1024,1024]{1,0:T(8,128)(2,1)} %copy-done.6), channel_id=1, source_target_pairs={{0,1},{1,0},{2,3},{3,2},{4,5},{5,4},{6,7},{7,6},{8,9},{9,8},{10,11... | collective-permute-start | bytes 6291464 | tf_op jit(solution)/shard_map/ppermute | solution.py:33
  135.2 49.9 %collective-permute-start.13 = (bf16[1024,1024]{1,0:T(8,128)(2,1)}, bf16[1024,1024]{1,0:T(8,128)(2,1)}, u32[]{:S(2)}, u32[]{:S(2)}) collective-permute-start(bf16[1024,1024]{1,0:T(8,128)(2,1)} %collective-permute-done.9.refs_2_), channel_id=1, source_target_pairs={{0,1},{1,0},{2,3},{3,2},{4,5},{5,4},{6,7},{7,6},{8,9},{9,8},{10,11... | collective-permute-start | bytes 6291464 | tf_op jit(solution)/shard_map/ppermute | solution.py:33
  175.9 9.1 %collective-permute-start.14 = (bf16[1024,1024]{1,0:T(8,128)(2,1)}, bf16[1024,1024]{1,0:T(8,128)(2,1)}, u32[]{:S(2)}, u32[]{:S(2)}) collective-permute-start(bf16[1024,1024]{1,0:T(8,128)(2,1)} %collective-permute-done.10.refs_3_), channel_id=1, source_target_pairs={{0,1},{1,0},{2,3},{3,2},{4,5},{5,4},{6,7},{7,6},{8,9},{9,8},{10,11... | collective-permute-start | bytes 6291464 | tf_op jit(solution)/shard_map/ppermute | solution.py:33
  181.2 34.9 %all-to-all-start.3 = ((bf16[32,72,512]{2,1,0:T(8,128)(2,1)}), bf16[32,72,512]{2,1,0:T(8,128)(2,1)S(1)}, u32[]{:S(2)}, u32[]{:S(2)}) async-start(bf16[32,72,512]{2,1,0:T(8,128)(2,1)} %sum_blocks.1), calls=%async_computation.3 | async-start | bytes 4718592 | tf_op jit(solution)/shard_map/all_to_all | solution.py:41

commit v5 on v4

--- a/solution.py
+++ b/solution.py
@@ -97,20 +97,40 @@
                 g_ref[f, b, rank:, :] = pack(g[f * cols : (f + 1) * cols], feats // rank)
 
 
-def base_kernel(blocks, pieces, f_ref, x_ref, dy_ref, u_ref, v_ref, up_ref, down_ref, *refs):
-    w_refs, (y_ref, dx_ref, acc_ref, w_buf, sem) = refs[:pieces], refs[pieces:]
+def base_kernel(blocks, quarter, f_ref, x_ref, dy_ref, u_ref, v_ref, up_ref, down_ref, *refs):
+    w_refs, (y_ref, dx_ref, acc_ref, w_buf, sem) = refs[:-5], refs[-5:]
     rows = dy_ref.shape[0] // blocks
     step, steps = pl.program_id(0), pl.num_programs(0)
     feats = w_buf.shape[1]
-    per = steps // pieces
+    per = steps // 2
 
     def fetch(i):
-        for k, w_ref in enumerate(w_refs):
-
-            @pl.when(i // per == k)
+        slot, m = i % 2, i % per
+
+        def start(src, k):
+            to = w_buf.at[slot, pl.ds(pl.multiple_of(f_ref[steps + k], quarter), quarter)]
+            pltpu.make_async_copy(src, to, sem.at[slot]).start()
+
+        for core in range(2):
+            own, x, ring, back, ahead, lo, hi = w_refs[7 * core : 7 * core + 7]
+            for k, w_ref in enumerate((own, x)):
+
+                @pl.when(i == core * per + k)
+                def _():
+                    pltpu.make_async_copy(w_ref, w_buf.at[slot], sem.at[slot]).start()
+
+            @pl.when((i // per == core) & (m >= 2))
             def _():
-                at = pl.ds(pl.multiple_of(i % per * feats, feats), feats)
-                pltpu.make_async_copy(w_ref.at[at], w_buf.at[i % 2], sem.at[i % 2]).start()
+                for k, w_ref in enumerate((ring, back, ahead)):
+                    start(w_ref.at[m - 2], k)
+
+            @pl.when((i // per == core) & (m >= 2) & (m < 5))
+            def _():
+                start(lo.at[m - 2], 3)
+
+            @pl.when((i // per == core) & (m >= 5))
+            def _():
+                start(hi.at[m - 5], 3)
 
     @pl.when(step == 0)
     def _():
@@ -122,7 +142,7 @@
         fetch(step + 1)
 
     slot = step % 2
-    pltpu.make_async_copy(w_refs[0].at[pl.ds(0, feats)], w_buf.at[slot], sem.at[slot]).wait()
+    pltpu.make_async_copy(w_refs[0], w_buf.at[slot], sem.at[slot]).wait()
     w = w_buf[slot]
     acc_ref[...] += nn(x_ref[...], w)
     wide = nt(dy_ref[...], w)
@@ -193,10 +213,6 @@
     adapters = slots * ys * xhs
     y_at, xh_at = lax.axis_index("y"), lax.axis_index("xh")
     z_at, xl_at, c_at = (lax.axis_index(a) for a in FSDP)
-    w_back, w_next = shift(weight, "z", 1), shift(weight, "z", -1)
-    mid = feats // 2
-    w_lo, w_hi = shift(w_back[:mid], "z", 1), shift(w_next[mid:], "z", -1)
-
     ids_out = jnp.broadcast_to(jnp.pad(ids, (0, 128 - blocks)), (steps, 8, 128))
     ids_all = exchange(ids_out, FSDP)
 
@@ -206,23 +222,31 @@
     own = jnp.concatenate([jnp.swapaxes(down, 1, 2), up_packed], axis=1)
     x_all = jnp.stack([own, shift(own, "xh", 1)])
     one, three = shift(x_all, "y", 1), shift(x_all, "y", -1)
-    lo, hi = shift(one[:, : slots // 2], "y", 1), shift(three[:, slots // 2 :], "y", -1)
+
+    w_x = lax.ppermute(gate(weight, x_all), X, [(0, 3), (3, 0), (1, 2), (2, 1)])
+    quarter = feats // ys
+    mine = lax.dynamic_slice_in_dim(jnp.stack([weight, w_x]), y_at * quarter, quarter, axis=1)
+    mine = gate(mine, ids_all)
+    z_back, z_next = shift(mine, "z", 1), shift(mine, "z", -1)
+
+    lo = shift(gate(one, ids_all)[:, : slots // 2], "y", 1)
+    hi = shift(gate(three, ids_all)[:, slots // 2 :], "y", -1)
     every = jnp.stack([x_all, one, jnp.concatenate([lo, hi], axis=1), three])
 
-    ids_all = gate(ids_all, lo, hi)[:, 0, :blocks]
+    ids_all = ids_all[:, 0, :blocks]
     want = ids_all.reshape(steps * blocks)
     owner = want // slots
     oy, ox = (y_at - owner // xhs) % ys, (xh_at - owner % xhs) % xhs
     at = (oy * xhs + ox) * slots + want % slots
-    every = gate(every, w_lo, w_hi)
+    every = gate(every, z_back, z_next)
     picked = every.reshape(adapters, *own.shape[1:])[at].reshape(steps, blocks, *own.shape[1:])
     low = exchange(picked, FSDP)
 
-    near = jnp.concatenate([gate(weight, picked), w_next])
-    far = jnp.concatenate([gate(w_back, picked), w_lo, w_hi])
-    across = [(0, 3), (3, 0), (1, 2), (2, 1)]
-    near_x = lax.ppermute(near, X, across)
-    low = gate(low, near_x)
+    z_lo = shift(gate(z_back, picked)[:1], "z", 1)
+    z_hi = shift(gate(z_next, picked)[1:], "z", -1)
+    ring = jnp.concatenate([z_back, z_next, z_lo, z_hi])
+    y_back, y_next = shift(ring, "y", 1), shift(ring, "y", -1)
+    low = gate(low, y_back, y_next)
 
     grid = 4
     per = steps // grid
@@ -255,22 +279,21 @@
         cost_estimate=cost(rows_dev * rank * 4 * (width + value), 16 << 20),
         name="low",
     )(fill, *(hbm(a) for a in (tokens, dy, low, low)))
-    far_x = lax.ppermute(gate(far, low_u), X, across)
+    y_lo = shift(gate(y_back, low_u)[:3], "y", 1)
+    y_hi = shift(gate(y_next, low_u)[3:], "y", -1)
     back = exchange(grads, FSDP)
 
-    w_own = [near, far, near_x, far_x]
-    w_other = [shift(gate(w, low_u), "c", 1) for w in w_own]
-    w_all = w_own + w_other
+    w_own = [weight, w_x, ring, y_back, y_next, y_lo, y_hi]
+    w_all = w_own + [shift(gate(w, low_u), "c", 1) for w in w_own]
     order = [
         (z_at + dz) % 4 * 4 + (xl_at + dx) % 2 * 2 + (c_at + dc) % 2
         for dc in (0, 1)
+        for dz in (0, 3, 1, 2)
         for dx in (0, 1)
-        for dz in (0, 1, 3, 2)
-    ]
-
+    ] + [(y_at + dy) % ys * quarter for dy in (0, 3, 1, 2)]
 
     values, input_gradient = pl.pallas_call(
-        functools.partial(base_kernel, blocks, len(w_all)),
+        functools.partial(base_kernel, blocks, quarter),
         grid_spec=pltpu.PrefetchScalarGridSpec(
             num_scalar_prefetch=1,
             grid=(steps,),

time: 220 us -> 252 us (1.15)
  waiting for transfers between devices: 114 us -> 146 us
    ppermute x13 -> x20, waiting for transfers between devices: 24.3 us -> 116 us  [shift(): return lax.ppermute(x, axis, [(i, (i + by) % n) for i in range(n)])]
    ppermute x2 -> x1, waiting for transfers between devices: 81.7 us -> 3.78 us  [body(): w_x = lax.ppermute(gate(weight, x_all), X, [(0, 3), (3, 0), (1, 2), (2, 1)])]
    all_to_all x4, waiting for transfers between devices: 8.01 us -> 26.6 us  [exchange(): return lax.all_to_all(x, axis, split_axis=0, concat_axis=0, tiled=True)]
    ppermute x13 -> x20, starting transfers between devices: 18 us -> 23.5 us  [shift(): return lax.ppermute(x, axis, [(i, (i + by) % n) for i in range(n)])]
    ppermute x2 -> x1, starting transfers between devices: 6.17 us -> 3.06 us  [body(): w_x = lax.ppermute(gate(weight, x_all), X, [(0, 3), (3, 0), (1, 2), (2, 1)])]
    unnamed x21 -> x17, local copies, waits for them, and re-layouts: 5.85 us -> 7.1 us
  transfers between devices with their start and end apart: 19 -> 25, of which waited for: 9 -> 15; matrix products, arithmetic and copies ran while one was open for 6% -> 5% of each run, Pallas kernels for 14% -> 12%
where the time goes in v5:
time: 252 us; the launch traced here: 251 us
  waiting for transfers between devices  146 us (58%)
  starting transfers between devices  44 us (17%)
  Pallas kernels  38.6 us (15%)
  local copies, waits for them, and re-layouts  16.8 us (7%)
  other arithmetic  3.98 us (2%)
    ppermute x20, waiting for transfers between devices, shift(): return lax.ppermute(x, axis, [(i, (i + by) % n) for i in range(n)])  116 us
    all_to_all x4, waiting for transfers between devices, exchange(): return lax.all_to_all(x, axis, split_axis=0, concat_axis=0, tiled=True)  26.6 us
    pallas_call x1, Pallas kernels, body(): pl.pallas_call(functools.partial(base_kernel, blocks, quarter), grid_spec...  25.9 us
    ppermute x20, starting transfers between devices, shift(): return lax.ppermute(x, axis, [(i, (i + by) % n) for i in range(n)])  23.5 us
    all_to_all x4, starting transfers between devices, exchange(): return lax.all_to_all(x, axis, split_axis=0, concat_axis=0, tiled=True)  17.4 us
    pallas_call x1, Pallas kernels, body(): pl.pallas_call(functools.partial(low_kernel, blocks, per), grid=(grid,),...  9.37 us
    unnamed x17, local copies, waits for them, and re-layouts  7.1 us
  transfers between devices with their start and end apart: 25, of which 15 were waited for; matrix products, arithmetic and copies ran while one was open for 5% of the time, Pallas kernels for 12%

profile of v5, /device:TPU:0, one launch (start us, length us, event | category | flops | bytes accessed | tf_op | source)
XLA Modules:
  0.0 250.5 jit_solution(3340647759312632768)
XLA Ops:
  2.7 3.2 %collective-permute-start = (bf16[4,72,512]{2,1,0:T(8,128)(2,1)S(1)}, bf16[4,72,512]{2,1,0:T(8,128)(2,1)S(1)}, u32[]{:S(2)}, u32[]{:S(2)}) collective-permute-start(bf16[4,72,512]{2,1,0:T(8,128)(2,1)S(1)} %get-tuple-element.63), channel_id=1, source_target_pairs={{0,16},{16,0},{1,17},{17,1},{2,18},{18,2},{3,19},{19,3},{4,20},{20... | collective-permute-start | bytes 884744 | tf_op jit(solution)/shard_map/ppermute | solution.py:33
  5.9 7.0 %collective-permute-done = bf16[4,72,512]{2,1,0:T(8,128)(2,1)S(1)} collective-permute-done((bf16[4,72,512]{2,1,0:T(8,128)(2,1)S(1)}, bf16[4,72,512]{2,1,0:T(8,128)(2,1)S(1)}, u32[]{:S(2)}, u32[]{:S(2)}) %collective-permute-start) | collective-permute-done | bytes 294944 | tf_op jit(solution)/shard_map/ppermute | solution.py:33
  13.0 3.1 %collective-permute-start.5 = (bf16[512,1024]{1,0:T(8,128)(2,1)}, bf16[512,1024]{1,0:T(8,128)(2,1)}, u32[]{:S(2)}, u32[]{:S(2)}) collective-permute-start(bf16[512,1024]{1,0:T(8,128)(2,1)} %refs_0_.1), channel_id=1, source_target_pairs={{0,18},{18,0},{2,16},{16,2},{1,19},{19,1},{3,17},{17,3},{4,22},{22... | collective-permute-start | bytes 3145736 | tf_op jit(solution)/shard_map/ppermute | solution.py:226
  16.1 3.0 %collective-permute-start.3 = (bf16[2,4,72,512]{3,2,1,0:T(8,128)(2,1)S(1)}, bf16[2,4,72,512]{3,2,1,0:T(8,128)(2,1)S(1)}, u32[]{:S(2)}, u32[]{:S(2)}) collective-permute-start(bf16[2,4,72,512]{3,2,1,0:T(8,128)(2,1)S(1)} %get-tuple-element.61), channel_id=1, source_target_pairs={{0,96},{32,0},{64,32},{96,64},{1,97},{33,1},{65,33},{97,65},{2,98}... | collective-permute-start | bytes 1769480 | tf_op jit(solution)/shard_map/ppermute | solution.py:33
  19.7 5.4 %all-to-all-start = ((s32[16,8,128]{2,1,0:T(8,128)}), s32[16,8,128]{2,1,0:T(8,128)S(1)}, u32[]{:S(2)}, u32[]{:S(2)}) async-start(s32[16,8,128]{2,1,0:T(8,128)} %broadcast_in_dim.4), calls=%async_computation | async-start | bytes 131072 | tf_op jit(solution)/shard_map/all_to_all | solution.py:41
  25.1 6.2 %all-to-all-done = s32[16,8,128]{2,1,0:T(8,128)S(1)} async-done(((s32[16,8,128]{2,1,0:T(8,128)}), s32[16,8,128]{2,1,0:T(8,128)S(1)}, u32[]{:S(2)}, u32[]{:S(2)}) %all-to-all-start) | async-done | bytes 65568 | tf_op jit(solution)/shard_map/all_to_all | solution.py:41
  31.5 3.3 %collective-permute-start.4 = (bf16[2,2,72,512]{3,2,1,0:T(8,128)(2,1)S(1)}, bf16[2,2,72,512]{3,2,1,0:T(8,128)(2,1)S(1)}, u32[]{:S(2)}, u32[]{:S(2)}) collective-permute-start(bf16[2,2,72,512]{3,2,1,0:T(8,128)(2,1)S(1)} %slice.28), channel_id=1, source_target_pairs={{0,96},{32,0},{64,32},{96,64},{1,97},{33,1},{65,33},{97,65},{2,98}... | collective-permute-start | bytes 884744 | tf_op jit(solution)/shard_map/ppermute | solution.py:33
  34.9 3.8 %collective-permute-done.5.refs_1_ = bf16[512,1024]{1,0:T(8,128)(2,1)} collective-permute-done((bf16[512,1024]{1,0:T(8,128)(2,1)}, bf16[512,1024]{1,0:T(8,128)(2,1)}, u32[]{:S(2)}, u32[]{:S(2)}) %collective-permute-start.5) | collective-permute-done | bytes 1048608 | tf_op jit(solution)/shard_map/ppermute | solution.py:226
  39.7 4.3 %collective-permute-start.7 = (bf16[2,128,1024]{2,1,0:T(8,128)(2,1)S(1)}, bf16[2,128,1024]{2,1,0:T(8,128)(2,1)}, u32[]{:S(2)}, u32[]{:S(2)}) collective-permute-start(bf16[2,128,1024]{2,1,0:T(8,128)(2,1)S(1)} %fusion), channel_id=1, source_target_pairs={{0,12},{4,0},{8,4},{12,8},{1,13},{5,1},{9,5},{13,9},{2,14},{6,2},{... | collective-permute-start | bytes 1572872 | tf_op jit(solution)/shard_map/ppermute | solution.py:33
  46.2 7.2 %collective-permute-done.7 = bf16[2,128,1024]{2,1,0:T(8,128)(2,1)} collective-permute-done((bf16[2,128,1024]{2,1,0:T(8,128)(2,1)S(1)}, bf16[2,128,1024]{2,1,0:T(8,128)(2,1)}, u32[]{:S(2)}, u32[]{:S(2)}) %collective-permute-start.7) | collective-permute-done | bytes 524320 | tf_op jit(solution)/shard_map/ppermute | solution.py:33
  53.4 3.5 %collective-permute-done.6 = bf16[2,128,1024]{2,1,0:T(8,128)(2,1)} collective-permute-done((bf16[2,128,1024]{2,1,0:T(8,128)(2,1)S(1)}, bf16[2,128,1024]{2,1,0:T(8,128)(2,1)}, u32[]{:S(2)}, u32[]{:S(2)}) %collective-permute-start.6) | collective-permute-done | bytes 524320 | tf_op jit(solution)/shard_map/ppermute | solution.py:33
  56.9 2.7 %gather_fusion = bf16[48,72,512]{2,1,0:T(8,128)(2,1)} fusion(bf16[32,72,512]{2,1,0:T(8,128)(2,1)S(1)} %bitcast.53, s32[1024]{0:T(1024)S(1)} %pad_clamp_fusion), kind=kCustom, calls=%fused_computation | custom fusion | bytes 7078080 | tf_op jit(solution)/shard_map/gather | solution.py:242
  59.6 4.5 %all-to-all-start.1 = ((bf16[16,3,72,512]{3,2,1,0:T(8,128)(2,1)}), bf16[16,3,72,512]{3,2,1,0:T(8,128)(2,1)}, u32[]{:S(2)}, u32[]{:S(2)}) async-start(bf16[16,3,72,512]{3,2,1,0:T(8,128)(2,1)} %bitcast.54), calls=%async_computation.1 | async-start | bytes 7077888 | tf_op jit(solution)/shard_map/all_to_all | solution.py:41
  65.1 1.8 collective-permute-start.8
  67.9 1.5 collective-permute-start.9
  69.5 1.9 constant_dynamic-update-slice_fusion.3
  71.3 1.9 constant_dynamic-update-slice_fusion.2
  73.2 38.7 %collective-permute-done.8 = bf16[1,128,1024]{2,1,0:T(8,128)(2,1)S(1)} collective-permute-done((bf16[1,128,1024]{2,1,0:T(8,128)(2,1)S(1)}, bf16[1,128,1024]{2,1,0:T(8,128)(2,1)S(1)}, u32[]{:S(2)}, u32[]{:S(2)}) %collective-permute-start.8) | collective-permute-done | bytes 262176 | tf_op jit(solution)/shard_map/ppermute | solution.py:33
  113.4 3.0 %collective-permute-start.11 = (bf16[6,128,1024]{2,1,0:T(8,128)(2,1)}, bf16[6,128,1024]{2,1,0:T(8,128)(2,1)}, u32[]{:S(2)}, u32[]{:S(2)}) collective-permute-start(bf16[6,128,1024]{2,1,0:T(8,128)(2,1)} %constant_dynamic-update-slice_fusion.refs_2_), channel_id=1, source_target_pairs={{0,96},{32,0},{64,32},{96,64},{1,97},{33,1},{65,33},{97,65},{2,98}... | collective-permute-start | bytes 4718600 | tf_op jit(solution)/shard_map/ppermute | solution.py:33
  116.4 33.8 %collective-permute-done.11.refs_4_ = bf16[6,128,1024]{2,1,0:T(8,128)(2,1)} collective-permute-done((bf16[6,128,1024]{2,1,0:T(8,128)(2,1)}, bf16[6,128,1024]{2,1,0:T(8,128)(2,1)}, u32[]{:S(2)}, u32[]{:S(2)}) %collective-permute-start.11) | collective-permute-done | bytes 1572896 | tf_op jit(solution)/shard_map/ppermute | solution.py:33
  150.1 3.4 %collective-permute-done.10.refs_3_ = bf16[6,128,1024]{2,1,0:T(8,128)(2,1)} collective-permute-done((bf16[6,128,1024]{2,1,0:T(8,128)(2,1)}, bf16[6,128,1024]{2,1,0:T(8,128)(2,1)}, u32[]{:S(2)}, u32[]{:S(2)}) %collective-permute-start.10) | collective-permute-done | bytes 1572896 | tf_op jit(solution)/shard_map/ppermute | solution.py:33
  153.6 9.4 %low.1 = (bf16[384,64]{1,0:T(8,128)(2,1)}, bf16[384,64]{1,0:T(8,128)(2,1)}, bf16[3,1024,64]{2,1,0:T(8,128)(2,1)}, bf16[16,3,72,512]{3,2,1,0:T(8,128)(2,1)}) custom-call(s32[3]{0:T(128)S(1)} %copy-done, bf16[384,8192]{1,0:T(8,128)(2,1)} %x_ref.3, bf16[384,1024]{1,0:T(8,128)(2,1)} %dy_ref.3, bf16[16,3,72,512]{3,2,1,0:T(8,128)(2,1)} %all-to-all-done.1.packed_ref.down_ref, ...), custom_call_target="tpu_custom_call" | custom-call | flops 905969664 | bytes 16777216 | tf_op jit(solution)/shard_map/low/pallas_call | solution.py:255
  162.9 3.8 %all-to-all-start.2 = ((bf16[16,3,72,512]{3,2,1,0:T(8,128)(2,1)}), bf16[16,3,72,512]{3,2,1,0:T(8,128)(2,1)S(1)}, u32[]{:S(2)}, u32[]{:S(2)}) async-start(bf16[16,3,72,512]{3,2,1,0:T(8,128)(2,1)} %get-tuple-element.46), calls=%async_computation.2 | async-start | bytes 7077888 | tf_op jit(solution)/shard_map/all_to_all | solution.py:41
  169.4 1.8 collective-permute-start.12
  171.8 15.9 %collective-permute-done.13.refs_6_ = bf16[3,128,1024]{2,1,0:T(8,128)(2,1)S(1)} collective-permute-done((bf16[3,128,1024]{2,1,0:T(8,128)(2,1)S(1)}, bf16[3,128,1024]{2,1,0:T(8,128)(2,1)S(1)}, u32[]{:S(2)}, u32[]{:S(2)}) %collective-permute-start.13) | collective-permute-done | bytes 786464 | tf_op jit(solution)/shard_map/ppermute | solution.py:33
  187.7 2.5 collective-permute-done.12.refs_5_
  191.1 18.9 %all-to-all-done.2.g_ref = bf16[16,3,72,512]{3,2,1,0:T(8,128)(2,1)S(1)} async-done(((bf16[16,3,72,512]{3,2,1,0:T(8,128)(2,1)}), bf16[16,3,72,512]{3,2,1,0:T(8,128)(2,1)S(1)}, u32[]{:S(2)}, u32[]{:S(2)}) %all-to-all-start.2) | async-done | bytes 3538976 | tf_op jit(solution)/shard_map/all_to_all | solution.py:41
  210.0 3.3 %sum_blocks.1 = bf16[32,72,512]{2,1,0:T(8,128)(2,1)} custom-call(s32[16,3]{1,0:T(8,128)S(1)} %bitcast.52, bf16[16,3,72,512]{3,2,1,0:T(8,128)(2,1)S(1)} %all-to-all-done.2.g_ref), custom_call_target="tpu_custom_call" | custom-call | flops 1769472 | bytes 7077888 | tf_op jit(solution)/shard_map/sum_blocks/pallas_call | solution.py:193
  213.3 3.7 %all-to-all-start.3 = ((bf16[32,72,512]{2,1,0:T(8,128)(2,1)}), bf16[32,72,512]{2,1,0:T(8,128)(2,1)S(1)}, u32[]{:S(2)}, u32[]{:S(2)}) async-start(bf16[32,72,512]{2,1,0:T(8,128)(2,1)} %sum_blocks.1), calls=%async_computation.3 | async-start | bytes 4718592 | tf_op jit(solution)/shard_map/all_to_all | solution.py:41
  217.8 1.9 collective-permute-done.20.refs_13_
  220.9 25.9 %base.1 = (bf16[384,1024]{1,0:T(8,128)(2,1)}, bf16[384,8192]{1,0:T(8,128)(2,1)}) custom-call(s32[20]{0:T(128)S(1)} %stack.116.f_ref, bf16[384,8192]{1,0:T(8,128)(2,1)} %x_ref.3, bf16[384,1024]{1,0:T(8,128)(2,1)} %dy_ref.3, bf16[384,64]{1,0:T(8,128)(2,1)} %get-tuple-element.34.u_ref, bf16[384,64]{1,0:T(8,128)(2,1)} %get-tuple-element.35.v_ref, ...), custom_call_target="tpu_custom_call" | custom-call | flops 12884901888 | bytes 37748736 | tf_op jit(solution)/shard_map/base/pallas_call | solution.py:295
  246.8 1.5 all-to-all-done.3
  (66 shorter events, 17.8 us)
Async XLA Ops:
  0.6 18.4 %copy-start.5 = (s32[3]{0:T(128)S(1)}, s32[3]{0:T(128)}, u32[]{:S(2)}) copy-start(s32[3]{0:T(128)} %param.12) | copy-start | bytes 40
  2.7 10.2 %collective-permute-start = (bf16[4,72,512]{2,1,0:T(8,128)(2,1)S(1)}, bf16[4,72,512]{2,1,0:T(8,128)(2,1)S(1)}, u32[]{:S(2)}, u32[]{:S(2)}) collective-permute-start(bf16[4,72,512]{2,1,0:T(8,128)(2,1)S(1)} %get-tuple-element.63), channel_id=1, source_target_pairs={{0,16},{16,0},{1,17},{17,1},{2,18},{18,2},{3,19},{19,3},{4,20},{20... | collective-permute-start | bytes 884744 | tf_op jit(solution)/shard_map/ppermute | solution.py:33
  13.0 25.7 %collective-permute-start.5 = (bf16[512,1024]{1,0:T(8,128)(2,1)}, bf16[512,1024]{1,0:T(8,128)(2,1)}, u32[]{:S(2)}, u32[]{:S(2)}) collective-permute-start(bf16[512,1024]{1,0:T(8,128)(2,1)} %refs_0_.1), channel_id=1, source_target_pairs={{0,18},{18,0},{2,16},{16,2},{1,19},{19,1},{3,17},{17,3},{4,22},{22... | collective-permute-start | bytes 3145736 | tf_op jit(solution)/shard_map/ppermute | solution.py:226
  16.1 15.4 %collective-permute-start.3 = (bf16[2,4,72,512]{3,2,1,0:T(8,128)(2,1)S(1)}, bf16[2,4,72,512]{3,2,1,0:T(8,128)(2,1)S(1)}, u32[]{:S(2)}, u32[]{:S(2)}) collective-permute-start(bf16[2,4,72,512]{3,2,1,0:T(8,128)(2,1)S(1)} %get-tuple-element.61), channel_id=1, source_target_pairs={{0,96},{32,0},{64,32},{96,64},{1,97},{33,1},{65,33},{97,65},{2,98}... | collective-permute-start | bytes 1769480 | tf_op jit(solution)/shard_map/ppermute | solution.py:33
  19.1 15.7 %collective-permute-start.1 = (bf16[2,4,72,512]{3,2,1,0:T(8,128)(2,1)S(1)}, bf16[2,4,72,512]{3,2,1,0:T(8,128)(2,1)S(1)}, u32[]{:S(2)}, u32[]{:S(2)}) collective-permute-start(bf16[2,4,72,512]{3,2,1,0:T(8,128)(2,1)S(1)} %get-tuple-element.61), channel_id=1, source_target_pairs={{0,32},{32,64},{64,96},{96,0},{1,33},{33,65},{65,97},{97,1},{2,34}... | collective-permute-start | bytes 1769480 | tf_op jit(solution)/shard_map/ppermute | solution.py:33
  19.7 11.6 %all-to-all-start = ((s32[16,8,128]{2,1,0:T(8,128)}), s32[16,8,128]{2,1,0:T(8,128)S(1)}, u32[]{:S(2)}, u32[]{:S(2)}) async-start(s32[16,8,128]{2,1,0:T(8,128)} %broadcast_in_dim.4), calls=%async_computation | async-start | bytes 131072 | tf_op jit(solution)/shard_map/all_to_all | solution.py:41
  31.5 12.6 %collective-permute-start.4 = (bf16[2,2,72,512]{3,2,1,0:T(8,128)(2,1)S(1)}, bf16[2,2,72,512]{3,2,1,0:T(8,128)(2,1)S(1)}, u32[]{:S(2)}, u32[]{:S(2)}) collective-permute-start(bf16[2,2,72,512]{3,2,1,0:T(8,128)(2,1)S(1)} %slice.28), channel_id=1, source_target_pairs={{0,96},{32,0},{64,32},{96,64},{1,97},{33,1},{65,33},{97,65},{2,98}... | collective-permute-start | bytes 884744 | tf_op jit(solution)/shard_map/ppermute | solution.py:33
  34.8 10.1 %copy-start.1 = (bf16[2,4,72,512]{3,2,1,0:T(8,128)(2,1)}, bf16[2,4,72,512]{3,2,1,0:T(8,128)(2,1)S(1)}, u32[]{:S(2)}) copy-start(bf16[2,4,72,512]{3,2,1,0:T(8,128)(2,1)S(1)} %collective-permute-done.1) | copy-start | bytes 1769476
  34.8 10.0 %collective-permute-start.2 = (bf16[2,2,72,512]{3,2,1,0:T(8,128)(2,1)S(1)}, bf16[2,2,72,512]{3,2,1,0:T(8,128)(2,1)S(1)}, u32[]{:S(2)}, u32[]{:S(2)}) collective-permute-start(bf16[2,2,72,512]{3,2,1,0:T(8,128)(2,1)S(1)} %slice.27), channel_id=1, source_target_pairs={{0,32},{32,64},{64,96},{96,0},{1,33},{33,65},{65,97},{97,1},{2,34}... | collective-permute-start | bytes 884744 | tf_op jit(solution)/shard_map/ppermute | solution.py:33
  39.7 13.7 %collective-permute-start.7 = (bf16[2,128,1024]{2,1,0:T(8,128)(2,1)S(1)}, bf16[2,128,1024]{2,1,0:T(8,128)(2,1)}, u32[]{:S(2)}, u32[]{:S(2)}) collective-permute-start(bf16[2,128,1024]{2,1,0:T(8,128)(2,1)S(1)} %fusion), channel_id=1, source_target_pairs={{0,12},{4,0},{8,4},{12,8},{1,13},{5,1},{9,5},{13,9},{2,14},{6,2},{... | collective-permute-start | bytes 1572872 | tf_op jit(solution)/shard_map/ppermute | solution.py:33
  44.0 12.9 %collective-permute-start.6 = (bf16[2,128,1024]{2,1,0:T(8,128)(2,1)S(1)}, bf16[2,128,1024]{2,1,0:T(8,128)(2,1)}, u32[]{:S(2)}, u32[]{:S(2)}) collective-permute-start(bf16[2,128,1024]{2,1,0:T(8,128)(2,1)S(1)} %fusion), channel_id=1, source_target_pairs={{0,4},{4,8},{8,12},{12,0},{1,5},{5,9},{9,13},{13,1},{2,6},{6,10},{... | collective-permute-start | bytes 1572872 | tf_op jit(solution)/shard_map/ppermute | solution.py:33
  59.6 94.0 %all-to-all-start.1 = ((bf16[16,3,72,512]{3,2,1,0:T(8,128)(2,1)}), bf16[16,3,72,512]{3,2,1,0:T(8,128)(2,1)}, u32[]{:S(2)}, u32[]{:S(2)}) async-start(bf16[16,3,72,512]{3,2,1,0:T(8,128)(2,1)} %bitcast.54), calls=%async_computation.1 | async-start | bytes 7077888 | tf_op jit(solution)/shard_map/all_to_all | solution.py:41
  64.1 89.4 %copy-start = (s32[3]{0:T(128)S(1)}, s32[3]{0:T(128)}, u32[]{:S(2)}) copy-start(s32[3]{0:T(128)} %fill_ref.1) | copy-start | bytes 40
  65.1 46.8 %collective-permute-start.8 = (bf16[1,128,1024]{2,1,0:T(8,128)(2,1)S(1)}, bf16[1,128,1024]{2,1,0:T(8,128)(2,1)S(1)}, u32[]{:S(2)}, u32[]{:S(2)}) collective-permute-start(bf16[1,128,1024]{2,1,0:T(8,128)(2,1)S(1)} %slice.30), channel_id=1, source_target_pairs={{0,4},{4,8},{8,12},{12,0},{1,5},{5,9},{9,13},{13,1},{2,6},{6,10},{... | collective-permute-start | bytes 786440 | tf_op jit(solution)/shard_map/ppermute | solution.py:33
  67.9 44.7 %collective-permute-start.9 = (bf16[1,128,1024]{2,1,0:T(8,128)(2,1)S(1)}, bf16[1,128,1024]{2,1,0:T(8,128)(2,1)S(1)}, u32[]{:S(2)}, u32[]{:S(2)}) collective-permute-start(bf16[1,128,1024]{2,1,0:T(8,128)(2,1)S(1)} %slice.31), channel_id=1, source_target_pairs={{0,12},{4,0},{8,4},{12,8},{1,13},{5,1},{9,5},{13,9},{2,14},{6,2},{... | collective-permute-start | bytes 786440 | tf_op jit(solution)/shard_map/ppermute | solution.py:33
  113.4 36.8 %collective-permute-start.11 = (bf16[6,128,1024]{2,1,0:T(8,128)(2,1)}, bf16[6,128,1024]{2,1,0:T(8,128)(2,1)}, u32[]{:S(2)}, u32[]{:S(2)}) collective-permute-start(bf16[6,128,1024]{2,1,0:T(8,128)(2,1)} %constant_dynamic-update-slice_fusion.refs_2_), channel_id=1, source_target_pairs={{0,96},{32,0},{64,32},{96,64},{1,97},{33,1},{65,33},{97,65},{2,98}... | collective-permute-start | bytes 4718600 | tf_op jit(solution)/shard_map/ppermute | solution.py:33
  116.4 37.2 %collective-permute-start.10 = (bf16[6,128,1024]{2,1,0:T(8,128)(2,1)}, bf16[6,128,1024]{2,1,0:T(8,128)(2,1)}, u32[]{:S(2)}, u32[]{:S(2)}) collective-permute-start(bf16[6,128,1024]{2,1,0:T(8,128)(2,1)} %constant_dynamic-update-slice_fusion.refs_2_), channel_id=1, source_target_pairs={{0,32},{32,64},{64,96},{96,0},{1,33},{33,65},{65,97},{97,1},{2,34}... | collective-permute-start | bytes 4718600 | tf_op jit(solution)/shard_map/ppermute | solution.py:33
  162.9 47.1 %all-to-all-start.2 = ((bf16[16,3,72,512]{3,2,1,0:T(8,128)(2,1)}), bf16[16,3,72,512]{3,2,1,0:T(8,128)(2,1)S(1)}, u32[]{:S(2)}, u32[]{:S(2)}) async-start(bf16[16,3,72,512]{3,2,1,0:T(8,128)(2,1)} %get-tuple-element.46), calls=%async_computation.2 | async-start | bytes 7077888 | tf_op jit(solution)/shard_map/all_to_all | solution.py:41
  167.9 19.8 %collective-permute-start.13 = (bf16[3,128,1024]{2,1,0:T(8,128)(2,1)S(1)}, bf16[3,128,1024]{2,1,0:T(8,128)(2,1)S(1)}, u32[]{:S(2)}, u32[]{:S(2)}) collective-permute-start(bf16[3,128,1024]{2,1,0:T(8,128)(2,1)S(1)} %slice.33), channel_id=1, source_target_pairs={{0,96},{32,0},{64,32},{96,64},{1,97},{33,1},{65,33},{97,65},{2,98}... | collective-permute-start | bytes 2359304 | tf_op jit(solution)/shard_map/ppermute | solution.py:33
  169.4 20.7 %collective-permute-start.12 = (bf16[3,128,1024]{2,1,0:T(8,128)(2,1)S(1)}, bf16[3,128,1024]{2,1,0:T(8,128)(2,1)S(1)}, u32[]{:S(2)}, u32[]{:S(2)}) collective-permute-start(bf16[3,128,1024]{2,1,0:T(8,128)(2,1)S(1)} %slice.32), channel_id=1, source_target_pairs={{0,32},{32,64},{64,96},{96,0},{1,33},{33,65},{65,97},{97,1},{2,34}... | collective-permute-start | bytes 2359304 | tf_op jit(solution)/shard_map/ppermute | solution.py:33
  171.2 45.8 %collective-permute-start.14 = (bf16[512,1024]{1,0:T(8,128)(2,1)}, bf16[512,1024]{1,0:T(8,128)(2,1)}, u32[]{:S(2)}, u32[]{:S(2)}) collective-permute-start(bf16[512,1024]{1,0:T(8,128)(2,1)} %refs_0_.1), channel_id=1, source_target_pairs={{0,1},{1,0},{2,3},{3,2},{4,5},{5,4},{6,7},{7,6},{8,9},{9,8},{10,11... | collective-permute-start | bytes 3145736 | tf_op jit(solution)/shard_map/ppermute | solution.py:33
  171.2 45.9 %collective-permute-start.15 = (bf16[512,1024]{1,0:T(8,128)(2,1)}, bf16[512,1024]{1,0:T(8,128)(2,1)}, u32[]{:S(2)}, u32[]{:S(2)}) collective-permute-start(bf16[512,1024]{1,0:T(8,128)(2,1)} %collective-permute-done.5.refs_1_), channel_id=1, source_target_pairs={{0,1},{1,0},{2,3},{3,2},{4,5},{5,4},{6,7},{7,6},{8,9},{9,8},{10,11... | collective-permute-start | bytes 3145736 | tf_op jit(solution)/shard_map/ppermute | solution.py:33
  171.8 49.2 %collective-permute-start.17 = (bf16[6,128,1024]{2,1,0:T(8,128)(2,1)}, bf16[6,128,1024]{2,1,0:T(8,128)(2,1)}, u32[]{:S(2)}, u32[]{:S(2)}) collective-permute-start(bf16[6,128,1024]{2,1,0:T(8,128)(2,1)} %collective-permute-done.10.refs_3_), channel_id=1, source_target_pairs={{0,1},{1,0},{2,3},{3,2},{4,5},{5,4},{6,7},{7,6},{8,9},{9,8},{10,11... | collective-permute-start | bytes 4718600 | tf_op jit(solution)/shard_map/ppermute | solution.py:33
  187.7 2.5 copy-start.2
  187.7 33.2 %collective-permute-start.18 = (bf16[6,128,1024]{2,1,0:T(8,128)(2,1)}, bf16[6,128,1024]{2,1,0:T(8,128)(2,1)}, u32[]{:S(2)}, u32[]{:S(2)}) collective-permute-start(bf16[6,128,1024]{2,1,0:T(8,128)(2,1)} %collective-permute-done.11.refs_4_), channel_id=1, source_target_pairs={{0,1},{1,0},{2,3},{3,2},{4,5},{5,4},{6,7},{7,6},{8,9},{9,8},{10,11... | collective-permute-start | bytes 4718600 | tf_op jit(solution)/shard_map/ppermute | solution.py:33
  190.2 0.9 copy-start.4
  191.1 29.8 %collective-permute-start.16 = (bf16[6,128,1024]{2,1,0:T(8,128)(2,1)}, bf16[6,128,1024]{2,1,0:T(8,128)(2,1)}, u32[]{:S(2)}, u32[]{:S(2)}) collective-permute-start(bf16[6,128,1024]{2,1,0:T(8,128)(2,1)} %constant_dynamic-update-slice_fusion.refs_2_), channel_id=1, source_target_pairs={{0,1},{1,0},{2,3},{3,2},{4,5},{5,4},{6,7},{7,6},{8,9},{9,8},{10,11... | collective-permute-start | bytes 4718600 | tf_op jit(solution)/shard_map/ppermute | solution.py:33
  213.3 3.8 %copy-start.3 = (bf16[3,128,1024]{2,1,0:T(8,128)(2,1)S(1)}, bf16[3,128,1024]{2,1,0:T(8,128)(2,1)}, u32[]{:S(2)}) copy-start(bf16[3,128,1024]{2,1,0:T(8,128)(2,1)} %copy-done.2) | copy-start | bytes 2359300
  213.3 35.1 %all-to-all-start.3 = ((bf16[32,72,512]{2,1,0:T(8,128)(2,1)}), bf16[32,72,512]{2,1,0:T(8,128)(2,1)S(1)}, u32[]{:S(2)}, u32[]{:S(2)}) async-start(bf16[32,72,512]{2,1,0:T(8,128)(2,1)} %sum_blocks.1), calls=%async_computation.3 | async-start | bytes 4718592 | tf_op jit(solution)/shard_map/all_to_all | solution.py:41
  217.1 2.6 %collective-permute-start.20 = (bf16[3,128,1024]{2,1,0:T(8,128)(2,1)S(1)}, bf16[3,128,1024]{2,1,0:T(8,128)(2,1)}, u32[]{:S(2)}, u32[]{:S(2)}) collective-permute-start(bf16[3,128,1024]{2,1,0:T(8,128)(2,1)S(1)} %copy-done.3), channel_id=1, source_target_pairs={{0,1},{1,0},{2,3},{3,2},{4,5},{5,4},{6,7},{7,6},{8,9},{9,8},{10,11... | collective-permute-start | bytes 2359304 | tf_op jit(solution)/shard_map/ppermute | solution.py:33
  217.2 3.7 %collective-permute-start.19 = (bf16[3,128,1024]{2,1,0:T(8,128)(2,1)}, bf16[3,128,1024]{2,1,0:T(8,128)(2,1)}, u32[]{:S(2)}, u32[]{:S(2)}) collective-permute-start(bf16[3,128,1024]{2,1,0:T(8,128)(2,1)} %copy-done.4), channel_id=1, source_target_pairs={{0,1},{1,0},{2,3},{3,2},{4,5},{5,4},{6,7},{7,6},{8,9},{9,8},{10,11... | collective-permute-start | bytes 2359304 | tf_op jit(solution)/shard_map/ppermute | solution.py:33

commit v6 on v5

--- a/solution.py
+++ b/solution.py
@@ -216,6 +216,10 @@
     ids_out = jnp.broadcast_to(jnp.pad(ids, (0, 128 - blocks)), (steps, 8, 128))
     ids_all = exchange(ids_out, FSDP)
 
+    quarter = feats // ys
+    mine = lax.dynamic_slice_in_dim(weight, y_at * quarter, quarter)
+    z_back, z_next = shift(mine, "z", 1), shift(mine, "z", -1)
+
     folds = feats // rank
     up_t = jnp.swapaxes(up, 1, 2).reshape(slots, folds, cols // folds, rank)
     up_packed = jnp.swapaxes(up_t, 1, 2).reshape(slots, cols // folds, feats)
@@ -223,14 +227,15 @@
     x_all = jnp.stack([own, shift(own, "xh", 1)])
     one, three = shift(x_all, "y", 1), shift(x_all, "y", -1)
 
-    w_x = lax.ppermute(gate(weight, x_all), X, [(0, 3), (3, 0), (1, 2), (2, 1)])
-    quarter = feats // ys
-    mine = lax.dynamic_slice_in_dim(jnp.stack([weight, w_x]), y_at * quarter, quarter, axis=1)
-    mine = gate(mine, ids_all)
-    z_back, z_next = shift(mine, "z", 1), shift(mine, "z", -1)
-
-    lo = shift(gate(one, ids_all)[:, : slots // 2], "y", 1)
-    hi = shift(gate(three, ids_all)[:, slots // 2 :], "y", -1)
+    across = [(0, 3), (3, 0), (1, 2), (2, 1)]
+    w_x = lax.ppermute(gate(weight, x_all), X, across)
+    z_lo = shift(z_back[: quarter // 2], "z", 1)
+    z_hi = shift(z_next[quarter // 2 :], "z", -1)
+    ring = jnp.concatenate([z_back, z_next, z_lo, z_hi]).reshape(3, quarter, value)
+    ring_x = lax.ppermute(ring, X, across)
+
+    lo = shift(gate(one, ids_all, z_back, z_next)[:, : slots // 2], "y", 1)
+    hi = shift(gate(three, ids_all, z_back, z_next)[:, slots // 2 :], "y", -1)
     every = jnp.stack([x_all, one, jnp.concatenate([lo, hi], axis=1), three])
 
     ids_all = ids_all[:, 0, :blocks]
@@ -238,13 +243,11 @@
     owner = want // slots
     oy, ox = (y_at - owner // xhs) % ys, (xh_at - owner % xhs) % xhs
     at = (oy * xhs + ox) * slots + want % slots
-    every = gate(every, z_back, z_next)
+    every = gate(every, w_x, ring_x)
     picked = every.reshape(adapters, *own.shape[1:])[at].reshape(steps, blocks, *own.shape[1:])
     low = exchange(picked, FSDP)
 
-    z_lo = shift(gate(z_back, picked)[:1], "z", 1)
-    z_hi = shift(gate(z_next, picked)[1:], "z", -1)
-    ring = jnp.concatenate([z_back, z_next, z_lo, z_hi])
+    ring = jnp.concatenate([gate(ring, picked), ring_x])
     y_back, y_next = shift(ring, "y", 1), shift(ring, "y", -1)
     low = gate(low, y_back, y_next)
 
@@ -288,8 +291,7 @@
     order = [
         (z_at + dz) % 4 * 4 + (xl_at + dx) % 2 * 2 + (c_at + dc) % 2
         for dc in (0, 1)
-        for dz in (0, 3, 1, 2)
-        for dx in (0, 1)
+        for dx, dz in ((0, 0), (1, 0), (0, 3), (0, 1), (0, 2), (1, 3), (1, 1), (1, 2))
     ] + [(y_at + dy) % ys * quarter for dy in (0, 3, 1, 2)]
 
     values, input_gradient = pl.pallas_call(

time: 252 us -> 215 us (0.85)
  waiting for transfers between devices: 146 us -> 108 us
  starting transfers between devices: 44 us -> 48.8 us
  local copies, waits for them, and re-layouts: 16.8 us -> 13.6 us
    ppermute x20, waiting for transfers between devices: 116 us -> 71.6 us  [shift(): return lax.ppermute(x, axis, [(i, (i + by) % n) for i in range(n)])]
    ppermute x1 -> x2, waiting for transfers between devices: 3.78 us -> 12.6 us  [the longest x1 12.6 us: body(): ring_x = lax.ppermute(ring, X, across)]
    unnamed x17 -> x19, local copies, waits for them, and re-layouts: 7.1 us -> 3.56 us
    all_to_all x4, waiting for transfers between devices: 26.6 us -> 23.8 us  [exchange(): return lax.all_to_all(x, axis, split_axis=0, concat_axis=0, tiled=True)]
  transfers between devices with their start and end apart: 25 -> 26, of which waited for: 15 -> 13; matrix products, arithmetic and copies ran while one was open for 5% -> 5% of each run, Pallas kernels for 12% -> 14%
where the time goes in v6:
time: 215 us; the launch traced here: 214 us
  waiting for transfers between devices  108 us (50%)
  starting transfers between devices  48.8 us (23%)
  Pallas kernels  38.6 us (18%)
  local copies, waits for them, and re-layouts  13.6 us (6%)
  other arithmetic  3.96 us (2%)
    ppermute x20, waiting for transfers between devices, shift(): return lax.ppermute(x, axis, [(i, (i + by) % n) for i in range(n)])  71.6 us
    pallas_call x1, Pallas kernels, body(): pl.pallas_call(functools.partial(base_kernel, blocks, quarter), grid_spec...  25.9 us
    ppermute x20, starting transfers between devices, shift(): return lax.ppermute(x, axis, [(i, (i + by) % n) for i in range(n)])  24.5 us
    all_to_all x4, waiting for transfers between devices, exchange(): return lax.all_to_all(x, axis, split_axis=0, concat_axis=0, tiled=True)  23.8 us
    all_to_all x4, starting transfers between devices, exchange(): return lax.all_to_all(x, axis, split_axis=0, concat_axis=0, tiled=True)  19.6 us
    ppermute x1, waiting for transfers between devices, body(): ring_x = lax.ppermute(ring, X, across)  12.6 us
    pallas_call x1, Pallas kernels, body(): pl.pallas_call(functools.partial(low_kernel, blocks, per), grid=(grid,),...  9.39 us
  transfers between devices with their start and end apart: 26, of which 13 were waited for; matrix products, arithmetic and copies ran while one was open for 5% of the time, Pallas kernels for 14%

profile of v6, /device:TPU:0, one launch (start us, length us, event | category | flops | bytes accessed | tf_op | source)
XLA Modules:
  0.0 214.0 jit_solution(6833030853296224444)
XLA Ops:
  2.7 3.2 %collective-permute-start = (bf16[4,72,512]{2,1,0:T(8,128)(2,1)S(1)}, bf16[4,72,512]{2,1,0:T(8,128)(2,1)S(1)}, u32[]{:S(2)}, u32[]{:S(2)}) collective-permute-start(bf16[4,72,512]{2,1,0:T(8,128)(2,1)S(1)} %get-tuple-element.59), channel_id=1, source_target_pairs={{0,16},{16,0},{1,17},{17,1},{2,18},{18,2},{3,19},{19,3},{4,20},{20... | collective-permute-start | bytes 884744 | tf_op jit(solution)/shard_map/ppermute | solution.py:33
  6.9 4.1 %collective-permute-start.3 = (bf16[128,1024]{1,0:T(8,128)(2,1)S(1)}, bf16[128,1024]{1,0:T(8,128)(2,1)S(1)}, u32[]{:S(2)}, u32[]{:S(2)}) collective-permute-start(bf16[128,1024]{1,0:T(8,128)(2,1)S(1)} %constant_dynamic-slice_fusion), channel_id=1, source_target_pairs={{0,12},{4,0},{8,4},{12,8},{1,13},{5,1},{9,5},{13,9},{2,14},{6,2},{... | collective-permute-start | bytes 786440 | tf_op jit(solution)/shard_map/ppermute | solution.py:33
  11.0 1.9 collective-permute-done
  13.8 3.2 %collective-permute-start.5 = (bf16[2,4,72,512]{3,2,1,0:T(8,128)(2,1)S(1)}, bf16[2,4,72,512]{3,2,1,0:T(8,128)(2,1)S(1)}, u32[]{:S(2)}, u32[]{:S(2)}) collective-permute-start(bf16[2,4,72,512]{3,2,1,0:T(8,128)(2,1)S(1)} %get-tuple-element.57), channel_id=1, source_target_pairs={{0,96},{32,0},{64,32},{96,64},{1,97},{33,1},{65,33},{97,65},{2,98}... | collective-permute-start | bytes 1769480 | tf_op jit(solution)/shard_map/ppermute | solution.py:33
  17.1 4.1 %collective-permute-start.9 = (bf16[64,1024]{1,0:T(8,128)(2,1)S(1)}, bf16[64,1024]{1,0:T(8,128)(2,1)S(1)}, u32[]{:S(2)}, u32[]{:S(2)}) collective-permute-start(bf16[64,1024]{1,0:T(8,128)(2,1)S(1)} %slice.39), channel_id=1, source_target_pairs={{0,12},{4,0},{8,4},{12,8},{1,13},{5,1},{9,5},{13,9},{2,14},{6,2},{... | collective-permute-start | bytes 393224 | tf_op jit(solution)/shard_map/ppermute | solution.py:33
  21.3 2.8 %collective-permute-start.7 = (bf16[512,1024]{1,0:T(8,128)(2,1)}, bf16[512,1024]{1,0:T(8,128)(2,1)}, u32[]{:S(2)}, u32[]{:S(2)}) collective-permute-start(bf16[512,1024]{1,0:T(8,128)(2,1)} %refs_0_.1), channel_id=1, source_target_pairs={{0,18},{18,0},{2,16},{16,2},{1,19},{19,1},{3,17},{17,3},{4,22},{22... | collective-permute-start | bytes 3145736 | tf_op jit(solution)/shard_map/ppermute | solution.py:231
  24.8 4.5 %all-to-all-start = ((s32[16,8,128]{2,1,0:T(8,128)}), s32[16,8,128]{2,1,0:T(8,128)S(1)}, u32[]{:S(2)}, u32[]{:S(2)}) async-start(s32[16,8,128]{2,1,0:T(8,128)} %broadcast_in_dim.4), calls=%async_computation | async-start | bytes 131072 | tf_op jit(solution)/shard_map/all_to_all | solution.py:41
  29.4 1.9 collective-permute-start.10
  31.3 4.2 %all-to-all-done = s32[16,8,128]{2,1,0:T(8,128)S(1)} async-done(((s32[16,8,128]{2,1,0:T(8,128)}), s32[16,8,128]{2,1,0:T(8,128)S(1)}, u32[]{:S(2)}, u32[]{:S(2)}) %all-to-all-start) | async-done | bytes 65568 | tf_op jit(solution)/shard_map/all_to_all | solution.py:41
  35.6 3.3 %collective-permute-start.6 = (bf16[2,2,72,512]{3,2,1,0:T(8,128)(2,1)S(1)}, bf16[2,2,72,512]{3,2,1,0:T(8,128)(2,1)S(1)}, u32[]{:S(2)}, u32[]{:S(2)}) collective-permute-start(bf16[2,2,72,512]{3,2,1,0:T(8,128)(2,1)S(1)} %slice.28), channel_id=1, source_target_pairs={{0,96},{32,0},{64,32},{96,64},{1,97},{33,1},{65,33},{97,65},{2,98}... | collective-permute-start | bytes 884744 | tf_op jit(solution)/shard_map/ppermute | solution.py:33
  39.1 6.3 %collective-permute-done.6 = bf16[2,2,72,512]{3,2,1,0:T(8,128)(2,1)S(1)} collective-permute-done((bf16[2,2,72,512]{3,2,1,0:T(8,128)(2,1)S(1)}, bf16[2,2,72,512]{3,2,1,0:T(8,128)(2,1)S(1)}, u32[]{:S(2)}, u32[]{:S(2)}) %collective-permute-start.6) | collective-permute-done | bytes 294944 | tf_op jit(solution)/shard_map/ppermute | solution.py:33
  45.4 3.5 %collective-permute-done.4 = bf16[2,2,72,512]{3,2,1,0:T(8,128)(2,1)S(1)} collective-permute-done((bf16[2,2,72,512]{3,2,1,0:T(8,128)(2,1)S(1)}, bf16[2,2,72,512]{3,2,1,0:T(8,128)(2,1)S(1)}, u32[]{:S(2)}, u32[]{:S(2)}) %collective-permute-start.4) | collective-permute-done | bytes 294944 | tf_op jit(solution)/shard_map/ppermute | solution.py:33
  49.0 1.5 pad_maximum_fusion
  50.6 12.6 %collective-permute-done.10 = bf16[3,128,1024]{2,1,0:T(8,128)(2,1)} collective-permute-done((bf16[3,128,1024]{2,1,0:T(8,128)(2,1)S(1)}, bf16[3,128,1024]{2,1,0:T(8,128)(2,1)}, u32[]{:S(2)}, u32[]{:S(2)}) %collective-permute-start.10) | collective-permute-done | bytes 786464 | tf_op jit(solution)/shard_map/ppermute | solution.py:235
  63.2 2.7 %gather_fusion = bf16[48,72,512]{2,1,0:T(8,128)(2,1)} fusion(bf16[32,72,512]{2,1,0:T(8,128)(2,1)S(1)} %bitcast.52, s32[1024]{0:T(1024)S(1)} %pad_clamp_fusion), kind=kCustom, calls=%fused_computation | custom fusion | bytes 7078080 | tf_op jit(solution)/shard_map/gather | solution.py:247
  65.9 4.5 %all-to-all-start.1 = ((bf16[16,3,72,512]{3,2,1,0:T(8,128)(2,1)}), bf16[16,3,72,512]{3,2,1,0:T(8,128)(2,1)}, u32[]{:S(2)}, u32[]{:S(2)}) async-start(bf16[16,3,72,512]{3,2,1,0:T(8,128)(2,1)} %bitcast.53), calls=%async_computation.1 | async-start | bytes 7077888 | tf_op jit(solution)/shard_map/all_to_all | solution.py:41
  71.3 2.1 constant_dynamic-update-slice_fusion.refs_2_
  73.4 3.0 %collective-permute-start.12 = (bf16[6,128,1024]{2,1,0:T(8,128)(2,1)}, bf16[6,128,1024]{2,1,0:T(8,128)(2,1)}, u32[]{:S(2)}, u32[]{:S(2)}) collective-permute-start(bf16[6,128,1024]{2,1,0:T(8,128)(2,1)} %constant_dynamic-update-slice_fusion.refs_2_), channel_id=1, source_target_pairs={{0,96},{32,0},{64,32},{96,64},{1,97},{33,1},{65,33},{97,65},{2,98}... | collective-permute-start | bytes 4718600 | tf_op jit(solution)/shard_map/ppermute | solution.py:33
  76.4 34.4 %collective-permute-done.12.refs_4_ = bf16[6,128,1024]{2,1,0:T(8,128)(2,1)} collective-permute-done((bf16[6,128,1024]{2,1,0:T(8,128)(2,1)}, bf16[6,128,1024]{2,1,0:T(8,128)(2,1)}, u32[]{:S(2)}, u32[]{:S(2)}) %collective-permute-start.12) | collective-permute-done | bytes 1572896 | tf_op jit(solution)/shard_map/ppermute | solution.py:33
  110.7 3.4 %collective-permute-done.11.refs_3_ = bf16[6,128,1024]{2,1,0:T(8,128)(2,1)} collective-permute-done((bf16[6,128,1024]{2,1,0:T(8,128)(2,1)}, bf16[6,128,1024]{2,1,0:T(8,128)(2,1)}, u32[]{:S(2)}, u32[]{:S(2)}) %collective-permute-start.11) | collective-permute-done | bytes 1572896 | tf_op jit(solution)/shard_map/ppermute | solution.py:33
  114.2 9.4 %low.1 = (bf16[384,64]{1,0:T(8,128)(2,1)}, bf16[384,64]{1,0:T(8,128)(2,1)}, bf16[3,1024,64]{2,1,0:T(8,128)(2,1)}, bf16[16,3,72,512]{3,2,1,0:T(8,128)(2,1)}) custom-call(s32[3]{0:T(128)S(1)} %copy-done, bf16[384,8192]{1,0:T(8,128)(2,1)} %x_ref.3, bf16[384,1024]{1,0:T(8,128)(2,1)} %dy_ref.3, bf16[16,3,72,512]{3,2,1,0:T(8,128)(2,1)} %all-to-all-done.1.packed_ref.down_ref, ...), custom_call_target="tpu_custom_call" | custom-call | flops 905969664 | bytes 16777216 | tf_op jit(solution)/shard_map/low/pallas_call | solution.py:258
  123.6 5.5 %all-to-all-start.2 = ((bf16[16,3,72,512]{3,2,1,0:T(8,128)(2,1)}), bf16[16,3,72,512]{3,2,1,0:T(8,128)(2,1)S(1)}, u32[]{:S(2)}, u32[]{:S(2)}) async-start(bf16[16,3,72,512]{3,2,1,0:T(8,128)(2,1)} %get-tuple-element.42), calls=%async_computation.2 | async-start | bytes 7077888 | tf_op jit(solution)/shard_map/all_to_all | solution.py:41
  129.1 1.2 slice.33
  132.3 1.3 collective-permute-start.13
  134.1 16.1 %collective-permute-done.14.refs_6_ = bf16[3,128,1024]{2,1,0:T(8,128)(2,1)S(1)} collective-permute-done((bf16[3,128,1024]{2,1,0:T(8,128)(2,1)S(1)}, bf16[3,128,1024]{2,1,0:T(8,128)(2,1)S(1)}, u32[]{:S(2)}, u32[]{:S(2)}) %collective-permute-start.14) | collective-permute-done | bytes 786464 | tf_op jit(solution)/shard_map/ppermute | solution.py:33
  150.2 2.8 %collective-permute-done.13.refs_5_ = bf16[3,128,1024]{2,1,0:T(8,128)(2,1)S(1)} collective-permute-done((bf16[3,128,1024]{2,1,0:T(8,128)(2,1)S(1)}, bf16[3,128,1024]{2,1,0:T(8,128)(2,1)S(1)}, u32[]{:S(2)}, u32[]{:S(2)}) %collective-permute-start.13) | collective-permute-done | bytes 786464 | tf_op jit(solution)/shard_map/ppermute | solution.py:33
  153.9 18.5 %all-to-all-done.2.g_ref = bf16[16,3,72,512]{3,2,1,0:T(8,128)(2,1)S(1)} async-done(((bf16[16,3,72,512]{3,2,1,0:T(8,128)(2,1)}), bf16[16,3,72,512]{3,2,1,0:T(8,128)(2,1)S(1)}, u32[]{:S(2)}, u32[]{:S(2)}) %all-to-all-start.2) | async-done | bytes 3538976 | tf_op jit(solution)/shard_map/all_to_all | solution.py:41
  172.4 3.3 %sum_blocks.1 = bf16[32,72,512]{2,1,0:T(8,128)(2,1)} custom-call(s32[16,3]{1,0:T(8,128)S(1)} %bitcast.51, bf16[16,3,72,512]{3,2,1,0:T(8,128)(2,1)S(1)} %all-to-all-done.2.g_ref), custom_call_target="tpu_custom_call" | custom-call | flops 1769472 | bytes 7077888 | tf_op jit(solution)/shard_map/sum_blocks/pallas_call | solution.py:193
  175.7 5.1 %all-to-all-start.3 = ((bf16[32,72,512]{2,1,0:T(8,128)(2,1)}), bf16[32,72,512]{2,1,0:T(8,128)(2,1)S(1)}, u32[]{:S(2)}, u32[]{:S(2)}) async-start(bf16[32,72,512]{2,1,0:T(8,128)(2,1)} %sum_blocks.1), calls=%async_computation.3 | async-start | bytes 4718592 | tf_op jit(solution)/shard_map/all_to_all | solution.py:41
  181.7 1.9 collective-permute-done.21.refs_13_
  183.5 1.3 collective-permute-done.20.refs_12_
  184.8 25.9 %base.1 = (bf16[384,1024]{1,0:T(8,128)(2,1)}, bf16[384,8192]{1,0:T(8,128)(2,1)}) custom-call(s32[20]{0:T(128)S(1)} %stack.107.f_ref, bf16[384,8192]{1,0:T(8,128)(2,1)} %x_ref.3, bf16[384,1024]{1,0:T(8,128)(2,1)} %dy_ref.3, bf16[384,64]{1,0:T(8,128)(2,1)} %get-tuple-element.30.u_ref, bf16[384,64]{1,0:T(8,128)(2,1)} %get-tuple-element.31.v_ref, ...), custom_call_target="tpu_custom_call" | custom-call | flops 12884901888 | bytes 37748736 | tf_op jit(solution)/shard_map/base/pallas_call | solution.py:297
  (71 shorter events, 13.6 us)
Async XLA Ops:
  0.6 23.5 %copy-start.7 = (s32[3]{0:T(128)S(1)}, s32[3]{0:T(128)}, u32[]{:S(2)}) copy-start(s32[3]{0:T(128)} %param.12) | copy-start | bytes 40
  2.7 10.2 %collective-permute-start = (bf16[4,72,512]{2,1,0:T(8,128)(2,1)S(1)}, bf16[4,72,512]{2,1,0:T(8,128)(2,1)S(1)}, u32[]{:S(2)}, u32[]{:S(2)}) collective-permute-start(bf16[4,72,512]{2,1,0:T(8,128)(2,1)S(1)} %get-tuple-element.59), channel_id=1, source_target_pairs={{0,16},{16,0},{1,17},{17,1},{2,18},{18,2},{3,19},{19,3},{4,20},{20... | collective-permute-start | bytes 884744 | tf_op jit(solution)/shard_map/ppermute | solution.py:33
  6.9 10.2 %collective-permute-start.3 = (bf16[128,1024]{1,0:T(8,128)(2,1)S(1)}, bf16[128,1024]{1,0:T(8,128)(2,1)S(1)}, u32[]{:S(2)}, u32[]{:S(2)}) collective-permute-start(bf16[128,1024]{1,0:T(8,128)(2,1)S(1)} %constant_dynamic-slice_fusion), channel_id=1, source_target_pairs={{0,12},{4,0},{8,4},{12,8},{1,13},{5,1},{9,5},{13,9},{2,14},{6,2},{... | collective-permute-start | bytes 786440 | tf_op jit(solution)/shard_map/ppermute | solution.py:33
  11.0 10.2 %collective-permute-start.2 = (bf16[128,1024]{1,0:T(8,128)(2,1)S(1)}, bf16[128,1024]{1,0:T(8,128)(2,1)S(1)}, u32[]{:S(2)}, u32[]{:S(2)}) collective-permute-start(bf16[128,1024]{1,0:T(8,128)(2,1)S(1)} %constant_dynamic-slice_fusion), channel_id=1, source_target_pairs={{0,4},{4,8},{8,12},{12,0},{1,5},{5,9},{9,13},{13,1},{2,6},{6,10},{... | collective-permute-start | bytes 786440 | tf_op jit(solution)/shard_map/ppermute | solution.py:33
  13.8 21.8 %collective-permute-start.5 = (bf16[2,4,72,512]{3,2,1,0:T(8,128)(2,1)S(1)}, bf16[2,4,72,512]{3,2,1,0:T(8,128)(2,1)S(1)}, u32[]{:S(2)}, u32[]{:S(2)}) collective-permute-start(bf16[2,4,72,512]{3,2,1,0:T(8,128)(2,1)S(1)} %get-tuple-element.57), channel_id=1, source_target_pairs={{0,96},{32,0},{64,32},{96,64},{1,97},{33,1},{65,33},{97,65},{2,98}... | collective-permute-start | bytes 1769480 | tf_op jit(solution)/shard_map/ppermute | solution.py:33
  17.0 21.9 %collective-permute-start.1 = (bf16[2,4,72,512]{3,2,1,0:T(8,128)(2,1)S(1)}, bf16[2,4,72,512]{3,2,1,0:T(8,128)(2,1)S(1)}, u32[]{:S(2)}, u32[]{:S(2)}) collective-permute-start(bf16[2,4,72,512]{3,2,1,0:T(8,128)(2,1)S(1)} %get-tuple-element.57), channel_id=1, source_target_pairs={{0,32},{32,64},{64,96},{96,0},{1,33},{33,65},{65,97},{97,1},{2,34}... | collective-permute-start | bytes 1769480 | tf_op jit(solution)/shard_map/ppermute | solution.py:33
  17.1 12.2 %collective-permute-start.9 = (bf16[64,1024]{1,0:T(8,128)(2,1)S(1)}, bf16[64,1024]{1,0:T(8,128)(2,1)S(1)}, u32[]{:S(2)}, u32[]{:S(2)}) collective-permute-start(bf16[64,1024]{1,0:T(8,128)(2,1)S(1)} %slice.39), channel_id=1, source_target_pairs={{0,12},{4,0},{8,4},{12,8},{1,13},{5,1},{9,5},{13,9},{2,14},{6,2},{... | collective-permute-start | bytes 393224 | tf_op jit(solution)/shard_map/ppermute | solution.py:33
  21.2 8.1 %collective-permute-start.8 = (bf16[64,1024]{1,0:T(8,128)(2,1)S(1)}, bf16[64,1024]{1,0:T(8,128)(2,1)S(1)}, u32[]{:S(2)}, u32[]{:S(2)}) collective-permute-start(bf16[64,1024]{1,0:T(8,128)(2,1)S(1)} %slice.38), channel_id=1, source_target_pairs={{0,4},{4,8},{8,12},{12,0},{1,5},{5,9},{9,13},{13,1},{2,6},{6,10},{... | collective-permute-start | bytes 393224 | tf_op jit(solution)/shard_map/ppermute | solution.py:33
  21.3 41.9 %collective-permute-start.7 = (bf16[512,1024]{1,0:T(8,128)(2,1)}, bf16[512,1024]{1,0:T(8,128)(2,1)}, u32[]{:S(2)}, u32[]{:S(2)}) collective-permute-start(bf16[512,1024]{1,0:T(8,128)(2,1)} %refs_0_.1), channel_id=1, source_target_pairs={{0,18},{18,0},{2,16},{16,2},{1,19},{19,1},{3,17},{17,3},{4,22},{22... | collective-permute-start | bytes 3145736 | tf_op jit(solution)/shard_map/ppermute | solution.py:231
  24.8 10.7 %all-to-all-start = ((s32[16,8,128]{2,1,0:T(8,128)}), s32[16,8,128]{2,1,0:T(8,128)S(1)}, u32[]{:S(2)}, u32[]{:S(2)}) async-start(s32[16,8,128]{2,1,0:T(8,128)} %broadcast_in_dim.4), calls=%async_computation | async-start | bytes 131072 | tf_op jit(solution)/shard_map/all_to_all | solution.py:41
  29.4 33.8 %collective-permute-start.10 = (bf16[3,128,1024]{2,1,0:T(8,128)(2,1)S(1)}, bf16[3,128,1024]{2,1,0:T(8,128)(2,1)}, u32[]{:S(2)}, u32[]{:S(2)}) collective-permute-start(bf16[3,128,1024]{2,1,0:T(8,128)(2,1)S(1)} %bitcast.55), channel_id=1, source_target_pairs={{0,18},{18,0},{2,16},{16,2},{1,19},{19,1},{3,17},{17,3},{4,22},{22... | collective-permute-start | bytes 2359304 | tf_op jit(solution)/shard_map/ppermute | solution.py:235
  35.6 13.5 %copy-start.1 = (bf16[1,2,4,72,512]{4,3,2,1,0:T(8,128)(2,1)S(1)}, bf16[1,2,4,72,512]{4,3,2,1,0:T(8,128)(2,1)}, u32[]{:S(2)}) copy-start(bf16[1,2,4,72,512]{4,3,2,1,0:T(8,128)(2,1)} %get-tuple-element.56) | copy-start | bytes 1769476
  35.6 13.4 %copy-start.2 = (bf16[2,4,72,512]{3,2,1,0:T(8,128)(2,1)}, bf16[2,4,72,512]{3,2,1,0:T(8,128)(2,1)S(1)}, u32[]{:S(2)}) copy-start(bf16[2,4,72,512]{3,2,1,0:T(8,128)(2,1)S(1)} %collective-permute-done.5) | copy-start | bytes 1769476
  35.6 9.8 %collective-permute-start.6 = (bf16[2,2,72,512]{3,2,1,0:T(8,128)(2,1)S(1)}, bf16[2,2,72,512]{3,2,1,0:T(8,128)(2,1)S(1)}, u32[]{:S(2)}, u32[]{:S(2)}) collective-permute-start(bf16[2,2,72,512]{3,2,1,0:T(8,128)(2,1)S(1)} %slice.28), channel_id=1, source_target_pairs={{0,96},{32,0},{64,32},{96,64},{1,97},{33,1},{65,33},{97,65},{2,98}... | collective-permute-start | bytes 884744 | tf_op jit(solution)/shard_map/ppermute | solution.py:33
  38.9 10.1 %copy-start.3 = (bf16[2,4,72,512]{3,2,1,0:T(8,128)(2,1)}, bf16[2,4,72,512]{3,2,1,0:T(8,128)(2,1)S(1)}, u32[]{:S(2)}) copy-start(bf16[2,4,72,512]{3,2,1,0:T(8,128)(2,1)S(1)} %collective-permute-done.1) | copy-start | bytes 1769476
  39.0 10.0 %collective-permute-start.4 = (bf16[2,2,72,512]{3,2,1,0:T(8,128)(2,1)S(1)}, bf16[2,2,72,512]{3,2,1,0:T(8,128)(2,1)S(1)}, u32[]{:S(2)}, u32[]{:S(2)}) collective-permute-start(bf16[2,2,72,512]{3,2,1,0:T(8,128)(2,1)S(1)} %slice.27), channel_id=1, source_target_pairs={{0,32},{32,64},{64,96},{96,0},{1,33},{33,65},{65,97},{97,1},{2,34}... | collective-permute-start | bytes 884744 | tf_op jit(solution)/shard_map/ppermute | solution.py:33
  65.9 48.3 %all-to-all-start.1 = ((bf16[16,3,72,512]{3,2,1,0:T(8,128)(2,1)}), bf16[16,3,72,512]{3,2,1,0:T(8,128)(2,1)}, u32[]{:S(2)}, u32[]{:S(2)}) async-start(bf16[16,3,72,512]{3,2,1,0:T(8,128)(2,1)} %bitcast.53), calls=%async_computation.1 | async-start | bytes 7077888 | tf_op jit(solution)/shard_map/all_to_all | solution.py:41
  70.4 43.8 %copy-start = (s32[3]{0:T(128)S(1)}, s32[3]{0:T(128)}, u32[]{:S(2)}) copy-start(s32[3]{0:T(128)} %fill_ref.1) | copy-start | bytes 40
  73.4 37.3 %collective-permute-start.12 = (bf16[6,128,1024]{2,1,0:T(8,128)(2,1)}, bf16[6,128,1024]{2,1,0:T(8,128)(2,1)}, u32[]{:S(2)}, u32[]{:S(2)}) collective-permute-start(bf16[6,128,1024]{2,1,0:T(8,128)(2,1)} %constant_dynamic-update-slice_fusion.refs_2_), channel_id=1, source_target_pairs={{0,96},{32,0},{64,32},{96,64},{1,97},{33,1},{65,33},{97,65},{2,98}... | collective-permute-start | bytes 4718600 | tf_op jit(solution)/shard_map/ppermute | solution.py:33
  76.4 37.8 %collective-permute-start.11 = (bf16[6,128,1024]{2,1,0:T(8,128)(2,1)}, bf16[6,128,1024]{2,1,0:T(8,128)(2,1)}, u32[]{:S(2)}, u32[]{:S(2)}) collective-permute-start(bf16[6,128,1024]{2,1,0:T(8,128)(2,1)} %constant_dynamic-update-slice_fusion.refs_2_), channel_id=1, source_target_pairs={{0,32},{32,64},{64,96},{96,0},{1,33},{33,65},{65,97},{97,1},{2,34}... | collective-permute-start | bytes 4718600 | tf_op jit(solution)/shard_map/ppermute | solution.py:33
  123.6 48.8 %all-to-all-start.2 = ((bf16[16,3,72,512]{3,2,1,0:T(8,128)(2,1)}), bf16[16,3,72,512]{3,2,1,0:T(8,128)(2,1)S(1)}, u32[]{:S(2)}, u32[]{:S(2)}) async-start(bf16[16,3,72,512]{3,2,1,0:T(8,128)(2,1)} %get-tuple-element.42), calls=%async_computation.2 | async-start | bytes 7077888 | tf_op jit(solution)/shard_map/all_to_all | solution.py:41
  130.2 19.9 %collective-permute-start.14 = (bf16[3,128,1024]{2,1,0:T(8,128)(2,1)S(1)}, bf16[3,128,1024]{2,1,0:T(8,128)(2,1)S(1)}, u32[]{:S(2)}, u32[]{:S(2)}) collective-permute-start(bf16[3,128,1024]{2,1,0:T(8,128)(2,1)S(1)} %slice.33), channel_id=1, source_target_pairs={{0,96},{32,0},{64,32},{96,64},{1,97},{33,1},{65,33},{97,65},{2,98}... | collective-permute-start | bytes 2359304 | tf_op jit(solution)/shard_map/ppermute | solution.py:33
  132.3 20.7 %collective-permute-start.13 = (bf16[3,128,1024]{2,1,0:T(8,128)(2,1)S(1)}, bf16[3,128,1024]{2,1,0:T(8,128)(2,1)S(1)}, u32[]{:S(2)}, u32[]{:S(2)}) collective-permute-start(bf16[3,128,1024]{2,1,0:T(8,128)(2,1)S(1)} %slice.32), channel_id=1, source_target_pairs={{0,32},{32,64},{64,96},{96,0},{1,33},{33,65},{65,97},{97,1},{2,34}... | collective-permute-start | bytes 2359304 | tf_op jit(solution)/shard_map/ppermute | solution.py:33
  133.6 47.2 %collective-permute-start.15 = (bf16[512,1024]{1,0:T(8,128)(2,1)}, bf16[512,1024]{1,0:T(8,128)(2,1)}, u32[]{:S(2)}, u32[]{:S(2)}) collective-permute-start(bf16[512,1024]{1,0:T(8,128)(2,1)} %refs_0_.1), channel_id=1, source_target_pairs={{0,1},{1,0},{2,3},{3,2},{4,5},{5,4},{6,7},{7,6},{8,9},{9,8},{10,11... | collective-permute-start | bytes 3145736 | tf_op jit(solution)/shard_map/ppermute | solution.py:33
  133.6 47.5 %collective-permute-start.16 = (bf16[512,1024]{1,0:T(8,128)(2,1)}, bf16[512,1024]{1,0:T(8,128)(2,1)}, u32[]{:S(2)}, u32[]{:S(2)}) collective-permute-start(bf16[512,1024]{1,0:T(8,128)(2,1)} %collective-permute-done.7.refs_1_), channel_id=1, source_target_pairs={{0,1},{1,0},{2,3},{3,2},{4,5},{5,4},{6,7},{7,6},{8,9},{9,8},{10,11... | collective-permute-start | bytes 3145736 | tf_op jit(solution)/shard_map/ppermute | solution.py:33
  134.1 50.7 %collective-permute-start.18 = (bf16[6,128,1024]{2,1,0:T(8,128)(2,1)}, bf16[6,128,1024]{2,1,0:T(8,128)(2,1)}, u32[]{:S(2)}, u32[]{:S(2)}) collective-permute-start(bf16[6,128,1024]{2,1,0:T(8,128)(2,1)} %collective-permute-done.11.refs_3_), channel_id=1, source_target_pairs={{0,1},{1,0},{2,3},{3,2},{4,5},{5,4},{6,7},{7,6},{8,9},{9,8},{10,11... | collective-permute-start | bytes 4718600 | tf_op jit(solution)/shard_map/ppermute | solution.py:33
  150.2 34.6 %collective-permute-start.19 = (bf16[6,128,1024]{2,1,0:T(8,128)(2,1)}, bf16[6,128,1024]{2,1,0:T(8,128)(2,1)}, u32[]{:S(2)}, u32[]{:S(2)}) collective-permute-start(bf16[6,128,1024]{2,1,0:T(8,128)(2,1)} %collective-permute-done.12.refs_4_), channel_id=1, source_target_pairs={{0,1},{1,0},{2,3},{3,2},{4,5},{5,4},{6,7},{7,6},{8,9},{9,8},{10,11... | collective-permute-start | bytes 4718600 | tf_op jit(solution)/shard_map/ppermute | solution.py:33
  153.9 30.9 %collective-permute-start.17 = (bf16[6,128,1024]{2,1,0:T(8,128)(2,1)}, bf16[6,128,1024]{2,1,0:T(8,128)(2,1)}, u32[]{:S(2)}, u32[]{:S(2)}) collective-permute-start(bf16[6,128,1024]{2,1,0:T(8,128)(2,1)} %constant_dynamic-update-slice_fusion.refs_2_), channel_id=1, source_target_pairs={{0,1},{1,0},{2,3},{3,2},{4,5},{5,4},{6,7},{7,6},{8,9},{9,8},{10,11... | collective-permute-start | bytes 4718600 | tf_op jit(solution)/shard_map/ppermute | solution.py:33
  175.7 5.1 %copy-start.5 = (bf16[3,128,1024]{2,1,0:T(8,128)(2,1)S(1)}, bf16[3,128,1024]{2,1,0:T(8,128)(2,1)}, u32[]{:S(2)}) copy-start(bf16[3,128,1024]{2,1,0:T(8,128)(2,1)} %copy-done.4) | copy-start | bytes 2359300
  175.7 36.2 %all-to-all-start.3 = ((bf16[32,72,512]{2,1,0:T(8,128)(2,1)}), bf16[32,72,512]{2,1,0:T(8,128)(2,1)S(1)}, u32[]{:S(2)}, u32[]{:S(2)}) async-start(bf16[32,72,512]{2,1,0:T(8,128)(2,1)} %sum_blocks.1), calls=%async_computation.3 | async-start | bytes 4718592 | tf_op jit(solution)/shard_map/all_to_all | solution.py:41
  180.8 2.8 %collective-permute-start.21 = (bf16[3,128,1024]{2,1,0:T(8,128)(2,1)S(1)}, bf16[3,128,1024]{2,1,0:T(8,128)(2,1)}, u32[]{:S(2)}, u32[]{:S(2)}) collective-permute-start(bf16[3,128,1024]{2,1,0:T(8,128)(2,1)S(1)} %copy-done.5), channel_id=1, source_target_pairs={{0,1},{1,0},{2,3},{3,2},{4,5},{5,4},{6,7},{7,6},{8,9},{9,8},{10,11... | collective-permute-start | bytes 2359304 | tf_op jit(solution)/shard_map/ppermute | solution.py:33
  181.1 3.7 %collective-permute-start.20 = (bf16[3,128,1024]{2,1,0:T(8,128)(2,1)}, bf16[3,128,1024]{2,1,0:T(8,128)(2,1)}, u32[]{:S(2)}, u32[]{:S(2)}) collective-permute-start(bf16[3,128,1024]{2,1,0:T(8,128)(2,1)} %copy-done.6), channel_id=1, source_target_pairs={{0,1},{1,0},{2,3},{3,2},{4,5},{5,4},{6,7},{7,6},{8,9},{9,8},{10,11... | collective-permute-start | bytes 2359304 | tf_op jit(solution)/shard_map/ppermute | solution.py:33
  (2 other events, 3.7 us)

commit v7 on v6

--- a/solution.py
+++ b/solution.py
@@ -218,6 +218,7 @@
 
     quarter = feats // ys
     mine = lax.dynamic_slice_in_dim(weight, y_at * quarter, quarter)
+    mine = gate(mine, ids_all)
     z_back, z_next = shift(mine, "z", 1), shift(mine, "z", -1)
 
     folds = feats // rank
@@ -234,8 +235,8 @@
     ring = jnp.concatenate([z_back, z_next, z_lo, z_hi]).reshape(3, quarter, value)
     ring_x = lax.ppermute(ring, X, across)
 
-    lo = shift(gate(one, ids_all, z_back, z_next)[:, : slots // 2], "y", 1)
-    hi = shift(gate(three, ids_all, z_back, z_next)[:, slots // 2 :], "y", -1)
+    lo = shift(gate(one, ids_all)[:, : slots // 2], "y", 1)
+    hi = shift(gate(three, ids_all)[:, slots // 2 :], "y", -1)
     every = jnp.stack([x_all, one, jnp.concatenate([lo, hi], axis=1), three])
 
     ids_all = ids_all[:, 0, :blocks]
@@ -243,13 +244,12 @@
     owner = want // slots
     oy, ox = (y_at - owner // xhs) % ys, (xh_at - owner % xhs) % xhs
     at = (oy * xhs + ox) * slots + want % slots
-    every = gate(every, w_x, ring_x)
+    every = gate(every, z_lo, z_hi)
     picked = every.reshape(adapters, *own.shape[1:])[at].reshape(steps, blocks, *own.shape[1:])
     low = exchange(picked, FSDP)
 
     ring = jnp.concatenate([gate(ring, picked), ring_x])
     y_back, y_next = shift(ring, "y", 1), shift(ring, "y", -1)
-    low = gate(low, y_back, y_next)
 
     grid = 4
     per = steps // grid
@@ -284,7 +284,7 @@
     )(fill, *(hbm(a) for a in (tokens, dy, low, low)))
     y_lo = shift(gate(y_back, low_u)[:3], "y", 1)
     y_hi = shift(gate(y_next, low_u)[3:], "y", -1)
-    back = exchange(grads, FSDP)
+    back = exchange(gate(grads, y_back, y_next), FSDP)
 
     w_own = [weight, w_x, ring, y_back, y_next, y_lo, y_hi]
     w_all = w_own + [shift(gate(w, low_u), "c", 1) for w in w_own]

time: 215 us -> 208 us (0.967)
  waiting for transfers between devices: 108 us -> 100 us
    ppermute x20, waiting for transfers between devices: 71.6 us -> 28.4 us  [shift(): return lax.ppermute(x, axis, [(i, (i + by) % n) for i in range(n)])]
    ppermute x1, waiting for transfers between devices: 0.01 us -> 19.2 us  [body(): w_x = lax.ppermute(gate(weight, x_all), X, across)]
    all_to_all x4, waiting for transfers between devices: 23.8 us -> 35.9 us  [exchange(): return lax.all_to_all(x, axis, split_axis=0, concat_axis=0, tiled=True)]
    ppermute x1, waiting for transfers between devices: 12.6 us -> 16.9 us  [body(): ring_x = lax.ppermute(ring, X, across)]
    ppermute x20, starting transfers between devices: 24.5 us -> 21.2 us  [shift(): return lax.ppermute(x, axis, [(i, (i + by) % n) for i in range(n)])]
    unnamed x19 -> x23, local copies, waits for them, and re-layouts: 3.56 us -> 4.35 us
  transfers between devices with their start and end apart: 26 -> 26, of which waited for: 13 -> 15; matrix products, arithmetic and copies ran while one was open for 5% -> 5% of each run, Pallas kernels for 14% -> 19%
where the time goes in v7:
time: 208 us; the launch traced here: 207 us
  waiting for transfers between devices  100 us (48%)
  starting transfers between devices  48.8 us (23%)
  Pallas kernels  38.6 us (19%)
  local copies, waits for them, and re-layouts  14 us (7%)
  other arithmetic  3.94 us (2%)
    all_to_all x4, waiting for transfers between devices, exchange(): return lax.all_to_all(x, axis, split_axis=0, concat_axis=0, tiled=True)  35.9 us
    ppermute x20, waiting for transfers between devices, shift(): return lax.ppermute(x, axis, [(i, (i + by) % n) for i in range(n)])  28.4 us
    pallas_call x1, Pallas kernels, body(): pl.pallas_call(functools.partial(base_kernel, blocks, quarter), grid_spec...  25.9 us
    ppermute x20, starting transfers between devices, shift(): return lax.ppermute(x, axis, [(i, (i + by) % n) for i in range(n)])  21.2 us
    all_to_all x4, starting transfers between devices, exchange(): return lax.all_to_all(x, axis, split_axis=0, concat_axis=0, tiled=True)  20.4 us
    ppermute x1, waiting for transfers between devices, body(): w_x = lax.ppermute(gate(weight, x_all), X, across)  19.2 us
    ppermute x1, waiting for transfers between devices, body(): ring_x = lax.ppermute(ring, X, across)  16.9 us
    pallas_call x1, Pallas kernels, body(): pl.pallas_call(functools.partial(low_kernel, blocks, per), grid=(grid,),...  9.37 us
  transfers between devices with their start and end apart: 26, of which 15 were waited for; matrix products, arithmetic and copies ran while one was open for 5% of the time, Pallas kernels for 19%

profile of v7, /device:TPU:0, one launch (start us, length us, event | category | flops | bytes accessed | tf_op | source)
XLA Modules:
  0.0 206.7 jit_solution(7165614778856179726)
XLA Ops:
  2.7 3.2 %collective-permute-start = (bf16[4,72,512]{2,1,0:T(8,128)(2,1)S(1)}, bf16[4,72,512]{2,1,0:T(8,128)(2,1)S(1)}, u32[]{:S(2)}, u32[]{:S(2)}) collective-permute-start(bf16[4,72,512]{2,1,0:T(8,128)(2,1)S(1)} %get-tuple-element.61), channel_id=1, source_target_pairs={{0,16},{16,0},{1,17},{17,1},{2,18},{18,2},{3,19},{19,3},{4,20},{20... | collective-permute-start | bytes 884744 | tf_op jit(solution)/shard_map/ppermute | solution.py:33
  5.9 7.0 %collective-permute-done = bf16[4,72,512]{2,1,0:T(8,128)(2,1)S(1)} collective-permute-done((bf16[4,72,512]{2,1,0:T(8,128)(2,1)S(1)}, bf16[4,72,512]{2,1,0:T(8,128)(2,1)S(1)}, u32[]{:S(2)}, u32[]{:S(2)}) %collective-permute-start) | collective-permute-done | bytes 294944 | tf_op jit(solution)/shard_map/ppermute | solution.py:33
  13.0 3.3 %collective-permute-start.3 = (bf16[2,4,72,512]{3,2,1,0:T(8,128)(2,1)S(1)}, bf16[2,4,72,512]{3,2,1,0:T(8,128)(2,1)S(1)}, u32[]{:S(2)}, u32[]{:S(2)}) collective-permute-start(bf16[2,4,72,512]{3,2,1,0:T(8,128)(2,1)S(1)} %get-tuple-element.59), channel_id=1, source_target_pairs={{0,96},{32,0},{64,32},{96,64},{1,97},{33,1},{65,33},{97,65},{2,98}... | collective-permute-start | bytes 1769480 | tf_op jit(solution)/shard_map/ppermute | solution.py:33
  16.9 6.3 %all-to-all-start = ((s32[16,8,128]{2,1,0:T(8,128)}), s32[16,8,128]{2,1,0:T(8,128)S(1)}, u32[]{:S(2)}, u32[]{:S(2)}) async-start(s32[16,8,128]{2,1,0:T(8,128)} %broadcast_in_dim.4), calls=%async_computation | async-start | bytes 131072 | tf_op jit(solution)/shard_map/all_to_all | solution.py:41
  23.3 1.7 constant_dynamic-slice_fusion
  25.0 4.5 %all-to-all-done = s32[16,8,128]{2,1,0:T(8,128)S(1)} async-done(((s32[16,8,128]{2,1,0:T(8,128)}), s32[16,8,128]{2,1,0:T(8,128)S(1)}, u32[]{:S(2)}, u32[]{:S(2)}) %all-to-all-start) | async-done | bytes 65568 | tf_op jit(solution)/shard_map/all_to_all | solution.py:41
  31.6 3.3 %collective-permute-start.4 = (bf16[2,2,72,512]{3,2,1,0:T(8,128)(2,1)S(1)}, bf16[2,2,72,512]{3,2,1,0:T(8,128)(2,1)S(1)}, u32[]{:S(2)}, u32[]{:S(2)}) collective-permute-start(bf16[2,2,72,512]{3,2,1,0:T(8,128)(2,1)S(1)} %slice.28), channel_id=1, source_target_pairs={{0,96},{32,0},{64,32},{96,64},{1,97},{33,1},{65,33},{97,65},{2,98}... | collective-permute-start | bytes 884744 | tf_op jit(solution)/shard_map/ppermute | solution.py:33
  35.1 2.8 %collective-permute-done.7 = bf16[128,1024]{1,0:T(8,128)(2,1)S(1)} collective-permute-done((bf16[128,1024]{1,0:T(8,128)(2,1)}, bf16[128,1024]{1,0:T(8,128)(2,1)S(1)}, u32[]{:S(2)}, u32[]{:S(2)}) %collective-permute-start.7) | collective-permute-done | bytes 262176 | tf_op jit(solution)/shard_map/ppermute | solution.py:33
  38.0 2.4 %collective-permute-start.8 = (bf16[64,1024]{1,0:T(8,128)(2,1)S(1)}, bf16[64,1024]{1,0:T(8,128)(2,1)}, u32[]{:S(2)}, u32[]{:S(2)}) collective-permute-start(bf16[64,1024]{1,0:T(8,128)(2,1)S(1)} %slice.39), channel_id=1, source_target_pairs={{0,12},{4,0},{8,4},{12,8},{1,13},{5,1},{9,5},{13,9},{2,14},{6,2},{... | collective-permute-start | bytes 393224 | tf_op jit(solution)/shard_map/ppermute | solution.py:33
  40.9 3.5 %collective-permute-done.2 = bf16[2,2,72,512]{3,2,1,0:T(8,128)(2,1)S(1)} collective-permute-done((bf16[2,2,72,512]{3,2,1,0:T(8,128)(2,1)S(1)}, bf16[2,2,72,512]{3,2,1,0:T(8,128)(2,1)S(1)}, u32[]{:S(2)}, u32[]{:S(2)}) %collective-permute-start.2) | collective-permute-done | bytes 294944 | tf_op jit(solution)/shard_map/ppermute | solution.py:33
  44.5 1.4 pad_maximum_fusion
  46.8 2.7 %gather_fusion = bf16[48,72,512]{2,1,0:T(8,128)(2,1)} fusion(bf16[32,72,512]{2,1,0:T(8,128)(2,1)S(1)} %bitcast.52, s32[1024]{0:T(1024)S(1)} %pad_clamp_fusion), kind=kCustom, calls=%fused_computation | custom fusion | bytes 7078080 | tf_op jit(solution)/shard_map/gather | solution.py:248
  49.5 4.6 %all-to-all-start.1 = ((bf16[16,3,72,512]{3,2,1,0:T(8,128)(2,1)}), bf16[16,3,72,512]{3,2,1,0:T(8,128)(2,1)}, u32[]{:S(2)}, u32[]{:S(2)}) async-start(bf16[16,3,72,512]{3,2,1,0:T(8,128)(2,1)} %bitcast.53), calls=%async_computation.1 | async-start | bytes 7077888 | tf_op jit(solution)/shard_map/all_to_all | solution.py:41
  55.2 3.1 %collective-permute-start.10 = (bf16[3,128,1024]{2,1,0:T(8,128)(2,1)S(1)}, bf16[3,128,1024]{2,1,0:T(8,128)(2,1)S(1)}, u32[]{:S(2)}, u32[]{:S(2)}) collective-permute-start(bf16[3,128,1024]{2,1,0:T(8,128)(2,1)S(1)} %bitcast.55), channel_id=1, source_target_pairs={{0,18},{18,0},{2,16},{16,2},{1,19},{19,1},{3,17},{17,3},{4,22},{22... | collective-permute-start | bytes 2359304 | tf_op jit(solution)/shard_map/ppermute | solution.py:236
  59.2 16.9 %collective-permute-done.10 = bf16[3,128,1024]{2,1,0:T(8,128)(2,1)S(1)} collective-permute-done((bf16[3,128,1024]{2,1,0:T(8,128)(2,1)S(1)}, bf16[3,128,1024]{2,1,0:T(8,128)(2,1)S(1)}, u32[]{:S(2)}, u32[]{:S(2)}) %collective-permute-start.10) | collective-permute-done | bytes 786464 | tf_op jit(solution)/shard_map/ppermute | solution.py:236
  77.1 3.2 %collective-permute-start.12 = (bf16[6,128,1024]{2,1,0:T(8,128)(2,1)}, bf16[6,128,1024]{2,1,0:T(8,128)(2,1)}, u32[]{:S(2)}, u32[]{:S(2)}) collective-permute-start(bf16[6,128,1024]{2,1,0:T(8,128)(2,1)} %constant_dynamic-update-slice_fusion.refs_2_), channel_id=1, source_target_pairs={{0,96},{32,0},{64,32},{96,64},{1,97},{33,1},{65,33},{97,65},{2,98}... | collective-permute-start | bytes 4718600 | tf_op jit(solution)/shard_map/ppermute | solution.py:33
  80.3 17.1 %all-to-all-done.1.packed_ref.down_ref = bf16[16,3,72,512]{3,2,1,0:T(8,128)(2,1)} async-done(((bf16[16,3,72,512]{3,2,1,0:T(8,128)(2,1)}), bf16[16,3,72,512]{3,2,1,0:T(8,128)(2,1)}, u32[]{:S(2)}, u32[]{:S(2)}) %all-to-all-start.1) | async-done | bytes 3538976 | tf_op jit(solution)/shard_map/all_to_all | solution.py:41
  97.5 9.4 %low.1 = (bf16[384,64]{1,0:T(8,128)(2,1)}, bf16[384,64]{1,0:T(8,128)(2,1)}, bf16[3,1024,64]{2,1,0:T(8,128)(2,1)}, bf16[16,3,72,512]{3,2,1,0:T(8,128)(2,1)}) custom-call(s32[3]{0:T(128)S(1)} %copy-done, bf16[384,8192]{1,0:T(8,128)(2,1)} %x_ref.3, bf16[384,1024]{1,0:T(8,128)(2,1)} %dy_ref.3, bf16[16,3,72,512]{3,2,1,0:T(8,128)(2,1)} %all-to-all-done.1.packed_ref.down_ref, ...), custom_call_target="tpu_custom_call" | custom-call | flops 905969664 | bytes 16777216 | tf_op jit(solution)/shard_map/low/pallas_call | solution.py:258
  106.8 7.1 %collective-permute-done.12.refs_4_ = bf16[6,128,1024]{2,1,0:T(8,128)(2,1)} collective-permute-done((bf16[6,128,1024]{2,1,0:T(8,128)(2,1)}, bf16[6,128,1024]{2,1,0:T(8,128)(2,1)}, u32[]{:S(2)}, u32[]{:S(2)}) %collective-permute-start.12) | collective-permute-done | bytes 1572896 | tf_op jit(solution)/shard_map/ppermute | solution.py:33
  114.0 3.4 %collective-permute-done.11.refs_3_ = bf16[6,128,1024]{2,1,0:T(8,128)(2,1)} collective-permute-done((bf16[6,128,1024]{2,1,0:T(8,128)(2,1)}, bf16[6,128,1024]{2,1,0:T(8,128)(2,1)}, u32[]{:S(2)}, u32[]{:S(2)}) %collective-permute-start.11) | collective-permute-done | bytes 1572896 | tf_op jit(solution)/shard_map/ppermute | solution.py:33
  117.4 4.4 %all-to-all-start.2 = ((bf16[16,3,72,512]{3,2,1,0:T(8,128)(2,1)}), bf16[16,3,72,512]{3,2,1,0:T(8,128)(2,1)S(1)}, u32[]{:S(2)}, u32[]{:S(2)}) async-start(bf16[16,3,72,512]{3,2,1,0:T(8,128)(2,1)} %get-tuple-element.44), calls=%async_computation.2 | async-start | bytes 7077888 | tf_op jit(solution)/shard_map/all_to_all | solution.py:41
  121.8 4.1 %collective-permute-start.9 = (bf16[512,1024]{1,0:T(8,128)(2,1)}, bf16[512,1024]{1,0:T(8,128)(2,1)}, u32[]{:S(2)}, u32[]{:S(2)}) collective-permute-start(bf16[512,1024]{1,0:T(8,128)(2,1)} %refs_0_.1), channel_id=1, source_target_pairs={{0,18},{18,0},{2,16},{16,2},{1,19},{19,1},{3,17},{17,3},{4,22},{22... | collective-permute-start | bytes 3145736 | tf_op jit(solution)/shard_map/ppermute | solution.py:232
  125.9 1.2 slice.33
  127.4 1.2 slice.32
  128.6 1.8 collective-permute-start.13
  130.4 19.2 %collective-permute-done.9.refs_1_ = bf16[512,1024]{1,0:T(8,128)(2,1)} collective-permute-done((bf16[512,1024]{1,0:T(8,128)(2,1)}, bf16[512,1024]{1,0:T(8,128)(2,1)}, u32[]{:S(2)}, u32[]{:S(2)}) %collective-permute-start.9) | collective-permute-done | bytes 1048608 | tf_op jit(solution)/shard_map/ppermute | solution.py:232
  152.0 13.2 %all-to-all-done.2.g_ref = bf16[16,3,72,512]{3,2,1,0:T(8,128)(2,1)S(1)} async-done(((bf16[16,3,72,512]{3,2,1,0:T(8,128)(2,1)}), bf16[16,3,72,512]{3,2,1,0:T(8,128)(2,1)S(1)}, u32[]{:S(2)}, u32[]{:S(2)}) %all-to-all-start.2) | async-done | bytes 3538976 | tf_op jit(solution)/shard_map/all_to_all | solution.py:41
  165.1 3.3 %sum_blocks.1 = bf16[32,72,512]{2,1,0:T(8,128)(2,1)} custom-call(s32[16,3]{1,0:T(8,128)S(1)} %bitcast.51, bf16[16,3,72,512]{3,2,1,0:T(8,128)(2,1)S(1)} %all-to-all-done.2.g_ref), custom_call_target="tpu_custom_call" | custom-call | flops 1769472 | bytes 7077888 | tf_op jit(solution)/shard_map/sum_blocks/pallas_call | solution.py:193
  168.4 5.1 %all-to-all-start.3 = ((bf16[32,72,512]{2,1,0:T(8,128)(2,1)}), bf16[32,72,512]{2,1,0:T(8,128)(2,1)S(1)}, u32[]{:S(2)}, u32[]{:S(2)}) async-start(bf16[32,72,512]{2,1,0:T(8,128)(2,1)} %sum_blocks.1), calls=%async_computation.3 | async-start | bytes 4718592 | tf_op jit(solution)/shard_map/all_to_all | solution.py:41
  174.4 1.9 collective-permute-done.21.refs_13_
  176.3 1.3 collective-permute-done.20.refs_12_
  177.5 25.9 %base.1 = (bf16[384,1024]{1,0:T(8,128)(2,1)}, bf16[384,8192]{1,0:T(8,128)(2,1)}) custom-call(s32[20]{0:T(128)S(1)} %stack.107.f_ref, bf16[384,8192]{1,0:T(8,128)(2,1)} %x_ref.3, bf16[384,1024]{1,0:T(8,128)(2,1)} %dy_ref.3, bf16[384,64]{1,0:T(8,128)(2,1)} %get-tuple-element.29.u_ref, bf16[384,64]{1,0:T(8,128)(2,1)} %get-tuple-element.30.v_ref, ...), custom_call_target="tpu_custom_call" | custom-call | flops 12884901888 | bytes 37748736 | tf_op jit(solution)/shard_map/base/pallas_call | solution.py:297
  (75 shorter events, 16.2 us)
Async XLA Ops:
  0.6 15.7 %copy-start.9 = (s32[3]{0:T(128)S(1)}, s32[3]{0:T(128)}, u32[]{:S(2)}) copy-start(s32[3]{0:T(128)} %param.12) | copy-start | bytes 40
  2.7 10.2 %collective-permute-start = (bf16[4,72,512]{2,1,0:T(8,128)(2,1)S(1)}, bf16[4,72,512]{2,1,0:T(8,128)(2,1)S(1)}, u32[]{:S(2)}, u32[]{:S(2)}) collective-permute-start(bf16[4,72,512]{2,1,0:T(8,128)(2,1)S(1)} %get-tuple-element.61), channel_id=1, source_target_pairs={{0,16},{16,0},{1,17},{17,1},{2,18},{18,2},{3,19},{19,3},{4,20},{20... | collective-permute-start | bytes 884744 | tf_op jit(solution)/shard_map/ppermute | solution.py:33
  13.0 18.6 %collective-permute-start.3 = (bf16[2,4,72,512]{3,2,1,0:T(8,128)(2,1)S(1)}, bf16[2,4,72,512]{3,2,1,0:T(8,128)(2,1)S(1)}, u32[]{:S(2)}, u32[]{:S(2)}) collective-permute-start(bf16[2,4,72,512]{3,2,1,0:T(8,128)(2,1)S(1)} %get-tuple-element.59), channel_id=1, source_target_pairs={{0,96},{32,0},{64,32},{96,64},{1,97},{33,1},{65,33},{97,65},{2,98}... | collective-permute-start | bytes 1769480 | tf_op jit(solution)/shard_map/ppermute | solution.py:33
  16.3 18.7 %collective-permute-start.1 = (bf16[2,4,72,512]{3,2,1,0:T(8,128)(2,1)S(1)}, bf16[2,4,72,512]{3,2,1,0:T(8,128)(2,1)S(1)}, u32[]{:S(2)}, u32[]{:S(2)}) collective-permute-start(bf16[2,4,72,512]{3,2,1,0:T(8,128)(2,1)S(1)} %get-tuple-element.59), channel_id=1, source_target_pairs={{0,32},{32,64},{64,96},{96,0},{1,33},{33,65},{65,97},{97,1},{2,34}... | collective-permute-start | bytes 1769480 | tf_op jit(solution)/shard_map/ppermute | solution.py:33
  16.9 12.5 %all-to-all-start = ((s32[16,8,128]{2,1,0:T(8,128)}), s32[16,8,128]{2,1,0:T(8,128)S(1)}, u32[]{:S(2)}, u32[]{:S(2)}) async-start(s32[16,8,128]{2,1,0:T(8,128)} %broadcast_in_dim.4), calls=%async_computation | async-start | bytes 131072 | tf_op jit(solution)/shard_map/all_to_all | solution.py:41
  29.5 8.5 %collective-permute-start.7 = (bf16[128,1024]{1,0:T(8,128)(2,1)}, bf16[128,1024]{1,0:T(8,128)(2,1)S(1)}, u32[]{:S(2)}, u32[]{:S(2)}) collective-permute-start(bf16[128,1024]{1,0:T(8,128)(2,1)} %constant_dynamic-slice_fusion), channel_id=1, source_target_pairs={{0,12},{4,0},{8,4},{12,8},{1,13},{5,1},{9,5},{13,9},{2,14},{6,2},{... | collective-permute-start | bytes 786440 | tf_op jit(solution)/shard_map/ppermute | solution.py:33
  30.6 9.8 %collective-permute-start.5 = (bf16[128,1024]{1,0:T(8,128)(2,1)}, bf16[128,1024]{1,0:T(8,128)(2,1)S(1)}, u32[]{:S(2)}, u32[]{:S(2)}) collective-permute-start(bf16[128,1024]{1,0:T(8,128)(2,1)} %constant_dynamic-slice_fusion), channel_id=1, source_target_pairs={{0,4},{4,8},{8,12},{12,0},{1,5},{5,9},{9,13},{13,1},{2,6},{6,10},{... | collective-permute-start | bytes 786440 | tf_op jit(solution)/shard_map/ppermute | solution.py:33
  31.6 9.2 %collective-permute-start.4 = (bf16[2,2,72,512]{3,2,1,0:T(8,128)(2,1)S(1)}, bf16[2,2,72,512]{3,2,1,0:T(8,128)(2,1)S(1)}, u32[]{:S(2)}, u32[]{:S(2)}) collective-permute-start(bf16[2,2,72,512]{3,2,1,0:T(8,128)(2,1)S(1)} %slice.28), channel_id=1, source_target_pairs={{0,96},{32,0},{64,32},{96,64},{1,97},{33,1},{65,33},{97,65},{2,98}... | collective-permute-start | bytes 884744 | tf_op jit(solution)/shard_map/ppermute | solution.py:33
  34.9 9.5 %copy-start.1 = (bf16[2,4,72,512]{3,2,1,0:T(8,128)(2,1)}, bf16[2,4,72,512]{3,2,1,0:T(8,128)(2,1)S(1)}, u32[]{:S(2)}) copy-start(bf16[2,4,72,512]{3,2,1,0:T(8,128)(2,1)S(1)} %collective-permute-done.1) | copy-start | bytes 1769476
  35.0 9.4 %collective-permute-start.2 = (bf16[2,2,72,512]{3,2,1,0:T(8,128)(2,1)S(1)}, bf16[2,2,72,512]{3,2,1,0:T(8,128)(2,1)S(1)}, u32[]{:S(2)}, u32[]{:S(2)}) collective-permute-start(bf16[2,2,72,512]{3,2,1,0:T(8,128)(2,1)S(1)} %slice.27), channel_id=1, source_target_pairs={{0,32},{32,64},{64,96},{96,0},{1,33},{33,65},{65,97},{97,1},{2,34}... | collective-permute-start | bytes 884744 | tf_op jit(solution)/shard_map/ppermute | solution.py:33
  38.0 6.5 %copy-start.2 = (bf16[128,1024]{1,0:T(8,128)(2,1)}, bf16[128,1024]{1,0:T(8,128)(2,1)S(1)}, u32[]{:S(2)}) copy-start(bf16[128,1024]{1,0:T(8,128)(2,1)S(1)} %collective-permute-done.7) | copy-start | bytes 786436
  38.0 7.9 %collective-permute-start.8 = (bf16[64,1024]{1,0:T(8,128)(2,1)S(1)}, bf16[64,1024]{1,0:T(8,128)(2,1)}, u32[]{:S(2)}, u32[]{:S(2)}) collective-permute-start(bf16[64,1024]{1,0:T(8,128)(2,1)S(1)} %slice.39), channel_id=1, source_target_pairs={{0,12},{4,0},{8,4},{12,8},{1,13},{5,1},{9,5},{13,9},{2,14},{6,2},{... | collective-permute-start | bytes 393224 | tf_op jit(solution)/shard_map/ppermute | solution.py:33
  40.4 6.4 %collective-permute-start.6 = (bf16[64,1024]{1,0:T(8,128)(2,1)S(1)}, bf16[64,1024]{1,0:T(8,128)(2,1)}, u32[]{:S(2)}, u32[]{:S(2)}) collective-permute-start(bf16[64,1024]{1,0:T(8,128)(2,1)S(1)} %slice.38), channel_id=1, source_target_pairs={{0,4},{4,8},{8,12},{12,0},{1,5},{5,9},{9,13},{13,1},{2,6},{6,10},{... | collective-permute-start | bytes 393224 | tf_op jit(solution)/shard_map/ppermute | solution.py:33
  49.5 4.7 %copy-start.5 = (bf16[128,1024]{1,0:T(8,128)(2,1)S(1)}, bf16[128,1024]{1,0:T(8,128)(2,1)}, u32[]{:S(2)}) copy-start(bf16[128,1024]{1,0:T(8,128)(2,1)} %copy-done.4) | copy-start | bytes 786436
  49.5 48.0 %all-to-all-start.1 = ((bf16[16,3,72,512]{3,2,1,0:T(8,128)(2,1)}), bf16[16,3,72,512]{3,2,1,0:T(8,128)(2,1)}, u32[]{:S(2)}, u32[]{:S(2)}) async-start(bf16[16,3,72,512]{3,2,1,0:T(8,128)(2,1)} %bitcast.53), calls=%async_computation.1 | async-start | bytes 7077888 | tf_op jit(solution)/shard_map/all_to_all | solution.py:41
  54.1 43.3 %copy-start = (s32[3]{0:T(128)S(1)}, s32[3]{0:T(128)}, u32[]{:S(2)}) copy-start(s32[3]{0:T(128)} %fill_ref.1) | copy-start | bytes 40
  55.2 21.0 %collective-permute-start.10 = (bf16[3,128,1024]{2,1,0:T(8,128)(2,1)S(1)}, bf16[3,128,1024]{2,1,0:T(8,128)(2,1)S(1)}, u32[]{:S(2)}, u32[]{:S(2)}) collective-permute-start(bf16[3,128,1024]{2,1,0:T(8,128)(2,1)S(1)} %bitcast.55), channel_id=1, source_target_pairs={{0,18},{18,0},{2,16},{16,2},{1,19},{19,1},{3,17},{17,3},{4,22},{22... | collective-permute-start | bytes 2359304 | tf_op jit(solution)/shard_map/ppermute | solution.py:236
  77.1 36.9 %collective-permute-start.12 = (bf16[6,128,1024]{2,1,0:T(8,128)(2,1)}, bf16[6,128,1024]{2,1,0:T(8,128)(2,1)}, u32[]{:S(2)}, u32[]{:S(2)}) collective-permute-start(bf16[6,128,1024]{2,1,0:T(8,128)(2,1)} %constant_dynamic-update-slice_fusion.refs_2_), channel_id=1, source_target_pairs={{0,96},{32,0},{64,32},{96,64},{1,97},{33,1},{65,33},{97,65},{2,98}... | collective-permute-start | bytes 4718600 | tf_op jit(solution)/shard_map/ppermute | solution.py:33
  80.3 37.1 %collective-permute-start.11 = (bf16[6,128,1024]{2,1,0:T(8,128)(2,1)}, bf16[6,128,1024]{2,1,0:T(8,128)(2,1)}, u32[]{:S(2)}, u32[]{:S(2)}) collective-permute-start(bf16[6,128,1024]{2,1,0:T(8,128)(2,1)} %constant_dynamic-update-slice_fusion.refs_2_), channel_id=1, source_target_pairs={{0,32},{32,64},{64,96},{96,0},{1,33},{33,65},{65,97},{97,1},{2,34}... | collective-permute-start | bytes 4718600 | tf_op jit(solution)/shard_map/ppermute | solution.py:33
  117.4 47.7 %all-to-all-start.2 = ((bf16[16,3,72,512]{3,2,1,0:T(8,128)(2,1)}), bf16[16,3,72,512]{3,2,1,0:T(8,128)(2,1)S(1)}, u32[]{:S(2)}, u32[]{:S(2)}) async-start(bf16[16,3,72,512]{3,2,1,0:T(8,128)(2,1)} %get-tuple-element.44), calls=%async_computation.2 | async-start | bytes 7077888 | tf_op jit(solution)/shard_map/all_to_all | solution.py:41
  121.8 27.9 %collective-permute-start.9 = (bf16[512,1024]{1,0:T(8,128)(2,1)}, bf16[512,1024]{1,0:T(8,128)(2,1)}, u32[]{:S(2)}, u32[]{:S(2)}) collective-permute-start(bf16[512,1024]{1,0:T(8,128)(2,1)} %refs_0_.1), channel_id=1, source_target_pairs={{0,18},{18,0},{2,16},{16,2},{1,19},{19,1},{3,17},{17,3},{4,22},{22... | collective-permute-start | bytes 3145736 | tf_op jit(solution)/shard_map/ppermute | solution.py:232
  127.1 23.1 %collective-permute-start.14 = (bf16[3,128,1024]{2,1,0:T(8,128)(2,1)S(1)}, bf16[3,128,1024]{2,1,0:T(8,128)(2,1)S(1)}, u32[]{:S(2)}, u32[]{:S(2)}) collective-permute-start(bf16[3,128,1024]{2,1,0:T(8,128)(2,1)S(1)} %slice.33), channel_id=1, source_target_pairs={{0,96},{32,0},{64,32},{96,64},{1,97},{33,1},{65,33},{97,65},{2,98}... | collective-permute-start | bytes 2359304 | tf_op jit(solution)/shard_map/ppermute | solution.py:33
  128.6 21.7 %collective-permute-start.13 = (bf16[3,128,1024]{2,1,0:T(8,128)(2,1)S(1)}, bf16[3,128,1024]{2,1,0:T(8,128)(2,1)S(1)}, u32[]{:S(2)}, u32[]{:S(2)}) collective-permute-start(bf16[3,128,1024]{2,1,0:T(8,128)(2,1)S(1)} %slice.32), channel_id=1, source_target_pairs={{0,32},{32,64},{64,96},{96,0},{1,33},{33,65},{65,97},{97,1},{2,34}... | collective-permute-start | bytes 2359304 | tf_op jit(solution)/shard_map/ppermute | solution.py:33
  130.4 43.0 %collective-permute-start.15 = (bf16[512,1024]{1,0:T(8,128)(2,1)}, bf16[512,1024]{1,0:T(8,128)(2,1)}, u32[]{:S(2)}, u32[]{:S(2)}) collective-permute-start(bf16[512,1024]{1,0:T(8,128)(2,1)} %refs_0_.1), channel_id=1, source_target_pairs={{0,1},{1,0},{2,3},{3,2},{4,5},{5,4},{6,7},{7,6},{8,9},{9,8},{10,11... | collective-permute-start | bytes 3145736 | tf_op jit(solution)/shard_map/ppermute | solution.py:33
  149.7 24.1 %collective-permute-start.16 = (bf16[512,1024]{1,0:T(8,128)(2,1)}, bf16[512,1024]{1,0:T(8,128)(2,1)}, u32[]{:S(2)}, u32[]{:S(2)}) collective-permute-start(bf16[512,1024]{1,0:T(8,128)(2,1)} %collective-permute-done.9.refs_1_), channel_id=1, source_target_pairs={{0,1},{1,0},{2,3},{3,2},{4,5},{5,4},{6,7},{7,6},{8,9},{9,8},{10,11... | collective-permute-start | bytes 3145736 | tf_op jit(solution)/shard_map/ppermute | solution.py:33
  149.7 27.8 %collective-permute-start.18 = (bf16[6,128,1024]{2,1,0:T(8,128)(2,1)}, bf16[6,128,1024]{2,1,0:T(8,128)(2,1)}, u32[]{:S(2)}, u32[]{:S(2)}) collective-permute-start(bf16[6,128,1024]{2,1,0:T(8,128)(2,1)} %collective-permute-done.11.refs_3_), channel_id=1, source_target_pairs={{0,1},{1,0},{2,3},{3,2},{4,5},{5,4},{6,7},{7,6},{8,9},{9,8},{10,11... | collective-permute-start | bytes 4718600 | tf_op jit(solution)/shard_map/ppermute | solution.py:33
  150.2 27.3 %collective-permute-start.19 = (bf16[6,128,1024]{2,1,0:T(8,128)(2,1)}, bf16[6,128,1024]{2,1,0:T(8,128)(2,1)}, u32[]{:S(2)}, u32[]{:S(2)}) collective-permute-start(bf16[6,128,1024]{2,1,0:T(8,128)(2,1)} %collective-permute-done.12.refs_4_), channel_id=1, source_target_pairs={{0,1},{1,0},{2,3},{3,2},{4,5},{5,4},{6,7},{7,6},{8,9},{9,8},{10,11... | collective-permute-start | bytes 4718600 | tf_op jit(solution)/shard_map/ppermute | solution.py:33
  152.0 25.6 %collective-permute-start.17 = (bf16[6,128,1024]{2,1,0:T(8,128)(2,1)}, bf16[6,128,1024]{2,1,0:T(8,128)(2,1)}, u32[]{:S(2)}, u32[]{:S(2)}) collective-permute-start(bf16[6,128,1024]{2,1,0:T(8,128)(2,1)} %constant_dynamic-update-slice_fusion.refs_2_), channel_id=1, source_target_pairs={{0,1},{1,0},{2,3},{3,2},{4,5},{5,4},{6,7},{7,6},{8,9},{9,8},{10,11... | collective-permute-start | bytes 4718600 | tf_op jit(solution)/shard_map/ppermute | solution.py:33
  168.4 5.1 %copy-start.7 = (bf16[3,128,1024]{2,1,0:T(8,128)(2,1)S(1)}, bf16[3,128,1024]{2,1,0:T(8,128)(2,1)}, u32[]{:S(2)}) copy-start(bf16[3,128,1024]{2,1,0:T(8,128)(2,1)} %copy-done.6) | copy-start | bytes 2359300
  168.4 36.1 %all-to-all-start.3 = ((bf16[32,72,512]{2,1,0:T(8,128)(2,1)}), bf16[32,72,512]{2,1,0:T(8,128)(2,1)S(1)}, u32[]{:S(2)}, u32[]{:S(2)}) async-start(bf16[32,72,512]{2,1,0:T(8,128)(2,1)} %sum_blocks.1), calls=%async_computation.3 | async-start | bytes 4718592 | tf_op jit(solution)/shard_map/all_to_all | solution.py:41
  173.5 2.8 %collective-permute-start.21 = (bf16[3,128,1024]{2,1,0:T(8,128)(2,1)S(1)}, bf16[3,128,1024]{2,1,0:T(8,128)(2,1)}, u32[]{:S(2)}, u32[]{:S(2)}) collective-permute-start(bf16[3,128,1024]{2,1,0:T(8,128)(2,1)S(1)} %copy-done.7), channel_id=1, source_target_pairs={{0,1},{1,0},{2,3},{3,2},{4,5},{5,4},{6,7},{7,6},{8,9},{9,8},{10,11... | collective-permute-start | bytes 2359304 | tf_op jit(solution)/shard_map/ppermute | solution.py:33
  173.8 3.7 %collective-permute-start.20 = (bf16[3,128,1024]{2,1,0:T(8,128)(2,1)}, bf16[3,128,1024]{2,1,0:T(8,128)(2,1)}, u32[]{:S(2)}, u32[]{:S(2)}) collective-permute-start(bf16[3,128,1024]{2,1,0:T(8,128)(2,1)} %copy-done.8), channel_id=1, source_target_pairs={{0,1},{1,0},{2,3},{3,2},{4,5},{5,4},{6,7},{7,6},{8,9},{9,8},{10,11... | collective-permute-start | bytes 2359304 | tf_op jit(solution)/shard_map/ppermute | solution.py:33
  (4 other events, 10.5 us)

commit v8 on v7

--- a/solution.py
+++ b/solution.py
@@ -218,8 +218,7 @@
 
     quarter = feats // ys
     mine = lax.dynamic_slice_in_dim(weight, y_at * quarter, quarter)
-    mine = gate(mine, ids_all)
-    z_back, z_next = shift(mine, "z", 1), shift(mine, "z", -1)
+    rest = [shift(mine, "z", by) for by in (1, -1, 2)]
 
     folds = feats // rank
     up_t = jnp.swapaxes(up, 1, 2).reshape(slots, folds, cols // folds, rank)
@@ -229,10 +228,7 @@
     one, three = shift(x_all, "y", 1), shift(x_all, "y", -1)
 
     across = [(0, 3), (3, 0), (1, 2), (2, 1)]
-    w_x = lax.ppermute(gate(weight, x_all), X, across)
-    z_lo = shift(z_back[: quarter // 2], "z", 1)
-    z_hi = shift(z_next[quarter // 2 :], "z", -1)
-    ring = jnp.concatenate([z_back, z_next, z_lo, z_hi]).reshape(3, quarter, value)
+    ring = jnp.stack(rest)
     ring_x = lax.ppermute(ring, X, across)
 
     lo = shift(gate(one, ids_all)[:, : slots // 2], "y", 1)
@@ -244,10 +240,11 @@
     owner = want // slots
     oy, ox = (y_at - owner // xhs) % ys, (xh_at - owner % xhs) % xhs
     at = (oy * xhs + ox) * slots + want % slots
-    every = gate(every, z_lo, z_hi)
+    every = gate(every, ring_x)
     picked = every.reshape(adapters, *own.shape[1:])[at].reshape(steps, blocks, *own.shape[1:])
     low = exchange(picked, FSDP)
 
+    w_x = lax.ppermute(gate(weight, picked), X, across)
     ring = jnp.concatenate([gate(ring, picked), ring_x])
     y_back, y_next = shift(ring, "y", 1), shift(ring, "y", -1)
 

time: 208 us -> 199 us (0.957)
  waiting for transfers between devices: 100 us -> 88.3 us
    ppermute x20 -> x19, waiting for transfers between devices: 28.4 us -> 10.2 us  [shift(): return lax.ppermute(x, axis, [(i, (i + by) % n) for i in range(n)])]
    all_to_all x4, waiting for transfers between devices: 35.9 us -> 54 us  [exchange(): return lax.all_to_all(x, axis, split_axis=0, concat_axis=0, tiled=True)]
    ppermute x1, waiting for transfers between devices: 16.9 us -> 4.81 us  [body(): ring_x = lax.ppermute(ring, X, across)]
    unnamed x23 -> x21, local copies, waits for them, and re-layouts: 4.35 us -> 4.87 us
    ppermute x20 -> x19, starting transfers between devices: 21.2 us -> 21.2 us  [shift(): return lax.ppermute(x, axis, [(i, (i + by) % n) for i in range(n)])]
  transfers between devices with their start and end apart: 26 -> 25, of which waited for: 15 -> 11; matrix products, arithmetic and copies ran while one was open for 5% -> 5% of each run, Pallas kernels for 19% -> 20%
where the time goes in v8:
time: 199 us; the launch traced here: 197 us
  waiting for transfers between devices  88.3 us (44%)
  starting transfers between devices  49.8 us (25%)
  Pallas kernels  38.6 us (19%)
  local copies, waits for them, and re-layouts  14.9 us (7%)
  other arithmetic  4.95 us (2%)
    all_to_all x4, waiting for transfers between devices, exchange(): return lax.all_to_all(x, axis, split_axis=0, concat_axis=0, tiled=True)  54 us
    pallas_call x1, Pallas kernels, body(): pl.pallas_call(functools.partial(base_kernel, blocks, quarter), grid_spec...  25.9 us
    all_to_all x4, starting transfers between devices, exchange(): return lax.all_to_all(x, axis, split_axis=0, concat_axis=0, tiled=True)  21.4 us
    ppermute x19, starting transfers between devices, shift(): return lax.ppermute(x, axis, [(i, (i + by) % n) for i in range(n)])  21.2 us
    ppermute x1, waiting for transfers between devices, body(): w_x = lax.ppermute(gate(weight, picked), X, across)  19.2 us
    ppermute x19, waiting for transfers between devices, shift(): return lax.ppermute(x, axis, [(i, (i + by) % n) for i in range(n)])  10.2 us
    pallas_call x1, Pallas kernels, body(): pl.pallas_call(functools.partial(low_kernel, blocks, per), grid=(grid,),...  9.38 us
    unnamed x21, local copies, waits for them, and re-layouts  4.87 us
  transfers between devices with their start and end apart: 25, of which 11 were waited for; matrix products, arithmetic and copies ran while one was open for 5% of the time, Pallas kernels for 20%

profile of v8, /device:TPU:0, one launch (start us, length us, event | category | flops | bytes accessed | tf_op | source)
XLA Modules:
  0.0 197.4 jit_solution(17844493699886915502)
XLA Ops:
  2.7 3.2 %collective-permute-start = (bf16[4,72,512]{2,1,0:T(8,128)(2,1)S(1)}, bf16[4,72,512]{2,1,0:T(8,128)(2,1)S(1)}, u32[]{:S(2)}, u32[]{:S(2)}) collective-permute-start(bf16[4,72,512]{2,1,0:T(8,128)(2,1)S(1)} %get-tuple-element.59), channel_id=1, source_target_pairs={{0,16},{16,0},{1,17},{17,1},{2,18},{18,2},{3,19},{19,3},{4,20},{20... | collective-permute-start | bytes 884744 | tf_op jit(solution)/shard_map/ppermute | solution.py:33
  6.9 4.0 %collective-permute-start.7 = (bf16[128,1024]{1,0:T(8,128)(2,1)S(1)}, bf16[128,1024]{1,0:T(8,128)(2,1)S(1)}, u32[]{:S(2)}, u32[]{:S(2)}) collective-permute-start(bf16[128,1024]{1,0:T(8,128)(2,1)S(1)} %constant_dynamic-slice_fusion), channel_id=1, source_target_pairs={{0,8},{4,12},{8,0},{12,4},{1,9},{5,13},{9,1},{13,5},{2,10},{6,14},... | collective-permute-start | bytes 786440 | tf_op jit(solution)/shard_map/ppermute | solution.py:33
  11.5 1.3 collective-permute-start.5
  13.8 1.8 collective-permute-start.1
  15.6 1.4 collective-permute-start.3
  17.7 6.6 %all-to-all-start = ((s32[16,8,128]{2,1,0:T(8,128)}), s32[16,8,128]{2,1,0:T(8,128)S(1)}, u32[]{:S(2)}, u32[]{:S(2)}) async-start(s32[16,8,128]{2,1,0:T(8,128)} %broadcast_in_dim.4), calls=%async_computation | async-start | bytes 131072 | tf_op jit(solution)/shard_map/all_to_all | solution.py:41
  25.0 1.0 pad_maximum_fusion.1
  26.0 3.3 %collective-permute-start.8 = (bf16[3,128,1024]{2,1,0:T(8,128)(2,1)S(1)}, bf16[3,128,1024]{2,1,0:T(8,128)(2,1)}, u32[]{:S(2)}, u32[]{:S(2)}) collective-permute-start(bf16[3,128,1024]{2,1,0:T(8,128)(2,1)S(1)} %pad_maximum_fusion.1), channel_id=1, source_target_pairs={{0,18},{18,0},{2,16},{16,2},{1,19},{19,1},{3,17},{17,3},{4,22},{22... | collective-permute-start | bytes 2359304 | tf_op jit(solution)/shard_map/ppermute | solution.py:232
  29.3 1.1 all-to-all-done
  31.1 2.9 %collective-permute-start.4 = (bf16[2,2,72,512]{3,2,1,0:T(8,128)(2,1)S(1)}, bf16[2,2,72,512]{3,2,1,0:T(8,128)(2,1)S(1)}, u32[]{:S(2)}, u32[]{:S(2)}) collective-permute-start(bf16[2,2,72,512]{3,2,1,0:T(8,128)(2,1)S(1)} %slice.22), channel_id=1, source_target_pairs={{0,96},{32,0},{64,32},{96,64},{1,97},{33,1},{65,33},{97,65},{2,98}... | collective-permute-start | bytes 884744 | tf_op jit(solution)/shard_map/ppermute | solution.py:33
  34.1 6.8 %collective-permute-done.2 = bf16[2,2,72,512]{3,2,1,0:T(8,128)(2,1)S(1)} collective-permute-done((bf16[2,2,72,512]{3,2,1,0:T(8,128)(2,1)S(1)}, bf16[2,2,72,512]{3,2,1,0:T(8,128)(2,1)S(1)}, u32[]{:S(2)}, u32[]{:S(2)}) %collective-permute-start.2) | collective-permute-done | bytes 294944 | tf_op jit(solution)/shard_map/ppermute | solution.py:33
  41.0 1.5 pad_maximum_fusion
  42.5 4.8 %collective-permute-done.8 = bf16[3,128,1024]{2,1,0:T(8,128)(2,1)} collective-permute-done((bf16[3,128,1024]{2,1,0:T(8,128)(2,1)S(1)}, bf16[3,128,1024]{2,1,0:T(8,128)(2,1)}, u32[]{:S(2)}, u32[]{:S(2)}) %collective-permute-start.8) | collective-permute-done | bytes 786464 | tf_op jit(solution)/shard_map/ppermute | solution.py:232
  47.3 2.7 %gather_fusion = bf16[48,72,512]{2,1,0:T(8,128)(2,1)} fusion(bf16[32,72,512]{2,1,0:T(8,128)(2,1)S(1)} %bitcast.54, s32[1024]{0:T(1024)S(1)} %pad_clamp_fusion), kind=kCustom, calls=%fused_computation | custom fusion | bytes 7078080 | tf_op jit(solution)/shard_map/gather | solution.py:244
  50.0 4.6 %all-to-all-start.1 = ((bf16[16,3,72,512]{3,2,1,0:T(8,128)(2,1)}), bf16[16,3,72,512]{3,2,1,0:T(8,128)(2,1)}, u32[]{:S(2)}, u32[]{:S(2)}) async-start(bf16[16,3,72,512]{3,2,1,0:T(8,128)(2,1)} %bitcast.55), calls=%async_computation.1 | async-start | bytes 7077888 | tf_op jit(solution)/shard_map/all_to_all | solution.py:41
  55.5 2.1 %constant_dynamic-update-slice_fusion.refs_2_ = bf16[6,128,1024]{2,1,0:T(8,128)(2,1)} fusion(bf16[6,128,1024]{2,1,0:T(8,128)(2,1)} %constant_dynamic-update-slice_fusion.1, bf16[3,128,1024]{2,1,0:T(8,128)(2,1)} %collective-permute-done.8), kind=kLoop, calls=%fused_computation.11 | loop fusion | bytes 1572864 | tf_op jit(solution)/shard_map/concatenate | solution.py:248
  57.6 1.8 collective-permute-start.11
  59.7 38.3 %all-to-all-done.1.packed_ref.down_ref = bf16[16,3,72,512]{3,2,1,0:T(8,128)(2,1)} async-done(((bf16[16,3,72,512]{3,2,1,0:T(8,128)(2,1)}), bf16[16,3,72,512]{3,2,1,0:T(8,128)(2,1)}, u32[]{:S(2)}, u32[]{:S(2)}) %all-to-all-start.1) | async-done | bytes 3538976 | tf_op jit(solution)/shard_map/all_to_all | solution.py:41
  98.0 9.4 %low.1 = (bf16[384,64]{1,0:T(8,128)(2,1)}, bf16[384,64]{1,0:T(8,128)(2,1)}, bf16[3,1024,64]{2,1,0:T(8,128)(2,1)}, bf16[16,3,72,512]{3,2,1,0:T(8,128)(2,1)}) custom-call(s32[3]{0:T(128)S(1)} %copy-done, bf16[384,8192]{1,0:T(8,128)(2,1)} %x_ref.3, bf16[384,1024]{1,0:T(8,128)(2,1)} %dy_ref.3, bf16[16,3,72,512]{3,2,1,0:T(8,128)(2,1)} %all-to-all-done.1.packed_ref.down_ref, ...), custom_call_target="tpu_custom_call" | custom-call | flops 905969664 | bytes 16777216 | tf_op jit(solution)/shard_map/low/pallas_call | solution.py:255
  107.4 3.8 %all-to-all-start.2 = ((bf16[16,3,72,512]{3,2,1,0:T(8,128)(2,1)}), bf16[16,3,72,512]{3,2,1,0:T(8,128)(2,1)S(1)}, u32[]{:S(2)}, u32[]{:S(2)}) async-start(bf16[16,3,72,512]{3,2,1,0:T(8,128)(2,1)} %get-tuple-element.42), calls=%async_computation.2 | async-start | bytes 7077888 | tf_op jit(solution)/shard_map/all_to_all | solution.py:41
  111.1 4.0 %collective-permute-start.9 = (bf16[512,1024]{1,0:T(8,128)(2,1)}, bf16[512,1024]{1,0:T(8,128)(2,1)}, u32[]{:S(2)}, u32[]{:S(2)}) collective-permute-start(bf16[512,1024]{1,0:T(8,128)(2,1)} %refs_0_.1), channel_id=1, source_target_pairs={{0,18},{18,0},{2,16},{16,2},{1,19},{19,1},{3,17},{17,3},{4,22},{22... | collective-permute-start | bytes 3145736 | tf_op jit(solution)/shard_map/ppermute | solution.py:247
  115.1 1.2 slice.25
  116.3 1.9 collective-permute-start.13
  118.2 1.2 slice.24
  119.7 19.2 %collective-permute-done.9.refs_1_ = bf16[512,1024]{1,0:T(8,128)(2,1)} collective-permute-done((bf16[512,1024]{1,0:T(8,128)(2,1)}, bf16[512,1024]{1,0:T(8,128)(2,1)}, u32[]{:S(2)}, u32[]{:S(2)}) %collective-permute-start.9) | collective-permute-done | bytes 1048608 | tf_op jit(solution)/shard_map/ppermute | solution.py:247
  141.2 13.2 %all-to-all-done.2.g_ref = bf16[16,3,72,512]{3,2,1,0:T(8,128)(2,1)S(1)} async-done(((bf16[16,3,72,512]{3,2,1,0:T(8,128)(2,1)}), bf16[16,3,72,512]{3,2,1,0:T(8,128)(2,1)S(1)}, u32[]{:S(2)}, u32[]{:S(2)}) %all-to-all-start.2) | async-done | bytes 3538976 | tf_op jit(solution)/shard_map/all_to_all | solution.py:41
  154.4 3.3 %sum_blocks.1 = bf16[32,72,512]{2,1,0:T(8,128)(2,1)} custom-call(s32[16,3]{1,0:T(8,128)S(1)} %bitcast.53, bf16[16,3,72,512]{3,2,1,0:T(8,128)(2,1)S(1)} %all-to-all-done.2.g_ref), custom_call_target="tpu_custom_call" | custom-call | flops 1769472 | bytes 7077888 | tf_op jit(solution)/shard_map/sum_blocks/pallas_call | solution.py:193
  157.7 6.5 %all-to-all-start.3 = ((bf16[32,72,512]{2,1,0:T(8,128)(2,1)}), bf16[32,72,512]{2,1,0:T(8,128)(2,1)S(1)}, u32[]{:S(2)}, u32[]{:S(2)}) async-start(bf16[32,72,512]{2,1,0:T(8,128)(2,1)} %sum_blocks.1), calls=%async_computation.3 | async-start | bytes 4718592 | tf_op jit(solution)/shard_map/all_to_all | solution.py:41
  164.9 1.9 collective-permute-done.20.refs_13_
  166.8 1.3 collective-permute-done.19.refs_12_
  168.1 25.9 %base.1 = (bf16[384,1024]{1,0:T(8,128)(2,1)}, bf16[384,8192]{1,0:T(8,128)(2,1)}) custom-call(s32[20]{0:T(128)S(1)} %stack.119.f_ref, bf16[384,8192]{1,0:T(8,128)(2,1)} %x_ref.3, bf16[384,1024]{1,0:T(8,128)(2,1)} %dy_ref.3, bf16[384,64]{1,0:T(8,128)(2,1)} %get-tuple-element.27.u_ref, bf16[384,64]{1,0:T(8,128)(2,1)} %get-tuple-element.28.v_ref, ...), custom_call_target="tpu_custom_call" | custom-call | flops 12884901888 | bytes 37748736 | tf_op jit(solution)/shard_map/base/pallas_call | solution.py:294
  194.0 1.3 all-to-all-done.3
  (69 shorter events, 13.3 us)
Async XLA Ops:
  0.6 16.4 %copy-start.8 = (s32[3]{0:T(128)S(1)}, s32[3]{0:T(128)}, u32[]{:S(2)}) copy-start(s32[3]{0:T(128)} %param.12) | copy-start | bytes 40
  2.7 10.2 %collective-permute-start = (bf16[4,72,512]{2,1,0:T(8,128)(2,1)S(1)}, bf16[4,72,512]{2,1,0:T(8,128)(2,1)S(1)}, u32[]{:S(2)}, u32[]{:S(2)}) collective-permute-start(bf16[4,72,512]{2,1,0:T(8,128)(2,1)S(1)} %get-tuple-element.59), channel_id=1, source_target_pairs={{0,16},{16,0},{1,17},{17,1},{2,18},{18,2},{3,19},{19,3},{4,20},{20... | collective-permute-start | bytes 884744 | tf_op jit(solution)/shard_map/ppermute | solution.py:33
  6.9 17.4 %collective-permute-start.7 = (bf16[128,1024]{1,0:T(8,128)(2,1)S(1)}, bf16[128,1024]{1,0:T(8,128)(2,1)S(1)}, u32[]{:S(2)}, u32[]{:S(2)}) collective-permute-start(bf16[128,1024]{1,0:T(8,128)(2,1)S(1)} %constant_dynamic-slice_fusion), channel_id=1, source_target_pairs={{0,8},{4,12},{8,0},{12,4},{1,9},{5,13},{9,1},{13,5},{2,10},{6,14},... | collective-permute-start | bytes 786440 | tf_op jit(solution)/shard_map/ppermute | solution.py:33
  10.8 13.4 %collective-permute-start.6 = (bf16[128,1024]{1,0:T(8,128)(2,1)S(1)}, bf16[128,1024]{1,0:T(8,128)(2,1)S(1)}, u32[]{:S(2)}, u32[]{:S(2)}) collective-permute-start(bf16[128,1024]{1,0:T(8,128)(2,1)S(1)} %constant_dynamic-slice_fusion), channel_id=1, source_target_pairs={{0,12},{4,0},{8,4},{12,8},{1,13},{5,1},{9,5},{13,9},{2,14},{6,2},{... | collective-permute-start | bytes 786440 | tf_op jit(solution)/shard_map/ppermute | solution.py:33
  11.5 12.7 %collective-permute-start.5 = (bf16[128,1024]{1,0:T(8,128)(2,1)S(1)}, bf16[128,1024]{1,0:T(8,128)(2,1)S(1)}, u32[]{:S(2)}, u32[]{:S(2)}) collective-permute-start(bf16[128,1024]{1,0:T(8,128)(2,1)S(1)} %constant_dynamic-slice_fusion), channel_id=1, source_target_pairs={{0,4},{4,8},{8,12},{12,0},{1,5},{5,9},{9,13},{13,1},{2,6},{6,10},{... | collective-permute-start | bytes 786440 | tf_op jit(solution)/shard_map/ppermute | solution.py:33
  13.8 16.7 %collective-permute-start.1 = (bf16[2,4,72,512]{3,2,1,0:T(8,128)(2,1)S(1)}, bf16[2,4,72,512]{3,2,1,0:T(8,128)(2,1)S(1)}, u32[]{:S(2)}, u32[]{:S(2)}) collective-permute-start(bf16[2,4,72,512]{3,2,1,0:T(8,128)(2,1)S(1)} %get-tuple-element.57), channel_id=1, source_target_pairs={{0,32},{32,64},{64,96},{96,0},{1,33},{33,65},{65,97},{97,1},{2,34}... | collective-permute-start | bytes 1769480 | tf_op jit(solution)/shard_map/ppermute | solution.py:33
  15.6 15.4 %collective-permute-start.3 = (bf16[2,4,72,512]{3,2,1,0:T(8,128)(2,1)S(1)}, bf16[2,4,72,512]{3,2,1,0:T(8,128)(2,1)S(1)}, u32[]{:S(2)}, u32[]{:S(2)}) collective-permute-start(bf16[2,4,72,512]{3,2,1,0:T(8,128)(2,1)S(1)} %get-tuple-element.57), channel_id=1, source_target_pairs={{0,96},{32,0},{64,32},{96,64},{1,97},{33,1},{65,33},{97,65},{2,98}... | collective-permute-start | bytes 1769480 | tf_op jit(solution)/shard_map/ppermute | solution.py:33
  17.7 12.7 %all-to-all-start = ((s32[16,8,128]{2,1,0:T(8,128)}), s32[16,8,128]{2,1,0:T(8,128)S(1)}, u32[]{:S(2)}, u32[]{:S(2)}) async-start(s32[16,8,128]{2,1,0:T(8,128)} %broadcast_in_dim.4), calls=%async_computation | async-start | bytes 131072 | tf_op jit(solution)/shard_map/all_to_all | solution.py:41
  26.0 21.3 %collective-permute-start.8 = (bf16[3,128,1024]{2,1,0:T(8,128)(2,1)S(1)}, bf16[3,128,1024]{2,1,0:T(8,128)(2,1)}, u32[]{:S(2)}, u32[]{:S(2)}) collective-permute-start(bf16[3,128,1024]{2,1,0:T(8,128)(2,1)S(1)} %pad_maximum_fusion.1), channel_id=1, source_target_pairs={{0,18},{18,0},{2,16},{16,2},{1,19},{19,1},{3,17},{17,3},{4,22},{22... | collective-permute-start | bytes 2359304 | tf_op jit(solution)/shard_map/ppermute | solution.py:232
  30.5 10.4 %copy-start.1 = (bf16[1,2,4,72,512]{4,3,2,1,0:T(8,128)(2,1)S(1)}, bf16[1,2,4,72,512]{4,3,2,1,0:T(8,128)(2,1)}, u32[]{:S(2)}) copy-start(bf16[1,2,4,72,512]{4,3,2,1,0:T(8,128)(2,1)} %get-tuple-element.56) | copy-start | bytes 1769476
  30.6 10.4 %copy-start.2 = (bf16[2,4,72,512]{3,2,1,0:T(8,128)(2,1)}, bf16[2,4,72,512]{3,2,1,0:T(8,128)(2,1)S(1)}, u32[]{:S(2)}) copy-start(bf16[2,4,72,512]{3,2,1,0:T(8,128)(2,1)S(1)} %collective-permute-done.1) | copy-start | bytes 1769476
  30.6 10.3 %collective-permute-start.2 = (bf16[2,2,72,512]{3,2,1,0:T(8,128)(2,1)S(1)}, bf16[2,2,72,512]{3,2,1,0:T(8,128)(2,1)S(1)}, u32[]{:S(2)}, u32[]{:S(2)}) collective-permute-start(bf16[2,2,72,512]{3,2,1,0:T(8,128)(2,1)S(1)} %slice.21), channel_id=1, source_target_pairs={{0,32},{32,64},{64,96},{96,0},{1,33},{33,65},{65,97},{97,1},{2,34}... | collective-permute-start | bytes 884744 | tf_op jit(solution)/shard_map/ppermute | solution.py:33
  31.0 9.9 %copy-start.3 = (bf16[2,4,72,512]{3,2,1,0:T(8,128)(2,1)}, bf16[2,4,72,512]{3,2,1,0:T(8,128)(2,1)S(1)}, u32[]{:S(2)}) copy-start(bf16[2,4,72,512]{3,2,1,0:T(8,128)(2,1)S(1)} %collective-permute-done.3) | copy-start | bytes 1769476
  31.1 9.8 %collective-permute-start.4 = (bf16[2,2,72,512]{3,2,1,0:T(8,128)(2,1)S(1)}, bf16[2,2,72,512]{3,2,1,0:T(8,128)(2,1)S(1)}, u32[]{:S(2)}, u32[]{:S(2)}) collective-permute-start(bf16[2,2,72,512]{3,2,1,0:T(8,128)(2,1)S(1)} %slice.22), channel_id=1, source_target_pairs={{0,96},{32,0},{64,32},{96,64},{1,97},{33,1},{65,33},{97,65},{2,98}... | collective-permute-start | bytes 884744 | tf_op jit(solution)/shard_map/ppermute | solution.py:33
  50.0 48.0 %all-to-all-start.1 = ((bf16[16,3,72,512]{3,2,1,0:T(8,128)(2,1)}), bf16[16,3,72,512]{3,2,1,0:T(8,128)(2,1)}, u32[]{:S(2)}, u32[]{:S(2)}) async-start(bf16[16,3,72,512]{3,2,1,0:T(8,128)(2,1)} %bitcast.55), calls=%async_computation.1 | async-start | bytes 7077888 | tf_op jit(solution)/shard_map/all_to_all | solution.py:41
  54.6 43.4 %copy-start = (s32[3]{0:T(128)S(1)}, s32[3]{0:T(128)}, u32[]{:S(2)}) copy-start(s32[3]{0:T(128)} %fill_ref.1) | copy-start | bytes 40
  57.6 49.7 %collective-permute-start.11 = (bf16[6,128,1024]{2,1,0:T(8,128)(2,1)}, bf16[6,128,1024]{2,1,0:T(8,128)(2,1)}, u32[]{:S(2)}, u32[]{:S(2)}) collective-permute-start(bf16[6,128,1024]{2,1,0:T(8,128)(2,1)} %constant_dynamic-update-slice_fusion.refs_2_), channel_id=1, source_target_pairs={{0,96},{32,0},{64,32},{96,64},{1,97},{33,1},{65,33},{97,65},{2,98}... | collective-permute-start | bytes 4718600 | tf_op jit(solution)/shard_map/ppermute | solution.py:33
  59.4 47.9 %collective-permute-start.10 = (bf16[6,128,1024]{2,1,0:T(8,128)(2,1)}, bf16[6,128,1024]{2,1,0:T(8,128)(2,1)}, u32[]{:S(2)}, u32[]{:S(2)}) collective-permute-start(bf16[6,128,1024]{2,1,0:T(8,128)(2,1)} %constant_dynamic-update-slice_fusion.refs_2_), channel_id=1, source_target_pairs={{0,32},{32,64},{64,96},{96,0},{1,33},{33,65},{65,97},{97,1},{2,34}... | collective-permute-start | bytes 4718600 | tf_op jit(solution)/shard_map/ppermute | solution.py:33
  107.4 47.1 %all-to-all-start.2 = ((bf16[16,3,72,512]{3,2,1,0:T(8,128)(2,1)}), bf16[16,3,72,512]{3,2,1,0:T(8,128)(2,1)S(1)}, u32[]{:S(2)}, u32[]{:S(2)}) async-start(bf16[16,3,72,512]{3,2,1,0:T(8,128)(2,1)} %get-tuple-element.42), calls=%async_computation.2 | async-start | bytes 7077888 | tf_op jit(solution)/shard_map/all_to_all | solution.py:41
  111.1 27.8 %collective-permute-start.9 = (bf16[512,1024]{1,0:T(8,128)(2,1)}, bf16[512,1024]{1,0:T(8,128)(2,1)}, u32[]{:S(2)}, u32[]{:S(2)}) collective-permute-start(bf16[512,1024]{1,0:T(8,128)(2,1)} %refs_0_.1), channel_id=1, source_target_pairs={{0,18},{18,0},{2,16},{16,2},{1,19},{19,1},{3,17},{17,3},{4,22},{22... | collective-permute-start | bytes 3145736 | tf_op jit(solution)/shard_map/ppermute | solution.py:247
  116.3 23.1 %collective-permute-start.13 = (bf16[3,128,1024]{2,1,0:T(8,128)(2,1)S(1)}, bf16[3,128,1024]{2,1,0:T(8,128)(2,1)S(1)}, u32[]{:S(2)}, u32[]{:S(2)}) collective-permute-start(bf16[3,128,1024]{2,1,0:T(8,128)(2,1)S(1)} %slice.25), channel_id=1, source_target_pairs={{0,96},{32,0},{64,32},{96,64},{1,97},{33,1},{65,33},{97,65},{2,98}... | collective-permute-start | bytes 2359304 | tf_op jit(solution)/shard_map/ppermute | solution.py:33
  119.4 20.3 %collective-permute-start.12 = (bf16[3,128,1024]{2,1,0:T(8,128)(2,1)S(1)}, bf16[3,128,1024]{2,1,0:T(8,128)(2,1)S(1)}, u32[]{:S(2)}, u32[]{:S(2)}) collective-permute-start(bf16[3,128,1024]{2,1,0:T(8,128)(2,1)S(1)} %slice.24), channel_id=1, source_target_pairs={{0,32},{32,64},{64,96},{96,0},{1,33},{33,65},{65,97},{97,1},{2,34}... | collective-permute-start | bytes 2359304 | tf_op jit(solution)/shard_map/ppermute | solution.py:33
  119.7 44.5 %collective-permute-start.14 = (bf16[512,1024]{1,0:T(8,128)(2,1)}, bf16[512,1024]{1,0:T(8,128)(2,1)}, u32[]{:S(2)}, u32[]{:S(2)}) collective-permute-start(bf16[512,1024]{1,0:T(8,128)(2,1)} %refs_0_.1), channel_id=1, source_target_pairs={{0,1},{1,0},{2,3},{3,2},{4,5},{5,4},{6,7},{7,6},{8,9},{9,8},{10,11... | collective-permute-start | bytes 3145736 | tf_op jit(solution)/shard_map/ppermute | solution.py:33
  138.9 25.4 %collective-permute-start.15 = (bf16[512,1024]{1,0:T(8,128)(2,1)}, bf16[512,1024]{1,0:T(8,128)(2,1)}, u32[]{:S(2)}, u32[]{:S(2)}) collective-permute-start(bf16[512,1024]{1,0:T(8,128)(2,1)} %collective-permute-done.9.refs_1_), channel_id=1, source_target_pairs={{0,1},{1,0},{2,3},{3,2},{4,5},{5,4},{6,7},{7,6},{8,9},{9,8},{10,11... | collective-permute-start | bytes 3145736 | tf_op jit(solution)/shard_map/ppermute | solution.py:33
  138.9 29.1 %collective-permute-start.17 = (bf16[6,128,1024]{2,1,0:T(8,128)(2,1)}, bf16[6,128,1024]{2,1,0:T(8,128)(2,1)}, u32[]{:S(2)}, u32[]{:S(2)}) collective-permute-start(bf16[6,128,1024]{2,1,0:T(8,128)(2,1)} %collective-permute-done.10.refs_3_), channel_id=1, source_target_pairs={{0,1},{1,0},{2,3},{3,2},{4,5},{5,4},{6,7},{7,6},{8,9},{9,8},{10,11... | collective-permute-start | bytes 4718600 | tf_op jit(solution)/shard_map/ppermute | solution.py:33
  139.4 28.6 %collective-permute-start.18 = (bf16[6,128,1024]{2,1,0:T(8,128)(2,1)}, bf16[6,128,1024]{2,1,0:T(8,128)(2,1)}, u32[]{:S(2)}, u32[]{:S(2)}) collective-permute-start(bf16[6,128,1024]{2,1,0:T(8,128)(2,1)} %collective-permute-done.11.refs_4_), channel_id=1, source_target_pairs={{0,1},{1,0},{2,3},{3,2},{4,5},{5,4},{6,7},{7,6},{8,9},{9,8},{10,11... | collective-permute-start | bytes 4718600 | tf_op jit(solution)/shard_map/ppermute | solution.py:33
  140.3 0.9 copy-start.7
  141.2 26.9 %collective-permute-start.16 = (bf16[6,128,1024]{2,1,0:T(8,128)(2,1)}, bf16[6,128,1024]{2,1,0:T(8,128)(2,1)}, u32[]{:S(2)}, u32[]{:S(2)}) collective-permute-start(bf16[6,128,1024]{2,1,0:T(8,128)(2,1)} %constant_dynamic-update-slice_fusion.refs_2_), channel_id=1, source_target_pairs={{0,1},{1,0},{2,3},{3,2},{4,5},{5,4},{6,7},{7,6},{8,9},{9,8},{10,11... | collective-permute-start | bytes 4718600 | tf_op jit(solution)/shard_map/ppermute | solution.py:33
  157.7 6.5 %copy-start.6 = (bf16[3,128,1024]{2,1,0:T(8,128)(2,1)S(1)}, bf16[3,128,1024]{2,1,0:T(8,128)(2,1)}, u32[]{:S(2)}) copy-start(bf16[3,128,1024]{2,1,0:T(8,128)(2,1)} %copy-done.5) | copy-start | bytes 2359300
  157.7 37.6 %all-to-all-start.3 = ((bf16[32,72,512]{2,1,0:T(8,128)(2,1)}), bf16[32,72,512]{2,1,0:T(8,128)(2,1)S(1)}, u32[]{:S(2)}, u32[]{:S(2)}) async-start(bf16[32,72,512]{2,1,0:T(8,128)(2,1)} %sum_blocks.1), calls=%async_computation.3 | async-start | bytes 4718592 | tf_op jit(solution)/shard_map/all_to_all | solution.py:41
  164.2 2.6 %collective-permute-start.20 = (bf16[3,128,1024]{2,1,0:T(8,128)(2,1)S(1)}, bf16[3,128,1024]{2,1,0:T(8,128)(2,1)}, u32[]{:S(2)}, u32[]{:S(2)}) collective-permute-start(bf16[3,128,1024]{2,1,0:T(8,128)(2,1)S(1)} %copy-done.6), channel_id=1, source_target_pairs={{0,1},{1,0},{2,3},{3,2},{4,5},{5,4},{6,7},{7,6},{8,9},{9,8},{10,11... | collective-permute-start | bytes 2359304 | tf_op jit(solution)/shard_map/ppermute | solution.py:33
  164.3 3.7 %collective-permute-start.19 = (bf16[3,128,1024]{2,1,0:T(8,128)(2,1)}, bf16[3,128,1024]{2,1,0:T(8,128)(2,1)}, u32[]{:S(2)}, u32[]{:S(2)}) collective-permute-start(bf16[3,128,1024]{2,1,0:T(8,128)(2,1)} %copy-done.7), channel_id=1, source_target_pairs={{0,1},{1,0},{2,3},{3,2},{4,5},{5,4},{6,7},{7,6},{8,9},{9,8},{10,11... | collective-permute-start | bytes 2359304 | tf_op jit(solution)/shard_map/ppermute | solution.py:33
  (2 other events, 1.6 us)

commit v9 on v8

--- a/solution.py
+++ b/solution.py
@@ -169,6 +169,28 @@
             acc_ref[ids_ref[m, b]] += g_ref[m, b].astype(F32)
 
     o_ref[...] = acc_ref[...].astype(BF16)
+
+
+def pick_kernel(members, blocks, oy_ref, ox_ref, slot_ref, own_ref, one_ref, lo_ref, hi_ref, three_ref, o_ref, sem):
+    mid = lo_ref.shape[1]
+
+    @pl.loop(0, members)
+    def _(m):
+        for b in range(blocks):
+            oy, ox, slot = oy_ref[m, b], ox_ref[m, b], slot_ref[m, b]
+            for here, ref, at in (
+                (oy == 0, own_ref, slot),
+                (oy == 1, one_ref, slot),
+                ((oy == 2) & (slot < mid), lo_ref, slot),
+                ((oy == 2) & (slot >= mid), hi_ref, slot - mid),
+                (oy == 3, three_ref, slot),
+            ):
+
+                @pl.when(here)
+                def _():
+                    pltpu.make_async_copy(ref.at[ox, at], o_ref.at[m, b], sem).start()
+
+    pltpu.make_async_copy(o_ref, o_ref, sem).wait()
 
 
 def vmem(mib):
@@ -229,19 +251,28 @@
 
     across = [(0, 3), (3, 0), (1, 2), (2, 1)]
     ring = jnp.stack(rest)
-    ring_x = lax.ppermute(ring, X, across)
+    beside = [(0, 1), (1, 0), (2, 3), (3, 2)]
+    mid = quarter // 2
+    ring_x = jnp.concatenate(
+        [lax.ppermute(ring[:, :mid], X, across), lax.ppermute(ring[:, mid:], X, beside)], axis=1
+    )
 
     lo = shift(gate(one, ids_all)[:, : slots // 2], "y", 1)
     hi = shift(gate(three, ids_all)[:, slots // 2 :], "y", -1)
-    every = jnp.stack([x_all, one, jnp.concatenate([lo, hi], axis=1), three])
-
     ids_all = ids_all[:, 0, :blocks]
-    want = ids_all.reshape(steps * blocks)
-    owner = want // slots
+    owner = ids_all // slots
     oy, ox = (y_at - owner // xhs) % ys, (xh_at - owner % xhs) % xhs
-    at = (oy * xhs + ox) * slots + want % slots
-    every = gate(every, ring_x)
-    picked = every.reshape(adapters, *own.shape[1:])[at].reshape(steps, blocks, *own.shape[1:])
+    any_spec = pl.BlockSpec(memory_space=pl.ANY)
+    picked = pl.pallas_call(
+        functools.partial(pick_kernel, steps, blocks),
+        in_specs=[SMEM] * 3 + [any_spec] * 5,
+        out_specs=any_spec,
+        out_shape=pltpu.HBM((steps, blocks, *own.shape[1:]), BF16),
+        scratch_shapes=[pltpu.SemaphoreType.DMA],
+        compiler_params=vmem(4),
+        cost_estimate=cost(0, 2 * steps * blocks * own[0].size * 2),
+        name="pick",
+    )(oy, ox, ids_all % slots, x_all, gate(one, ring_x), lo, hi, three)
     low = exchange(picked, FSDP)
 
     w_x = lax.ppermute(gate(weight, picked), X, across)

time: 199 us -> 198 us (level)
  waiting for transfers between devices: 88.3 us -> 97.6 us
  starting transfers between devices: 49.8 us -> 44.1 us
  local copies, waits for them, and re-layouts: 14.9 us -> 10.5 us
  Pallas kernels: 38.6 us -> 41.3 us
  other arithmetic: 4.95 us -> 2.85 us
    all_to_all x4, waiting for transfers between devices: 54 us -> 60.6 us  [exchange(): return lax.all_to_all(x, axis, split_axis=0, concat_axis=0, tiled=True)]
    ppermute x19, waiting for transfers between devices: 10.2 us -> 16.1 us  [shift(): return lax.ppermute(x, axis, [(i, (i + by) % n) for i in range(n)])]
    all_to_all x4, starting transfers between devices: 21.4 us -> 16.7 us  [exchange(): return lax.all_to_all(x, axis, split_axis=0, concat_axis=0, tiled=True)]
    ppermute x1 -> x2, waiting for transfers between devices: 4.81 us -> 1.64 us  [the longest x1 1.63 us: body(): lax.ppermute(ring[:, mid:], X, beside)]
    pallas_call x0 -> x1, Pallas kernels: none -> 2.72 us  [body(): pl.pallas_call(functools.partial(pick_kernel, steps, blocks), in_specs=[S...]
    gather x1 -> x0, local copies, waits for them, and re-layouts: 2.68 us -> none  [body(): every.reshape(adapters, *own.shape[1:])[at]]
    another operation x3 -> x0, other arithmetic: 2.49 us -> none  [body(): every = jnp.stack([x_all, one, jnp.concatenate([lo, hi], axis=1), three])]
    unnamed x21 -> x11, local copies, waits for them, and re-layouts: 4.87 us -> 3.5 us
  transfers between devices with their start and end apart: 25 -> 26, of which waited for: 11 -> 12; matrix products, arithmetic and copies ran while one was open for 5% -> 4% of each run, Pallas kernels for 20% -> 20%
where the time goes in v9:
time: 198 us; the launch traced here: 197 us
  waiting for transfers between devices  97.6 us (49%)
  starting transfers between devices  44.1 us (22%)
  Pallas kernels  41.3 us (21%)
  local copies, waits for them, and re-layouts  10.5 us (5%)
  other arithmetic  2.85 us (1%)
    all_to_all x4, waiting for transfers between devices, exchange(): return lax.all_to_all(x, axis, split_axis=0, concat_axis=0, tiled=True)  60.6 us
    pallas_call x1, Pallas kernels, body(): pl.pallas_call(functools.partial(base_kernel, blocks, quarter), grid_spec...  25.9 us
    ppermute x19, starting transfers between devices, shift(): return lax.ppermute(x, axis, [(i, (i + by) % n) for i in range(n)])  21 us
    ppermute x1, waiting for transfers between devices, body(): w_x = lax.ppermute(gate(weight, picked), X, across)  19.2 us
    all_to_all x4, starting transfers between devices, exchange(): return lax.all_to_all(x, axis, split_axis=0, concat_axis=0, tiled=True)  16.7 us
    ppermute x19, waiting for transfers between devices, shift(): return lax.ppermute(x, axis, [(i, (i + by) % n) for i in range(n)])  16.1 us
    pallas_call x1, Pallas kernels, body(): pl.pallas_call(functools.partial(low_kernel, blocks, per), grid=(grid,),...  9.38 us
  transfers between devices with their start and end apart: 26, of which 12 were waited for; matrix products, arithmetic and copies ran while one was open for 4% of the time, Pallas kernels for 20%

profile of v9, /device:TPU:0, one launch (start us, length us, event | category | flops | bytes accessed | tf_op | source)
XLA Modules:
  0.0 197.2 jit_solution(10911039006045602823)
XLA Ops:
  2.7 3.2 %collective-permute-start = (bf16[4,72,512]{2,1,0:T(8,128)(2,1)S(1)}, bf16[4,72,512]{2,1,0:T(8,128)(2,1)S(1)}, u32[]{:S(2)}, u32[]{:S(2)}) collective-permute-start(bf16[4,72,512]{2,1,0:T(8,128)(2,1)S(1)} %get-tuple-element.59), channel_id=1, source_target_pairs={{0,16},{16,0},{1,17},{17,1},{2,18},{18,2},{3,19},{19,3},{4,20},{20... | collective-permute-start | bytes 884744 | tf_op jit(solution)/shard_map/ppermute | solution.py:33
  6.9 4.0 %collective-permute-start.4 = (bf16[128,1024]{1,0:T(8,128)(2,1)S(1)}, bf16[128,1024]{1,0:T(8,128)(2,1)S(1)}, u32[]{:S(2)}, u32[]{:S(2)}) collective-permute-start(bf16[128,1024]{1,0:T(8,128)(2,1)S(1)} %constant_dynamic-slice_fusion), channel_id=1, source_target_pairs={{0,8},{4,12},{8,0},{12,4},{1,9},{5,13},{9,1},{13,5},{2,10},{6,14},... | collective-permute-start | bytes 786440 | tf_op jit(solution)/shard_map/ppermute | solution.py:33
  11.5 1.3 collective-permute-start.2
  13.0 3.3 %collective-permute-start.8 = (bf16[2,4,72,512]{3,2,1,0:T(8,128)(2,1)S(1)}, bf16[2,4,72,512]{3,2,1,0:T(8,128)(2,1)S(1)}, u32[]{:S(2)}, u32[]{:S(2)}) collective-permute-start(bf16[2,4,72,512]{3,2,1,0:T(8,128)(2,1)S(1)} %pad_maximum_fusion.2.own_ref), channel_id=1, source_target_pairs={{0,96},{32,0},{64,32},{96,64},{1,97},{33,1},{65,33},{97,65},{2,98}... | collective-permute-start | bytes 1769480 | tf_op jit(solution)/shard_map/ppermute | solution.py:33
  16.3 1.7 collective-permute-done.4
  18.0 5.2 %collective-permute-done.3 = bf16[128,1024]{1,0:T(8,128)(2,1)S(1)} collective-permute-done((bf16[128,1024]{1,0:T(8,128)(2,1)S(1)}, bf16[128,1024]{1,0:T(8,128)(2,1)S(1)}, u32[]{:S(2)}, u32[]{:S(2)}) %collective-permute-start.3) | collective-permute-done | bytes 262176 | tf_op jit(solution)/shard_map/ppermute | solution.py:33
  25.9 4.0 %all-to-all-start = ((s32[16,8,128]{2,1,0:T(8,128)}), s32[16,8,128]{2,1,0:T(8,128)S(1)}, u32[]{:S(2)}, u32[]{:S(2)}) async-start(s32[16,8,128]{2,1,0:T(8,128)} %broadcast_in_dim.3), calls=%async_computation | async-start | bytes 131072 | tf_op jit(solution)/shard_map/all_to_all | solution.py:41
  29.9 1.9 collective-permute-start.6
  31.9 4.5 %all-to-all-done = s32[16,8,128]{2,1,0:T(8,128)S(1)} async-done(((s32[16,8,128]{2,1,0:T(8,128)}), s32[16,8,128]{2,1,0:T(8,128)S(1)}, u32[]{:S(2)}, u32[]{:S(2)}) %all-to-all-start) | async-done | bytes 65568 | tf_op jit(solution)/shard_map/all_to_all | solution.py:41
  36.4 3.1 %collective-permute-start.9 = (bf16[2,2,72,512]{3,2,1,0:T(8,128)(2,1)S(1)}, bf16[2,2,72,512]{3,2,1,0:T(8,128)(2,1)S(1)}, u32[]{:S(2)}, u32[]{:S(2)}) collective-permute-start(bf16[2,2,72,512]{3,2,1,0:T(8,128)(2,1)S(1)} %slice.31), channel_id=1, source_target_pairs={{0,96},{32,0},{64,32},{96,64},{1,97},{33,1},{65,33},{97,65},{2,98}... | collective-permute-start | bytes 884744 | tf_op jit(solution)/shard_map/ppermute | solution.py:33
  40.7 1.6 collective-permute-done.6
  43.3 2.4 %collective-permute-done.9.hi_ref = bf16[2,2,72,512]{3,2,1,0:T(8,128)(2,1)S(1)} collective-permute-done((bf16[2,2,72,512]{3,2,1,0:T(8,128)(2,1)S(1)}, bf16[2,2,72,512]{3,2,1,0:T(8,128)(2,1)S(1)}, u32[]{:S(2)}, u32[]{:S(2)}) %collective-permute-start.9) | collective-permute-done | bytes 294944 | tf_op jit(solution)/shard_map/ppermute | solution.py:33
  45.7 3.5 %collective-permute-done.7.lo_ref = bf16[2,2,72,512]{3,2,1,0:T(8,128)(2,1)S(1)} collective-permute-done((bf16[2,2,72,512]{3,2,1,0:T(8,128)(2,1)S(1)}, bf16[2,2,72,512]{3,2,1,0:T(8,128)(2,1)S(1)}, u32[]{:S(2)}, u32[]{:S(2)}) %collective-permute-start.7) | collective-permute-done | bytes 294944 | tf_op jit(solution)/shard_map/ppermute | solution.py:33
  49.3 2.7 %pick.1 = bf16[16,3,72,512]{3,2,1,0:T(8,128)(2,1)} custom-call(s32[16,3]{1,0:T(8,128)S(1)} %get-tuple-element.62.oy_ref, s32[16,3]{1,0:T(8,128)S(1)} %get-tuple-element.61.ox_ref, s32[16,3]{1,0:T(8,128)S(1)} %get-tuple-element.60.slot_ref, bf16[2,4,72,512]{3,2,1,0:T(8,128)(2,1)S(1)} %pad_maximum_fusion.2.own_ref, ...), custom_call_target="tpu_custom_call" | custom-call | bytes 7077888 | tf_op jit(solution)/shard_map/pick/pallas_call | solution.py:266
  52.0 4.5 %all-to-all-start.1 = ((bf16[16,3,72,512]{3,2,1,0:T(8,128)(2,1)}), bf16[16,3,72,512]{3,2,1,0:T(8,128)(2,1)}, u32[]{:S(2)}, u32[]{:S(2)}) async-start(bf16[16,3,72,512]{3,2,1,0:T(8,128)(2,1)} %pick.1), calls=%async_computation.1 | async-start | bytes 7077888 | tf_op jit(solution)/shard_map/all_to_all | solution.py:41
  56.5 1.3 pad_maximum_fusion.refs_2_
  58.0 1.8 collective-permute-start.11
  59.8 40.0 %all-to-all-done.1.packed_ref.down_ref = bf16[16,3,72,512]{3,2,1,0:T(8,128)(2,1)} async-done(((bf16[16,3,72,512]{3,2,1,0:T(8,128)(2,1)}), bf16[16,3,72,512]{3,2,1,0:T(8,128)(2,1)}, u32[]{:S(2)}, u32[]{:S(2)}) %all-to-all-start.1) | async-done | bytes 3538976 | tf_op jit(solution)/shard_map/all_to_all | solution.py:41
  99.9 9.4 %low.1 = (bf16[384,64]{1,0:T(8,128)(2,1)}, bf16[384,64]{1,0:T(8,128)(2,1)}, bf16[3,1024,64]{2,1,0:T(8,128)(2,1)}, bf16[16,3,72,512]{3,2,1,0:T(8,128)(2,1)}) custom-call(s32[3]{0:T(128)S(1)} %copy-done, bf16[384,8192]{1,0:T(8,128)(2,1)} %x_ref.3, bf16[384,1024]{1,0:T(8,128)(2,1)} %dy_ref.3, bf16[16,3,72,512]{3,2,1,0:T(8,128)(2,1)} %all-to-all-done.1.packed_ref.down_ref, ...), custom_call_target="tpu_custom_call" | custom-call | flops 905969664 | bytes 16777216 | tf_op jit(solution)/shard_map/low/pallas_call | solution.py:286
  109.2 3.8 %all-to-all-start.2 = ((bf16[16,3,72,512]{3,2,1,0:T(8,128)(2,1)}), bf16[16,3,72,512]{3,2,1,0:T(8,128)(2,1)S(1)}, u32[]{:S(2)}, u32[]{:S(2)}) async-start(bf16[16,3,72,512]{3,2,1,0:T(8,128)(2,1)} %get-tuple-element.42), calls=%async_computation.2 | async-start | bytes 7077888 | tf_op jit(solution)/shard_map/all_to_all | solution.py:41
  113.0 3.3 %collective-permute-start.10 = (bf16[512,1024]{1,0:T(8,128)(2,1)}, bf16[512,1024]{1,0:T(8,128)(2,1)}, u32[]{:S(2)}, u32[]{:S(2)}) collective-permute-start(bf16[512,1024]{1,0:T(8,128)(2,1)} %refs_0_.1), channel_id=1, source_target_pairs={{0,18},{18,0},{2,16},{16,2},{1,19},{19,1},{3,17},{17,3},{4,22},{22... | collective-permute-start | bytes 3145736 | tf_op jit(solution)/shard_map/ppermute | solution.py:278
  116.4 1.2 slice.33
  117.8 1.2 slice.32
  119.0 1.9 collective-permute-start.13
  120.9 19.2 %collective-permute-done.10.refs_1_ = bf16[512,1024]{1,0:T(8,128)(2,1)} collective-permute-done((bf16[512,1024]{1,0:T(8,128)(2,1)}, bf16[512,1024]{1,0:T(8,128)(2,1)}, u32[]{:S(2)}, u32[]{:S(2)}) %collective-permute-start.10) | collective-permute-done | bytes 1048608 | tf_op jit(solution)/shard_map/ppermute | solution.py:278
  141.5 14.8 %all-to-all-done.2.g_ref = bf16[16,3,72,512]{3,2,1,0:T(8,128)(2,1)S(1)} async-done(((bf16[16,3,72,512]{3,2,1,0:T(8,128)(2,1)}), bf16[16,3,72,512]{3,2,1,0:T(8,128)(2,1)S(1)}, u32[]{:S(2)}, u32[]{:S(2)}) %all-to-all-start.2) | async-done | bytes 3538976 | tf_op jit(solution)/shard_map/all_to_all | solution.py:41
  156.3 3.3 %sum_blocks.1 = bf16[32,72,512]{2,1,0:T(8,128)(2,1)} custom-call(s32[16,3]{1,0:T(8,128)S(1)} %bitcast.44, bf16[16,3,72,512]{3,2,1,0:T(8,128)(2,1)S(1)} %all-to-all-done.2.g_ref), custom_call_target="tpu_custom_call" | custom-call | flops 1769472 | bytes 7077888 | tf_op jit(solution)/shard_map/sum_blocks/pallas_call | solution.py:215
  159.6 4.4 %all-to-all-start.3 = ((bf16[32,72,512]{2,1,0:T(8,128)(2,1)}), bf16[32,72,512]{2,1,0:T(8,128)(2,1)S(1)}, u32[]{:S(2)}, u32[]{:S(2)}) async-start(bf16[32,72,512]{2,1,0:T(8,128)(2,1)} %sum_blocks.1), calls=%async_computation.3 | async-start | bytes 4718592 | tf_op jit(solution)/shard_map/all_to_all | solution.py:41
  164.7 1.9 collective-permute-done.21.refs_13_
  166.6 1.3 collective-permute-done.20.refs_12_
  167.9 25.9 %base.1 = (bf16[384,1024]{1,0:T(8,128)(2,1)}, bf16[384,8192]{1,0:T(8,128)(2,1)}) custom-call(s32[20]{0:T(128)S(1)} %stack.104.f_ref, bf16[384,8192]{1,0:T(8,128)(2,1)} %x_ref.3, bf16[384,1024]{1,0:T(8,128)(2,1)} %dy_ref.3, bf16[384,64]{1,0:T(8,128)(2,1)} %get-tuple-element.27.u_ref, bf16[384,64]{1,0:T(8,128)(2,1)} %get-tuple-element.28.v_ref, ...), custom_call_target="tpu_custom_call" | custom-call | flops 12884901888 | bytes 37748736 | tf_op jit(solution)/shard_map/base/pallas_call | solution.py:325
  193.8 1.3 all-to-all-done.3
  (59 shorter events, 13.4 us)
Async XLA Ops:
  2.7 10.2 %collective-permute-start = (bf16[4,72,512]{2,1,0:T(8,128)(2,1)S(1)}, bf16[4,72,512]{2,1,0:T(8,128)(2,1)S(1)}, u32[]{:S(2)}, u32[]{:S(2)}) collective-permute-start(bf16[4,72,512]{2,1,0:T(8,128)(2,1)S(1)} %get-tuple-element.59), channel_id=1, source_target_pairs={{0,16},{16,0},{1,17},{17,1},{2,18},{18,2},{3,19},{19,3},{4,20},{20... | collective-permute-start | bytes 884744 | tf_op jit(solution)/shard_map/ppermute | solution.py:33
  5.9 19.4 %copy-start.3 = (s32[3]{0:T(128)S(1)}, s32[3]{0:T(128)}, u32[]{:S(2)}) copy-start(s32[3]{0:T(128)} %param.12) | copy-start | bytes 40
  6.9 11.1 %collective-permute-start.4 = (bf16[128,1024]{1,0:T(8,128)(2,1)S(1)}, bf16[128,1024]{1,0:T(8,128)(2,1)S(1)}, u32[]{:S(2)}, u32[]{:S(2)}) collective-permute-start(bf16[128,1024]{1,0:T(8,128)(2,1)S(1)} %constant_dynamic-slice_fusion), channel_id=1, source_target_pairs={{0,8},{4,12},{8,0},{12,4},{1,9},{5,13},{9,1},{13,5},{2,10},{6,14},... | collective-permute-start | bytes 786440 | tf_op jit(solution)/shard_map/ppermute | solution.py:33
  10.8 12.4 %collective-permute-start.3 = (bf16[128,1024]{1,0:T(8,128)(2,1)S(1)}, bf16[128,1024]{1,0:T(8,128)(2,1)S(1)}, u32[]{:S(2)}, u32[]{:S(2)}) collective-permute-start(bf16[128,1024]{1,0:T(8,128)(2,1)S(1)} %constant_dynamic-slice_fusion), channel_id=1, source_target_pairs={{0,12},{4,0},{8,4},{12,8},{1,13},{5,1},{9,5},{13,9},{2,14},{6,2},{... | collective-permute-start | bytes 786440 | tf_op jit(solution)/shard_map/ppermute | solution.py:33
  11.5 11.7 %collective-permute-start.2 = (bf16[128,1024]{1,0:T(8,128)(2,1)S(1)}, bf16[128,1024]{1,0:T(8,128)(2,1)S(1)}, u32[]{:S(2)}, u32[]{:S(2)}) collective-permute-start(bf16[128,1024]{1,0:T(8,128)(2,1)S(1)} %constant_dynamic-slice_fusion), channel_id=1, source_target_pairs={{0,4},{4,8},{8,12},{12,0},{1,5},{5,9},{9,13},{13,1},{2,6},{6,10},{... | collective-permute-start | bytes 786440 | tf_op jit(solution)/shard_map/ppermute | solution.py:33
  13.0 23.4 %collective-permute-start.8 = (bf16[2,4,72,512]{3,2,1,0:T(8,128)(2,1)S(1)}, bf16[2,4,72,512]{3,2,1,0:T(8,128)(2,1)S(1)}, u32[]{:S(2)}, u32[]{:S(2)}) collective-permute-start(bf16[2,4,72,512]{3,2,1,0:T(8,128)(2,1)S(1)} %pad_maximum_fusion.2.own_ref), channel_id=1, source_target_pairs={{0,96},{32,0},{64,32},{96,64},{1,97},{33,1},{65,33},{97,65},{2,98}... | collective-permute-start | bytes 1769480 | tf_op jit(solution)/shard_map/ppermute | solution.py:33
  16.3 23.2 %collective-permute-start.1 = (bf16[2,4,72,512]{3,2,1,0:T(8,128)(2,1)S(1)}, bf16[2,4,72,512]{3,2,1,0:T(8,128)(2,1)S(1)}, u32[]{:S(2)}, u32[]{:S(2)}) collective-permute-start(bf16[2,4,72,512]{3,2,1,0:T(8,128)(2,1)S(1)} %pad_maximum_fusion.2.own_ref), channel_id=1, source_target_pairs={{0,32},{32,64},{64,96},{96,0},{1,33},{33,65},{65,97},{97,1},{2,34}... | collective-permute-start | bytes 1769480 | tf_op jit(solution)/shard_map/ppermute | solution.py:33
  24.1 15.5 %collective-permute-start.5 = (bf16[3,64,1024]{2,1,0:T(8,128)(2,1)S(1)}, bf16[3,64,1024]{2,1,0:T(8,128)(2,1)}, u32[]{:S(2)}, u32[]{:S(2)}) collective-permute-start(bf16[3,64,1024]{2,1,0:T(8,128)(2,1)S(1)} %get-tuple-element.57), channel_id=1, source_target_pairs={{0,18},{18,0},{2,16},{16,2},{1,19},{19,1},{3,17},{17,3},{4,22},{22... | collective-permute-start | bytes 1179656 | tf_op jit(solution)/shard_map/ppermute | solution.py:257
  25.9 10.4 %all-to-all-start = ((s32[16,8,128]{2,1,0:T(8,128)}), s32[16,8,128]{2,1,0:T(8,128)S(1)}, u32[]{:S(2)}, u32[]{:S(2)}) async-start(s32[16,8,128]{2,1,0:T(8,128)} %broadcast_in_dim.3), calls=%async_computation | async-start | bytes 131072 | tf_op jit(solution)/shard_map/all_to_all | solution.py:41
  29.9 12.4 %collective-permute-start.6 = (bf16[3,64,1024]{2,1,0:T(8,128)(2,1)}, bf16[3,64,1024]{2,1,0:T(8,128)(2,1)}, u32[]{:S(2)}, u32[]{:S(2)}) collective-permute-start(bf16[3,64,1024]{2,1,0:T(8,128)(2,1)} %get-tuple-element.56), channel_id=1, source_target_pairs={{0,2},{2,0},{16,18},{18,16},{1,3},{3,1},{17,19},{19,17},{4,6},{6,4... | collective-permute-start | bytes 1179656 | tf_op jit(solution)/shard_map/ppermute | solution.py:257
  36.4 9.4 %collective-permute-start.9 = (bf16[2,2,72,512]{3,2,1,0:T(8,128)(2,1)S(1)}, bf16[2,2,72,512]{3,2,1,0:T(8,128)(2,1)S(1)}, u32[]{:S(2)}, u32[]{:S(2)}) collective-permute-start(bf16[2,2,72,512]{3,2,1,0:T(8,128)(2,1)S(1)} %slice.31), channel_id=1, source_target_pairs={{0,96},{32,0},{64,32},{96,64},{1,97},{33,1},{65,33},{97,65},{2,98}... | collective-permute-start | bytes 884744 | tf_op jit(solution)/shard_map/ppermute | solution.py:33
  39.5 9.8 %collective-permute-start.7 = (bf16[2,2,72,512]{3,2,1,0:T(8,128)(2,1)S(1)}, bf16[2,2,72,512]{3,2,1,0:T(8,128)(2,1)S(1)}, u32[]{:S(2)}, u32[]{:S(2)}) collective-permute-start(bf16[2,2,72,512]{3,2,1,0:T(8,128)(2,1)S(1)} %slice.30), channel_id=1, source_target_pairs={{0,32},{32,64},{64,96},{96,0},{1,33},{33,65},{65,97},{97,1},{2,34}... | collective-permute-start | bytes 884744 | tf_op jit(solution)/shard_map/ppermute | solution.py:33
  52.0 47.9 %all-to-all-start.1 = ((bf16[16,3,72,512]{3,2,1,0:T(8,128)(2,1)}), bf16[16,3,72,512]{3,2,1,0:T(8,128)(2,1)}, u32[]{:S(2)}, u32[]{:S(2)}) async-start(bf16[16,3,72,512]{3,2,1,0:T(8,128)(2,1)} %pick.1), calls=%async_computation.1 | async-start | bytes 7077888 | tf_op jit(solution)/shard_map/all_to_all | solution.py:41
  56.5 43.4 %copy-start = (s32[3]{0:T(128)S(1)}, s32[3]{0:T(128)}, u32[]{:S(2)}) copy-start(s32[3]{0:T(128)} %fill_ref.1) | copy-start | bytes 40
  57.8 51.4 %collective-permute-start.12 = (bf16[6,128,1024]{2,1,0:T(8,128)(2,1)}, bf16[6,128,1024]{2,1,0:T(8,128)(2,1)}, u32[]{:S(2)}, u32[]{:S(2)}) collective-permute-start(bf16[6,128,1024]{2,1,0:T(8,128)(2,1)} %pad_maximum_fusion.refs_2_), channel_id=1, source_target_pairs={{0,96},{32,0},{64,32},{96,64},{1,97},{33,1},{65,33},{97,65},{2,98}... | collective-permute-start | bytes 4718600 | tf_op jit(solution)/shard_map/ppermute | solution.py:33
  58.0 51.2 %collective-permute-start.11 = (bf16[6,128,1024]{2,1,0:T(8,128)(2,1)}, bf16[6,128,1024]{2,1,0:T(8,128)(2,1)}, u32[]{:S(2)}, u32[]{:S(2)}) collective-permute-start(bf16[6,128,1024]{2,1,0:T(8,128)(2,1)} %pad_maximum_fusion.refs_2_), channel_id=1, source_target_pairs={{0,32},{32,64},{64,96},{96,0},{1,33},{33,65},{65,97},{97,1},{2,34}... | collective-permute-start | bytes 4718600 | tf_op jit(solution)/shard_map/ppermute | solution.py:33
  109.2 47.1 %all-to-all-start.2 = ((bf16[16,3,72,512]{3,2,1,0:T(8,128)(2,1)}), bf16[16,3,72,512]{3,2,1,0:T(8,128)(2,1)S(1)}, u32[]{:S(2)}, u32[]{:S(2)}) async-start(bf16[16,3,72,512]{3,2,1,0:T(8,128)(2,1)} %get-tuple-element.42), calls=%async_computation.2 | async-start | bytes 7077888 | tf_op jit(solution)/shard_map/all_to_all | solution.py:41
  113.0 27.1 %collective-permute-start.10 = (bf16[512,1024]{1,0:T(8,128)(2,1)}, bf16[512,1024]{1,0:T(8,128)(2,1)}, u32[]{:S(2)}, u32[]{:S(2)}) collective-permute-start(bf16[512,1024]{1,0:T(8,128)(2,1)} %refs_0_.1), channel_id=1, source_target_pairs={{0,18},{18,0},{2,16},{16,2},{1,19},{19,1},{3,17},{17,3},{4,22},{22... | collective-permute-start | bytes 3145736 | tf_op jit(solution)/shard_map/ppermute | solution.py:278
  117.5 23.1 %collective-permute-start.14 = (bf16[3,128,1024]{2,1,0:T(8,128)(2,1)S(1)}, bf16[3,128,1024]{2,1,0:T(8,128)(2,1)S(1)}, u32[]{:S(2)}, u32[]{:S(2)}) collective-permute-start(bf16[3,128,1024]{2,1,0:T(8,128)(2,1)S(1)} %slice.33), channel_id=1, source_target_pairs={{0,96},{32,0},{64,32},{96,64},{1,97},{33,1},{65,33},{97,65},{2,98}... | collective-permute-start | bytes 2359304 | tf_op jit(solution)/shard_map/ppermute | solution.py:33
  119.0 21.7 %collective-permute-start.13 = (bf16[3,128,1024]{2,1,0:T(8,128)(2,1)S(1)}, bf16[3,128,1024]{2,1,0:T(8,128)(2,1)}, u32[]{:S(2)}, u32[]{:S(2)}) collective-permute-start(bf16[3,128,1024]{2,1,0:T(8,128)(2,1)S(1)} %slice.32), channel_id=1, source_target_pairs={{0,32},{32,64},{64,96},{96,0},{1,33},{33,65},{65,97},{97,1},{2,34}... | collective-permute-start | bytes 2359304 | tf_op jit(solution)/shard_map/ppermute | solution.py:33
  120.9 43.1 %collective-permute-start.15 = (bf16[512,1024]{1,0:T(8,128)(2,1)}, bf16[512,1024]{1,0:T(8,128)(2,1)}, u32[]{:S(2)}, u32[]{:S(2)}) collective-permute-start(bf16[512,1024]{1,0:T(8,128)(2,1)} %refs_0_.1), channel_id=1, source_target_pairs={{0,1},{1,0},{2,3},{3,2},{4,5},{5,4},{6,7},{7,6},{8,9},{9,8},{10,11... | collective-permute-start | bytes 3145736 | tf_op jit(solution)/shard_map/ppermute | solution.py:33
  140.1 24.0 %collective-permute-start.16 = (bf16[512,1024]{1,0:T(8,128)(2,1)}, bf16[512,1024]{1,0:T(8,128)(2,1)}, u32[]{:S(2)}, u32[]{:S(2)}) collective-permute-start(bf16[512,1024]{1,0:T(8,128)(2,1)} %collective-permute-done.10.refs_1_), channel_id=1, source_target_pairs={{0,1},{1,0},{2,3},{3,2},{4,5},{5,4},{6,7},{7,6},{8,9},{9,8},{10,11... | collective-permute-start | bytes 3145736 | tf_op jit(solution)/shard_map/ppermute | solution.py:33
  140.1 27.7 %collective-permute-start.18 = (bf16[6,128,1024]{2,1,0:T(8,128)(2,1)}, bf16[6,128,1024]{2,1,0:T(8,128)(2,1)}, u32[]{:S(2)}, u32[]{:S(2)}) collective-permute-start(bf16[6,128,1024]{2,1,0:T(8,128)(2,1)} %collective-permute-done.11.refs_3_), channel_id=1, source_target_pairs={{0,1},{1,0},{2,3},{3,2},{4,5},{5,4},{6,7},{7,6},{8,9},{9,8},{10,11... | collective-permute-start | bytes 4718600 | tf_op jit(solution)/shard_map/ppermute | solution.py:33
  140.7 0.9 copy-start.1
  140.7 27.2 %collective-permute-start.19 = (bf16[6,128,1024]{2,1,0:T(8,128)(2,1)}, bf16[6,128,1024]{2,1,0:T(8,128)(2,1)}, u32[]{:S(2)}, u32[]{:S(2)}) collective-permute-start(bf16[6,128,1024]{2,1,0:T(8,128)(2,1)} %collective-permute-done.12.refs_4_), channel_id=1, source_target_pairs={{0,1},{1,0},{2,3},{3,2},{4,5},{5,4},{6,7},{7,6},{8,9},{9,8},{10,11... | collective-permute-start | bytes 4718600 | tf_op jit(solution)/shard_map/ppermute | solution.py:33
  141.5 26.3 %collective-permute-start.17 = (bf16[6,128,1024]{2,1,0:T(8,128)(2,1)}, bf16[6,128,1024]{2,1,0:T(8,128)(2,1)}, u32[]{:S(2)}, u32[]{:S(2)}) collective-permute-start(bf16[6,128,1024]{2,1,0:T(8,128)(2,1)} %pad_maximum_fusion.refs_2_), channel_id=1, source_target_pairs={{0,1},{1,0},{2,3},{3,2},{4,5},{5,4},{6,7},{7,6},{8,9},{9,8},{10,11... | collective-permute-start | bytes 4718600 | tf_op jit(solution)/shard_map/ppermute | solution.py:33
  159.6 4.4 %copy-start.2 = (bf16[3,128,1024]{2,1,0:T(8,128)(2,1)S(1)}, bf16[3,128,1024]{2,1,0:T(8,128)(2,1)}, u32[]{:S(2)}) copy-start(bf16[3,128,1024]{2,1,0:T(8,128)(2,1)} %copy-done.1) | copy-start | bytes 2359300
  159.6 35.5 %all-to-all-start.3 = ((bf16[32,72,512]{2,1,0:T(8,128)(2,1)}), bf16[32,72,512]{2,1,0:T(8,128)(2,1)S(1)}, u32[]{:S(2)}, u32[]{:S(2)}) async-start(bf16[32,72,512]{2,1,0:T(8,128)(2,1)} %sum_blocks.1), calls=%async_computation.3 | async-start | bytes 4718592 | tf_op jit(solution)/shard_map/all_to_all | solution.py:41
  164.0 2.6 %collective-permute-start.21 = (bf16[3,128,1024]{2,1,0:T(8,128)(2,1)S(1)}, bf16[3,128,1024]{2,1,0:T(8,128)(2,1)}, u32[]{:S(2)}, u32[]{:S(2)}) collective-permute-start(bf16[3,128,1024]{2,1,0:T(8,128)(2,1)S(1)} %copy-done.2), channel_id=1, source_target_pairs={{0,1},{1,0},{2,3},{3,2},{4,5},{5,4},{6,7},{7,6},{8,9},{9,8},{10,11... | collective-permute-start | bytes 2359304 | tf_op jit(solution)/shard_map/ppermute | solution.py:33
  164.1 3.7 %collective-permute-start.20 = (bf16[3,128,1024]{2,1,0:T(8,128)(2,1)}, bf16[3,128,1024]{2,1,0:T(8,128)(2,1)}, u32[]{:S(2)}, u32[]{:S(2)}) collective-permute-start(bf16[3,128,1024]{2,1,0:T(8,128)(2,1)} %collective-permute-done.13.refs_5_), channel_id=1, source_target_pairs={{0,1},{1,0},{2,3},{3,2},{4,5},{5,4},{6,7},{7,6},{8,9},{9,8},{10,11... | collective-permute-start | bytes 2359304 | tf_op jit(solution)/shard_map/ppermute | solution.py:33

commit v10 on v8

--- a/solution.py
+++ b/solution.py
@@ -240,15 +240,14 @@
     owner = want // slots
     oy, ox = (y_at - owner // xhs) % ys, (xh_at - owner % xhs) % xhs
     at = (oy * xhs + ox) * slots + want % slots
-    every = gate(every, ring_x)
     picked = every.reshape(adapters, *own.shape[1:])[at].reshape(steps, blocks, *own.shape[1:])
-    low = exchange(picked, FSDP)
+    low = exchange(gate(picked, ring_x), FSDP)
 
     w_x = lax.ppermute(gate(weight, picked), X, across)
     ring = jnp.concatenate([gate(ring, picked), ring_x])
     y_back, y_next = shift(ring, "y", 1), shift(ring, "y", -1)
 
-    grid = 4
+    grid = 2
     per = steps // grid
     x_spec = pl.BlockSpec((rows_dev, per * feats), lambda i: (0, i))
     up_rows = cols // folds

time: 199 us -> 195 us (0.980)
  waiting for transfers between devices: 88.3 us -> 85.4 us
    ppermute x1, waiting for transfers between devices: 4.81 us -> 2.12 us  [body(): ring_x = lax.ppermute(ring, X, across)]
  transfers between devices with their start and end apart: 25 -> 25, of which waited for: 11 -> 11; matrix products, arithmetic and copies ran while one was open for 5% -> 7% of each run, Pallas kernels for 20% -> 20%
where the time goes in v10:
time: 195 us; the launch traced here: 194 us
  waiting for transfers between devices  85.4 us (44%)
  starting transfers between devices  50 us (26%)
  Pallas kernels  37.9 us (19%)
  local copies, waits for them, and re-layouts  14.9 us (8%)
  other arithmetic  4.95 us (3%)
    all_to_all x4, waiting for transfers between devices, exchange(): return lax.all_to_all(x, axis, split_axis=0, concat_axis=0, tiled=True)  53.8 us
    pallas_call x1, Pallas kernels, body(): pl.pallas_call(functools.partial(base_kernel, blocks, quarter), grid_spec...  25.9 us
    all_to_all x4, starting transfers between devices, exchange(): return lax.all_to_all(x, axis, split_axis=0, concat_axis=0, tiled=True)  21.4 us
    ppermute x19, starting transfers between devices, shift(): return lax.ppermute(x, axis, [(i, (i + by) % n) for i in range(n)])  21.3 us
    ppermute x1, waiting for transfers between devices, body(): w_x = lax.ppermute(gate(weight, picked), X, across)  19.2 us
    ppermute x19, waiting for transfers between devices, shift(): return lax.ppermute(x, axis, [(i, (i + by) % n) for i in range(n)])  10.2 us
    pallas_call x1, Pallas kernels, body(): pl.pallas_call(functools.partial(low_kernel, blocks, per), grid=(grid,),...  8.7 us
    unnamed x21, local copies, waits for them, and re-layouts  4.87 us
  transfers between devices with their start and end apart: 25, of which 11 were waited for; matrix products, arithmetic and copies ran while one was open for 7% of the time, Pallas kernels for 20%

profile of v10, /device:TPU:0, one launch (start us, length us, event | category | flops | bytes accessed | tf_op | source)
XLA Modules:
  0.0 194.1 jit_solution(7546787255234024227)
XLA Ops:
  2.7 3.2 %collective-permute-start = (bf16[4,72,512]{2,1,0:T(8,128)(2,1)S(1)}, bf16[4,72,512]{2,1,0:T(8,128)(2,1)S(1)}, u32[]{:S(2)}, u32[]{:S(2)}) collective-permute-start(bf16[4,72,512]{2,1,0:T(8,128)(2,1)S(1)} %get-tuple-element.59), channel_id=1, source_target_pairs={{0,16},{16,0},{1,17},{17,1},{2,18},{18,2},{3,19},{19,3},{4,20},{20... | collective-permute-start | bytes 884744 | tf_op jit(solution)/shard_map/ppermute | solution.py:33
  6.9 4.0 %collective-permute-start.7 = (bf16[128,1024]{1,0:T(8,128)(2,1)S(1)}, bf16[128,1024]{1,0:T(8,128)(2,1)S(1)}, u32[]{:S(2)}, u32[]{:S(2)}) collective-permute-start(bf16[128,1024]{1,0:T(8,128)(2,1)S(1)} %constant_dynamic-slice_fusion), channel_id=1, source_target_pairs={{0,8},{4,12},{8,0},{12,4},{1,9},{5,13},{9,1},{13,5},{2,10},{6,14},... | collective-permute-start | bytes 786440 | tf_op jit(solution)/shard_map/ppermute | solution.py:33
  11.5 1.3 collective-permute-start.5
  13.8 1.8 collective-permute-start.1
  15.6 1.4 collective-permute-start.3
  17.7 6.6 %all-to-all-start = ((s32[16,8,128]{2,1,0:T(8,128)}), s32[16,8,128]{2,1,0:T(8,128)S(1)}, u32[]{:S(2)}, u32[]{:S(2)}) async-start(s32[16,8,128]{2,1,0:T(8,128)} %broadcast_in_dim.4), calls=%async_computation | async-start | bytes 131072 | tf_op jit(solution)/shard_map/all_to_all | solution.py:41
  25.0 1.0 pad_maximum_fusion.1
  26.0 3.3 %collective-permute-start.8 = (bf16[3,128,1024]{2,1,0:T(8,128)(2,1)S(1)}, bf16[3,128,1024]{2,1,0:T(8,128)(2,1)}, u32[]{:S(2)}, u32[]{:S(2)}) collective-permute-start(bf16[3,128,1024]{2,1,0:T(8,128)(2,1)S(1)} %pad_maximum_fusion.1), channel_id=1, source_target_pairs={{0,18},{18,0},{2,16},{16,2},{1,19},{19,1},{3,17},{17,3},{4,22},{22... | collective-permute-start | bytes 2359304 | tf_op jit(solution)/shard_map/ppermute | solution.py:232
  29.3 1.1 all-to-all-done
  31.1 2.9 %collective-permute-start.4 = (bf16[2,2,72,512]{3,2,1,0:T(8,128)(2,1)S(1)}, bf16[2,2,72,512]{3,2,1,0:T(8,128)(2,1)S(1)}, u32[]{:S(2)}, u32[]{:S(2)}) collective-permute-start(bf16[2,2,72,512]{3,2,1,0:T(8,128)(2,1)S(1)} %slice.22), channel_id=1, source_target_pairs={{0,96},{32,0},{64,32},{96,64},{1,97},{33,1},{65,33},{97,65},{2,98}... | collective-permute-start | bytes 884744 | tf_op jit(solution)/shard_map/ppermute | solution.py:33
  34.1 6.8 %collective-permute-done.2 = bf16[2,2,72,512]{3,2,1,0:T(8,128)(2,1)S(1)} collective-permute-done((bf16[2,2,72,512]{3,2,1,0:T(8,128)(2,1)S(1)}, bf16[2,2,72,512]{3,2,1,0:T(8,128)(2,1)S(1)}, u32[]{:S(2)}, u32[]{:S(2)}) %collective-permute-start.2) | collective-permute-done | bytes 294944 | tf_op jit(solution)/shard_map/ppermute | solution.py:33
  41.0 1.5 pad_maximum_fusion
  42.5 2.7 %gather_fusion = bf16[48,72,512]{2,1,0:T(8,128)(2,1)} fusion(bf16[32,72,512]{2,1,0:T(8,128)(2,1)S(1)} %bitcast.54, s32[1024]{0:T(1024)S(1)} %pad_clamp_fusion), kind=kCustom, calls=%fused_computation | custom fusion | bytes 7078080 | tf_op jit(solution)/shard_map/gather | solution.py:243
  45.2 2.1 %collective-permute-done.8 = bf16[3,128,1024]{2,1,0:T(8,128)(2,1)} collective-permute-done((bf16[3,128,1024]{2,1,0:T(8,128)(2,1)S(1)}, bf16[3,128,1024]{2,1,0:T(8,128)(2,1)}, u32[]{:S(2)}, u32[]{:S(2)}) %collective-permute-start.8) | collective-permute-done | bytes 786464 | tf_op jit(solution)/shard_map/ppermute | solution.py:232
  47.3 4.6 %all-to-all-start.1 = ((bf16[16,3,72,512]{3,2,1,0:T(8,128)(2,1)}), bf16[16,3,72,512]{3,2,1,0:T(8,128)(2,1)}, u32[]{:S(2)}, u32[]{:S(2)}) async-start(bf16[16,3,72,512]{3,2,1,0:T(8,128)(2,1)} %bitcast.55), calls=%async_computation.1 | async-start | bytes 7077888 | tf_op jit(solution)/shard_map/all_to_all | solution.py:41
  52.9 2.1 %constant_dynamic-update-slice_fusion.refs_2_ = bf16[6,128,1024]{2,1,0:T(8,128)(2,1)} fusion(bf16[6,128,1024]{2,1,0:T(8,128)(2,1)} %constant_dynamic-update-slice_fusion.1, bf16[3,128,1024]{2,1,0:T(8,128)(2,1)} %collective-permute-done.8), kind=kLoop, calls=%fused_computation.11 | loop fusion | bytes 1572864 | tf_op jit(solution)/shard_map/concatenate | solution.py:247
  54.9 1.8 collective-permute-start.11
  57.0 38.3 %all-to-all-done.1.packed_ref.down_ref = bf16[16,3,72,512]{3,2,1,0:T(8,128)(2,1)} async-done(((bf16[16,3,72,512]{3,2,1,0:T(8,128)(2,1)}), bf16[16,3,72,512]{3,2,1,0:T(8,128)(2,1)}, u32[]{:S(2)}, u32[]{:S(2)}) %all-to-all-start.1) | async-done | bytes 3538976 | tf_op jit(solution)/shard_map/all_to_all | solution.py:41
  95.3 8.7 %low.1 = (bf16[384,64]{1,0:T(8,128)(2,1)}, bf16[384,64]{1,0:T(8,128)(2,1)}, bf16[3,1024,64]{2,1,0:T(8,128)(2,1)}, bf16[16,3,72,512]{3,2,1,0:T(8,128)(2,1)}) custom-call(s32[3]{0:T(128)S(1)} %copy-done, bf16[384,8192]{1,0:T(8,128)(2,1)} %x_ref.3, bf16[384,1024]{1,0:T(8,128)(2,1)} %dy_ref.3, bf16[16,3,72,512]{3,2,1,0:T(8,128)(2,1)} %all-to-all-done.1.packed_ref.down_ref, ...), custom_call_target="tpu_custom_call" | custom-call | flops 905969664 | bytes 16777216 | tf_op jit(solution)/shard_map/low/pallas_call | solution.py:254
  104.0 3.8 %all-to-all-start.2 = ((bf16[16,3,72,512]{3,2,1,0:T(8,128)(2,1)}), bf16[16,3,72,512]{3,2,1,0:T(8,128)(2,1)S(1)}, u32[]{:S(2)}, u32[]{:S(2)}) async-start(bf16[16,3,72,512]{3,2,1,0:T(8,128)(2,1)} %get-tuple-element.42), calls=%async_computation.2 | async-start | bytes 7077888 | tf_op jit(solution)/shard_map/all_to_all | solution.py:41
  107.8 4.0 %collective-permute-start.9 = (bf16[512,1024]{1,0:T(8,128)(2,1)}, bf16[512,1024]{1,0:T(8,128)(2,1)}, u32[]{:S(2)}, u32[]{:S(2)}) collective-permute-start(bf16[512,1024]{1,0:T(8,128)(2,1)} %refs_0_.1), channel_id=1, source_target_pairs={{0,18},{18,0},{2,16},{16,2},{1,19},{19,1},{3,17},{17,3},{4,22},{22... | collective-permute-start | bytes 3145736 | tf_op jit(solution)/shard_map/ppermute | solution.py:246
  111.7 1.2 slice.25
  112.9 1.9 collective-permute-start.13
  114.8 1.2 slice.24
  116.3 19.2 %collective-permute-done.9.refs_1_ = bf16[512,1024]{1,0:T(8,128)(2,1)} collective-permute-done((bf16[512,1024]{1,0:T(8,128)(2,1)}, bf16[512,1024]{1,0:T(8,128)(2,1)}, u32[]{:S(2)}, u32[]{:S(2)}) %collective-permute-start.9) | collective-permute-done | bytes 1048608 | tf_op jit(solution)/shard_map/ppermute | solution.py:246
  137.8 13.2 %all-to-all-done.2.g_ref = bf16[16,3,72,512]{3,2,1,0:T(8,128)(2,1)S(1)} async-done(((bf16[16,3,72,512]{3,2,1,0:T(8,128)(2,1)}), bf16[16,3,72,512]{3,2,1,0:T(8,128)(2,1)S(1)}, u32[]{:S(2)}, u32[]{:S(2)}) %all-to-all-start.2) | async-done | bytes 3538976 | tf_op jit(solution)/shard_map/all_to_all | solution.py:41
  151.1 3.3 %sum_blocks.1 = bf16[32,72,512]{2,1,0:T(8,128)(2,1)} custom-call(s32[16,3]{1,0:T(8,128)S(1)} %bitcast.53, bf16[16,3,72,512]{3,2,1,0:T(8,128)(2,1)S(1)} %all-to-all-done.2.g_ref), custom_call_target="tpu_custom_call" | custom-call | flops 1769472 | bytes 7077888 | tf_op jit(solution)/shard_map/sum_blocks/pallas_call | solution.py:193
  154.4 6.5 %all-to-all-start.3 = ((bf16[32,72,512]{2,1,0:T(8,128)(2,1)}), bf16[32,72,512]{2,1,0:T(8,128)(2,1)S(1)}, u32[]{:S(2)}, u32[]{:S(2)}) async-start(bf16[32,72,512]{2,1,0:T(8,128)(2,1)} %sum_blocks.1), calls=%async_computation.3 | async-start | bytes 4718592 | tf_op jit(solution)/shard_map/all_to_all | solution.py:41
  161.7 1.9 collective-permute-done.20.refs_13_
  163.6 1.3 collective-permute-done.19.refs_12_
  164.9 25.9 %base.1 = (bf16[384,1024]{1,0:T(8,128)(2,1)}, bf16[384,8192]{1,0:T(8,128)(2,1)}) custom-call(s32[20]{0:T(128)S(1)} %stack.119.f_ref, bf16[384,8192]{1,0:T(8,128)(2,1)} %x_ref.3, bf16[384,1024]{1,0:T(8,128)(2,1)} %dy_ref.3, bf16[384,64]{1,0:T(8,128)(2,1)} %get-tuple-element.27.u_ref, bf16[384,64]{1,0:T(8,128)(2,1)} %get-tuple-element.28.v_ref, ...), custom_call_target="tpu_custom_call" | custom-call | flops 12884901888 | bytes 37748736 | tf_op jit(solution)/shard_map/base/pallas_call | solution.py:293
  190.8 1.1 all-to-all-done.3
  (69 shorter events, 13.5 us)
Async XLA Ops:
  0.6 16.4 %copy-start.8 = (s32[3]{0:T(128)S(1)}, s32[3]{0:T(128)}, u32[]{:S(2)}) copy-start(s32[3]{0:T(128)} %param.12) | copy-start | bytes 40
  2.7 10.2 %collective-permute-start = (bf16[4,72,512]{2,1,0:T(8,128)(2,1)S(1)}, bf16[4,72,512]{2,1,0:T(8,128)(2,1)S(1)}, u32[]{:S(2)}, u32[]{:S(2)}) collective-permute-start(bf16[4,72,512]{2,1,0:T(8,128)(2,1)S(1)} %get-tuple-element.59), channel_id=1, source_target_pairs={{0,16},{16,0},{1,17},{17,1},{2,18},{18,2},{3,19},{19,3},{4,20},{20... | collective-permute-start | bytes 884744 | tf_op jit(solution)/shard_map/ppermute | solution.py:33
  6.9 17.4 %collective-permute-start.7 = (bf16[128,1024]{1,0:T(8,128)(2,1)S(1)}, bf16[128,1024]{1,0:T(8,128)(2,1)S(1)}, u32[]{:S(2)}, u32[]{:S(2)}) collective-permute-start(bf16[128,1024]{1,0:T(8,128)(2,1)S(1)} %constant_dynamic-slice_fusion), channel_id=1, source_target_pairs={{0,8},{4,12},{8,0},{12,4},{1,9},{5,13},{9,1},{13,5},{2,10},{6,14},... | collective-permute-start | bytes 786440 | tf_op jit(solution)/shard_map/ppermute | solution.py:33
  10.8 13.4 %collective-permute-start.6 = (bf16[128,1024]{1,0:T(8,128)(2,1)S(1)}, bf16[128,1024]{1,0:T(8,128)(2,1)S(1)}, u32[]{:S(2)}, u32[]{:S(2)}) collective-permute-start(bf16[128,1024]{1,0:T(8,128)(2,1)S(1)} %constant_dynamic-slice_fusion), channel_id=1, source_target_pairs={{0,12},{4,0},{8,4},{12,8},{1,13},{5,1},{9,5},{13,9},{2,14},{6,2},{... | collective-permute-start | bytes 786440 | tf_op jit(solution)/shard_map/ppermute | solution.py:33
  11.5 12.7 %collective-permute-start.5 = (bf16[128,1024]{1,0:T(8,128)(2,1)S(1)}, bf16[128,1024]{1,0:T(8,128)(2,1)S(1)}, u32[]{:S(2)}, u32[]{:S(2)}) collective-permute-start(bf16[128,1024]{1,0:T(8,128)(2,1)S(1)} %constant_dynamic-slice_fusion), channel_id=1, source_target_pairs={{0,4},{4,8},{8,12},{12,0},{1,5},{5,9},{9,13},{13,1},{2,6},{6,10},{... | collective-permute-start | bytes 786440 | tf_op jit(solution)/shard_map/ppermute | solution.py:33
  13.8 16.7 %collective-permute-start.1 = (bf16[2,4,72,512]{3,2,1,0:T(8,128)(2,1)S(1)}, bf16[2,4,72,512]{3,2,1,0:T(8,128)(2,1)S(1)}, u32[]{:S(2)}, u32[]{:S(2)}) collective-permute-start(bf16[2,4,72,512]{3,2,1,0:T(8,128)(2,1)S(1)} %get-tuple-element.57), channel_id=1, source_target_pairs={{0,32},{32,64},{64,96},{96,0},{1,33},{33,65},{65,97},{97,1},{2,34}... | collective-permute-start | bytes 1769480 | tf_op jit(solution)/shard_map/ppermute | solution.py:33
  15.6 15.4 %collective-permute-start.3 = (bf16[2,4,72,512]{3,2,1,0:T(8,128)(2,1)S(1)}, bf16[2,4,72,512]{3,2,1,0:T(8,128)(2,1)S(1)}, u32[]{:S(2)}, u32[]{:S(2)}) collective-permute-start(bf16[2,4,72,512]{3,2,1,0:T(8,128)(2,1)S(1)} %get-tuple-element.57), channel_id=1, source_target_pairs={{0,96},{32,0},{64,32},{96,64},{1,97},{33,1},{65,33},{97,65},{2,98}... | collective-permute-start | bytes 1769480 | tf_op jit(solution)/shard_map/ppermute | solution.py:33
  17.7 12.7 %all-to-all-start = ((s32[16,8,128]{2,1,0:T(8,128)}), s32[16,8,128]{2,1,0:T(8,128)S(1)}, u32[]{:S(2)}, u32[]{:S(2)}) async-start(s32[16,8,128]{2,1,0:T(8,128)} %broadcast_in_dim.4), calls=%async_computation | async-start | bytes 131072 | tf_op jit(solution)/shard_map/all_to_all | solution.py:41
  26.0 21.3 %collective-permute-start.8 = (bf16[3,128,1024]{2,1,0:T(8,128)(2,1)S(1)}, bf16[3,128,1024]{2,1,0:T(8,128)(2,1)}, u32[]{:S(2)}, u32[]{:S(2)}) collective-permute-start(bf16[3,128,1024]{2,1,0:T(8,128)(2,1)S(1)} %pad_maximum_fusion.1), channel_id=1, source_target_pairs={{0,18},{18,0},{2,16},{16,2},{1,19},{19,1},{3,17},{17,3},{4,22},{22... | collective-permute-start | bytes 2359304 | tf_op jit(solution)/shard_map/ppermute | solution.py:232
  30.5 10.4 %copy-start.1 = (bf16[1,2,4,72,512]{4,3,2,1,0:T(8,128)(2,1)S(1)}, bf16[1,2,4,72,512]{4,3,2,1,0:T(8,128)(2,1)}, u32[]{:S(2)}) copy-start(bf16[1,2,4,72,512]{4,3,2,1,0:T(8,128)(2,1)} %get-tuple-element.56) | copy-start | bytes 1769476
  30.6 10.4 %copy-start.2 = (bf16[2,4,72,512]{3,2,1,0:T(8,128)(2,1)}, bf16[2,4,72,512]{3,2,1,0:T(8,128)(2,1)S(1)}, u32[]{:S(2)}) copy-start(bf16[2,4,72,512]{3,2,1,0:T(8,128)(2,1)S(1)} %collective-permute-done.1) | copy-start | bytes 1769476
  30.6 10.3 %collective-permute-start.2 = (bf16[2,2,72,512]{3,2,1,0:T(8,128)(2,1)S(1)}, bf16[2,2,72,512]{3,2,1,0:T(8,128)(2,1)S(1)}, u32[]{:S(2)}, u32[]{:S(2)}) collective-permute-start(bf16[2,2,72,512]{3,2,1,0:T(8,128)(2,1)S(1)} %slice.21), channel_id=1, source_target_pairs={{0,32},{32,64},{64,96},{96,0},{1,33},{33,65},{65,97},{97,1},{2,34}... | collective-permute-start | bytes 884744 | tf_op jit(solution)/shard_map/ppermute | solution.py:33
  31.0 9.9 %copy-start.3 = (bf16[2,4,72,512]{3,2,1,0:T(8,128)(2,1)}, bf16[2,4,72,512]{3,2,1,0:T(8,128)(2,1)S(1)}, u32[]{:S(2)}) copy-start(bf16[2,4,72,512]{3,2,1,0:T(8,128)(2,1)S(1)} %collective-permute-done.3) | copy-start | bytes 1769476
  31.1 9.8 %collective-permute-start.4 = (bf16[2,2,72,512]{3,2,1,0:T(8,128)(2,1)S(1)}, bf16[2,2,72,512]{3,2,1,0:T(8,128)(2,1)S(1)}, u32[]{:S(2)}, u32[]{:S(2)}) collective-permute-start(bf16[2,2,72,512]{3,2,1,0:T(8,128)(2,1)S(1)} %slice.22), channel_id=1, source_target_pairs={{0,96},{32,0},{64,32},{96,64},{1,97},{33,1},{65,33},{97,65},{2,98}... | collective-permute-start | bytes 884744 | tf_op jit(solution)/shard_map/ppermute | solution.py:33
  47.3 48.0 %all-to-all-start.1 = ((bf16[16,3,72,512]{3,2,1,0:T(8,128)(2,1)}), bf16[16,3,72,512]{3,2,1,0:T(8,128)(2,1)}, u32[]{:S(2)}, u32[]{:S(2)}) async-start(bf16[16,3,72,512]{3,2,1,0:T(8,128)(2,1)} %bitcast.55), calls=%async_computation.1 | async-start | bytes 7077888 | tf_op jit(solution)/shard_map/all_to_all | solution.py:41
  51.9 43.4 %copy-start = (s32[3]{0:T(128)S(1)}, s32[3]{0:T(128)}, u32[]{:S(2)}) copy-start(s32[3]{0:T(128)} %fill_ref.1) | copy-start | bytes 40
  54.9 49.1 %collective-permute-start.11 = (bf16[6,128,1024]{2,1,0:T(8,128)(2,1)}, bf16[6,128,1024]{2,1,0:T(8,128)(2,1)}, u32[]{:S(2)}, u32[]{:S(2)}) collective-permute-start(bf16[6,128,1024]{2,1,0:T(8,128)(2,1)} %constant_dynamic-update-slice_fusion.refs_2_), channel_id=1, source_target_pairs={{0,96},{32,0},{64,32},{96,64},{1,97},{33,1},{65,33},{97,65},{2,98}... | collective-permute-start | bytes 4718600 | tf_op jit(solution)/shard_map/ppermute | solution.py:33
  56.7 47.2 %collective-permute-start.10 = (bf16[6,128,1024]{2,1,0:T(8,128)(2,1)}, bf16[6,128,1024]{2,1,0:T(8,128)(2,1)}, u32[]{:S(2)}, u32[]{:S(2)}) collective-permute-start(bf16[6,128,1024]{2,1,0:T(8,128)(2,1)} %constant_dynamic-update-slice_fusion.refs_2_), channel_id=1, source_target_pairs={{0,32},{32,64},{64,96},{96,0},{1,33},{33,65},{65,97},{97,1},{2,34}... | collective-permute-start | bytes 4718600 | tf_op jit(solution)/shard_map/ppermute | solution.py:33
  104.0 47.1 %all-to-all-start.2 = ((bf16[16,3,72,512]{3,2,1,0:T(8,128)(2,1)}), bf16[16,3,72,512]{3,2,1,0:T(8,128)(2,1)S(1)}, u32[]{:S(2)}, u32[]{:S(2)}) async-start(bf16[16,3,72,512]{3,2,1,0:T(8,128)(2,1)} %get-tuple-element.42), calls=%async_computation.2 | async-start | bytes 7077888 | tf_op jit(solution)/shard_map/all_to_all | solution.py:41
  107.8 27.8 %collective-permute-start.9 = (bf16[512,1024]{1,0:T(8,128)(2,1)}, bf16[512,1024]{1,0:T(8,128)(2,1)}, u32[]{:S(2)}, u32[]{:S(2)}) collective-permute-start(bf16[512,1024]{1,0:T(8,128)(2,1)} %refs_0_.1), channel_id=1, source_target_pairs={{0,18},{18,0},{2,16},{16,2},{1,19},{19,1},{3,17},{17,3},{4,22},{22... | collective-permute-start | bytes 3145736 | tf_op jit(solution)/shard_map/ppermute | solution.py:246
  112.9 23.1 %collective-permute-start.13 = (bf16[3,128,1024]{2,1,0:T(8,128)(2,1)S(1)}, bf16[3,128,1024]{2,1,0:T(8,128)(2,1)S(1)}, u32[]{:S(2)}, u32[]{:S(2)}) collective-permute-start(bf16[3,128,1024]{2,1,0:T(8,128)(2,1)S(1)} %slice.25), channel_id=1, source_target_pairs={{0,96},{32,0},{64,32},{96,64},{1,97},{33,1},{65,33},{97,65},{2,98}... | collective-permute-start | bytes 2359304 | tf_op jit(solution)/shard_map/ppermute | solution.py:33
  116.0 20.3 %collective-permute-start.12 = (bf16[3,128,1024]{2,1,0:T(8,128)(2,1)S(1)}, bf16[3,128,1024]{2,1,0:T(8,128)(2,1)S(1)}, u32[]{:S(2)}, u32[]{:S(2)}) collective-permute-start(bf16[3,128,1024]{2,1,0:T(8,128)(2,1)S(1)} %slice.24), channel_id=1, source_target_pairs={{0,32},{32,64},{64,96},{96,0},{1,33},{33,65},{65,97},{97,1},{2,34}... | collective-permute-start | bytes 2359304 | tf_op jit(solution)/shard_map/ppermute | solution.py:33
  116.3 44.5 %collective-permute-start.14 = (bf16[512,1024]{1,0:T(8,128)(2,1)}, bf16[512,1024]{1,0:T(8,128)(2,1)}, u32[]{:S(2)}, u32[]{:S(2)}) collective-permute-start(bf16[512,1024]{1,0:T(8,128)(2,1)} %refs_0_.1), channel_id=1, source_target_pairs={{0,1},{1,0},{2,3},{3,2},{4,5},{5,4},{6,7},{7,6},{8,9},{9,8},{10,11... | collective-permute-start | bytes 3145736 | tf_op jit(solution)/shard_map/ppermute | solution.py:33
  135.5 25.6 %collective-permute-start.15 = (bf16[512,1024]{1,0:T(8,128)(2,1)}, bf16[512,1024]{1,0:T(8,128)(2,1)}, u32[]{:S(2)}, u32[]{:S(2)}) collective-permute-start(bf16[512,1024]{1,0:T(8,128)(2,1)} %collective-permute-done.9.refs_1_), channel_id=1, source_target_pairs={{0,1},{1,0},{2,3},{3,2},{4,5},{5,4},{6,7},{7,6},{8,9},{9,8},{10,11... | collective-permute-start | bytes 3145736 | tf_op jit(solution)/shard_map/ppermute | solution.py:33
  135.5 29.3 %collective-permute-start.17 = (bf16[6,128,1024]{2,1,0:T(8,128)(2,1)}, bf16[6,128,1024]{2,1,0:T(8,128)(2,1)}, u32[]{:S(2)}, u32[]{:S(2)}) collective-permute-start(bf16[6,128,1024]{2,1,0:T(8,128)(2,1)} %collective-permute-done.10.refs_3_), channel_id=1, source_target_pairs={{0,1},{1,0},{2,3},{3,2},{4,5},{5,4},{6,7},{7,6},{8,9},{9,8},{10,11... | collective-permute-start | bytes 4718600 | tf_op jit(solution)/shard_map/ppermute | solution.py:33
  136.1 28.8 %collective-permute-start.18 = (bf16[6,128,1024]{2,1,0:T(8,128)(2,1)}, bf16[6,128,1024]{2,1,0:T(8,128)(2,1)}, u32[]{:S(2)}, u32[]{:S(2)}) collective-permute-start(bf16[6,128,1024]{2,1,0:T(8,128)(2,1)} %collective-permute-done.11.refs_4_), channel_id=1, source_target_pairs={{0,1},{1,0},{2,3},{3,2},{4,5},{5,4},{6,7},{7,6},{8,9},{9,8},{10,11... | collective-permute-start | bytes 4718600 | tf_op jit(solution)/shard_map/ppermute | solution.py:33
  136.9 0.9 copy-start.7
  137.8 27.1 %collective-permute-start.16 = (bf16[6,128,1024]{2,1,0:T(8,128)(2,1)}, bf16[6,128,1024]{2,1,0:T(8,128)(2,1)}, u32[]{:S(2)}, u32[]{:S(2)}) collective-permute-start(bf16[6,128,1024]{2,1,0:T(8,128)(2,1)} %constant_dynamic-update-slice_fusion.refs_2_), channel_id=1, source_target_pairs={{0,1},{1,0},{2,3},{3,2},{4,5},{5,4},{6,7},{7,6},{8,9},{9,8},{10,11... | collective-permute-start | bytes 4718600 | tf_op jit(solution)/shard_map/ppermute | solution.py:33
  154.4 6.5 %copy-start.6 = (bf16[3,128,1024]{2,1,0:T(8,128)(2,1)S(1)}, bf16[3,128,1024]{2,1,0:T(8,128)(2,1)}, u32[]{:S(2)}) copy-start(bf16[3,128,1024]{2,1,0:T(8,128)(2,1)} %copy-done.5) | copy-start | bytes 2359300
  154.4 37.6 %all-to-all-start.3 = ((bf16[32,72,512]{2,1,0:T(8,128)(2,1)}), bf16[32,72,512]{2,1,0:T(8,128)(2,1)S(1)}, u32[]{:S(2)}, u32[]{:S(2)}) async-start(bf16[32,72,512]{2,1,0:T(8,128)(2,1)} %sum_blocks.1), calls=%async_computation.3 | async-start | bytes 4718592 | tf_op jit(solution)/shard_map/all_to_all | solution.py:41
  160.8 2.8 %collective-permute-start.20 = (bf16[3,128,1024]{2,1,0:T(8,128)(2,1)S(1)}, bf16[3,128,1024]{2,1,0:T(8,128)(2,1)}, u32[]{:S(2)}, u32[]{:S(2)}) collective-permute-start(bf16[3,128,1024]{2,1,0:T(8,128)(2,1)S(1)} %copy-done.6), channel_id=1, source_target_pairs={{0,1},{1,0},{2,3},{3,2},{4,5},{5,4},{6,7},{7,6},{8,9},{9,8},{10,11... | collective-permute-start | bytes 2359304 | tf_op jit(solution)/shard_map/ppermute | solution.py:33
  161.1 3.7 %collective-permute-start.19 = (bf16[3,128,1024]{2,1,0:T(8,128)(2,1)}, bf16[3,128,1024]{2,1,0:T(8,128)(2,1)}, u32[]{:S(2)}, u32[]{:S(2)}) collective-permute-start(bf16[3,128,1024]{2,1,0:T(8,128)(2,1)} %copy-done.7), channel_id=1, source_target_pairs={{0,1},{1,0},{2,3},{3,2},{4,5},{5,4},{6,7},{7,6},{8,9},{9,8},{10,11... | collective-permute-start | bytes 2359304 | tf_op jit(solution)/shard_map/ppermute | solution.py:33
  (2 other events, 1.6 us)

commit v11 on v10

--- a/solution.py
+++ b/solution.py
@@ -284,6 +284,7 @@
 
     w_own = [weight, w_x, ring, y_back, y_next, y_lo, y_hi]
     w_all = w_own + [shift(gate(w, low_u), "c", 1) for w in w_own]
+    back = gate(back, *w_all)
     order = [
         (z_at + dz) % 4 * 4 + (xl_at + dx) % 2 * 2 + (c_at + dc) % 2
         for dc in (0, 1)

time: 195 us -> 197 us (1.010)
  local copies, waits for them, and re-layouts: 14.9 us -> 17.6 us
    all_to_all x4, waiting for transfers between devices: 53.8 us -> 45.8 us  [exchange(): return lax.all_to_all(x, axis, split_axis=0, concat_axis=0, tiled=True)]
    ppermute x19, waiting for transfers between devices: 10.2 us -> 17.2 us  [shift(): return lax.ppermute(x, axis, [(i, (i + by) % n) for i in range(n)])]
    unnamed x21 -> x41, local copies, waits for them, and re-layouts: 4.87 us -> 7.55 us
  transfers between devices with their start and end apart: 25 -> 25, of which waited for: 11 -> 12; matrix products, arithmetic and copies ran while one was open for 7% -> 7% of each run, Pallas kernels for 20% -> 18%
where the time goes in v11:
time: 197 us; the launch traced here: 196 us
  waiting for transfers between devices  84.3 us (43%)
  starting transfers between devices  49.8 us (25%)
  Pallas kernels  37.9 us (19%)
  local copies, waits for them, and re-layouts  17.6 us (9%)
  other arithmetic  4.95 us (3%)
    all_to_all x4, waiting for transfers between devices, exchange(): return lax.all_to_all(x, axis, split_axis=0, concat_axis=0, tiled=True)  45.8 us
    pallas_call x1, Pallas kernels, body(): pl.pallas_call(functools.partial(base_kernel, blocks, quarter), grid_spec...  25.9 us
    ppermute x19, starting transfers between devices, shift(): return lax.ppermute(x, axis, [(i, (i + by) % n) for i in range(n)])  21.3 us
    all_to_all x4, starting transfers between devices, exchange(): return lax.all_to_all(x, axis, split_axis=0, concat_axis=0, tiled=True)  21.2 us
    ppermute x1, waiting for transfers between devices, body(): w_x = lax.ppermute(gate(weight, picked), X, across)  19.1 us
    ppermute x19, waiting for transfers between devices, shift(): return lax.ppermute(x, axis, [(i, (i + by) % n) for i in range(n)])  17.2 us
    pallas_call x1, Pallas kernels, body(): pl.pallas_call(functools.partial(low_kernel, blocks, per), grid=(grid,),...  8.7 us
    unnamed x41, local copies, waits for them, and re-layouts  7.55 us
  transfers between devices with their start and end apart: 25, of which 12 were waited for; matrix products, arithmetic and copies ran while one was open for 7% of the time, Pallas kernels for 18%

profile of v11, /device:TPU:0, one launch (start us, length us, event | category | flops | bytes accessed | tf_op | source)
XLA Modules:
  0.0 195.6 jit_solution(16309353654808070932)
XLA Ops:
  2.7 3.2 %collective-permute-start = (bf16[4,72,512]{2,1,0:T(8,128)(2,1)S(1)}, bf16[4,72,512]{2,1,0:T(8,128)(2,1)S(1)}, u32[]{:S(2)}, u32[]{:S(2)}) collective-permute-start(bf16[4,72,512]{2,1,0:T(8,128)(2,1)S(1)} %get-tuple-element.61), channel_id=1, source_target_pairs={{0,16},{16,0},{1,17},{17,1},{2,18},{18,2},{3,19},{19,3},{4,20},{20... | collective-permute-start | bytes 884744 | tf_op jit(solution)/shard_map/ppermute | solution.py:33
  6.9 4.0 %collective-permute-start.7 = (bf16[128,1024]{1,0:T(8,128)(2,1)S(1)}, bf16[128,1024]{1,0:T(8,128)(2,1)S(1)}, u32[]{:S(2)}, u32[]{:S(2)}) collective-permute-start(bf16[128,1024]{1,0:T(8,128)(2,1)S(1)} %constant_dynamic-slice_fusion), channel_id=1, source_target_pairs={{0,8},{4,12},{8,0},{12,4},{1,9},{5,13},{9,1},{13,5},{2,10},{6,14},... | collective-permute-start | bytes 786440 | tf_op jit(solution)/shard_map/ppermute | solution.py:33
  11.5 1.3 collective-permute-start.5
  13.8 1.8 collective-permute-start.1
  15.6 1.4 collective-permute-start.3
  17.7 6.6 %all-to-all-start = ((s32[16,8,128]{2,1,0:T(8,128)}), s32[16,8,128]{2,1,0:T(8,128)S(1)}, u32[]{:S(2)}, u32[]{:S(2)}) async-start(s32[16,8,128]{2,1,0:T(8,128)} %broadcast_in_dim.4), calls=%async_computation | async-start | bytes 131072 | tf_op jit(solution)/shard_map/all_to_all | solution.py:41
  26.0 3.3 %collective-permute-start.8 = (bf16[3,128,1024]{2,1,0:T(8,128)(2,1)S(1)}, bf16[3,128,1024]{2,1,0:T(8,128)(2,1)}, u32[]{:S(2)}, u32[]{:S(2)}) collective-permute-start(bf16[3,128,1024]{2,1,0:T(8,128)(2,1)S(1)} %pad_maximum_fusion.1), channel_id=1, source_target_pairs={{0,18},{18,0},{2,16},{16,2},{1,19},{19,1},{3,17},{17,3},{4,22},{22... | collective-permute-start | bytes 2359304 | tf_op jit(solution)/shard_map/ppermute | solution.py:232
  31.1 2.9 %collective-permute-start.4 = (bf16[2,2,72,512]{3,2,1,0:T(8,128)(2,1)S(1)}, bf16[2,2,72,512]{3,2,1,0:T(8,128)(2,1)S(1)}, u32[]{:S(2)}, u32[]{:S(2)}) collective-permute-start(bf16[2,2,72,512]{3,2,1,0:T(8,128)(2,1)S(1)} %slice.22), channel_id=1, source_target_pairs={{0,96},{32,0},{64,32},{96,64},{1,97},{33,1},{65,33},{97,65},{2,98}... | collective-permute-start | bytes 884744 | tf_op jit(solution)/shard_map/ppermute | solution.py:33
  34.1 6.8 %collective-permute-done.2 = bf16[2,2,72,512]{3,2,1,0:T(8,128)(2,1)S(1)} collective-permute-done((bf16[2,2,72,512]{3,2,1,0:T(8,128)(2,1)S(1)}, bf16[2,2,72,512]{3,2,1,0:T(8,128)(2,1)S(1)}, u32[]{:S(2)}, u32[]{:S(2)}) %collective-permute-start.2) | collective-permute-done | bytes 294944 | tf_op jit(solution)/shard_map/ppermute | solution.py:33
  41.0 1.5 pad_maximum_fusion
  42.5 2.7 %gather_fusion = bf16[48,72,512]{2,1,0:T(8,128)(2,1)} fusion(bf16[32,72,512]{2,1,0:T(8,128)(2,1)S(1)} %bitcast.54, s32[1024]{0:T(1024)S(1)} %pad_clamp_fusion), kind=kCustom, calls=%fused_computation | custom fusion | bytes 7078080 | tf_op jit(solution)/shard_map/gather | solution.py:243
  45.2 2.1 %collective-permute-done.8 = bf16[3,128,1024]{2,1,0:T(8,128)(2,1)} collective-permute-done((bf16[3,128,1024]{2,1,0:T(8,128)(2,1)S(1)}, bf16[3,128,1024]{2,1,0:T(8,128)(2,1)}, u32[]{:S(2)}, u32[]{:S(2)}) %collective-permute-start.8) | collective-permute-done | bytes 786464 | tf_op jit(solution)/shard_map/ppermute | solution.py:232
  47.3 4.6 %all-to-all-start.1 = ((bf16[16,3,72,512]{3,2,1,0:T(8,128)(2,1)}), bf16[16,3,72,512]{3,2,1,0:T(8,128)(2,1)}, u32[]{:S(2)}, u32[]{:S(2)}) async-start(bf16[16,3,72,512]{3,2,1,0:T(8,128)(2,1)} %bitcast.55), calls=%async_computation.1 | async-start | bytes 7077888 | tf_op jit(solution)/shard_map/all_to_all | solution.py:41
  52.9 2.1 %constant_dynamic-update-slice_fusion.refs_2_ = bf16[6,128,1024]{2,1,0:T(8,128)(2,1)} fusion(bf16[6,128,1024]{2,1,0:T(8,128)(2,1)} %constant_dynamic-update-slice_fusion.1, bf16[3,128,1024]{2,1,0:T(8,128)(2,1)} %collective-permute-done.8), kind=kLoop, calls=%fused_computation.11 | loop fusion | bytes 1572864 | tf_op jit(solution)/shard_map/concatenate | solution.py:247
  54.9 1.8 collective-permute-start.11
  57.0 38.3 %all-to-all-done.1.packed_ref.down_ref = bf16[16,3,72,512]{3,2,1,0:T(8,128)(2,1)} async-done(((bf16[16,3,72,512]{3,2,1,0:T(8,128)(2,1)}), bf16[16,3,72,512]{3,2,1,0:T(8,128)(2,1)}, u32[]{:S(2)}, u32[]{:S(2)}) %all-to-all-start.1) | async-done | bytes 3538976 | tf_op jit(solution)/shard_map/all_to_all | solution.py:41
  95.3 8.7 %low.1 = (bf16[384,64]{1,0:T(8,128)(2,1)}, bf16[384,64]{1,0:T(8,128)(2,1)}, bf16[3,1024,64]{2,1,0:T(8,128)(2,1)}, bf16[16,3,72,512]{3,2,1,0:T(8,128)(2,1)}) custom-call(s32[3]{0:T(128)S(1)} %copy-done, bf16[384,8192]{1,0:T(8,128)(2,1)} %x_ref.3, bf16[384,1024]{1,0:T(8,128)(2,1)} %dy_ref.3, bf16[16,3,72,512]{3,2,1,0:T(8,128)(2,1)} %all-to-all-done.1.packed_ref.down_ref, ...), custom_call_target="tpu_custom_call" | custom-call | flops 905969664 | bytes 16777216 | tf_op jit(solution)/shard_map/low/pallas_call | solution.py:254
  104.0 1.2 copy-done.4
  105.6 3.8 %all-to-all-start.2 = ((bf16[16,3,72,512]{3,2,1,0:T(8,128)(2,1)}), bf16[16,3,72,512]{3,2,1,0:T(8,128)(2,1)S(1)}, u32[]{:S(2)}, u32[]{:S(2)}) async-start(bf16[16,3,72,512]{3,2,1,0:T(8,128)(2,1)} %get-tuple-element.43), calls=%async_computation.2 | async-start | bytes 7077888 | tf_op jit(solution)/shard_map/all_to_all | solution.py:41
  109.4 4.1 %collective-permute-start.9 = (bf16[512,1024]{1,0:T(8,128)(2,1)}, bf16[512,1024]{1,0:T(8,128)(2,1)S(1)}, u32[]{:S(2)}, u32[]{:S(2)}) collective-permute-start(bf16[512,1024]{1,0:T(8,128)(2,1)} %refs_0_.1), channel_id=1, source_target_pairs={{0,18},{18,0},{2,16},{16,2},{1,19},{19,1},{3,17},{17,3},{4,22},{22... | collective-permute-start | bytes 3145736 | tf_op jit(solution)/shard_map/ppermute | solution.py:246
  113.5 1.2 slice.25
  114.7 1.9 collective-permute-start.13
  116.5 1.2 slice.24
  118.0 19.1 %collective-permute-done.9.refs_1_ = bf16[512,1024]{1,0:T(8,128)(2,1)S(1)} collective-permute-done((bf16[512,1024]{1,0:T(8,128)(2,1)}, bf16[512,1024]{1,0:T(8,128)(2,1)S(1)}, u32[]{:S(2)}, u32[]{:S(2)}) %collective-permute-start.9) | collective-permute-done | bytes 1048608 | tf_op jit(solution)/shard_map/ppermute | solution.py:246
  138.6 1.3 collective-permute-done.15.refs_8_
  140.0 7.7 %collective-permute-done.20.refs_13_ = bf16[3,128,1024]{2,1,0:T(8,128)(2,1)S(1)} collective-permute-done((bf16[3,128,1024]{2,1,0:T(8,128)(2,1)S(1)}, bf16[3,128,1024]{2,1,0:T(8,128)(2,1)S(1)}, u32[]{:S(2)}, u32[]{:S(2)}) %collective-permute-start.20) | collective-permute-done | bytes 786464 | tf_op jit(solution)/shard_map/ppermute | solution.py:33
  150.2 1.2 copy-done.10
  151.4 1.3 all-to-all-done.2.g_ref
  152.7 3.3 %sum_blocks.1 = bf16[32,72,512]{2,1,0:T(8,128)(2,1)} custom-call(s32[16,3]{1,0:T(8,128)S(1)} %bitcast.53, bf16[16,3,72,512]{3,2,1,0:T(8,128)(2,1)S(1)} %all-to-all-done.2.g_ref), custom_call_target="tpu_custom_call" | custom-call | flops 1769472 | bytes 7077888 | tf_op jit(solution)/shard_map/sum_blocks/pallas_call | solution.py:193
  156.0 6.3 %all-to-all-start.3 = ((bf16[32,72,512]{2,1,0:T(8,128)(2,1)}), bf16[32,72,512]{2,1,0:T(8,128)(2,1)S(1)}, u32[]{:S(2)}, u32[]{:S(2)}) async-start(bf16[32,72,512]{2,1,0:T(8,128)(2,1)} %sum_blocks.1), calls=%async_computation.3 | async-start | bytes 4718592 | tf_op jit(solution)/shard_map/all_to_all | solution.py:41
  162.4 25.9 %base.1 = (bf16[384,1024]{1,0:T(8,128)(2,1)}, bf16[384,8192]{1,0:T(8,128)(2,1)}) custom-call(s32[20]{0:T(128)S(1)} %stack.119.f_ref, bf16[384,8192]{1,0:T(8,128)(2,1)} %x_ref.3, bf16[384,1024]{1,0:T(8,128)(2,1)} %dy_ref.3, bf16[384,64]{1,0:T(8,128)(2,1)} %get-tuple-element.28.u_ref, bf16[384,64]{1,0:T(8,128)(2,1)} %get-tuple-element.29.v_ref, ...), custom_call_target="tpu_custom_call" | custom-call | flops 12884901888 | bytes 37748736 | tf_op jit(solution)/shard_map/base/pallas_call | solution.py:294
  188.3 5.1 %all-to-all-done.3 = bf16[32,72,512]{2,1,0:T(8,128)(2,1)S(1)} async-done(((bf16[32,72,512]{2,1,0:T(8,128)(2,1)}), bf16[32,72,512]{2,1,0:T(8,128)(2,1)S(1)}, u32[]{:S(2)}, u32[]{:S(2)}) %all-to-all-start.3) | async-done | bytes 2359328 | tf_op jit(solution)/shard_map/all_to_all | solution.py:41
  (89 shorter events, 17.0 us)
Async XLA Ops:
  0.6 16.4 %copy-start.18 = (s32[3]{0:T(128)S(1)}, s32[3]{0:T(128)}, u32[]{:S(2)}) copy-start(s32[3]{0:T(128)} %param.12) | copy-start | bytes 40
  2.7 10.2 %collective-permute-start = (bf16[4,72,512]{2,1,0:T(8,128)(2,1)S(1)}, bf16[4,72,512]{2,1,0:T(8,128)(2,1)S(1)}, u32[]{:S(2)}, u32[]{:S(2)}) collective-permute-start(bf16[4,72,512]{2,1,0:T(8,128)(2,1)S(1)} %get-tuple-element.61), channel_id=1, source_target_pairs={{0,16},{16,0},{1,17},{17,1},{2,18},{18,2},{3,19},{19,3},{4,20},{20... | collective-permute-start | bytes 884744 | tf_op jit(solution)/shard_map/ppermute | solution.py:33
  6.9 17.4 %collective-permute-start.7 = (bf16[128,1024]{1,0:T(8,128)(2,1)S(1)}, bf16[128,1024]{1,0:T(8,128)(2,1)S(1)}, u32[]{:S(2)}, u32[]{:S(2)}) collective-permute-start(bf16[128,1024]{1,0:T(8,128)(2,1)S(1)} %constant_dynamic-slice_fusion), channel_id=1, source_target_pairs={{0,8},{4,12},{8,0},{12,4},{1,9},{5,13},{9,1},{13,5},{2,10},{6,14},... | collective-permute-start | bytes 786440 | tf_op jit(solution)/shard_map/ppermute | solution.py:33
  10.8 13.4 %collective-permute-start.6 = (bf16[128,1024]{1,0:T(8,128)(2,1)S(1)}, bf16[128,1024]{1,0:T(8,128)(2,1)S(1)}, u32[]{:S(2)}, u32[]{:S(2)}) collective-permute-start(bf16[128,1024]{1,0:T(8,128)(2,1)S(1)} %constant_dynamic-slice_fusion), channel_id=1, source_target_pairs={{0,12},{4,0},{8,4},{12,8},{1,13},{5,1},{9,5},{13,9},{2,14},{6,2},{... | collective-permute-start | bytes 786440 | tf_op jit(solution)/shard_map/ppermute | solution.py:33
  11.5 12.7 %collective-permute-start.5 = (bf16[128,1024]{1,0:T(8,128)(2,1)S(1)}, bf16[128,1024]{1,0:T(8,128)(2,1)S(1)}, u32[]{:S(2)}, u32[]{:S(2)}) collective-permute-start(bf16[128,1024]{1,0:T(8,128)(2,1)S(1)} %constant_dynamic-slice_fusion), channel_id=1, source_target_pairs={{0,4},{4,8},{8,12},{12,0},{1,5},{5,9},{9,13},{13,1},{2,6},{6,10},{... | collective-permute-start | bytes 786440 | tf_op jit(solution)/shard_map/ppermute | solution.py:33
  13.8 16.7 %collective-permute-start.1 = (bf16[2,4,72,512]{3,2,1,0:T(8,128)(2,1)S(1)}, bf16[2,4,72,512]{3,2,1,0:T(8,128)(2,1)S(1)}, u32[]{:S(2)}, u32[]{:S(2)}) collective-permute-start(bf16[2,4,72,512]{3,2,1,0:T(8,128)(2,1)S(1)} %get-tuple-element.59), channel_id=1, source_target_pairs={{0,32},{32,64},{64,96},{96,0},{1,33},{33,65},{65,97},{97,1},{2,34}... | collective-permute-start | bytes 1769480 | tf_op jit(solution)/shard_map/ppermute | solution.py:33
  15.6 15.4 %collective-permute-start.3 = (bf16[2,4,72,512]{3,2,1,0:T(8,128)(2,1)S(1)}, bf16[2,4,72,512]{3,2,1,0:T(8,128)(2,1)S(1)}, u32[]{:S(2)}, u32[]{:S(2)}) collective-permute-start(bf16[2,4,72,512]{3,2,1,0:T(8,128)(2,1)S(1)} %get-tuple-element.59), channel_id=1, source_target_pairs={{0,96},{32,0},{64,32},{96,64},{1,97},{33,1},{65,33},{97,65},{2,98}... | collective-permute-start | bytes 1769480 | tf_op jit(solution)/shard_map/ppermute | solution.py:33
  17.7 12.7 %all-to-all-start = ((s32[16,8,128]{2,1,0:T(8,128)}), s32[16,8,128]{2,1,0:T(8,128)S(1)}, u32[]{:S(2)}, u32[]{:S(2)}) async-start(s32[16,8,128]{2,1,0:T(8,128)} %broadcast_in_dim.4), calls=%async_computation | async-start | bytes 131072 | tf_op jit(solution)/shard_map/all_to_all | solution.py:41
  26.0 21.3 %collective-permute-start.8 = (bf16[3,128,1024]{2,1,0:T(8,128)(2,1)S(1)}, bf16[3,128,1024]{2,1,0:T(8,128)(2,1)}, u32[]{:S(2)}, u32[]{:S(2)}) collective-permute-start(bf16[3,128,1024]{2,1,0:T(8,128)(2,1)S(1)} %pad_maximum_fusion.1), channel_id=1, source_target_pairs={{0,18},{18,0},{2,16},{16,2},{1,19},{19,1},{3,17},{17,3},{4,22},{22... | collective-permute-start | bytes 2359304 | tf_op jit(solution)/shard_map/ppermute | solution.py:232
  30.6 10.3 %collective-permute-start.2 = (bf16[2,2,72,512]{3,2,1,0:T(8,128)(2,1)S(1)}, bf16[2,2,72,512]{3,2,1,0:T(8,128)(2,1)S(1)}, u32[]{:S(2)}, u32[]{:S(2)}) collective-permute-start(bf16[2,2,72,512]{3,2,1,0:T(8,128)(2,1)S(1)} %slice.21), channel_id=1, source_target_pairs={{0,32},{32,64},{64,96},{96,0},{1,33},{33,65},{65,97},{97,1},{2,34}... | collective-permute-start | bytes 884744 | tf_op jit(solution)/shard_map/ppermute | solution.py:33
  31.1 9.8 %collective-permute-start.4 = (bf16[2,2,72,512]{3,2,1,0:T(8,128)(2,1)S(1)}, bf16[2,2,72,512]{3,2,1,0:T(8,128)(2,1)S(1)}, u32[]{:S(2)}, u32[]{:S(2)}) collective-permute-start(bf16[2,2,72,512]{3,2,1,0:T(8,128)(2,1)S(1)} %slice.22), channel_id=1, source_target_pairs={{0,96},{32,0},{64,32},{96,64},{1,97},{33,1},{65,33},{97,65},{2,98}... | collective-permute-start | bytes 884744 | tf_op jit(solution)/shard_map/ppermute | solution.py:33
  47.3 48.0 %all-to-all-start.1 = ((bf16[16,3,72,512]{3,2,1,0:T(8,128)(2,1)}), bf16[16,3,72,512]{3,2,1,0:T(8,128)(2,1)}, u32[]{:S(2)}, u32[]{:S(2)}) async-start(bf16[16,3,72,512]{3,2,1,0:T(8,128)(2,1)} %bitcast.55), calls=%async_computation.1 | async-start | bytes 7077888 | tf_op jit(solution)/shard_map/all_to_all | solution.py:41
  51.9 43.4 %copy-start = (s32[3]{0:T(128)S(1)}, s32[3]{0:T(128)}, u32[]{:S(2)}) copy-start(s32[3]{0:T(128)} %fill_ref.1) | copy-start | bytes 40
  54.9 49.0 %collective-permute-start.11 = (bf16[6,128,1024]{2,1,0:T(8,128)(2,1)}, bf16[6,128,1024]{2,1,0:T(8,128)(2,1)S(1)}, u32[]{:S(2)}, u32[]{:S(2)}) collective-permute-start(bf16[6,128,1024]{2,1,0:T(8,128)(2,1)} %constant_dynamic-update-slice_fusion.refs_2_), channel_id=1, source_target_pairs={{0,96},{32,0},{64,32},{96,64},{1,97},{33,1},{65,33},{97,65},{2,98}... | collective-permute-start | bytes 4718600 | tf_op jit(solution)/shard_map/ppermute | solution.py:33
  56.8 47.2 %collective-permute-start.10 = (bf16[6,128,1024]{2,1,0:T(8,128)(2,1)}, bf16[6,128,1024]{2,1,0:T(8,128)(2,1)S(1)}, u32[]{:S(2)}, u32[]{:S(2)}) collective-permute-start(bf16[6,128,1024]{2,1,0:T(8,128)(2,1)} %constant_dynamic-update-slice_fusion.refs_2_), channel_id=1, source_target_pairs={{0,32},{32,64},{64,96},{96,0},{1,33},{33,65},{65,97},{97,1},{2,34}... | collective-permute-start | bytes 4718600 | tf_op jit(solution)/shard_map/ppermute | solution.py:33
  105.6 47.1 %all-to-all-start.2 = ((bf16[16,3,72,512]{3,2,1,0:T(8,128)(2,1)}), bf16[16,3,72,512]{3,2,1,0:T(8,128)(2,1)S(1)}, u32[]{:S(2)}, u32[]{:S(2)}) async-start(bf16[16,3,72,512]{3,2,1,0:T(8,128)(2,1)} %get-tuple-element.43), calls=%async_computation.2 | async-start | bytes 7077888 | tf_op jit(solution)/shard_map/all_to_all | solution.py:41
  109.4 27.8 %copy-start.7 = (bf16[6,128,1024]{2,1,0:T(8,128)(2,1)S(1)}, bf16[6,128,1024]{2,1,0:T(8,128)(2,1)}, u32[]{:S(2)}) copy-start(bf16[6,128,1024]{2,1,0:T(8,128)(2,1)} %copy-done.6) | copy-start | bytes 4718596
  109.4 28.3 %copy-start.5 = (bf16[6,128,1024]{2,1,0:T(8,128)(2,1)S(1)}, bf16[6,128,1024]{2,1,0:T(8,128)(2,1)}, u32[]{:S(2)}) copy-start(bf16[6,128,1024]{2,1,0:T(8,128)(2,1)} %copy-done.4) | copy-start | bytes 4718596
  109.4 27.7 %collective-permute-start.9 = (bf16[512,1024]{1,0:T(8,128)(2,1)}, bf16[512,1024]{1,0:T(8,128)(2,1)S(1)}, u32[]{:S(2)}, u32[]{:S(2)}) collective-permute-start(bf16[512,1024]{1,0:T(8,128)(2,1)} %refs_0_.1), channel_id=1, source_target_pairs={{0,18},{18,0},{2,16},{16,2},{1,19},{19,1},{3,17},{17,3},{4,22},{22... | collective-permute-start | bytes 3145736 | tf_op jit(solution)/shard_map/ppermute | solution.py:246
  114.7 23.0 %collective-permute-start.13 = (bf16[3,128,1024]{2,1,0:T(8,128)(2,1)S(1)}, bf16[3,128,1024]{2,1,0:T(8,128)(2,1)S(1)}, u32[]{:S(2)}, u32[]{:S(2)}) collective-permute-start(bf16[3,128,1024]{2,1,0:T(8,128)(2,1)S(1)} %slice.25), channel_id=1, source_target_pairs={{0,96},{32,0},{64,32},{96,64},{1,97},{33,1},{65,33},{97,65},{2,98}... | collective-permute-start | bytes 2359304 | tf_op jit(solution)/shard_map/ppermute | solution.py:33
  117.7 20.3 %collective-permute-start.12 = (bf16[3,128,1024]{2,1,0:T(8,128)(2,1)S(1)}, bf16[3,128,1024]{2,1,0:T(8,128)(2,1)S(1)}, u32[]{:S(2)}, u32[]{:S(2)}) collective-permute-start(bf16[3,128,1024]{2,1,0:T(8,128)(2,1)S(1)} %slice.24), channel_id=1, source_target_pairs={{0,32},{32,64},{64,96},{96,0},{1,33},{33,65},{65,97},{97,1},{2,34}... | collective-permute-start | bytes 2359304 | tf_op jit(solution)/shard_map/ppermute | solution.py:33
  118.0 20.3 %collective-permute-start.14 = (bf16[512,1024]{1,0:T(8,128)(2,1)}, bf16[512,1024]{1,0:T(8,128)(2,1)S(1)}, u32[]{:S(2)}, u32[]{:S(2)}) collective-permute-start(bf16[512,1024]{1,0:T(8,128)(2,1)} %refs_0_.1), channel_id=1, source_target_pairs={{0,1},{1,0},{2,3},{3,2},{4,5},{5,4},{6,7},{7,6},{8,9},{9,8},{10,11... | collective-permute-start | bytes 3145736 | tf_op jit(solution)/shard_map/ppermute | solution.py:33
  137.2 11.7 %copy-start.11 = (bf16[512,1024]{1,0:T(8,128)(2,1)}, bf16[512,1024]{1,0:T(8,128)(2,1)S(1)}, u32[]{:S(2)}) copy-start(bf16[512,1024]{1,0:T(8,128)(2,1)S(1)} %collective-permute-done.9.refs_1_) | copy-start | bytes 3145732
  137.2 2.7 %collective-permute-start.15 = (bf16[512,1024]{1,0:T(8,128)(2,1)S(1)}, bf16[512,1024]{1,0:T(8,128)(2,1)S(1)}, u32[]{:S(2)}, u32[]{:S(2)}) collective-permute-start(bf16[512,1024]{1,0:T(8,128)(2,1)S(1)} %collective-permute-done.9.refs_1_), channel_id=1, source_target_pairs={{0,1},{1,0},{2,3},{3,2},{4,5},{5,4},{6,7},{7,6},{8,9},{9,8},{10,11... | collective-permute-start | bytes 3145736 | tf_op jit(solution)/shard_map/ppermute | solution.py:33
  137.2 11.7 %collective-permute-start.17 = (bf16[6,128,1024]{2,1,0:T(8,128)(2,1)S(1)}, bf16[6,128,1024]{2,1,0:T(8,128)(2,1)S(1)}, u32[]{:S(2)}, u32[]{:S(2)}) collective-permute-start(bf16[6,128,1024]{2,1,0:T(8,128)(2,1)S(1)} %copy-done.7), channel_id=1, source_target_pairs={{0,1},{1,0},{2,3},{3,2},{4,5},{5,4},{6,7},{7,6},{8,9},{9,8},{10,11... | collective-permute-start | bytes 4718600 | tf_op jit(solution)/shard_map/ppermute | solution.py:33
  137.7 11.2 %copy-start.14 = (bf16[3,128,1024]{2,1,0:T(8,128)(2,1)}, bf16[3,128,1024]{2,1,0:T(8,128)(2,1)S(1)}, u32[]{:S(2)}) copy-start(bf16[3,128,1024]{2,1,0:T(8,128)(2,1)S(1)} %collective-permute-done.13.refs_6_) | copy-start | bytes 2359300
  137.7 11.1 %collective-permute-start.18 = (bf16[6,128,1024]{2,1,0:T(8,128)(2,1)S(1)}, bf16[6,128,1024]{2,1,0:T(8,128)(2,1)S(1)}, u32[]{:S(2)}, u32[]{:S(2)}) collective-permute-start(bf16[6,128,1024]{2,1,0:T(8,128)(2,1)S(1)} %copy-done.5), channel_id=1, source_target_pairs={{0,1},{1,0},{2,3},{3,2},{4,5},{5,4},{6,7},{7,6},{8,9},{9,8},{10,11... | collective-permute-start | bytes 4718600 | tf_op jit(solution)/shard_map/ppermute | solution.py:33
  138.0 10.8 %copy-start.15 = (bf16[3,128,1024]{2,1,0:T(8,128)(2,1)}, bf16[3,128,1024]{2,1,0:T(8,128)(2,1)S(1)}, u32[]{:S(2)}) copy-start(bf16[3,128,1024]{2,1,0:T(8,128)(2,1)S(1)} %collective-permute-done.12.refs_5_) | copy-start | bytes 2359300
  138.1 13.4 %collective-permute-start.16 = (bf16[6,128,1024]{2,1,0:T(8,128)(2,1)}, bf16[6,128,1024]{2,1,0:T(8,128)(2,1)}, u32[]{:S(2)}, u32[]{:S(2)}) collective-permute-start(bf16[6,128,1024]{2,1,0:T(8,128)(2,1)} %constant_dynamic-update-slice_fusion.refs_2_), channel_id=1, source_target_pairs={{0,1},{1,0},{2,3},{3,2},{4,5},{5,4},{6,7},{7,6},{8,9},{9,8},{10,11... | collective-permute-start | bytes 4718600 | tf_op jit(solution)/shard_map/ppermute | solution.py:33
  138.3 9.4 %collective-permute-start.20 = (bf16[3,128,1024]{2,1,0:T(8,128)(2,1)S(1)}, bf16[3,128,1024]{2,1,0:T(8,128)(2,1)S(1)}, u32[]{:S(2)}, u32[]{:S(2)}) collective-permute-start(bf16[3,128,1024]{2,1,0:T(8,128)(2,1)S(1)} %collective-permute-done.13.refs_6_), channel_id=1, source_target_pairs={{0,1},{1,0},{2,3},{3,2},{4,5},{5,4},{6,7},{7,6},{8,9},{9,8},{10,11... | collective-permute-start | bytes 2359304 | tf_op jit(solution)/shard_map/ppermute | solution.py:33
  139.8 9.0 %collective-permute-start.19 = (bf16[3,128,1024]{2,1,0:T(8,128)(2,1)S(1)}, bf16[3,128,1024]{2,1,0:T(8,128)(2,1)S(1)}, u32[]{:S(2)}, u32[]{:S(2)}) collective-permute-start(bf16[3,128,1024]{2,1,0:T(8,128)(2,1)S(1)} %collective-permute-done.12.refs_5_), channel_id=1, source_target_pairs={{0,1},{1,0},{2,3},{3,2},{4,5},{5,4},{6,7},{7,6},{8,9},{9,8},{10,11... | collective-permute-start | bytes 2359304 | tf_op jit(solution)/shard_map/ppermute | solution.py:33
  156.0 37.4 %all-to-all-start.3 = ((bf16[32,72,512]{2,1,0:T(8,128)(2,1)}), bf16[32,72,512]{2,1,0:T(8,128)(2,1)S(1)}, u32[]{:S(2)}, u32[]{:S(2)}) async-start(bf16[32,72,512]{2,1,0:T(8,128)(2,1)} %sum_blocks.1), calls=%async_computation.3 | async-start | bytes 4718592 | tf_op jit(solution)/shard_map/all_to_all | solution.py:41
  (12 other events, 58.6 us)

commit v12 on v10

--- a/solution.py
+++ b/solution.py
@@ -229,7 +229,8 @@
 
     across = [(0, 3), (3, 0), (1, 2), (2, 1)]
     ring = jnp.stack(rest)
-    ring_x = lax.ppermute(ring, X, across)
+    early = quarter * 7 // 8
+    x_early = lax.ppermute(jnp.stack([r[:early] for r in rest]), X, across)
 
     lo = shift(gate(one, ids_all)[:, : slots // 2], "y", 1)
     hi = shift(gate(three, ids_all)[:, slots // 2 :], "y", -1)
@@ -241,10 +242,11 @@
     oy, ox = (y_at - owner // xhs) % ys, (xh_at - owner % xhs) % xhs
     at = (oy * xhs + ox) * slots + want % slots
     picked = every.reshape(adapters, *own.shape[1:])[at].reshape(steps, blocks, *own.shape[1:])
-    low = exchange(gate(picked, ring_x), FSDP)
+    low = exchange(gate(picked, x_early), FSDP)
 
     w_x = lax.ppermute(gate(weight, picked), X, across)
-    ring = jnp.concatenate([gate(ring, picked), ring_x])
+    x_late = lax.ppermute(gate(ring, picked)[:, early:], X, across)
+    ring = jnp.concatenate([gate(ring, picked), jnp.concatenate([x_early, x_late], axis=1)])
     y_back, y_next = shift(ring, "y", 1), shift(ring, "y", -1)
 
     grid = 2

time: 195 us -> 205 us (1.051)
  waiting for transfers between devices: 85.4 us -> 93 us
  starting transfers between devices: 50 us -> 52.7 us
    ppermute x19, waiting for transfers between devices: 10.2 us -> 25.9 us  [shift(): return lax.ppermute(x, axis, [(i, (i + by) % n) for i in range(n)])]
    all_to_all x4, waiting for transfers between devices: 53.8 us -> 45.9 us  [exchange(): return lax.all_to_all(x, axis, split_axis=0, concat_axis=0, tiled=True)]
    ppermute x1 -> x2, starting transfers between devices: 3.26 us -> 6.4 us  [the longest x1 3.42 us: body(): x_late = lax.ppermute(gate(ring, picked)[:, early:], X, across)]
    concatenate x0 -> x1, other arithmetic: none -> 2.4 us  [body(): jnp.concatenate([gate(ring, picked), jnp.concatenate([x_early, x_late], a...]
    unnamed x21 -> x24, local copies, waits for them, and re-layouts: 4.87 us -> 2.61 us
    concatenate x1 -> x0, local copies, waits for them, and re-layouts: 2.08 us -> none  [body(): ring = jnp.concatenate([gate(ring, picked), ring_x])]
  transfers between devices with their start and end apart: 25 -> 26, of which waited for: 11 -> 12; matrix products, arithmetic and copies ran while one was open for 7% -> 7% of each run, Pallas kernels for 20% -> 19%
where the time goes in v12:
time: 205 us; the launch traced here: 204 us
  waiting for transfers between devices  93 us (45%)
  starting transfers between devices  52.7 us (26%)
  Pallas kernels  37.9 us (18%)
  local copies, waits for them, and re-layouts  12.9 us (6%)
  other arithmetic  6.34 us (3%)
    all_to_all x4, waiting for transfers between devices, exchange(): return lax.all_to_all(x, axis, split_axis=0, concat_axis=0, tiled=True)  45.9 us
    ppermute x19, waiting for transfers between devices, shift(): return lax.ppermute(x, axis, [(i, (i + by) % n) for i in range(n)])  25.9 us
    pallas_call x1, Pallas kernels, body(): pl.pallas_call(functools.partial(base_kernel, blocks, quarter), grid_spec...  25.9 us
    ppermute x19, starting transfers between devices, shift(): return lax.ppermute(x, axis, [(i, (i + by) % n) for i in range(n)])  23.2 us
    all_to_all x4, starting transfers between devices, exchange(): return lax.all_to_all(x, axis, split_axis=0, concat_axis=0, tiled=True)  19.9 us
    ppermute x1, waiting for transfers between devices, body(): w_x = lax.ppermute(gate(weight, picked), X, across)  18.1 us
    pallas_call x1, Pallas kernels, body(): pl.pallas_call(functools.partial(low_kernel, blocks, per), grid=(grid,),...  8.7 us
  transfers between devices with their start and end apart: 26, of which 12 were waited for; matrix products, arithmetic and copies ran while one was open for 7% of the time, Pallas kernels for 19%

profile of v12, /device:TPU:0, one launch (start us, length us, event | category | flops | bytes accessed | tf_op | source)
XLA Modules:
  0.0 203.8 jit_solution(7129731226594254657)
XLA Ops:
  0.6 1.7 constant_dynamic-slice_fusion
  2.3 4.0 %collective-permute-start.7 = (bf16[128,1024]{1,0:T(8,128)(2,1)}, bf16[128,1024]{1,0:T(8,128)(2,1)S(1)}, u32[]{:S(2)}, u32[]{:S(2)}) collective-permute-start(bf16[128,1024]{1,0:T(8,128)(2,1)} %constant_dynamic-slice_fusion), channel_id=1, source_target_pairs={{0,8},{4,12},{8,0},{12,4},{1,9},{5,13},{9,1},{13,5},{2,10},{6,14},... | collective-permute-start | bytes 786440 | tf_op jit(solution)/shard_map/ppermute | solution.py:33
  7.0 1.3 collective-permute-start.5
  9.6 4.3 %all-to-all-start = ((s32[16,8,128]{2,1,0:T(8,128)}), s32[16,8,128]{2,1,0:T(8,128)}, u32[]{:S(2)}, u32[]{:S(2)}) async-start(s32[16,8,128]{2,1,0:T(8,128)} %broadcast_in_dim.4), calls=%async_computation | async-start | bytes 131072 | tf_op jit(solution)/shard_map/all_to_all | solution.py:41
  16.0 3.0 %collective-permute-start = (bf16[4,72,512]{2,1,0:T(8,128)(2,1)S(1)}, bf16[4,72,512]{2,1,0:T(8,128)(2,1)S(1)}, u32[]{:S(2)}, u32[]{:S(2)}) collective-permute-start(bf16[4,72,512]{2,1,0:T(8,128)(2,1)S(1)} %get-tuple-element.59), channel_id=1, source_target_pairs={{0,16},{16,0},{1,17},{17,1},{2,18},{18,2},{3,19},{19,3},{4,20},{20... | collective-permute-start | bytes 884744 | tf_op jit(solution)/shard_map/ppermute | solution.py:33
  19.7 7.1 %collective-permute-done = bf16[4,72,512]{2,1,0:T(8,128)(2,1)S(1)} collective-permute-done((bf16[4,72,512]{2,1,0:T(8,128)(2,1)S(1)}, bf16[4,72,512]{2,1,0:T(8,128)(2,1)S(1)}, u32[]{:S(2)}, u32[]{:S(2)}) %collective-permute-start) | collective-permute-done | bytes 294944 | tf_op jit(solution)/shard_map/ppermute | solution.py:33
  26.9 1.6 collective-permute-start.1
  28.6 1.7 collective-permute-start.3
  31.2 3.0 %collective-permute-start.8 = (bf16[3,112,1024]{2,1,0:T(8,128)(2,1)}, bf16[3,112,1024]{2,1,0:T(8,128)(2,1)}, u32[]{:S(2)}, u32[]{:S(2)}) collective-permute-start(bf16[3,112,1024]{2,1,0:T(8,128)(2,1)} %pad_maximum_fusion.2), channel_id=1, source_target_pairs={{0,18},{18,0},{2,16},{16,2},{1,19},{19,1},{3,17},{17,3},{4,22},{22... | collective-permute-start | bytes 2064392 | tf_op jit(solution)/shard_map/ppermute | solution.py:233
  35.1 7.9 %collective-permute-done.1 = bf16[2,4,72,512]{3,2,1,0:T(8,128)(2,1)S(1)} collective-permute-done((bf16[2,4,72,512]{3,2,1,0:T(8,128)(2,1)S(1)}, bf16[2,4,72,512]{3,2,1,0:T(8,128)(2,1)S(1)}, u32[]{:S(2)}, u32[]{:S(2)}) %collective-permute-start.1) | collective-permute-done | bytes 589856 | tf_op jit(solution)/shard_map/ppermute | solution.py:33
  43.5 3.0 %collective-permute-start.4 = (bf16[2,2,72,512]{3,2,1,0:T(8,128)(2,1)S(1)}, bf16[2,2,72,512]{3,2,1,0:T(8,128)(2,1)S(1)}, u32[]{:S(2)}, u32[]{:S(2)}) collective-permute-start(bf16[2,2,72,512]{3,2,1,0:T(8,128)(2,1)S(1)} %slice.34), channel_id=1, source_target_pairs={{0,96},{32,0},{64,32},{96,64},{1,97},{33,1},{65,33},{97,65},{2,98}... | collective-permute-start | bytes 884744 | tf_op jit(solution)/shard_map/ppermute | solution.py:33
  46.5 5.6 %collective-permute-done.2 = bf16[2,2,72,512]{3,2,1,0:T(8,128)(2,1)S(1)} collective-permute-done((bf16[2,2,72,512]{3,2,1,0:T(8,128)(2,1)S(1)}, bf16[2,2,72,512]{3,2,1,0:T(8,128)(2,1)S(1)}, u32[]{:S(2)}, u32[]{:S(2)}) %collective-permute-start.2) | collective-permute-done | bytes 294944 | tf_op jit(solution)/shard_map/ppermute | solution.py:33
  52.2 1.4 pad_maximum_fusion
  53.5 2.7 %gather_fusion = bf16[48,72,512]{2,1,0:T(8,128)(2,1)} fusion(bf16[32,72,512]{2,1,0:T(8,128)(2,1)S(1)} %bitcast.60, s32[1024]{0:T(1024)S(1)} %pad_clamp_fusion), kind=kCustom, calls=%fused_computation | custom fusion | bytes 7078080 | tf_op jit(solution)/shard_map/gather | solution.py:244
  56.2 5.0 %all-to-all-start.1 = ((bf16[16,3,72,512]{3,2,1,0:T(8,128)(2,1)}), bf16[16,3,72,512]{3,2,1,0:T(8,128)(2,1)}, u32[]{:S(2)}, u32[]{:S(2)}) async-start(bf16[16,3,72,512]{3,2,1,0:T(8,128)(2,1)} %bitcast.61), calls=%async_computation.1 | async-start | bytes 7077888 | tf_op jit(solution)/shard_map/all_to_all | solution.py:41
  61.4 3.4 %collective-permute-start.10 = (bf16[3,16,1024]{2,1,0:T(8,128)(2,1)S(1)}, bf16[3,16,1024]{2,1,0:T(8,128)(2,1)S(1)}, u32[]{:S(2)}, u32[]{:S(2)}) collective-permute-start(bf16[3,16,1024]{2,1,0:T(8,128)(2,1)S(1)} %slice.39), channel_id=1, source_target_pairs={{0,18},{18,0},{2,16},{16,2},{1,19},{19,1},{3,17},{17,3},{4,22},{22... | collective-permute-start | bytes 294920 | tf_op jit(solution)/shard_map/ppermute | solution.py:248
  64.9 3.1 %collective-permute-done.10 = bf16[3,16,1024]{2,1,0:T(8,128)(2,1)S(1)} collective-permute-done((bf16[3,16,1024]{2,1,0:T(8,128)(2,1)S(1)}, bf16[3,16,1024]{2,1,0:T(8,128)(2,1)S(1)}, u32[]{:S(2)}, u32[]{:S(2)}) %collective-permute-start.10) | collective-permute-done | bytes 98336 | tf_op jit(solution)/shard_map/ppermute | solution.py:248
  68.0 2.4 %maximum_maximum_fusion.refs_2_ = bf16[6,128,1024]{2,1,0:T(8,128)(2,1)} fusion(bf16[3,16,1024]{2,1,0:T(8,128)(2,1)S(1)} %collective-permute-done.10, bf16[3,112,1024]{2,1,0:T(8,128)(2,1)} %collective-permute-done.8, bf16[3,128,1024]{2,1,0:T(8,128)(2,1)S(1)} %pad_maximum_fusion.1), kind=kLoop, calls=%fused_computation.3 | loop fusion | flops 4718592 | bytes 3145728 | tf_op jit(solution)/shard_map/concatenate | solution.py:249
  70.4 3.1 %collective-permute-start.12 = (bf16[6,128,1024]{2,1,0:T(8,128)(2,1)}, bf16[6,128,1024]{2,1,0:T(8,128)(2,1)}, u32[]{:S(2)}, u32[]{:S(2)}) collective-permute-start(bf16[6,128,1024]{2,1,0:T(8,128)(2,1)} %maximum_maximum_fusion.refs_2_), channel_id=1, source_target_pairs={{0,96},{32,0},{64,32},{96,64},{1,97},{33,1},{65,33},{97,65},{2,98}... | collective-permute-start | bytes 4718600 | tf_op jit(solution)/shard_map/ppermute | solution.py:33
  73.4 31.2 %all-to-all-done.1.packed_ref.down_ref = bf16[16,3,72,512]{3,2,1,0:T(8,128)(2,1)} async-done(((bf16[16,3,72,512]{3,2,1,0:T(8,128)(2,1)}), bf16[16,3,72,512]{3,2,1,0:T(8,128)(2,1)}, u32[]{:S(2)}, u32[]{:S(2)}) %all-to-all-start.1) | async-done | bytes 3538976 | tf_op jit(solution)/shard_map/all_to_all | solution.py:41
  104.7 8.7 %low.1 = (bf16[384,64]{1,0:T(8,128)(2,1)}, bf16[384,64]{1,0:T(8,128)(2,1)}, bf16[3,1024,64]{2,1,0:T(8,128)(2,1)}, bf16[16,3,72,512]{3,2,1,0:T(8,128)(2,1)}) custom-call(s32[3]{0:T(128)S(1)} %copy-done, bf16[384,8192]{1,0:T(8,128)(2,1)} %x_ref.3, bf16[384,1024]{1,0:T(8,128)(2,1)} %dy_ref.3, bf16[16,3,72,512]{3,2,1,0:T(8,128)(2,1)} %all-to-all-done.1.packed_ref.down_ref, ...), custom_call_target="tpu_custom_call" | custom-call | flops 905969664 | bytes 16777216 | tf_op jit(solution)/shard_map/low/pallas_call | solution.py:256
  113.4 3.8 %all-to-all-start.2 = ((bf16[16,3,72,512]{3,2,1,0:T(8,128)(2,1)}), bf16[16,3,72,512]{3,2,1,0:T(8,128)(2,1)S(1)}, u32[]{:S(2)}, u32[]{:S(2)}) async-start(bf16[16,3,72,512]{3,2,1,0:T(8,128)(2,1)} %get-tuple-element.42), calls=%async_computation.2 | async-start | bytes 7077888 | tf_op jit(solution)/shard_map/all_to_all | solution.py:41
  117.2 3.3 %collective-permute-start.9 = (bf16[512,1024]{1,0:T(8,128)(2,1)}, bf16[512,1024]{1,0:T(8,128)(2,1)}, u32[]{:S(2)}, u32[]{:S(2)}) collective-permute-start(bf16[512,1024]{1,0:T(8,128)(2,1)} %refs_0_.1), channel_id=1, source_target_pairs={{0,18},{18,0},{2,16},{16,2},{1,19},{19,1},{3,17},{17,3},{4,22},{22... | collective-permute-start | bytes 3145736 | tf_op jit(solution)/shard_map/ppermute | solution.py:247
  121.6 3.1 %collective-permute-start.14 = (bf16[3,128,1024]{2,1,0:T(8,128)(2,1)S(1)}, bf16[3,128,1024]{2,1,0:T(8,128)(2,1)S(1)}, u32[]{:S(2)}, u32[]{:S(2)}) collective-permute-start(bf16[3,128,1024]{2,1,0:T(8,128)(2,1)S(1)} %slice.41), channel_id=1, source_target_pairs={{0,96},{32,0},{64,32},{96,64},{1,97},{33,1},{65,33},{97,65},{2,98}... | collective-permute-start | bytes 2359304 | tf_op jit(solution)/shard_map/ppermute | solution.py:33
  126.1 18.1 %collective-permute-done.9.refs_1_ = bf16[512,1024]{1,0:T(8,128)(2,1)} collective-permute-done((bf16[512,1024]{1,0:T(8,128)(2,1)}, bf16[512,1024]{1,0:T(8,128)(2,1)}, u32[]{:S(2)}, u32[]{:S(2)}) %collective-permute-start.9) | collective-permute-done | bytes 1048608 | tf_op jit(solution)/shard_map/ppermute | solution.py:247
  144.8 1.4 collective-permute-done.13.refs_5_
  147.1 13.3 %all-to-all-done.2.g_ref = bf16[16,3,72,512]{3,2,1,0:T(8,128)(2,1)S(1)} async-done(((bf16[16,3,72,512]{3,2,1,0:T(8,128)(2,1)}), bf16[16,3,72,512]{3,2,1,0:T(8,128)(2,1)S(1)}, u32[]{:S(2)}, u32[]{:S(2)}) %all-to-all-start.2) | async-done | bytes 3538976 | tf_op jit(solution)/shard_map/all_to_all | solution.py:41
  160.5 3.3 %sum_blocks.1 = bf16[32,72,512]{2,1,0:T(8,128)(2,1)} custom-call(s32[16,3]{1,0:T(8,128)S(1)} %bitcast.59, bf16[16,3,72,512]{3,2,1,0:T(8,128)(2,1)S(1)} %all-to-all-done.2.g_ref), custom_call_target="tpu_custom_call" | custom-call | flops 1769472 | bytes 7077888 | tf_op jit(solution)/shard_map/sum_blocks/pallas_call | solution.py:193
  163.8 6.8 %all-to-all-start.3 = ((bf16[32,72,512]{2,1,0:T(8,128)(2,1)}), bf16[32,72,512]{2,1,0:T(8,128)(2,1)S(1)}, u32[]{:S(2)}, u32[]{:S(2)}) async-start(bf16[32,72,512]{2,1,0:T(8,128)(2,1)} %sum_blocks.1), calls=%async_computation.3 | async-start | bytes 4718592 | tf_op jit(solution)/shard_map/all_to_all | solution.py:41
  171.3 1.9 collective-permute-done.21.refs_13_
  174.5 25.9 %base.1 = (bf16[384,1024]{1,0:T(8,128)(2,1)}, bf16[384,8192]{1,0:T(8,128)(2,1)}) custom-call(s32[20]{0:T(128)S(1)} %stack.131.f_ref, bf16[384,8192]{1,0:T(8,128)(2,1)} %x_ref.3, bf16[384,1024]{1,0:T(8,128)(2,1)} %dy_ref.3, bf16[384,64]{1,0:T(8,128)(2,1)} %get-tuple-element.27.u_ref, bf16[384,64]{1,0:T(8,128)(2,1)} %get-tuple-element.28.v_ref, ...), custom_call_target="tpu_custom_call" | custom-call | flops 12884901888 | bytes 37748736 | tf_op jit(solution)/shard_map/base/pallas_call | solution.py:295
  200.4 1.3 all-to-all-done.3
  (79 shorter events, 15.5 us)
Async XLA Ops:
  2.3 16.6 %collective-permute-start.7 = (bf16[128,1024]{1,0:T(8,128)(2,1)}, bf16[128,1024]{1,0:T(8,128)(2,1)S(1)}, u32[]{:S(2)}, u32[]{:S(2)}) collective-permute-start(bf16[128,1024]{1,0:T(8,128)(2,1)} %constant_dynamic-slice_fusion), channel_id=1, source_target_pairs={{0,8},{4,12},{8,0},{12,4},{1,9},{5,13},{9,1},{13,5},{2,10},{6,14},... | collective-permute-start | bytes 786440 | tf_op jit(solution)/shard_map/ppermute | solution.py:33
  6.3 13.4 %collective-permute-start.6 = (bf16[128,1024]{1,0:T(8,128)(2,1)}, bf16[128,1024]{1,0:T(8,128)(2,1)S(1)}, u32[]{:S(2)}, u32[]{:S(2)}) collective-permute-start(bf16[128,1024]{1,0:T(8,128)(2,1)} %constant_dynamic-slice_fusion), channel_id=1, source_target_pairs={{0,12},{4,0},{8,4},{12,8},{1,13},{5,1},{9,5},{13,9},{2,14},{6,2},{... | collective-permute-start | bytes 786440 | tf_op jit(solution)/shard_map/ppermute | solution.py:33
  7.0 23.2 %collective-permute-start.5 = (bf16[128,1024]{1,0:T(8,128)(2,1)}, bf16[128,1024]{1,0:T(8,128)(2,1)S(1)}, u32[]{:S(2)}, u32[]{:S(2)}) collective-permute-start(bf16[128,1024]{1,0:T(8,128)(2,1)} %constant_dynamic-slice_fusion), channel_id=1, source_target_pairs={{0,4},{4,8},{8,12},{12,0},{1,5},{5,9},{9,13},{13,1},{2,6},{6,10},{... | collective-permute-start | bytes 786440 | tf_op jit(solution)/shard_map/ppermute | solution.py:33
  9.6 24.6 %all-to-all-start = ((s32[16,8,128]{2,1,0:T(8,128)}), s32[16,8,128]{2,1,0:T(8,128)}, u32[]{:S(2)}, u32[]{:S(2)}) async-start(s32[16,8,128]{2,1,0:T(8,128)} %broadcast_in_dim.4), calls=%async_computation | async-start | bytes 131072 | tf_op jit(solution)/shard_map/all_to_all | solution.py:41
  16.0 10.9 %collective-permute-start = (bf16[4,72,512]{2,1,0:T(8,128)(2,1)S(1)}, bf16[4,72,512]{2,1,0:T(8,128)(2,1)S(1)}, u32[]{:S(2)}, u32[]{:S(2)}) collective-permute-start(bf16[4,72,512]{2,1,0:T(8,128)(2,1)S(1)} %get-tuple-element.59), channel_id=1, source_target_pairs={{0,16},{16,0},{1,17},{17,1},{2,18},{18,2},{3,19},{19,3},{4,20},{20... | collective-permute-start | bytes 884744 | tf_op jit(solution)/shard_map/ppermute | solution.py:33
  18.9 8.0 %copy-start.2 = (bf16[128,1024]{1,0:T(8,128)(2,1)}, bf16[128,1024]{1,0:T(8,128)(2,1)S(1)}, u32[]{:S(2)}) copy-start(bf16[128,1024]{1,0:T(8,128)(2,1)S(1)} %collective-permute-done.7) | copy-start | bytes 786436
  19.7 7.2 %copy-start.4 = (bf16[128,1024]{1,0:T(8,128)(2,1)}, bf16[128,1024]{1,0:T(8,128)(2,1)S(1)}, u32[]{:S(2)}) copy-start(bf16[128,1024]{1,0:T(8,128)(2,1)S(1)} %collective-permute-done.6) | copy-start | bytes 786436
  26.9 16.1 %collective-permute-start.1 = (bf16[2,4,72,512]{3,2,1,0:T(8,128)(2,1)S(1)}, bf16[2,4,72,512]{3,2,1,0:T(8,128)(2,1)S(1)}, u32[]{:S(2)}, u32[]{:S(2)}) collective-permute-start(bf16[2,4,72,512]{3,2,1,0:T(8,128)(2,1)S(1)} %get-tuple-element.57), channel_id=1, source_target_pairs={{0,32},{32,64},{64,96},{96,0},{1,33},{33,65},{65,97},{97,1},{2,34}... | collective-permute-start | bytes 1769480 | tf_op jit(solution)/shard_map/ppermute | solution.py:33
  28.6 14.9 %collective-permute-start.3 = (bf16[2,4,72,512]{3,2,1,0:T(8,128)(2,1)S(1)}, bf16[2,4,72,512]{3,2,1,0:T(8,128)(2,1)S(1)}, u32[]{:S(2)}, u32[]{:S(2)}) collective-permute-start(bf16[2,4,72,512]{3,2,1,0:T(8,128)(2,1)S(1)} %get-tuple-element.57), channel_id=1, source_target_pairs={{0,96},{32,0},{64,32},{96,64},{1,97},{33,1},{65,33},{97,65},{2,98}... | collective-permute-start | bytes 1769480 | tf_op jit(solution)/shard_map/ppermute | solution.py:33
  30.2 21.9 %copy-start.6 = (bf16[128,1024]{1,0:T(8,128)(2,1)}, bf16[128,1024]{1,0:T(8,128)(2,1)S(1)}, u32[]{:S(2)}) copy-start(bf16[128,1024]{1,0:T(8,128)(2,1)S(1)} %collective-permute-done.5) | copy-start | bytes 786436
  31.2 25.0 %collective-permute-start.8 = (bf16[3,112,1024]{2,1,0:T(8,128)(2,1)}, bf16[3,112,1024]{2,1,0:T(8,128)(2,1)}, u32[]{:S(2)}, u32[]{:S(2)}) collective-permute-start(bf16[3,112,1024]{2,1,0:T(8,128)(2,1)} %pad_maximum_fusion.2), channel_id=1, source_target_pairs={{0,18},{18,0},{2,16},{16,2},{1,19},{19,1},{3,17},{17,3},{4,22},{22... | collective-permute-start | bytes 2064392 | tf_op jit(solution)/shard_map/ppermute | solution.py:233
  43.1 9.0 %collective-permute-start.2 = (bf16[2,2,72,512]{3,2,1,0:T(8,128)(2,1)S(1)}, bf16[2,2,72,512]{3,2,1,0:T(8,128)(2,1)S(1)}, u32[]{:S(2)}, u32[]{:S(2)}) collective-permute-start(bf16[2,2,72,512]{3,2,1,0:T(8,128)(2,1)S(1)} %slice.33), channel_id=1, source_target_pairs={{0,32},{32,64},{64,96},{96,0},{1,33},{33,65},{65,97},{97,1},{2,34}... | collective-permute-start | bytes 884744 | tf_op jit(solution)/shard_map/ppermute | solution.py:33
  43.4 8.7 %copy-start.1 = (bf16[2,4,72,512]{3,2,1,0:T(8,128)(2,1)}, bf16[2,4,72,512]{3,2,1,0:T(8,128)(2,1)S(1)}, u32[]{:S(2)}) copy-start(bf16[2,4,72,512]{3,2,1,0:T(8,128)(2,1)S(1)} %collective-permute-done.3) | copy-start | bytes 1769476
  43.5 8.6 %collective-permute-start.4 = (bf16[2,2,72,512]{3,2,1,0:T(8,128)(2,1)S(1)}, bf16[2,2,72,512]{3,2,1,0:T(8,128)(2,1)S(1)}, u32[]{:S(2)}, u32[]{:S(2)}) collective-permute-start(bf16[2,2,72,512]{3,2,1,0:T(8,128)(2,1)S(1)} %slice.34), channel_id=1, source_target_pairs={{0,96},{32,0},{64,32},{96,64},{1,97},{33,1},{65,33},{97,65},{2,98}... | collective-permute-start | bytes 884744 | tf_op jit(solution)/shard_map/ppermute | solution.py:33
  56.2 48.4 %all-to-all-start.1 = ((bf16[16,3,72,512]{3,2,1,0:T(8,128)(2,1)}), bf16[16,3,72,512]{3,2,1,0:T(8,128)(2,1)}, u32[]{:S(2)}, u32[]{:S(2)}) async-start(bf16[16,3,72,512]{3,2,1,0:T(8,128)(2,1)} %bitcast.61), calls=%async_computation.1 | async-start | bytes 7077888 | tf_op jit(solution)/shard_map/all_to_all | solution.py:41
  61.3 43.4 %copy-start = (s32[3]{0:T(128)S(1)}, s32[3]{0:T(128)}, u32[]{:S(2)}) copy-start(s32[3]{0:T(128)} %fill_ref.1) | copy-start | bytes 40
  61.4 6.5 %collective-permute-start.10 = (bf16[3,16,1024]{2,1,0:T(8,128)(2,1)S(1)}, bf16[3,16,1024]{2,1,0:T(8,128)(2,1)S(1)}, u32[]{:S(2)}, u32[]{:S(2)}) collective-permute-start(bf16[3,16,1024]{2,1,0:T(8,128)(2,1)S(1)} %slice.39), channel_id=1, source_target_pairs={{0,18},{18,0},{2,16},{16,2},{1,19},{19,1},{3,17},{17,3},{4,22},{22... | collective-permute-start | bytes 294920 | tf_op jit(solution)/shard_map/ppermute | solution.py:248
  70.4 43.0 %collective-permute-start.12 = (bf16[6,128,1024]{2,1,0:T(8,128)(2,1)}, bf16[6,128,1024]{2,1,0:T(8,128)(2,1)}, u32[]{:S(2)}, u32[]{:S(2)}) collective-permute-start(bf16[6,128,1024]{2,1,0:T(8,128)(2,1)} %maximum_maximum_fusion.refs_2_), channel_id=1, source_target_pairs={{0,96},{32,0},{64,32},{96,64},{1,97},{33,1},{65,33},{97,65},{2,98}... | collective-permute-start | bytes 4718600 | tf_op jit(solution)/shard_map/ppermute | solution.py:33
  73.4 40.0 %collective-permute-start.11 = (bf16[6,128,1024]{2,1,0:T(8,128)(2,1)}, bf16[6,128,1024]{2,1,0:T(8,128)(2,1)}, u32[]{:S(2)}, u32[]{:S(2)}) collective-permute-start(bf16[6,128,1024]{2,1,0:T(8,128)(2,1)} %maximum_maximum_fusion.refs_2_), channel_id=1, source_target_pairs={{0,32},{32,64},{64,96},{96,0},{1,33},{33,65},{65,97},{97,1},{2,34}... | collective-permute-start | bytes 4718600 | tf_op jit(solution)/shard_map/ppermute | solution.py:33
  113.4 47.1 %all-to-all-start.2 = ((bf16[16,3,72,512]{3,2,1,0:T(8,128)(2,1)}), bf16[16,3,72,512]{3,2,1,0:T(8,128)(2,1)S(1)}, u32[]{:S(2)}, u32[]{:S(2)}) async-start(bf16[16,3,72,512]{3,2,1,0:T(8,128)(2,1)} %get-tuple-element.42), calls=%async_computation.2 | async-start | bytes 7077888 | tf_op jit(solution)/shard_map/all_to_all | solution.py:41
  117.2 27.1 %collective-permute-start.9 = (bf16[512,1024]{1,0:T(8,128)(2,1)}, bf16[512,1024]{1,0:T(8,128)(2,1)}, u32[]{:S(2)}, u32[]{:S(2)}) collective-permute-start(bf16[512,1024]{1,0:T(8,128)(2,1)} %refs_0_.1), channel_id=1, source_target_pairs={{0,18},{18,0},{2,16},{16,2},{1,19},{19,1},{3,17},{17,3},{4,22},{22... | collective-permute-start | bytes 3145736 | tf_op jit(solution)/shard_map/ppermute | solution.py:247
  121.6 23.1 %collective-permute-start.14 = (bf16[3,128,1024]{2,1,0:T(8,128)(2,1)S(1)}, bf16[3,128,1024]{2,1,0:T(8,128)(2,1)S(1)}, u32[]{:S(2)}, u32[]{:S(2)}) collective-permute-start(bf16[3,128,1024]{2,1,0:T(8,128)(2,1)S(1)} %slice.41), channel_id=1, source_target_pairs={{0,96},{32,0},{64,32},{96,64},{1,97},{33,1},{65,33},{97,65},{2,98}... | collective-permute-start | bytes 2359304 | tf_op jit(solution)/shard_map/ppermute | solution.py:33
  125.9 20.3 %collective-permute-start.13 = (bf16[3,128,1024]{2,1,0:T(8,128)(2,1)S(1)}, bf16[3,128,1024]{2,1,0:T(8,128)(2,1)S(1)}, u32[]{:S(2)}, u32[]{:S(2)}) collective-permute-start(bf16[3,128,1024]{2,1,0:T(8,128)(2,1)S(1)} %slice.40), channel_id=1, source_target_pairs={{0,32},{32,64},{64,96},{96,0},{1,33},{33,65},{65,97},{97,1},{2,34}... | collective-permute-start | bytes 2359304 | tf_op jit(solution)/shard_map/ppermute | solution.py:33
  126.0 44.6 %collective-permute-start.15 = (bf16[512,1024]{1,0:T(8,128)(2,1)}, bf16[512,1024]{1,0:T(8,128)(2,1)}, u32[]{:S(2)}, u32[]{:S(2)}) collective-permute-start(bf16[512,1024]{1,0:T(8,128)(2,1)} %refs_0_.1), channel_id=1, source_target_pairs={{0,1},{1,0},{2,3},{3,2},{4,5},{5,4},{6,7},{7,6},{8,9},{9,8},{10,11... | collective-permute-start | bytes 3145736 | tf_op jit(solution)/shard_map/ppermute | solution.py:33
  144.2 26.5 %collective-permute-start.16 = (bf16[512,1024]{1,0:T(8,128)(2,1)}, bf16[512,1024]{1,0:T(8,128)(2,1)}, u32[]{:S(2)}, u32[]{:S(2)}) collective-permute-start(bf16[512,1024]{1,0:T(8,128)(2,1)} %collective-permute-done.9.refs_1_), channel_id=1, source_target_pairs={{0,1},{1,0},{2,3},{3,2},{4,5},{5,4},{6,7},{7,6},{8,9},{9,8},{10,11... | collective-permute-start | bytes 3145736 | tf_op jit(solution)/shard_map/ppermute | solution.py:33
  144.2 30.2 %collective-permute-start.18 = (bf16[6,128,1024]{2,1,0:T(8,128)(2,1)}, bf16[6,128,1024]{2,1,0:T(8,128)(2,1)}, u32[]{:S(2)}, u32[]{:S(2)}) collective-permute-start(bf16[6,128,1024]{2,1,0:T(8,128)(2,1)} %collective-permute-done.11.refs_3_), channel_id=1, source_target_pairs={{0,1},{1,0},{2,3},{3,2},{4,5},{5,4},{6,7},{7,6},{8,9},{9,8},{10,11... | collective-permute-start | bytes 4718600 | tf_op jit(solution)/shard_map/ppermute | solution.py:33
  144.7 29.7 %collective-permute-start.19 = (bf16[6,128,1024]{2,1,0:T(8,128)(2,1)}, bf16[6,128,1024]{2,1,0:T(8,128)(2,1)}, u32[]{:S(2)}, u32[]{:S(2)}) collective-permute-start(bf16[6,128,1024]{2,1,0:T(8,128)(2,1)} %collective-permute-done.12.refs_4_), channel_id=1, source_target_pairs={{0,1},{1,0},{2,3},{3,2},{4,5},{5,4},{6,7},{7,6},{8,9},{9,8},{10,11... | collective-permute-start | bytes 4718600 | tf_op jit(solution)/shard_map/ppermute | solution.py:33
  147.1 27.3 %collective-permute-start.17 = (bf16[6,128,1024]{2,1,0:T(8,128)(2,1)}, bf16[6,128,1024]{2,1,0:T(8,128)(2,1)}, u32[]{:S(2)}, u32[]{:S(2)}) collective-permute-start(bf16[6,128,1024]{2,1,0:T(8,128)(2,1)} %maximum_maximum_fusion.refs_2_), channel_id=1, source_target_pairs={{0,1},{1,0},{2,3},{3,2},{4,5},{5,4},{6,7},{7,6},{8,9},{9,8},{10,11... | collective-permute-start | bytes 4718600 | tf_op jit(solution)/shard_map/ppermute | solution.py:33
  163.8 6.8 %copy-start.9 = (bf16[3,128,1024]{2,1,0:T(8,128)(2,1)S(1)}, bf16[3,128,1024]{2,1,0:T(8,128)(2,1)}, u32[]{:S(2)}) copy-start(bf16[3,128,1024]{2,1,0:T(8,128)(2,1)} %copy-done.8) | copy-start | bytes 2359300
  163.8 37.9 %all-to-all-start.3 = ((bf16[32,72,512]{2,1,0:T(8,128)(2,1)}), bf16[32,72,512]{2,1,0:T(8,128)(2,1)S(1)}, u32[]{:S(2)}, u32[]{:S(2)}) async-start(bf16[32,72,512]{2,1,0:T(8,128)(2,1)} %sum_blocks.1), calls=%async_computation.3 | async-start | bytes 4718592 | tf_op jit(solution)/shard_map/all_to_all | solution.py:41
  170.6 2.6 %collective-permute-start.21 = (bf16[3,128,1024]{2,1,0:T(8,128)(2,1)S(1)}, bf16[3,128,1024]{2,1,0:T(8,128)(2,1)}, u32[]{:S(2)}, u32[]{:S(2)}) collective-permute-start(bf16[3,128,1024]{2,1,0:T(8,128)(2,1)S(1)} %copy-done.9), channel_id=1, source_target_pairs={{0,1},{1,0},{2,3},{3,2},{4,5},{5,4},{6,7},{7,6},{8,9},{9,8},{10,11... | collective-permute-start | bytes 2359304 | tf_op jit(solution)/shard_map/ppermute | solution.py:33
  170.7 3.7 %collective-permute-start.20 = (bf16[3,128,1024]{2,1,0:T(8,128)(2,1)}, bf16[3,128,1024]{2,1,0:T(8,128)(2,1)}, u32[]{:S(2)}, u32[]{:S(2)}) collective-permute-start(bf16[3,128,1024]{2,1,0:T(8,128)(2,1)} %copy-done.10), channel_id=1, source_target_pairs={{0,1},{1,0},{2,3},{3,2},{4,5},{5,4},{6,7},{7,6},{8,9},{9,8},{10,11... | collective-permute-start | bytes 2359304 | tf_op jit(solution)/shard_map/ppermute | solution.py:33
  (5 other events, 17.6 us)
